TPU v7x, 512 devices: a whole 4x8x8 slice. The times are simulated.
512 devices in a mesh: wide: 128 (over y, z, core), rep: 4 (over x).
Axes of the slice: x: 4, y: 8, z: 8, core: 2. Of those that a mesh axis runs over, the one named last changes fastest.
Arguments:
- node_feats: bfloat16 [131072, 512], P('wide'), may hold values from -6 to 6
- w_self: bfloat16 [512, 512], replicated, may hold values from -0.25 to 0.25
- w_neigh: bfloat16 [512, 512], replicated, may hold values from -0.25 to 0.25
- send_rows: int32 [128, 128, 32], P('wide', None, 'rep'), may hold values from 0 to 1023
- tile_dst: int32 [128, 4, 128], P('wide', 'rep'), may hold values from 0 to 15
- tile_src: int32 [128, 4, 128], P('wide', 'rep'), may hold values from 0 to 31
- tile_bits: int32 [128, 4, 32768], P('wide', 'rep'), may hold values from 0 to 65280
- norm_count: int32 [131072], P('wide'), may hold values from 512 to 2048
- grad_out: bfloat16 [131072, 512], P(('wide', 'rep')), may hold values from -6 to 6
Outputs:
- out_feats: bfloat16 [131072, 512], P(('wide', 'rep'))
- grad_feats: bfloat16 [131072, 512], P(('wide', 'rep'))
- grad_self: bfloat16 [512, 512], replicated
- grad_neigh: bfloat16 [512, 512], replicated
All inputs are finite; a program needn't handle non-finite values.
Results may differ from a plain program's by a relative error of at most 0.014.
Values may be sent and summed in bfloat16 or wider, within the bound.
No kernel may reach another device: no remote copies, remote signals or barrier semaphores. Data moves between devices by JAX's collectives and lax.ppermute only.
A program may use at most 64 MiB of HBM per device.

v0:
```python
import math

import jax
import jax.numpy as jnp
from jax import lax
from jax.sharding import PartitionSpec as P

BLOCK = 64


def unpack_bits(packed, tile_count, block_size):
    shaped = packed.reshape(tile_count, block_size, block_size // 16)
    shift_list = jnp.arange(16, dtype=jnp.int32)
    bit_grid = jnp.bitwise_and(jnp.right_shift(shaped[..., None], shift_list), 1)
    return bit_grid.reshape(tile_count, block_size, block_size)


def times_transposed(left, right):
    return lax.dot_general(
        left, right, (((1,), (1,)), ((), ())), preferred_element_type=jnp.float32
    )


def on_device(
    node_feats, w_self, w_neigh, send_rows, tile_dst, tile_src, tile_bits, norm_count, grad_out
):
    node_rows, feat_width = node_feats.shape
    peer_count = lax.axis_size("wide")
    replicas = lax.axis_size("rep")
    slot_count = send_rows.shape[2]
    tile_total = tile_dst.shape[2]
    block_size = BLOCK
    quarter = node_rows // replicas
    rep_index = lax.axis_index("rep")
    dst_count = node_rows // block_size
    group_size = math.gcd(tile_total, 32)
    send_index = send_rows[0]
    outgoing = jnp.take(node_feats, send_index.reshape(-1), axis=0).reshape(
        peer_count, slot_count, feat_width
    )
    incoming = lax.all_to_all(outgoing, "wide", split_axis=0, concat_axis=0, tiled=True)
    src_table = jnp.concatenate(
        [node_feats, incoming.reshape(peer_count * slot_count, feat_width)], axis=0
    )
    source_blocks = src_table.reshape(-1, block_size, feat_width)
    src_count = source_blocks.shape[0]
    tile_masks = unpack_bits(tile_bits[0, 0], tile_total, block_size).astype(jnp.bfloat16)
    grouped_masks = tile_masks.reshape(-1, group_size, block_size, block_size)
    grouped_dst = tile_dst[0, 0].reshape(-1, group_size)
    grouped_src = tile_src[0, 0].reshape(-1, group_size)

    def forward_group(running, group_items):
        mask_part, dst_part, src_part = group_items
        picked = jnp.take(source_blocks, src_part, axis=0)
        products = jnp.einsum("tij,tjf->tif", mask_part, picked, preferred_element_type=jnp.float32)
        return (running.at[dst_part].add(products), None)

    partial_sum, _ = lax.scan(
        forward_group,
        jnp.zeros((dst_count, block_size, feat_width), jnp.float32),
        (grouped_masks, grouped_dst, grouped_src),
    )
    partial_sum = partial_sum.reshape(node_rows, feat_width)
    summed = lax.psum(partial_sum, "rep")
    own_sums = lax.dynamic_slice_in_dim(summed, rep_index * quarter, quarter, 0)
    scale_all = lax.rsqrt(norm_count.astype(jnp.float32))
    own_scale = lax.dynamic_slice_in_dim(scale_all, rep_index * quarter, quarter, 0)
    own_feats = lax.dynamic_slice_in_dim(node_feats, rep_index * quarter, quarter, 0)
    own_agg = (own_sums * own_scale[:, None]).astype(jnp.bfloat16)
    pre_act = jnp.dot(own_feats, w_self, preferred_element_type=jnp.float32) + jnp.dot(
        own_agg, w_neigh, preferred_element_type=jnp.float32
    )
    sigmoid = jax.nn.sigmoid(pre_act)
    out_feats = (pre_act * sigmoid).astype(jnp.bfloat16)
    grad_pre = (grad_out.astype(jnp.float32) * sigmoid * (1.0 + pre_act * (1.0 - sigmoid))).astype(
        jnp.bfloat16
    )
    dims_rows = (((0,), (0,)), ((), ()))
    self_term = lax.dot_general(own_feats, grad_pre, dims_rows, preferred_element_type=jnp.float32)
    neigh_term = lax.dot_general(own_agg, grad_pre, dims_rows, preferred_element_type=jnp.float32)
    summed_self, summed_neigh = lax.psum((self_term, neigh_term), ("wide", "rep"))
    own_grad_agg = (times_transposed(grad_pre, w_neigh) * own_scale[:, None]).astype(jnp.bfloat16)
    grad_agg = lax.all_gather(own_grad_agg, "rep", axis=0, tiled=True)
    agg_blocks = grad_agg.reshape(dst_count, block_size, feat_width)

    def backward_group(running, group_items):
        mask_part, dst_part, src_part = group_items
        picked = jnp.take(agg_blocks, dst_part, axis=0)
        products = jnp.einsum("tij,tif->tjf", mask_part, picked, preferred_element_type=jnp.float32)
        return (running.at[src_part].add(products), None)

    table_grad, _ = lax.scan(
        backward_group,
        jnp.zeros((src_count, block_size, feat_width), jnp.float32),
        (grouped_masks, grouped_dst, grouped_src),
    )
    table_grad = table_grad.reshape(src_count * block_size, feat_width)
    local_grad = table_grad[:node_rows]
    halo_grad = (
        table_grad[node_rows:].astype(jnp.bfloat16).reshape(peer_count, slot_count, feat_width)
    )
    returned = lax.all_to_all(halo_grad, "wide", split_axis=0, concat_axis=0, tiled=True)
    returned_rows = (
        jnp.zeros((node_rows, feat_width), jnp.float32)
        .at[send_index.reshape(-1)]
        .add(returned.reshape(-1, feat_width).astype(jnp.float32))
    )
    own_total = lax.psum_scatter(
        (local_grad + returned_rows).astype(jnp.bfloat16), "rep", scatter_dimension=0, tiled=True
    ).astype(jnp.float32)
    grad_feats = (own_total + times_transposed(grad_pre, w_self)).astype(jnp.bfloat16)
    return (
        out_feats,
        grad_feats,
        summed_self.astype(jnp.bfloat16),
        summed_neigh.astype(jnp.bfloat16),
    )


def solution(mesh):
    in_specs = (
        P("wide", None),
        P(),
        P(),
        P("wide", None, "rep"),
        P("wide", "rep", None),
        P("wide", "rep", None),
        P("wide", "rep", None),
        P("wide"),
        P(("wide", "rep"), None),
    )
    out_specs = (P(("wide", "rep"), None), P(("wide", "rep"), None), P(), P())
    return jax.shard_map(
        on_device, mesh=mesh, in_specs=in_specs, out_specs=out_specs, check_vma=False
    )
```

profile of v0, /device:TPU:1, one launch (start us, length us, event | category | flops | bytes accessed | tf_op | source)
XLA Modules:
  0.0 460.0 jit_solution(16109861953868291241)
XLA Ops:
  9.0 5.4 %gather_fusion.2 = bf16[1024,512]{1,0:T(8,128)(2,1)S(1)} fusion(bf16[1024,512]{1,0:T(8,128)(2,1)} %param.13, s32[1024]{0:T(1024)S(1)} %broadcast_clamp_fusion), kind=kCustom, calls=%fused_computation.2 | custom fusion | bytes 2101248 | tf_op jit(solution)/shard_map/jit(_take)/gather | solution.py:38
  15.5 18.4 %all-to-all-start = ((bf16[128,8,512]{2,1,0:T(8,128)(2,1)}), bf16[128,8,512]{2,1,0:T(8,128)(2,1)S(1)}, u32[]{:S(2)}, u32[]{:S(2)}) async-start(bf16[128,8,512]{2,1,0:T(8,128)(2,1)} %bitcast_select_fusion), calls=%async_computation | async-start | bytes 2097152 | tf_op jit(solution)/shard_map/all_to_all | solution.py:41
  37.1 5.7 %shift_right_arithmetic.23 = s32[128,64,4]{2,1,0:T(8,128)} reshape(s32[32768]{0:T(1024)S(1)} %reduce.10) | data formatting | bytes 262144 | tf_op jit(solution)/shard_map/shift_right_arithmetic | solution.py:14
  48.2 16.2 %all-to-all-done = bf16[128,8,512]{2,1,0:T(8,128)(2,1)S(1)} async-done(((bf16[128,8,512]{2,1,0:T(8,128)(2,1)}), bf16[128,8,512]{2,1,0:T(8,128)(2,1)S(1)}, u32[]{:S(2)}, u32[]{:S(2)}) %all-to-all-start) | async-done | bytes 1048608 | tf_op jit(solution)/shard_map/all_to_all | solution.py:41
  66.1 58.5 %while.20 = (s32[]{:T(128)}, f32[16,64,512]{2,1,0:T(8,128)S(1)}, s32[4,32]{1,0:T(4,128)S(1)}, bf16[4,32,64,64]{2,3,1,0:T(8,128)(2,1)}, s32[4,32]{1,0:T(4,128)S(1)}, /*index=5*/bf16[32,64,512]{2,1,0:T(8,128)(2,1)}, s32[]{:T(128)}) while((s32[]{:T(128)}, f32[16,64,512]{2,1,0:T(8,128)S(1)}, s32[4,32]{1,0:T(4,128)S(1)}, ...), condition=%wide.region_2.3_spmd, body=%wide.region_0.0_spmd.sunk | while | flops 136316288 | bytes 23598240 | solution.py:58
  69.8 4.5 fusion.53
  74.3 6.5 %scatter_fusion = f32[16,64,512]{2,1,0:T(8,128)S(1)} fusion(f32[16,64,512]{2,1,0:T(8,128)S(1)} %get-tuple-element.204, s32[32]{0:T(128)S(1)} %get-tuple-element.186, f32[32,64,512]{2,1,0:T(8,128)} %fusion.53), kind=kCustom, calls=%fused_computation.3.clone.1 | custom fusion | flops 1048576 | bytes 12583040 | tf_op jit(solution)/shard_map/while/body/eval_jaxpr/scatter-add | solution.py:56
  84.4 4.5 fusion.53
  88.9 6.5 %scatter_fusion = f32[16,64,512]{2,1,0:T(8,128)S(1)} fusion(f32[16,64,512]{2,1,0:T(8,128)S(1)} %get-tuple-element.204, s32[32]{0:T(128)S(1)} %get-tuple-element.186, f32[32,64,512]{2,1,0:T(8,128)} %fusion.53), kind=kCustom, calls=%fused_computation.3.clone.1 | custom fusion | flops 1048576 | bytes 12583040 | tf_op jit(solution)/shard_map/while/body/eval_jaxpr/scatter-add | solution.py:56
  99.1 4.5 fusion.53
  103.5 6.5 %scatter_fusion = f32[16,64,512]{2,1,0:T(8,128)S(1)} fusion(f32[16,64,512]{2,1,0:T(8,128)S(1)} %get-tuple-element.204, s32[32]{0:T(128)S(1)} %get-tuple-element.186, f32[32,64,512]{2,1,0:T(8,128)} %fusion.53), kind=kCustom, calls=%fused_computation.3.clone.1 | custom fusion | flops 1048576 | bytes 12583040 | tf_op jit(solution)/shard_map/while/body/eval_jaxpr/scatter-add | solution.py:56
  113.7 4.5 fusion.53
  118.1 6.5 %scatter_fusion = f32[16,64,512]{2,1,0:T(8,128)S(1)} fusion(f32[16,64,512]{2,1,0:T(8,128)S(1)} %get-tuple-element.204, s32[32]{0:T(128)S(1)} %get-tuple-element.186, f32[32,64,512]{2,1,0:T(8,128)} %fusion.53), kind=kCustom, calls=%fused_computation.3.clone.1 | custom fusion | flops 1048576 | bytes 12583040 | tf_op jit(solution)/shard_map/while/body/eval_jaxpr/scatter-add | solution.py:56
  127.6 62.1 %all-reduce.4.cloned.1.call-done = f32[1024,512]{1,0:T(8,128)} async-done(((f32[1024,512]{1,0:T(8,128)}), f32[1024,512]{1,0:T(8,128)}) %all-reduce.4.cloned.1.call-update) | async-done | bytes 2097168 | tf_op jit(solution)/shard_map/psum | solution.py:64
  193.1 28.4 %all-gather.2.cloned.1.call-done = bf16[1024,512]{1,0:T(8,128)(2,1)} async-done(((bf16[256,512]{1,0:T(8,128)(2,1)}), bf16[1024,512]{1,0:T(8,128)(2,1)}) %all-gather.2.cloned.1.call-update) | async-done | bytes 1048592 | tf_op jit(solution)/shard_map/all_gather | solution.py:83
  224.0 62.5 %while.21 = (s32[]{:T(128)}, f32[32,64,512]{2,1,0:T(8,128)}, s32[4,32]{1,0:T(4,128)S(1)}, bf16[4,32,64,64]{2,3,1,0:T(8,128)(2,1)}, s32[4,32]{1,0:T(4,128)S(1)}, /*index=5*/bf16[16,64,512]{2,1,0:T(8,128)(2,1)}, s32[]{:T(128)}) while((s32[]{:T(128)}, f32[32,64,512]{2,1,0:T(8,128)}, s32[4,32]{1,0:T(4,128)S(1)}, ...), condition=%wide.region_6.7_spmd, body=%wide.region_4.6_spmd.sunk | while | flops 136316288 | bytes 23598240 | solution.py:92
  229.7 9.9 %scatter_fusion.1 = f32[32,64,512]{2,1,0:T(8,128)} fusion(f32[32,64,512]{2,1,0:T(8,128)} %get-tuple-element.225, s32[32]{0:T(128)S(1)} %get-tuple-element.194, f32[32,64,512]{2,1,0:T(8,128)} %fusion.57), kind=kCustom, calls=%fused_computation.4.clone.1 | custom fusion | flops 1048576 | bytes 12583040 | tf_op jit(solution)/shard_map/while/body/eval_jaxpr/scatter-add | solution.py:90
  245.3 9.9 %scatter_fusion.1 = f32[32,64,512]{2,1,0:T(8,128)} fusion(f32[32,64,512]{2,1,0:T(8,128)} %get-tuple-element.225, s32[32]{0:T(128)S(1)} %get-tuple-element.194, f32[32,64,512]{2,1,0:T(8,128)} %fusion.57), kind=kCustom, calls=%fused_computation.4.clone.1 | custom fusion | flops 1048576 | bytes 12583040 | tf_op jit(solution)/shard_map/while/body/eval_jaxpr/scatter-add | solution.py:90
  260.9 10.0 %scatter_fusion.1 = f32[32,64,512]{2,1,0:T(8,128)} fusion(f32[32,64,512]{2,1,0:T(8,128)} %get-tuple-element.225, s32[32]{0:T(128)S(1)} %get-tuple-element.194, f32[32,64,512]{2,1,0:T(8,128)} %fusion.57), kind=kCustom, calls=%fused_computation.4.clone.1 | custom fusion | flops 1048576 | bytes 12583040 | tf_op jit(solution)/shard_map/while/body/eval_jaxpr/scatter-add | solution.py:90
  276.6 9.8 %scatter_fusion.1 = f32[32,64,512]{2,1,0:T(8,128)} fusion(f32[32,64,512]{2,1,0:T(8,128)} %get-tuple-element.225, s32[32]{0:T(128)S(1)} %get-tuple-element.194, f32[32,64,512]{2,1,0:T(8,128)} %fusion.57), kind=kCustom, calls=%fused_computation.4.clone.1 | custom fusion | flops 1048576 | bytes 12583040 | tf_op jit(solution)/shard_map/while/body/eval_jaxpr/scatter-add | solution.py:90
  289.2 15.9 %all-to-all-start.1 = ((bf16[128,8,512]{2,1,0:T(8,128)(2,1)}), bf16[128,8,512]{2,1,0:T(8,128)(2,1)}, u32[]{:S(2)}, u32[]{:S(2)}) async-start(bf16[128,8,512]{2,1,0:T(8,128)(2,1)} %bitcast.21), calls=%async_computation.1 | async-start | bytes 2097152 | tf_op jit(solution)/shard_map/all_to_all | solution.py:102
  307.0 28.2 %all-to-all-done.1 = bf16[128,8,512]{2,1,0:T(8,128)(2,1)} async-done(((bf16[128,8,512]{2,1,0:T(8,128)(2,1)}), bf16[128,8,512]{2,1,0:T(8,128)(2,1)}, u32[]{:S(2)}, u32[]{:S(2)}) %all-to-all-start.1) | async-done | bytes 1048608 | tf_op jit(solution)/shard_map/all_to_all | solution.py:102
  335.2 8.0 %scatter_custom_fusion.2 = f32[1024,512]{1,0:T(8,128)S(1)} fusion(f32[1024,512]{1,0:T(8,128)S(1)} %bitcast.83, s32[1024]{0:T(1024)S(1)} %bitcast.86, bf16[128,8,512]{2,1,0:T(8,128)(2,1)} %all-to-all-done.1), kind=kCustom, calls=%fused_computation.45 | custom fusion | flops 1048576 | bytes 3145728 | tf_op jit(solution)/shard_map/scatter-add | solution.py:106
  347.1 104.5 %all-reduce.5 = (bf16[512,512]{1,0:T(8,128)(2,1)}, bf16[512,512]{1,0:T(8,128)(2,1)}) all-reduce(f32[512,512]{1,0:T(8,128)S(1)} %fusion.27, f32[512,512]{1,0:T(8,128)S(1)} %fusion.33), channel_id=1, replica_groups=mesh['wide'=128,'rep'=4] {'wide','rep'}, use_global_device_ids=true, to_apply=%region_9.10 | all-reduce | flops 524288 | bytes 3145728 | tf_op jit(solution)/shard_map/psum | solution.py:81
  (91 shorter events, 69.8 us)
Async XLA Ops:
  7.2 182.5 %copy-start = (bf16[512,512]{1,0:T(8,128)(2,1)S(1)}, bf16[512,512]{1,0:T(8,128)(2,1)}, u32[]{:S(2)}) copy-start(bf16[512,512]{1,0:T(8,128)(2,1)} %param.15) | copy-start | bytes 1572868
  14.3 20.2 %copy-start.6 = (s32[1,1,128]{2,1,0:T(1,128)S(1)}, s32[1,1,128]{2,1,0:T(1,128)}, u32[]{:S(2)}) copy-start(s32[1,1,128]{2,1,0:T(1,128)} %param.17) | copy-start | bytes 1540
  14.3 20.9 %copy-start.7 = (s32[1,1,128]{2,1,0:T(1,128)S(1)}, s32[1,1,128]{2,1,0:T(1,128)}, u32[]{:S(2)}) copy-start(s32[1,1,128]{2,1,0:T(1,128)} %param.18) | copy-start | bytes 1540
  14.4 21.8 %copy-start.4 = (s32[1,1,32768]{2,1,0:T(1,128)S(1)}, s32[1,1,32768]{2,1,0:T(1,128)}, u32[]{:S(2)}) copy-start(s32[1,1,32768]{2,1,0:T(1,128)} %param.19) | copy-start | bytes 393220
  15.5 48.9 %all-to-all-start = ((bf16[128,8,512]{2,1,0:T(8,128)(2,1)}), bf16[128,8,512]{2,1,0:T(8,128)(2,1)S(1)}, u32[]{:S(2)}, u32[]{:S(2)}) async-start(bf16[128,8,512]{2,1,0:T(8,128)(2,1)} %bitcast_select_fusion), calls=%async_computation | async-start | bytes 2097152 | tf_op jit(solution)/shard_map/all_to_all | solution.py:41
  34.0 155.7 %all-reduce.4.cloned.1.call-start = ((), (), s32[]{:S(2)}) async-start(), calls=%async_computation.3 | async-start | bytes 4194304 | tf_op jit(solution)/shard_map/psum | solution.py:64
  46.1 18.3 %copy-start.2 = (bf16[1024,512]{1,0:T(8,128)(2,1)S(1)}, bf16[1024,512]{1,0:T(8,128)(2,1)}, u32[]{:S(2)}) copy-start(bf16[1024,512]{1,0:T(8,128)(2,1)} %param.13) | copy-start | bytes 3145732
  124.7 1.3 copy-start.1
  124.7 1.6 copy-start.5
  124.7 1.7 copy-start.3
  126.0 95.5 %all-gather.2.cloned.1.call-start = ((), (), s32[]{:S(2)}) async-start(), calls=%async_computation.4 | async-start | bytes 1310720 | tf_op jit(solution)/shard_map/all_gather | solution.py:83
  289.2 46.0 %all-to-all-start.1 = ((bf16[128,8,512]{2,1,0:T(8,128)(2,1)}), bf16[128,8,512]{2,1,0:T(8,128)(2,1)}, u32[]{:S(2)}, u32[]{:S(2)}) async-start(bf16[128,8,512]{2,1,0:T(8,128)(2,1)} %bitcast.21), calls=%async_computation.1 | async-start | bytes 2097152 | tf_op jit(solution)/shard_map/all_to_all | solution.py:102
  305.1 146.4 %reduce-scatter.2.cloned.1.call-start = ((), (), s32[]{:S(2)}) async-start(), calls=%async_computation.5 | async-start | bytes 1310720 | tf_op jit(solution)/shard_map/reduce_scatter | solution.py:108
Sparse Core Ops, SparseCore 0:
  126.2 63.4 all-reduce.3
  193.2 28.2 all-gather.1
  344.4 19.7 reduce-scatter.1
where the time goes:
time: 462 us; the launch traced here: 460 us
  waiting for transfers between devices  135 us (29%)
  blocking collectives  104 us (23%)
  other arithmetic  82.7 us (18%)
  local copies, waits for them, and re-layouts  47 us (10%)
  matrix products  42.2 us (9%)
  starting transfers between devices  34.6 us (7%)
  between operations  14 us (3%)
    psum x1, blocking collectives, on_device(): lax.psum((self_term, neigh_term), ('wide', 'rep'))  104 us
    psum x1, waiting for transfers between devices, on_device(): summed = lax.psum(partial_sum, 'rep')  62.1 us
    scatter-add x4, other arithmetic, backward_group(): return (running.at[src_part].add(products), None)  39.7 us
    all_gather x1, waiting for transfers between devices, on_device(): grad_agg = lax.all_gather(own_grad_agg, 'rep', axis=0, tiled=True)  28.4 us
    all_to_all x1, waiting for transfers between devices, on_device(): lax.all_to_all(halo_grad, 'wide', split_axis=0, concat_axis=0, tiled=True)  28.2 us
    scatter-add x4, other arithmetic, forward_group(): return (running.at[dst_part].add(products), None)  25.9 us
    all_to_all x1, starting transfers between devices, on_device(): lax.all_to_all(outgoing, 'wide', split_axis=0, concat_axis=0, tiled=True)  18.4 us
    dot_general x4, matrix products, forward_group(): jnp.einsum('tij,tjf->tif', mask_part, picked, preferred_element_type=jnp....  17.9 us
  transfers between devices with their start and end apart: 5, of which 4 were waited for; matrix products, arithmetic and copies ran while one was open for 4% of the time, Pallas kernels for 0%

commit v1 on v0

v1 whole, which is shorter than its diff:
```python
import jax
import jax.numpy as jnp
from jax import lax
from jax.experimental import pallas as pl
from jax.experimental.pallas import tpu as pltpu
from jax.sharding import PartitionSpec as P

BLOCK = 64
LANES = 128
F32 = jnp.float32
BF16 = jnp.bfloat16


def dot(left, right, left_dim, right_dim):
    dims = (((left_dim,), (right_dim,)), ((), ()))
    return lax.dot_general(left, right, dims, preferred_element_type=F32)


def count_kernel(place_ref, words_ref, counts_ref):
    counts_ref[...] = jnp.zeros_like(counts_ref)
    row = lax.broadcasted_iota(jnp.int32, (BLOCK, LANES), 0)
    lane = lax.broadcasted_iota(jnp.int32, (BLOCK, LANES), 1)
    word_lane = (row % 32) * 4 + (lane % BLOCK) // 16
    shift = lane % 16
    half = lane // BLOCK

    def add_tile(t, carry):
        place = place_ref[t]
        dst = pl.multiple_of((place // 64) * BLOCK, BLOCK)
        src = place % 64
        upper = jnp.broadcast_to(words_ref[pl.ds(2 * t, 1), :], (32, LANES))
        lower = jnp.broadcast_to(words_ref[pl.ds(2 * t + 1, 1), :], (32, LANES))
        words = jnp.concatenate([upper, lower], axis=0)
        picked = jnp.take_along_axis(words, word_lane, axis=1)
        bits = jnp.right_shift(picked, shift) & 1
        tile = jnp.where(half == src % 2, bits, 0).astype(F32).astype(BF16)
        rows = pl.ds(dst, BLOCK)
        cols = pl.ds(pl.multiple_of((src // 2) * LANES, LANES), LANES)
        counts_ref[rows, cols] = counts_ref[rows, cols] + tile
        return carry

    lax.fori_loop(0, place_ref.shape[0], add_tile, 0, unroll=4)


def dense_counts(place, words, rows, cols):
    return pl.pallas_call(
        count_kernel,
        out_shape=jax.ShapeDtypeStruct((rows, cols), BF16),
        in_specs=[
            pl.BlockSpec(memory_space=pltpu.SMEM),
            pl.BlockSpec(memory_space=pltpu.VMEM),
        ],
        out_specs=pl.BlockSpec(memory_space=pltpu.VMEM),
        compiler_params=pltpu.CompilerParams(vmem_limit_bytes=16 << 20),
        cost_estimate=pl.CostEstimate(
            flops=20_000_000, bytes_accessed=rows * cols * 4, transcendentals=0
        ),
        name="dense_counts",
    )(place, words)


def send_to(x, step, replicas):
    return lax.ppermute(x, "rep", [(i, (i + step) % replicas) for i in range(replicas)])


def on_device(
    node_feats, w_self, w_neigh, send_rows, tile_dst, tile_src, tile_bits, norm_count, grad_out
):
    node_rows, feat_width = node_feats.shape
    peer_count = lax.axis_size("wide")
    replicas = lax.axis_size("rep")
    slot_count = send_rows.shape[2]
    tile_total = tile_dst.shape[2]
    quarter = node_rows // replicas
    rep_index = lax.axis_index("rep")
    dst_count = node_rows // BLOCK
    halo_rows = peer_count * slot_count
    first_row = rep_index * quarter
    first_block = rep_index * (quarter // BLOCK)

    def turned(x, axis=0):
        twice = jnp.concatenate([x, x], axis=axis)
        return lax.dynamic_slice_in_dim(twice, first_row, node_rows, axis)

    slot_rows = send_rows[0].reshape(-1)
    every_row = lax.broadcasted_iota(jnp.int32, (node_rows, halo_rows), 0)
    send_pick = (every_row == slot_rows[None, :]).astype(BF16)
    outgoing = dot(send_pick, node_feats, 0, 0).astype(BF16)
    incoming = lax.all_to_all(
        outgoing.reshape(peer_count, slot_count, feat_width), "wide", 0, 0, tiled=True
    ).reshape(halo_rows, feat_width)

    feats = turned(node_feats)
    scale = turned(lax.rsqrt(norm_count.astype(F32)))[:, None]
    grad_out_parts = [grad_out] + [send_to(grad_out, replicas - k, replicas) for k in range(1, replicas)]
    grad_out_all = jnp.concatenate(grad_out_parts, axis=0)
    dst = (tile_dst[0, 0] - first_block) % dst_count
    src = tile_src[0, 0]
    src = jnp.where(src < dst_count, (src - first_block) % dst_count, src)
    counts = dense_counts(
        dst * 64 + src, tile_bits.reshape(tile_total * 2, LANES), node_rows, node_rows + halo_rows
    )
    counts_local = counts[:, :node_rows]
    counts_halo = counts[:, node_rows:]
    sums_local = dot(counts_local, feats, 1, 0)
    pre_self = dot(feats, w_self, 1, 0)

    sums = sums_local + dot(counts_halo, incoming, 1, 0)
    own_sums = sums[:quarter]
    for k in range(1, replicas):
        own_sums = own_sums + send_to(
            sums[k * quarter : (k + 1) * quarter].astype(BF16), k, replicas
        ).astype(F32)
    own_agg = (own_sums * scale[:quarter]).astype(BF16)
    agg = jnp.concatenate(
        [own_agg] + [send_to(own_agg, replicas - k, replicas) for k in range(1, replicas)], axis=0
    )
    pre = pre_self + dot(agg, w_neigh, 1, 0)
    sigmoid = jax.nn.sigmoid(pre)
    out_feats = (pre[:quarter] * sigmoid[:quarter]).astype(BF16)
    grad_pre = (grad_out_all.astype(F32) * sigmoid * (1.0 + pre * (1.0 - sigmoid))).astype(BF16)
    grad_agg = (dot(grad_pre, w_neigh, 1, 1) * scale).astype(BF16)

    halo_grad = dot(counts_halo, grad_agg, 0, 0).astype(BF16)
    returned = lax.all_to_all(
        halo_grad.reshape(peer_count, slot_count, feat_width), "wide", 0, 0, tiled=True
    ).reshape(halo_rows, feat_width)

    share = feat_width // replicas
    share_of = lambda x: lax.dynamic_slice_in_dim(x, rep_index * share, share, 1)
    weight_part = jnp.concatenate(
        [dot(share_of(feats), grad_pre, 0, 0), dot(share_of(agg), grad_pre, 0, 0)], axis=0
    )
    weight_share = lax.psum(weight_part, "wide").astype(BF16)
    weight_all = lax.all_gather(weight_share, "rep", axis=0)
    grad_self = weight_all[:, :share].reshape(feat_width, feat_width)
    grad_neigh = weight_all[:, share:].reshape(feat_width, feat_width)

    grad_local = dot(counts_local, grad_agg, 0, 0)
    turned_slots = (slot_rows - first_row) % node_rows
    return_pick = (every_row == turned_slots[None, :]).astype(BF16)
    block_grad = grad_local + dot(return_pick, returned, 1, 0)
    own_grad = block_grad[:quarter] + dot(grad_pre[:quarter], w_self, 1, 1)
    for k in range(1, replicas):
        own_grad = own_grad + send_to(
            block_grad[k * quarter : (k + 1) * quarter].astype(BF16), k, replicas
        ).astype(F32)
    return out_feats, own_grad.astype(BF16), grad_self, grad_neigh


def solution(mesh):
    in_specs = (
        P("wide", None),
        P(),
        P(),
        P("wide", None, "rep"),
        P("wide", "rep", None),
        P("wide", "rep", None),
        P("wide", "rep", None),
        P("wide"),
        P(("wide", "rep"), None),
    )
    out_specs = (P(("wide", "rep"), None), P(("wide", "rep"), None), P(), P())
    return jax.shard_map(
        on_device, mesh=mesh, in_specs=in_specs, out_specs=out_specs, check_vma=False
    )
```

time: 462 us -> 679 us (1.47)
  blocking collectives: 104 us -> 502 us
  waiting for transfers between devices: 135 us -> 48.9 us
  other arithmetic: 82.7 us -> 3.45 us
  local copies, waits for them, and re-layouts: 47 us -> 6.21 us
  starting transfers between devices: 34.6 us -> 67.3 us
  matrix products: 42.2 us -> 30.7 us
    psum x1, blocking collectives: 104 us -> 502 us  [on_device(): weight_share = lax.psum(weight_part, 'wide').astype(BF16)]
    scatter-add x9 -> x0, other arithmetic: 73.6 us -> none  [the longest x4 39.7 us: backward_group(): return (running.at[src_part].add(products), None)]
    psum x1 -> x0, waiting for transfers between devices: 62.1 us -> none  [on_device(): summed = lax.psum(partial_sum, 'rep')]
    ppermute x0 -> x12, starting transfers between devices: none -> 39.4 us  [send_to(): lax.ppermute(x, 'rep', [(i, (i + step) % replicas) for i in range(replica...]
    all_to_all x2, waiting for transfers between devices: 44.4 us -> 14.4 us  [the longest x1 14.4 us: on_device(): lax.all_to_all(outgoing.reshape(peer_count, slot_count, feat_width), 'wid...]
    gather x9 -> x0, local copies, waits for them, and re-layouts: 27.4 us -> none  [the longest x4 14.4 us: forward_group(): picked = jnp.take(source_blocks, src_part, axis=0)]
    ppermute x0 -> x12, waiting for transfers between devices: none -> 15.5 us  [send_to(): lax.ppermute(x, 'rep', [(i, (i + step) % replicas) for i in range(replica...]
    dot_general x14 -> x12, matrix products: 42.2 us -> 30.7 us  [dot(): return lax.dot_general(left, right, dims, preferred_element_type=F32)]
  transfers between devices with their start and end apart: 5 -> 15, of which waited for: 4 -> 5; matrix products, arithmetic and copies ran while one was open for 4% -> 3% of each run, Pallas kernels for 0% -> 1%
where the time goes in v1:
time: 679 us
  blocking collectives  502 us (74%)
  starting transfers between devices  67.3 us (10%)
  waiting for transfers between devices  48.9 us (7%)
  matrix products  30.7 us (5%)
  between operations  14.4 us (2%)
    psum x1, blocking collectives, on_device(): weight_share = lax.psum(weight_part, 'wide').astype(BF16)  502 us
    ppermute x12, starting transfers between devices, send_to(): lax.ppermute(x, 'rep', [(i, (i + step) % replicas) for i in range(replica...  39.4 us
    dot_general x12, matrix products, dot(): return lax.dot_general(left, right, dims, preferred_element_type=F32)  30.7 us
    all_to_all x1, starting transfers between devices, on_device(): lax.all_to_all(outgoing.reshape(peer_count, slot_count, feat_width), 'wid...  19 us
    all_gather x1, waiting for transfers between devices, on_device(): weight_all = lax.all_gather(weight_share, 'rep', axis=0)  19 us
    ppermute x12, waiting for transfers between devices, send_to(): lax.ppermute(x, 'rep', [(i, (i + step) % replicas) for i in range(replica...  15.5 us
    all_to_all x1, waiting for transfers between devices, on_device(): lax.all_to_all(outgoing.reshape(peer_count, slot_count, feat_width), 'wid...  14.4 us
  transfers between devices with their start and end apart: 15, of which 5 were waited for; matrix products, arithmetic and copies ran while one was open for 3% of the time, Pallas kernels for 1%

profile of v1, /device:TPU:1, one launch (start us, length us, event | category | flops | bytes accessed | tf_op | source)
XLA Modules:
  0.0 678.6 jit_solution(16392462383498679393)
XLA Ops:
  8.1 3.5 fusion.20
  11.7 19.0 %all-to-all-start = ((bf16[128,8,512]{2,1,0:T(8,128)(2,1)}), bf16[128,8,512]{2,1,0:T(8,128)(2,1)}, u32[]{:S(2)}, u32[]{:S(2)}) async-start(bf16[128,8,512]{2,1,0:T(8,128)(2,1)} %fusion.20), calls=%async_computation | async-start | bytes 2097152 | tf_op jit(solution)/shard_map/all_to_all | solution.py:89
  30.7 3.1 collective-permute-start.8
  33.8 4.4 collective-permute-start.7
  38.3 6.0 dense_counts.1
  46.4 14.4 %all-to-all-done = bf16[128,8,512]{2,1,0:T(8,128)(2,1)} async-done(((bf16[128,8,512]{2,1,0:T(8,128)(2,1)}), bf16[128,8,512]{2,1,0:T(8,128)(2,1)}, u32[]{:S(2)}, u32[]{:S(2)}) %all-to-all-start) | async-done | bytes 1048608 | tf_op jit(solution)/shard_map/all_to_all | solution.py:89
  60.8 3.2 fusion.6
  65.4 4.5 collective-permute-start.2
  69.9 2.4 collective-permute-start.1
  72.3 2.5 collective-permute-start
  75.0 5.4 collective-permute-start.6
  80.4 6.3 collective-permute-done
  88.8 2.3 collective-permute-start.4
  91.1 4.1 collective-permute-start.3
  96.0 6.4 collective-permute-done.5
  102.4 2.9 collective-permute-done.3
  105.3 5.7 multiply_convert_fusion.1
  114.1 8.8 %all-to-all-start.1 = ((bf16[128,8,512]{2,1,0:T(8,128)(2,1)}), bf16[128,8,512]{2,1,0:T(8,128)(2,1)}, u32[]{:S(2)}, u32[]{:S(2)}) async-start(bf16[128,8,512]{2,1,0:T(8,128)(2,1)} %fusion.21), calls=%async_computation.1 | async-start | bytes 2097152 | tf_op jit(solution)/shard_map/all_to_all | solution.py:125
  126.1 501.6 %all-reduce.1 = bf16[256,512]{1,0:T(8,128)(2,1)} all-reduce(f32[256,512]{1,0:T(8,128)S(1)} %pad_maximum_fusion.1), channel_id=1, replica_groups=mesh['wide'=128,'rep'=4] {'wide'}, use_global_device_ids=true, to_apply=%region_0.1 | all-reduce | flops 131072 | bytes 786432 | tf_op jit(solution)/shard_map/psum | solution.py:134
  629.7 4.5 fusion.8
  634.2 4.6 fusion.56
  639.7 4.2 collective-permute-start.11
  645.8 2.5 collective-permute-start.9
  648.3 19.0 %all-gather.3.cloned.1.call-done = bf16[1024,512]{1,0:T(8,128)(2,1)} async-done(((bf16[256,512]{1,0:T(8,128)(2,1)}), bf16[1024,512]{1,0:T(8,128)(2,1)}) %all-gather.3.cloned.1.call-update) | async-done | bytes 1048592 | tf_op jit(solution)/shard_map/all_gather | solution.py:135
  (65 shorter events, 22.6 us)
Async XLA Ops:
  7.2 98.1 %copy-start = (bf16[512,512]{1,0:T(8,128)(2,1)S(1)}, bf16[512,512]{1,0:T(8,128)(2,1)}, u32[]{:S(2)}) copy-start(bf16[512,512]{1,0:T(8,128)(2,1)} %param.11) | copy-start | bytes 1572868
  11.7 26.5 %copy-start.11 = (s32[1,1,128]{2,1,0:T(1,128)S(1)}, s32[1,1,128]{2,1,0:T(1,128)}, u32[]{:S(2)}) copy-start(s32[1,1,128]{2,1,0:T(1,128)} %param.14) | copy-start | bytes 1540
  11.7 26.5 %copy-start.12 = (s32[1,1,128]{2,1,0:T(1,128)S(1)}, s32[1,1,128]{2,1,0:T(1,128)}, u32[]{:S(2)}) copy-start(s32[1,1,128]{2,1,0:T(1,128)} %param.13) | copy-start | bytes 1540
  11.7 26.6 %copy-start.3 = (s32[1,1,32768]{2,1,0:T(1,128)S(1)}, s32[1,1,32768]{2,1,0:T(1,128)}, u32[]{:S(2)}) copy-start(s32[1,1,32768]{2,1,0:T(1,128)} %param.15) | copy-start | bytes 393220
  11.7 49.1 %all-to-all-start = ((bf16[128,8,512]{2,1,0:T(8,128)(2,1)}), bf16[128,8,512]{2,1,0:T(8,128)(2,1)}, u32[]{:S(2)}, u32[]{:S(2)}) async-start(bf16[128,8,512]{2,1,0:T(8,128)(2,1)} %fusion.20), calls=%async_computation | async-start | bytes 2097152 | tf_op jit(solution)/shard_map/all_to_all | solution.py:89
  30.7 60.4 %collective-permute-start.8 = (bf16[256,512]{1,0:T(8,128)(2,1)}, bf16[256,512]{1,0:T(8,128)(2,1)}, u32[]{:S(2)}, u32[]{:S(2)}) collective-permute-start(bf16[256,512]{1,0:T(8,128)(2,1)} %param.17), channel_id=1, source_target_pairs={{0,1},{1,2},{2,3},{3,0},{4,5},{5,6},{6,7},{7,4},{8,9},{9,10},{10,1... | collective-permute-start | bytes 786440 | tf_op jit(solution)/shard_map/ppermute | solution.py:63
  33.8 62.2 %collective-permute-start.7 = (bf16[256,512]{1,0:T(8,128)(2,1)}, bf16[256,512]{1,0:T(8,128)(2,1)}, u32[]{:S(2)}, u32[]{:S(2)}) collective-permute-start(bf16[256,512]{1,0:T(8,128)(2,1)} %param.17), channel_id=1, source_target_pairs={{0,2},{1,3},{2,0},{3,1},{4,6},{5,7},{6,4},{7,5},{8,10},{9,11},{10,... | collective-permute-start | bytes 786440 | tf_op jit(solution)/shard_map/ppermute | solution.py:63
  46.4 48.9 %copy-start.5 = (bf16[2048,512]{1,0:T(8,128)(2,1)}, bf16[2048,512]{1,0:T(8,128)(2,1)S(1)}, u32[]{:S(2)}) copy-start(bf16[2048,512]{1,0:T(8,128)(2,1)S(1)} %constant_dynamic-update-slice_fusion) | copy-start | bytes 6291460
  64.0 10.8 %copy-start.10 = (s32[1024]{0:T(1024)S(1)}, s32[1024]{0:T(1024)}, u32[]{:S(2)}) copy-start(s32[1024]{0:T(1024)} %param.16) | copy-start | bytes 12292
  65.3 30.0 %copy-start.6 = (bf16[512,512]{1,0:T(8,128)(2,1)S(1)}, bf16[512,512]{1,0:T(8,128)(2,1)}, u32[]{:S(2)}) copy-start(bf16[512,512]{1,0:T(8,128)(2,1)} %param.10) | copy-start | bytes 1572868
  65.4 9.6 %collective-permute-start.2 = (bf16[256,512]{1,0:T(8,128)(2,1)S(1)}, bf16[256,512]{1,0:T(8,128)(2,1)S(1)}, u32[]{:S(2)}, u32[]{:S(2)}) collective-permute-start(bf16[256,512]{1,0:T(8,128)(2,1)S(1)} %get-tuple-element.12), channel_id=1, source_target_pairs={{0,3},{1,0},{2,1},{3,2},{4,7},{5,4},{6,5},{7,6},{8,11},{9,8},{10,9... | collective-permute-start | bytes 786440 | tf_op jit(solution)/shard_map/ppermute | solution.py:63
  69.9 10.5 %collective-permute-start.1 = (bf16[256,512]{1,0:T(8,128)(2,1)S(1)}, bf16[256,512]{1,0:T(8,128)(2,1)S(1)}, u32[]{:S(2)}, u32[]{:S(2)}) collective-permute-start(bf16[256,512]{1,0:T(8,128)(2,1)S(1)} %get-tuple-element.13), channel_id=1, source_target_pairs={{0,2},{1,3},{2,0},{3,1},{4,6},{5,7},{6,4},{7,5},{8,10},{9,11},{10,... | collective-permute-start | bytes 786440 | tf_op jit(solution)/shard_map/ppermute | solution.py:63
  72.3 14.3 %collective-permute-start = (bf16[256,512]{1,0:T(8,128)(2,1)S(1)}, bf16[256,512]{1,0:T(8,128)(2,1)S(1)}, u32[]{:S(2)}, u32[]{:S(2)}) collective-permute-start(bf16[256,512]{1,0:T(8,128)(2,1)S(1)} %get-tuple-element.11), channel_id=1, source_target_pairs={{0,1},{1,2},{2,3},{3,0},{4,5},{5,6},{6,7},{7,4},{8,9},{9,10},{10,1... | collective-permute-start | bytes 786440 | tf_op jit(solution)/shard_map/ppermute | solution.py:63
  75.0 21.0 %collective-permute-start.6 = (bf16[256,512]{1,0:T(8,128)(2,1)}, bf16[256,512]{1,0:T(8,128)(2,1)S(1)}, u32[]{:S(2)}, u32[]{:S(2)}) collective-permute-start(bf16[256,512]{1,0:T(8,128)(2,1)} %param.17), channel_id=1, source_target_pairs={{0,3},{1,0},{2,1},{3,2},{4,7},{5,4},{6,5},{7,6},{8,11},{9,8},{10,9... | collective-permute-start | bytes 786440 | tf_op jit(solution)/shard_map/ppermute | solution.py:63
  86.8 15.6 %collective-permute-start.5 = (bf16[256,512]{1,0:T(8,128)(2,1)S(1)}, bf16[256,512]{1,0:T(8,128)(2,1)S(1)}, u32[]{:S(2)}, u32[]{:S(2)}) collective-permute-start(bf16[256,512]{1,0:T(8,128)(2,1)S(1)} %fusion.37), channel_id=1, source_target_pairs={{0,1},{1,2},{2,3},{3,0},{4,5},{5,6},{6,7},{7,4},{8,9},{9,10},{10,1... | collective-permute-start | bytes 786440 | tf_op jit(solution)/shard_map/ppermute | solution.py:63
  88.8 13.6 %collective-permute-start.4 = (bf16[256,512]{1,0:T(8,128)(2,1)S(1)}, bf16[256,512]{1,0:T(8,128)(2,1)S(1)}, u32[]{:S(2)}, u32[]{:S(2)}) collective-permute-start(bf16[256,512]{1,0:T(8,128)(2,1)S(1)} %fusion.37), channel_id=1, source_target_pairs={{0,2},{1,3},{2,0},{3,1},{4,6},{5,7},{6,4},{7,5},{8,10},{9,11},{10,... | collective-permute-start | bytes 786440 | tf_op jit(solution)/shard_map/ppermute | solution.py:63
  91.1 14.1 %collective-permute-start.3 = (bf16[256,512]{1,0:T(8,128)(2,1)S(1)}, bf16[256,512]{1,0:T(8,128)(2,1)S(1)}, u32[]{:S(2)}, u32[]{:S(2)}) collective-permute-start(bf16[256,512]{1,0:T(8,128)(2,1)S(1)} %fusion.37), channel_id=1, source_target_pairs={{0,3},{1,0},{2,1},{3,2},{4,7},{5,4},{6,5},{7,6},{8,11},{9,8},{10,9... | collective-permute-start | bytes 786440 | tf_op jit(solution)/shard_map/ppermute | solution.py:63
  102.4 8.6 %copy-start.7 = (bf16[256,512]{1,0:T(8,128)(2,1)}, bf16[256,512]{1,0:T(8,128)(2,1)S(1)}, u32[]{:S(2)}) copy-start(bf16[256,512]{1,0:T(8,128)(2,1)S(1)} %collective-permute-done.5) | copy-start | bytes 786436
  102.4 8.6 %copy-start.8 = (bf16[256,512]{1,0:T(8,128)(2,1)}, bf16[256,512]{1,0:T(8,128)(2,1)S(1)}, u32[]{:S(2)}) copy-start(bf16[256,512]{1,0:T(8,128)(2,1)S(1)} %collective-permute-done.4) | copy-start | bytes 786436
  114.1 520.2 %all-to-all-start.1 = ((bf16[128,8,512]{2,1,0:T(8,128)(2,1)}), bf16[128,8,512]{2,1,0:T(8,128)(2,1)}, u32[]{:S(2)}, u32[]{:S(2)}) async-start(bf16[128,8,512]{2,1,0:T(8,128)(2,1)} %fusion.21), calls=%async_computation.1 | async-start | bytes 2097152 | tf_op jit(solution)/shard_map/all_to_all | solution.py:125
  122.9 544.4 %all-gather.3.cloned.1.call-start = ((), (), s32[]{:S(2)}) async-start(), calls=%async_computation.2 | async-start | bytes 1310720 | tf_op jit(solution)/shard_map/all_gather | solution.py:135
  639.7 29.9 %collective-permute-start.11 = (bf16[256,512]{1,0:T(8,128)(2,1)}, bf16[256,512]{1,0:T(8,128)(2,1)S(1)}, u32[]{:S(2)}, u32[]{:S(2)}) collective-permute-start(bf16[256,512]{1,0:T(8,128)(2,1)} %get-tuple-element.9), channel_id=1, source_target_pairs={{0,3},{1,0},{2,1},{3,2},{4,7},{5,4},{6,5},{7,6},{8,11},{9,8},{10,9... | collective-permute-start | bytes 786440 | tf_op jit(solution)/shard_map/ppermute | solution.py:63
  643.9 25.6 %collective-permute-start.10 = (bf16[256,512]{1,0:T(8,128)(2,1)}, bf16[256,512]{1,0:T(8,128)(2,1)S(1)}, u32[]{:S(2)}, u32[]{:S(2)}) collective-permute-start(bf16[256,512]{1,0:T(8,128)(2,1)} %get-tuple-element.10), channel_id=1, source_target_pairs={{0,2},{1,3},{2,0},{3,1},{4,6},{5,7},{6,4},{7,5},{8,10},{9,11},{10,... | collective-permute-start | bytes 786440 | tf_op jit(solution)/shard_map/ppermute | solution.py:63
  645.8 23.7 %collective-permute-start.9 = (bf16[256,512]{1,0:T(8,128)(2,1)S(1)}, bf16[256,512]{1,0:T(8,128)(2,1)S(1)}, u32[]{:S(2)}, u32[]{:S(2)}) collective-permute-start(bf16[256,512]{1,0:T(8,128)(2,1)S(1)} %get-tuple-element.8), channel_id=1, source_target_pairs={{0,1},{1,2},{2,3},{3,0},{4,5},{5,6},{6,7},{7,4},{8,9},{9,10},{10,1... | collective-permute-start | bytes 786440 | tf_op jit(solution)/shard_map/ppermute | solution.py:63
  (5 other events, 21.2 us)
Sparse Core Ops, SparseCore 0:
  627.8 39.4 all-gather.2

commit v2 on v1

--- a/solution.py
+++ b/solution.py
@@ -3,10 +3,12 @@
 from jax import lax
 from jax.experimental import pallas as pl
 from jax.experimental.pallas import tpu as pltpu
+from jax.sharding import Mesh
 from jax.sharding import PartitionSpec as P
 
 BLOCK = 64
 LANES = 128
+WIDE = ("y", "z", "core")
 F32 = jnp.float32
 BF16 = jnp.bfloat16
 
@@ -63,11 +65,16 @@
     return lax.ppermute(x, "rep", [(i, (i + step) % replicas) for i in range(replicas)])
 
 
+def gather_wide(tile, peer_count):
+    copies = jnp.broadcast_to(tile, (peer_count,) + tile.shape)
+    return lax.all_to_all(copies, WIDE, 0, 0, tiled=True)
+
+
 def on_device(
     node_feats, w_self, w_neigh, send_rows, tile_dst, tile_src, tile_bits, norm_count, grad_out
 ):
     node_rows, feat_width = node_feats.shape
-    peer_count = lax.axis_size("wide")
+    peer_count = lax.axis_size(WIDE)
     replicas = lax.axis_size("rep")
     slot_count = send_rows.shape[2]
     tile_total = tile_dst.shape[2]
@@ -87,13 +94,12 @@
     send_pick = (every_row == slot_rows[None, :]).astype(BF16)
     outgoing = dot(send_pick, node_feats, 0, 0).astype(BF16)
     incoming = lax.all_to_all(
-        outgoing.reshape(peer_count, slot_count, feat_width), "wide", 0, 0, tiled=True
+        outgoing.reshape(peer_count, slot_count, feat_width), WIDE, 0, 0, tiled=True
     ).reshape(halo_rows, feat_width)
 
     feats = turned(node_feats)
     scale = turned(lax.rsqrt(norm_count.astype(F32)))[:, None]
-    grad_out_parts = [grad_out] + [send_to(grad_out, replicas - k, replicas) for k in range(1, replicas)]
-    grad_out_all = jnp.concatenate(grad_out_parts, axis=0)
+    grad_out_all = turned(lax.all_gather(grad_out, "rep", axis=0, tiled=True))
     dst = (tile_dst[0, 0] - first_block) % dst_count
     src = tile_src[0, 0]
     src = jnp.where(src < dst_count, (src - first_block) % dst_count, src)
@@ -121,17 +127,39 @@
     grad_pre = (grad_out_all.astype(F32) * sigmoid * (1.0 + pre * (1.0 - sigmoid))).astype(BF16)
     grad_agg = (dot(grad_pre, w_neigh, 1, 1) * scale).astype(BF16)
 
-    halo_grad = dot(counts_halo, grad_agg, 0, 0).astype(BF16)
-    returned = lax.all_to_all(
-        halo_grad.reshape(peer_count, slot_count, feat_width), "wide", 0, 0, tiled=True
-    ).reshape(halo_rows, feat_width)
-
     share = feat_width // replicas
     share_of = lambda x: lax.dynamic_slice_in_dim(x, rep_index * share, share, 1)
     weight_part = jnp.concatenate(
         [dot(share_of(feats), grad_pre, 0, 0), dot(share_of(agg), grad_pre, 0, 0)], axis=0
+    ).astype(BF16)
+    lane_tiles = feat_width // LANES
+    weight_tiles = (
+        weight_part.reshape(-1, slot_count, lane_tiles, LANES)
+        .transpose(0, 2, 1, 3)
+        .reshape(peer_count, -1, slot_count, LANES)
+        .transpose(0, 2, 1, 3)
+        .reshape(peer_count, slot_count, -1)
     )
-    weight_share = lax.psum(weight_part, "wide").astype(BF16)
+    halo_grad = dot(counts_halo, grad_agg, 0, 0).astype(BF16)
+    returned = lax.all_to_all(
+        jnp.concatenate(
+            [halo_grad.reshape(peer_count, slot_count, feat_width), weight_tiles], axis=2
+        ),
+        WIDE,
+        0,
+        0,
+        tiled=True,
+    )
+    own_tile = returned[:, :, feat_width:].astype(F32).sum(axis=0).astype(BF16)
+    returned = returned[:, :, :feat_width].reshape(halo_rows, feat_width)
+    all_tiles = gather_wide(own_tile, peer_count)
+    weight_share = (
+        all_tiles.reshape(peer_count, slot_count, -1, LANES)
+        .transpose(0, 2, 1, 3)
+        .reshape(-1, lane_tiles, slot_count, LANES)
+        .transpose(0, 2, 1, 3)
+        .reshape(2 * share, feat_width)
+    )
     weight_all = lax.all_gather(weight_share, "rep", axis=0)
     grad_self = weight_all[:, :share].reshape(feat_width, feat_width)
     grad_neigh = weight_all[:, share:].reshape(feat_width, feat_width)
@@ -149,18 +177,21 @@
 
 
 def solution(mesh):
+    fine = Mesh(
+        mesh.devices.reshape(8, mesh.shape["wide"] // 16, 2, mesh.shape["rep"]), WIDE + ("rep",)
+    )
     in_specs = (
-        P("wide", None),
+        P(WIDE, None),
         P(),
         P(),
-        P("wide", None, "rep"),
-        P("wide", "rep", None),
-        P("wide", "rep", None),
-        P("wide", "rep", None),
-        P("wide"),
-        P(("wide", "rep"), None),
+        P(WIDE, None, "rep"),
+        P(WIDE, "rep", None),
+        P(WIDE, "rep", None),
+        P(WIDE, "rep", None),
+        P(WIDE),
+        P(WIDE + ("rep",), None),
     )
-    out_specs = (P(("wide", "rep"), None), P(("wide", "rep"), None), P(), P())
+    out_specs = (P(WIDE + ("rep",), None), P(WIDE + ("rep",), None), P(), P())
     return jax.shard_map(
-        on_device, mesh=mesh, in_specs=in_specs, out_specs=out_specs, check_vma=False
+        on_device, mesh=fine, in_specs=in_specs, out_specs=out_specs, check_vma=False
     )

time: 679 us -> 230 us (0.34)
  blocking collectives: 502 us -> 65.9 us
  starting transfers between devices: 67.3 us -> 45.4 us
  waiting for transfers between devices: 48.9 us -> 57.7 us
    psum x1 -> x0, blocking collectives: 502 us -> none  [on_device(): weight_share = lax.psum(weight_part, 'wide').astype(BF16)]
    all_to_all x0 -> x2, blocking collectives: none -> 65.9 us  [the longest x1 44 us: on_device(): lax.all_to_all(jnp.concatenate([halo_grad.reshape(peer_count, slot_count,...]
    ppermute x12 -> x9, waiting for transfers between devices: 15.5 us -> 35.9 us  [send_to(): lax.ppermute(x, 'rep', [(i, (i + step) % replicas) for i in range(replica...]
    all_gather x1, waiting for transfers between devices: 19 us -> 0.01 us  [on_device(): weight_all = lax.all_gather(weight_share, 'rep', axis=0)]
    ppermute x12 -> x9, starting transfers between devices: 39.4 us -> 26.3 us  [send_to(): lax.ppermute(x, 'rep', [(i, (i + step) % replicas) for i in range(replica...]
    all_to_all x2 -> x1, starting transfers between devices: 27.8 us -> 19 us  [on_device(): lax.all_to_all(outgoing.reshape(peer_count, slot_count, feat_width), WIDE...]
    all_to_all x2 -> x1, waiting for transfers between devices: 14.4 us -> 21.1 us  [on_device(): lax.all_to_all(outgoing.reshape(peer_count, slot_count, feat_width), WIDE...]
  transfers between devices with their start and end apart: 15 -> 12, of which waited for: 5 -> 8; matrix products, arithmetic and copies ran while one was open for 3% -> 8% of each run, Pallas kernels for 1% -> 3%
where the time goes in v2:
time: 230 us; the launch traced here: 229 us
  blocking collectives  65.9 us (29%)
  waiting for transfers between devices  57.7 us (25%)
  starting transfers between devices  45.4 us (20%)
  matrix products  26.7 us (12%)
  between operations  14.4 us (6%)
  local copies, waits for them, and re-layouts  7.44 us (3%)
  Pallas kernels  5.98 us (3%)
  other arithmetic  5.69 us (2%)
    all_to_all x1, blocking collectives, on_device(): lax.all_to_all(jnp.concatenate([halo_grad.reshape(peer_count, slot_count,...  44 us
    ppermute x9, waiting for transfers between devices, send_to(): lax.ppermute(x, 'rep', [(i, (i + step) % replicas) for i in range(replica...  35.9 us
    dot_general x12, matrix products, dot(): return lax.dot_general(left, right, dims, preferred_element_type=F32)  26.7 us
    ppermute x9, starting transfers between devices, send_to(): lax.ppermute(x, 'rep', [(i, (i + step) % replicas) for i in range(replica...  26.3 us
    all_to_all x1, blocking collectives, gather_wide(): return lax.all_to_all(copies, WIDE, 0, 0, tiled=True)  21.9 us
    all_to_all x1, waiting for transfers between devices, on_device(): lax.all_to_all(outgoing.reshape(peer_count, slot_count, feat_width), WIDE...  21.1 us
    all_to_all x1, starting transfers between devices, on_device(): lax.all_to_all(outgoing.reshape(peer_count, slot_count, feat_width), WIDE...  19 us
    pallas_call x1, Pallas kernels, dense_counts(): pl.pallas_call(count_kernel, out_shape=jax.ShapeDtypeStruct((rows, cols),...  5.98 us
  transfers between devices with their start and end apart: 12, of which 8 were waited for; matrix products, arithmetic and copies ran while one was open for 8% of the time, Pallas kernels for 3%

profile of v2, /device:TPU:1, one launch (start us, length us, event | category | flops | bytes accessed | tf_op | source)
XLA Modules:
  0.0 229.2 jit_solution(17668546867694947179)
XLA Ops:
  8.1 3.6 %fusion.20 = bf16[128,8,512]{2,1,0:T(8,128)(2,1)} fusion(bf16[1024,512]{1,0:T(8,128)(2,1)} %param.9, s32[1024]{0:T(1024)S(1)} %eq.23), kind=kOutput, calls=%fused_computation.24 | convolution fusion | flops 1075314688 | bytes 2101248 | tf_op jit(solution)/shard_map/dot_general | solution.py:18
  11.7 19.0 %all-to-all-start = ((bf16[128,8,512]{2,1,0:T(8,128)(2,1)}), bf16[128,8,512]{2,1,0:T(8,128)(2,1)}, u32[]{:S(2)}, u32[]{:S(2)}) async-start(bf16[128,8,512]{2,1,0:T(8,128)(2,1)} %fusion.20), calls=%async_computation | async-start | bytes 2097152 | tf_op jit(solution)/shard_map/all_to_all | solution.py:96
  31.6 6.0 %dense_counts.1 = bf16[1024,2048]{1,0:T(8,128)(2,1)S(1)} custom-call(s32[128]{0:T(128)S(1)} %fusion.45.place_ref, s32[256,128]{1,0:T(8,128)S(1)} %bitcast.42), custom_call_target="tpu_custom_call" | custom-call | flops 20000000 | bytes 8388608 | tf_op jit(solution)/shard_map/dense_counts/pallas_call | solution.py:48
  39.7 21.1 %all-to-all-done = bf16[128,8,512]{2,1,0:T(8,128)(2,1)} async-done(((bf16[128,8,512]{2,1,0:T(8,128)(2,1)}), bf16[128,8,512]{2,1,0:T(8,128)(2,1)}, u32[]{:S(2)}, u32[]{:S(2)}) %all-to-all-start) | async-done | bytes 1048608 | tf_op jit(solution)/shard_map/all_to_all | solution.py:96
  60.8 3.2 %fusion.6 = f32[1024,512]{1,0:T(8,128)S(1)} fusion(bf16[1024,2048]{1,0:T(8,128)(2,1)} %copy-done.1, bf16[128,8,512]{2,1,0:T(8,128)(2,1)} %all-to-all-done), kind=kOutput, calls=%fused_computation.13 | convolution fusion | flops 1073741824 | bytes 5242880 | tf_op jit(solution)/shard_map/dot_general | solution.py:18
  64.1 2.7 %fusion.51 = (bf16[1024,512]{1,0:T(8,128)(2,1)S(1)}, f32[1024,512]{1,0:T(8,128)}) fusion(f32[1024,512]{1,0:T(8,128)S(1)} %fusion.6, bf16[2048,512]{1,0:T(8,128)(2,1)S(1)} %constant_dynamic-update-slice_fusion, s32[]{:T(128)S(6)} %select_n.38, bf16[1024,2048]{1,0:T(8,128)(2,1)S(1)} %copy-done.2), kind=kOutput, calls=%fused_computation.78 | convolution fusion | flops 1074790400 | bytes 8388612 | tf_op jit(solution)/shard_map/dot_general | solution.py:18
  67.7 4.4 %collective-permute-start.2 = (bf16[256,512]{1,0:T(8,128)(2,1)}, bf16[256,512]{1,0:T(8,128)(2,1)S(1)}, u32[]{:S(2)}, u32[]{:S(2)}) collective-permute-start(bf16[256,512]{1,0:T(8,128)(2,1)} %get-tuple-element.12), channel_id=1, source_target_pairs={{0,3},{1,0},{2,1},{3,2},{4,7},{5,4},{6,5},{7,6},{8,11},{9,8},{10,9... | collective-permute-start | bytes 786440 | tf_op jit(solution)/shard_map/ppermute | solution.py:65
  72.1 2.4 %collective-permute-start.1 = (bf16[256,512]{1,0:T(8,128)(2,1)}, bf16[256,512]{1,0:T(8,128)(2,1)}, u32[]{:S(2)}, u32[]{:S(2)}) collective-permute-start(bf16[256,512]{1,0:T(8,128)(2,1)} %get-tuple-element.13), channel_id=1, source_target_pairs={{0,2},{1,3},{2,0},{3,1},{4,6},{5,7},{6,4},{7,5},{8,10},{9,11},{10,... | collective-permute-start | bytes 786440 | tf_op jit(solution)/shard_map/ppermute | solution.py:65
  74.5 2.5 %collective-permute-start = (bf16[256,512]{1,0:T(8,128)(2,1)}, bf16[256,512]{1,0:T(8,128)(2,1)}, u32[]{:S(2)}, u32[]{:S(2)}) collective-permute-start(bf16[256,512]{1,0:T(8,128)(2,1)} %get-tuple-element.11), channel_id=1, source_target_pairs={{0,1},{1,2},{2,3},{3,0},{4,5},{5,6},{6,7},{7,4},{8,9},{9,10},{10,1... | collective-permute-start | bytes 786440 | tf_op jit(solution)/shard_map/ppermute | solution.py:65
  77.2 4.8 %collective-permute-done.1 = bf16[256,512]{1,0:T(8,128)(2,1)} collective-permute-done((bf16[256,512]{1,0:T(8,128)(2,1)}, bf16[256,512]{1,0:T(8,128)(2,1)}, u32[]{:S(2)}, u32[]{:S(2)}) %collective-permute-start.1) | collective-permute-done | bytes 262176 | tf_op jit(solution)/shard_map/ppermute | solution.py:65
  82.0 7.2 %collective-permute-done = bf16[256,512]{1,0:T(8,128)(2,1)} collective-permute-done((bf16[256,512]{1,0:T(8,128)(2,1)}, bf16[256,512]{1,0:T(8,128)(2,1)}, u32[]{:S(2)}, u32[]{:S(2)}) %collective-permute-start) | collective-permute-done | bytes 262176 | tf_op jit(solution)/shard_map/ppermute | solution.py:65
  92.5 2.3 %collective-permute-start.4 = (bf16[256,512]{1,0:T(8,128)(2,1)S(1)}, bf16[256,512]{1,0:T(8,128)(2,1)}, u32[]{:S(2)}, u32[]{:S(2)}) collective-permute-start(bf16[256,512]{1,0:T(8,128)(2,1)S(1)} %fusion.33), channel_id=1, source_target_pairs={{0,2},{1,3},{2,0},{3,1},{4,6},{5,7},{6,4},{7,5},{8,10},{9,11},{10,... | collective-permute-start | bytes 786440 | tf_op jit(solution)/shard_map/ppermute | solution.py:65
  94.8 4.2 %collective-permute-start.3 = (bf16[256,512]{1,0:T(8,128)(2,1)S(1)}, bf16[256,512]{1,0:T(8,128)(2,1)}, u32[]{:S(2)}, u32[]{:S(2)}) collective-permute-start(bf16[256,512]{1,0:T(8,128)(2,1)S(1)} %fusion.33), channel_id=1, source_target_pairs={{0,3},{1,0},{2,1},{3,2},{4,7},{5,4},{6,5},{7,6},{8,11},{9,8},{10,9... | collective-permute-start | bytes 786440 | tf_op jit(solution)/shard_map/ppermute | solution.py:65
  101.1 5.1 %collective-permute-done.5 = bf16[256,512]{1,0:T(8,128)(2,1)} collective-permute-done((bf16[256,512]{1,0:T(8,128)(2,1)S(1)}, bf16[256,512]{1,0:T(8,128)(2,1)}, u32[]{:S(2)}, u32[]{:S(2)}) %collective-permute-start.5) | collective-permute-done | bytes 262176 | tf_op jit(solution)/shard_map/ppermute | solution.py:65
  106.2 2.8 %collective-permute-done.3 = bf16[256,512]{1,0:T(8,128)(2,1)} collective-permute-done((bf16[256,512]{1,0:T(8,128)(2,1)S(1)}, bf16[256,512]{1,0:T(8,128)(2,1)}, u32[]{:S(2)}, u32[]{:S(2)}) %collective-permute-start.3) | collective-permute-done | bytes 262176 | tf_op jit(solution)/shard_map/ppermute | solution.py:65
  109.0 5.8 %multiply_convert_fusion.1 = (bf16[1024,512]{1,0:T(8,128)(2,1)S(1)}, f32[1024,512]{1,0:T(8,128)}, f32[1024,512]{1,0:T(8,128)}) fusion(s32[]{:T(128)S(6)} %select_n.38, bf16[1024,512]{1,0:T(8,128)(2,1)} %all-gather.3.cloned.1.call-done, f32[1024,512]{1,0:T(8,128)} %fusion.27, bf16[512,512]{1,0:T(8,128)(2,1)S(1)} %copy-done, ...), kind=kOutput, calls=%fused_computation.8 | convolution fusion | flops 548405248 | bytes 9961476 | tf_op jit(solution)/shard_map/dot_general | solution.py:18
  120.8 44.0 %all_to_all.15 = bf16[128,8,640]{2,1,0:T(8,128)(2,1)S(1)} all-to-all(bf16[128,8,640]{2,1,0:T(8,128)(2,1)S(1)} %pad_maximum_fusion), channel_id=1, replica_groups=mesh['y'=8,'z'=8,'core'=2,'rep'=4] {'y','z','core'}, dimensions={0} | all-to-all | bytes 2621440 | tf_op jit(solution)/shard_map/all_to_all | solution.py:144
  166.1 21.9 %all_to_all.16 = bf16[128,8,128]{2,1,0:T(8,128)(2,1)} all-to-all(bf16[128,8,128]{2,1,0:T(8,128)(2,1)S(1)} %broadcast_in_dim.2), channel_id=1, replica_groups=mesh['y'=8,'z'=8,'core'=2,'rep'=4] {'y','z','core'}, dimensions={0} | all-to-all | bytes 524288 | tf_op jit(solution)/shard_map/all_to_all | solution.py:70
  188.1 3.0 %fusion.8 = f32[1024,512]{1,0:T(8,128)S(1)} fusion(bf16[1024,512]{1,0:T(8,128)(2,1)S(1)} %copy-done.15, bf16[1024,2048]{1,0:T(8,128)(2,1)} %copy-done.1), kind=kOutput, calls=%fused_computation.15 | convolution fusion | flops 1073741824 | bytes 5242880 | tf_op jit(solution)/shard_map/dot_general | solution.py:18
  192.4 4.2 %collective-permute-start.8 = (bf16[256,512]{1,0:T(8,128)(2,1)S(1)}, bf16[256,512]{1,0:T(8,128)(2,1)S(1)}, u32[]{:S(2)}, u32[]{:S(2)}) collective-permute-start(bf16[256,512]{1,0:T(8,128)(2,1)S(1)} %get-tuple-element.9), channel_id=1, source_target_pairs={{0,3},{1,0},{2,1},{3,2},{4,7},{5,4},{6,5},{7,6},{8,11},{9,8},{10,9... | collective-permute-start | bytes 786440 | tf_op jit(solution)/shard_map/ppermute | solution.py:65
  198.5 2.5 %collective-permute-start.6 = (bf16[256,512]{1,0:T(8,128)(2,1)S(1)}, bf16[256,512]{1,0:T(8,128)(2,1)S(1)}, u32[]{:S(2)}, u32[]{:S(2)}) collective-permute-start(bf16[256,512]{1,0:T(8,128)(2,1)S(1)} %get-tuple-element.8), channel_id=1, source_target_pairs={{0,1},{1,2},{2,3},{3,0},{4,5},{5,6},{6,7},{7,4},{8,9},{9,10},{10,1... | collective-permute-start | bytes 786440 | tf_op jit(solution)/shard_map/ppermute | solution.py:65
  203.0 3.8 %collective-permute-done.8 = bf16[256,512]{1,0:T(8,128)(2,1)S(1)} collective-permute-done((bf16[256,512]{1,0:T(8,128)(2,1)S(1)}, bf16[256,512]{1,0:T(8,128)(2,1)S(1)}, u32[]{:S(2)}, u32[]{:S(2)}) %collective-permute-start.8) | collective-permute-done | bytes 262176 | tf_op jit(solution)/shard_map/ppermute | solution.py:65
  206.8 5.1 %collective-permute-done.7 = bf16[256,512]{1,0:T(8,128)(2,1)S(1)} collective-permute-done((bf16[256,512]{1,0:T(8,128)(2,1)S(1)}, bf16[256,512]{1,0:T(8,128)(2,1)S(1)}, u32[]{:S(2)}, u32[]{:S(2)}) %collective-permute-start.7) | collective-permute-done | bytes 262176 | tf_op jit(solution)/shard_map/ppermute | solution.py:65
  211.9 7.1 %collective-permute-done.6 = bf16[256,512]{1,0:T(8,128)(2,1)S(1)} collective-permute-done((bf16[256,512]{1,0:T(8,128)(2,1)S(1)}, bf16[256,512]{1,0:T(8,128)(2,1)S(1)}, u32[]{:S(2)}, u32[]{:S(2)}) %collective-permute-start.6) | collective-permute-done | bytes 262176 | tf_op jit(solution)/shard_map/ppermute | solution.py:65
  (68 shorter events, 26.1 us)
Async XLA Ops:
  7.2 101.8 %copy-start = (bf16[512,512]{1,0:T(8,128)(2,1)S(1)}, bf16[512,512]{1,0:T(8,128)(2,1)}, u32[]{:S(2)}) copy-start(bf16[512,512]{1,0:T(8,128)(2,1)} %param.11) | copy-start | bytes 1572868
  11.7 19.8 %copy-start.12 = (s32[1,1,128]{2,1,0:T(1,128)S(1)}, s32[1,1,128]{2,1,0:T(1,128)}, u32[]{:S(2)}) copy-start(s32[1,1,128]{2,1,0:T(1,128)} %param.14) | copy-start | bytes 1540
  11.7 19.8 %copy-start.13 = (s32[1,1,128]{2,1,0:T(1,128)S(1)}, s32[1,1,128]{2,1,0:T(1,128)}, u32[]{:S(2)}) copy-start(s32[1,1,128]{2,1,0:T(1,128)} %param.13) | copy-start | bytes 1540
  11.7 19.9 %copy-start.4 = (s32[1,1,32768]{2,1,0:T(1,128)S(1)}, s32[1,1,32768]{2,1,0:T(1,128)}, u32[]{:S(2)}) copy-start(s32[1,1,32768]{2,1,0:T(1,128)} %param.15) | copy-start | bytes 393220
  11.7 49.1 %all-to-all-start = ((bf16[128,8,512]{2,1,0:T(8,128)(2,1)}), bf16[128,8,512]{2,1,0:T(8,128)(2,1)}, u32[]{:S(2)}, u32[]{:S(2)}) async-start(bf16[128,8,512]{2,1,0:T(8,128)(2,1)} %fusion.20), calls=%async_computation | async-start | bytes 2097152 | tf_op jit(solution)/shard_map/all_to_all | solution.py:96
  30.8 70.4 %all-gather.3.cloned.1.call-start = ((), (), s32[]{:S(2)}) async-start(), calls=%async_computation.3 | async-start | bytes 1310720 | tf_op jit(solution)/shard_map/all_gather | solution.py:102
  31.5 188.6 %all-gather.5.cloned.1.call-start = ((), (), s32[]{:S(2)}) async-start(), calls=%async_computation.4 | async-start | bytes 1310720 | tf_op jit(solution)/shard_map/all_gather | solution.py:163
  31.6 8.0 %copy-start.5 = (bf16[1024,512]{1,0:T(8,128)(2,1)S(1)}, bf16[1024,512]{1,0:T(8,128)(2,1)}, u32[]{:S(2)}) copy-start(bf16[1024,512]{1,0:T(8,128)(2,1)} %param.9) | copy-start | bytes 3145732
  39.7 59.3 %copy-start.6 = (bf16[2048,512]{1,0:T(8,128)(2,1)}, bf16[2048,512]{1,0:T(8,128)(2,1)S(1)}, u32[]{:S(2)}) copy-start(bf16[2048,512]{1,0:T(8,128)(2,1)S(1)} %constant_dynamic-update-slice_fusion) | copy-start | bytes 6291460
  60.8 3.3 %copy-start.2 = (bf16[1024,2048]{1,0:T(8,128)(2,1)S(1)}, bf16[1024,2048]{1,0:T(8,128)(2,1)}, u32[]{:S(2)}) copy-start(bf16[1024,2048]{1,0:T(8,128)(2,1)} %copy-done.1) | copy-start | bytes 12582916
  64.1 12.9 %copy-start.11 = (s32[1024]{0:T(1024)S(1)}, s32[1024]{0:T(1024)}, u32[]{:S(2)}) copy-start(s32[1024]{0:T(1024)} %param.16) | copy-start | bytes 12292
  66.8 32.2 %copy-start.7 = (bf16[512,512]{1,0:T(8,128)(2,1)S(1)}, bf16[512,512]{1,0:T(8,128)(2,1)}, u32[]{:S(2)}) copy-start(bf16[512,512]{1,0:T(8,128)(2,1)} %param.10) | copy-start | bytes 1572868
  67.7 9.5 %collective-permute-start.2 = (bf16[256,512]{1,0:T(8,128)(2,1)}, bf16[256,512]{1,0:T(8,128)(2,1)S(1)}, u32[]{:S(2)}, u32[]{:S(2)}) collective-permute-start(bf16[256,512]{1,0:T(8,128)(2,1)} %get-tuple-element.12), channel_id=1, source_target_pairs={{0,3},{1,0},{2,1},{3,2},{4,7},{5,4},{6,5},{7,6},{8,11},{9,8},{10,9... | collective-permute-start | bytes 786440 | tf_op jit(solution)/shard_map/ppermute | solution.py:65
  72.1 9.9 %collective-permute-start.1 = (bf16[256,512]{1,0:T(8,128)(2,1)}, bf16[256,512]{1,0:T(8,128)(2,1)}, u32[]{:S(2)}, u32[]{:S(2)}) collective-permute-start(bf16[256,512]{1,0:T(8,128)(2,1)} %get-tuple-element.13), channel_id=1, source_target_pairs={{0,2},{1,3},{2,0},{3,1},{4,6},{5,7},{6,4},{7,5},{8,10},{9,11},{10,... | collective-permute-start | bytes 786440 | tf_op jit(solution)/shard_map/ppermute | solution.py:65
  74.5 14.7 %collective-permute-start = (bf16[256,512]{1,0:T(8,128)(2,1)}, bf16[256,512]{1,0:T(8,128)(2,1)}, u32[]{:S(2)}, u32[]{:S(2)}) collective-permute-start(bf16[256,512]{1,0:T(8,128)(2,1)} %get-tuple-element.11), channel_id=1, source_target_pairs={{0,1},{1,2},{2,3},{3,0},{4,5},{5,6},{6,7},{7,4},{8,9},{9,10},{10,1... | collective-permute-start | bytes 786440 | tf_op jit(solution)/shard_map/ppermute | solution.py:65
  77.1 12.0 %copy-start.10 = (bf16[256,512]{1,0:T(8,128)(2,1)}, bf16[256,512]{1,0:T(8,128)(2,1)S(1)}, u32[]{:S(2)}) copy-start(bf16[256,512]{1,0:T(8,128)(2,1)S(1)} %collective-permute-done.2) | copy-start | bytes 786436
  90.6 15.7 %collective-permute-start.5 = (bf16[256,512]{1,0:T(8,128)(2,1)S(1)}, bf16[256,512]{1,0:T(8,128)(2,1)}, u32[]{:S(2)}, u32[]{:S(2)}) collective-permute-start(bf16[256,512]{1,0:T(8,128)(2,1)S(1)} %fusion.33), channel_id=1, source_target_pairs={{0,1},{1,2},{2,3},{3,0},{4,5},{5,6},{6,7},{7,4},{8,9},{9,10},{10,1... | collective-permute-start | bytes 786440 | tf_op jit(solution)/shard_map/ppermute | solution.py:65
  92.5 13.7 %collective-permute-start.4 = (bf16[256,512]{1,0:T(8,128)(2,1)S(1)}, bf16[256,512]{1,0:T(8,128)(2,1)}, u32[]{:S(2)}, u32[]{:S(2)}) collective-permute-start(bf16[256,512]{1,0:T(8,128)(2,1)S(1)} %fusion.33), channel_id=1, source_target_pairs={{0,2},{1,3},{2,0},{3,1},{4,6},{5,7},{6,4},{7,5},{8,10},{9,11},{10,... | collective-permute-start | bytes 786440 | tf_op jit(solution)/shard_map/ppermute | solution.py:65
  94.8 14.1 %collective-permute-start.3 = (bf16[256,512]{1,0:T(8,128)(2,1)S(1)}, bf16[256,512]{1,0:T(8,128)(2,1)}, u32[]{:S(2)}, u32[]{:S(2)}) collective-permute-start(bf16[256,512]{1,0:T(8,128)(2,1)S(1)} %fusion.33), channel_id=1, source_target_pairs={{0,3},{1,0},{2,1},{3,2},{4,7},{5,4},{6,5},{7,6},{8,11},{9,8},{10,9... | collective-permute-start | bytes 786440 | tf_op jit(solution)/shard_map/ppermute | solution.py:65
  115.5 3.6 %copy-start.14 = (bf16[1024,512]{1,0:T(8,128)(2,1)}, bf16[1024,512]{1,0:T(8,128)(2,1)S(1)}, u32[]{:S(2)}) copy-start(bf16[1024,512]{1,0:T(8,128)(2,1)S(1)} %multiply_convert_fusion) | copy-start | bytes 3145732
  120.8 67.2 %copy-start.15 = (bf16[1024,512]{1,0:T(8,128)(2,1)S(1)}, bf16[1024,512]{1,0:T(8,128)(2,1)}, u32[]{:S(2)}) copy-start(bf16[1024,512]{1,0:T(8,128)(2,1)} %copy-done.14) | copy-start | bytes 3145732
  192.4 14.4 %collective-permute-start.8 = (bf16[256,512]{1,0:T(8,128)(2,1)S(1)}, bf16[256,512]{1,0:T(8,128)(2,1)S(1)}, u32[]{:S(2)}, u32[]{:S(2)}) collective-permute-start(bf16[256,512]{1,0:T(8,128)(2,1)S(1)} %get-tuple-element.9), channel_id=1, source_target_pairs={{0,3},{1,0},{2,1},{3,2},{4,7},{5,4},{6,5},{7,6},{8,11},{9,8},{10,9... | collective-permute-start | bytes 786440 | tf_op jit(solution)/shard_map/ppermute | solution.py:65
  196.6 15.3 %collective-permute-start.7 = (bf16[256,512]{1,0:T(8,128)(2,1)S(1)}, bf16[256,512]{1,0:T(8,128)(2,1)S(1)}, u32[]{:S(2)}, u32[]{:S(2)}) collective-permute-start(bf16[256,512]{1,0:T(8,128)(2,1)S(1)} %get-tuple-element.10), channel_id=1, source_target_pairs={{0,2},{1,3},{2,0},{3,1},{4,6},{5,7},{6,4},{7,5},{8,10},{9,11},{10,... | collective-permute-start | bytes 786440 | tf_op jit(solution)/shard_map/ppermute | solution.py:65
  198.5 20.5 %collective-permute-start.6 = (bf16[256,512]{1,0:T(8,128)(2,1)S(1)}, bf16[256,512]{1,0:T(8,128)(2,1)S(1)}, u32[]{:S(2)}, u32[]{:S(2)}) collective-permute-start(bf16[256,512]{1,0:T(8,128)(2,1)S(1)} %get-tuple-element.8), channel_id=1, source_target_pairs={{0,1},{1,2},{2,3},{3,0},{4,5},{5,6},{6,7},{7,4},{8,9},{9,10},{10,1... | collective-permute-start | bytes 786440 | tf_op jit(solution)/shard_map/ppermute | solution.py:65
  (4 other events, 9.1 us)
Sparse Core Ops, SparseCore 0:
  33.7 29.1 all-gather.2
  188.2 29.2 all-gather.4

commit v3 on v2

v3 whole, which is shorter than its diff:
```python
import jax
import jax.numpy as jnp
from jax import lax
from jax.experimental import pallas as pl
from jax.experimental.pallas import tpu as pltpu
from jax.sharding import Mesh
from jax.sharding import PartitionSpec as P

BLOCK = 64
LANES = 128
WIDE = ("y", "z", "core")
F32 = jnp.float32
BF16 = jnp.bfloat16
VMEM = pl.BlockSpec(memory_space=pltpu.VMEM)
SMEM = pl.BlockSpec(memory_space=pltpu.SMEM)


def dot(left, right, left_dim, right_dim):
    dims = (((left_dim,), (right_dim,)), ((), ()))
    return lax.dot_general(left, right, dims, preferred_element_type=F32)


def call(kernel, name, outs, in_specs, args, flops, scratch=(), vmem=24):
    moved = sum(a.size * a.dtype.itemsize for a in args) + sum(
        o.size * o.dtype.itemsize for o in outs
    )
    return pl.pallas_call(
        kernel,
        out_shape=outs,
        in_specs=in_specs,
        out_specs=[VMEM] * len(outs),
        scratch_shapes=scratch,
        compiler_params=pltpu.CompilerParams(vmem_limit_bytes=vmem << 20),
        cost_estimate=pl.CostEstimate(flops=flops, bytes_accessed=moved, transcendentals=0),
        name=name,
    )(*args)


def shape(rows, cols, dtype):
    return jax.ShapeDtypeStruct((rows, cols), dtype)


def count_kernel(place_ref, words_ref, local_ref, halo_ref, counts_ref):
    counts_ref[...] = jnp.zeros_like(counts_ref)
    row = lax.broadcasted_iota(jnp.int32, (BLOCK, LANES), 0)
    lane = lax.broadcasted_iota(jnp.int32, (BLOCK, LANES), 1)
    word_lane = (row % 32) * 4 + (lane % BLOCK) // 16
    shift = lane % 16
    half = lane // BLOCK

    def add_tile(t, carry):
        place = place_ref[t]
        dst = pl.multiple_of((place // 64) * BLOCK, BLOCK)
        src = place % 64
        upper = jnp.broadcast_to(words_ref[pl.ds(2 * t, 1), :], (32, LANES))
        lower = jnp.broadcast_to(words_ref[pl.ds(2 * t + 1, 1), :], (32, LANES))
        words = jnp.concatenate([upper, lower], axis=0)
        picked = jnp.take_along_axis(words, word_lane, axis=1)
        bits = jnp.right_shift(picked, shift) & 1
        tile = jnp.where(half == src % 2, bits, 0).astype(F32).astype(BF16)
        rows = pl.ds(dst, BLOCK)
        cols = pl.ds(pl.multiple_of((src // 2) * LANES, LANES), LANES)
        counts_ref[rows, cols] = counts_ref[rows, cols] + tile
        return carry

    lax.fori_loop(0, place_ref.shape[0], add_tile, 0, unroll=4)
    split = local_ref.shape[1]
    local_ref[...] = counts_ref[:, :split]
    halo_ref[...] = counts_ref[:, split:]


def sum_kernel(counts_ref, incoming_ref, local_ref, own_ref, *send_refs):
    quarter = own_ref.shape[0]
    for k in (*range(1, 1 + len(send_refs)), 0):
        rows = pl.ds(k * quarter, quarter)
        total = dot(counts_ref[rows, :], incoming_ref[...], 1, 0) + local_ref[rows, :]
        if k:
            send_refs[k - 1][...] = total.astype(BF16)
        else:
            own_ref[...] = total


def dense_kernel(
    rep_ref, agg0, agg1, agg2, agg3, pre_ref, grad_ref, w_self_ref, w_neigh_ref, scale_ref,
    share_ref, halo_t_ref, out_ref, own_ref, grad_agg_ref, joint_ref,
):
    aggs = (agg0, agg1, agg2, agg3)
    quarter, feat_width = agg0.shape
    share = feat_width // len(aggs)
    share_cols = pl.ds(pl.multiple_of(rep_ref[0] * share, LANES), share)
    w_neigh = w_neigh_ref[...]
    grad_self = jnp.zeros((share, feat_width), F32)
    grad_neigh = jnp.zeros((share, feat_width), F32)
    for k, agg_ref in enumerate(aggs):
        rows = pl.ds(k * quarter, quarter)
        pre = pre_ref[rows, :] + dot(agg_ref[...], w_neigh, 1, 0)
        sigmoid = jax.nn.sigmoid(pre)
        grad_pre = (
            grad_ref[rows, :].astype(F32) * sigmoid * (1.0 + pre * (1.0 - sigmoid))
        ).astype(BF16)
        if k == 0:
            out_ref[...] = (pre * sigmoid).astype(BF16)
            own_ref[...] = dot(grad_pre, w_self_ref[...], 1, 1)
        grad_agg_ref[rows, :] = (dot(grad_pre, w_neigh, 1, 1) * scale_ref[rows, :]).astype(BF16)
        grad_self = grad_self + dot(share_ref[rows, :], grad_pre, 0, 0)
        grad_neigh = grad_neigh + dot(agg_ref[:, share_cols], grad_pre, 0, 0)
    tile = 0
    peers = joint_ref.shape[0] // 8
    lanes = joint_ref.shape[1] - feat_width
    per_peer = lanes // LANES
    for part in (grad_self, grad_neigh):
        for g in range(0, share, 8):
            for c in range(0, feat_width, LANES):
                peer, slot = tile // per_peer, tile % per_peer
                joint_ref[peer * 8 : peer * 8 + 8, feat_width + slot * LANES : feat_width + (slot + 1) * LANES] = (
                    part[g : g + 8, c : c + LANES].astype(BF16)
                )
                tile += 1
    halo_rows = halo_t_ref.shape[0]
    step = min(256, halo_rows)
    for at in range(0, halo_rows, step):
        rows = pl.ds(at, step)
        joint_ref[rows, :feat_width] = dot(halo_t_ref[rows, :], grad_agg_ref[...], 1, 0).astype(BF16)


def return_kernel(slots_ref, joint_ref, local_ref, base_ref, tile_ref, own_ref, *send_refs):
    quarter, feat_width = own_ref.shape
    halo_rows = joint_ref.shape[0]
    slots = jnp.broadcast_to(slots_ref[...], (quarter, halo_rows))
    row = lax.broadcasted_iota(jnp.int32, (quarter, halo_rows), 0)
    for k in (*range(1, 1 + len(send_refs)), 0):
        rows = pl.ds(k * quarter, quarter)
        pick = jnp.where(row + k * quarter == slots, 1.0, 0.0).astype(BF16)
        total = dot(pick, joint_ref[:, :feat_width], 1, 0) + local_ref[rows, :]
        if k:
            send_refs[k - 1][...] = total.astype(BF16)
        else:
            own_ref[...] = total + base_ref[...]
    tiles = joint_ref[:, feat_width:].astype(F32)
    tile_ref[...] = tiles.reshape(halo_rows // 8, 8, tiles.shape[1]).sum(axis=0).astype(BF16)


def place_kernel(rep_ref, part0, part1, part2, part3, self_ref, neigh_ref):
    parts = (part0, part1, part2, part3)
    share = part0.shape[0] // 2
    for k, part in enumerate(parts):
        at = pl.ds(pl.multiple_of(((rep_ref[0] + k) % len(parts)) * share, share), share)
        self_ref[at, :] = part[:share, :]
        neigh_ref[at, :] = part[share:, :]


def send_to(x, step, replicas):
    return lax.ppermute(x, "rep", [(i, (i + step) % replicas) for i in range(replicas)])


def from_ahead(x, replicas):
    return [send_to(x, replicas - k, replicas) for k in range(1, replicas)]


def on_device(
    node_feats, w_self, w_neigh, send_rows, tile_dst, tile_src, tile_bits, norm_count, grad_out
):
    node_rows, feat_width = node_feats.shape
    peer_count = lax.axis_size(WIDE)
    replicas = lax.axis_size("rep")
    slot_count = send_rows.shape[2]
    tile_total = tile_dst.shape[2]
    quarter = node_rows // replicas
    share = feat_width // replicas
    rep_index = lax.axis_index("rep")
    rep_ref = rep_index.reshape(1).astype(jnp.int32)
    dst_count = node_rows // BLOCK
    halo_rows = peer_count * slot_count
    first_row = rep_index * quarter
    first_block = rep_index * (quarter // BLOCK)
    send_outs = [shape(quarter, feat_width, BF16)] * (replicas - 1)

    def turned(x, axis=0):
        twice = jnp.concatenate([x, x], axis=axis)
        return lax.dynamic_slice_in_dim(twice, first_row, node_rows, axis)

    slot_rows = send_rows[0].reshape(-1)
    every_row = lax.broadcasted_iota(jnp.int32, (node_rows, halo_rows), 0)
    send_pick = (every_row == slot_rows[None, :]).astype(BF16)
    outgoing = dot(send_pick, node_feats, 0, 0).astype(BF16)
    incoming = lax.all_to_all(outgoing, WIDE, 0, 0, tiled=True)

    feats = turned(node_feats)
    scale = turned(lax.rsqrt(norm_count.astype(F32)))[:, None]
    grad_out_all = jnp.concatenate([grad_out] + from_ahead(grad_out, replicas), axis=0)
    dst = (tile_dst[0, 0] - first_block) % dst_count
    src = tile_src[0, 0]
    src = jnp.where(src < dst_count, (src - first_block) % dst_count, src)
    counts_local, counts_halo = call(
        count_kernel,
        "tile_counts",
        [shape(node_rows, node_rows, BF16), shape(node_rows, halo_rows, BF16)],
        [SMEM, VMEM],
        (dst * 64 + src, tile_bits.reshape(tile_total * 2, LANES)),
        tile_total * BLOCK * LANES * 20,
        scratch=[pltpu.VMEM((node_rows, node_rows + halo_rows), BF16)],
    )
    sums_local = dot(counts_local, feats, 1, 0)
    pre_self = dot(feats, w_self, 1, 0)
    feats_share = lax.dynamic_slice_in_dim(feats, rep_index * share, share, 1)
    turned_slots = ((slot_rows - first_row) % node_rows)[None, :]
    halo_t = counts_halo.T
    (
        incoming, sums_local, pre_self, feats_share, halo_t, counts_local, counts_halo, grad_out_all, scale,
        turned_slots,
    ) = lax.optimization_barrier(
        (
            incoming, sums_local, pre_self, feats_share, halo_t, counts_local, counts_halo, grad_out_all, scale,
            turned_slots,
        )
    )

    block_flops = 2 * node_rows * halo_rows * feat_width
    own_sums, *sends = call(
        sum_kernel,
        "neighbour_sums",
        [shape(quarter, feat_width, F32)] + send_outs,
        [VMEM] * 3,
        (counts_halo, incoming, sums_local),
        block_flops,
    )
    for k in range(1, replicas):
        own_sums = own_sums + send_to(sends[k - 1], k, replicas).astype(F32)
    own_agg = (own_sums * scale[:quarter]).astype(BF16)
    aggs = [own_agg] + from_ahead(own_agg, replicas)
    out_feats, own_base, grad_agg, joint = call(
        dense_kernel,
        "dense",
        [
            shape(quarter, feat_width, BF16),
            shape(quarter, feat_width, F32),
            shape(node_rows, feat_width, BF16),
            shape(halo_rows, feat_width + 2 * share * feat_width // halo_rows, BF16),
        ],
        [SMEM] + [VMEM] * 11,
        (rep_ref, *aggs, pre_self, grad_out_all, w_self, w_neigh, scale, feats_share, halo_t),
        2 * block_flops,
    )
    returned = lax.all_to_all(joint, WIDE, 0, 0, tiled=True)
    grad_local = dot(counts_local, grad_agg, 0, 0)
    returned, grad_local = lax.optimization_barrier((returned, grad_local))

    tile, own_grad, *sends = call(
        return_kernel,
        "returned_rows",
        [shape(slot_count, joint.shape[1] - feat_width, BF16), shape(quarter, feat_width, F32)]
        + send_outs,
        [VMEM] * 4,
        (turned_slots, returned, grad_local, own_base),
        block_flops,
    )
    for k in range(1, replicas):
        own_grad = own_grad + send_to(sends[k - 1], k, replicas).astype(F32)

    copies = jnp.broadcast_to(tile, (peer_count,) + tile.shape)
    tiles = lax.all_to_all(copies, WIDE, 0, 0, tiled=True)
    lane_tiles = feat_width // LANES
    own_share = (
        tiles.reshape(peer_count, slot_count, -1, LANES)
        .transpose(0, 2, 1, 3)
        .reshape(-1, lane_tiles, slot_count, LANES)
        .transpose(0, 2, 1, 3)
        .reshape(2 * share, feat_width)
    )
    grad_self, grad_neigh = call(
        place_kernel,
        "place",
        [shape(feat_width, feat_width, BF16)] * 2,
        [SMEM] + [VMEM] * replicas,
        (rep_ref, own_share, *from_ahead(own_share, replicas)),
        0,
    )
    return out_feats, own_grad.astype(BF16), grad_self, grad_neigh


def solution(mesh):
    fine = Mesh(
        mesh.devices.reshape(8, mesh.shape["wide"] // 16, 2, mesh.shape["rep"]), WIDE + ("rep",)
    )
    in_specs = (
        P(WIDE, None),
        P(),
        P(),
        P(WIDE, None, "rep"),
        P(WIDE, "rep", None),
        P(WIDE, "rep", None),
        P(WIDE, "rep", None),
        P(WIDE),
        P(WIDE + ("rep",), None),
    )
    out_specs = (P(WIDE + ("rep",), None), P(WIDE + ("rep",), None), P(), P())
    return jax.shard_map(
        on_device, mesh=fine, in_specs=in_specs, out_specs=out_specs, check_vma=False
    )
```

time: 230 us -> 205 us (0.89)
  blocking collectives: 65.9 us -> 0 us
  starting transfers between devices: 45.4 us -> 93.8 us
  matrix products: 26.7 us -> 12.1 us
  between operations: 14.4 us -> 1.02 us
  local copies, waits for them, and re-layouts: 7.44 us -> 20.8 us
  Pallas kernels: 5.98 us -> 14.4 us
  other arithmetic: 5.69 us -> 3.35 us
    all_to_all x2 -> x0, blocking collectives: 65.9 us -> none  [the longest x1 44 us: on_device(): lax.all_to_all(jnp.concatenate([halo_grad.reshape(peer_count, slot_count,...]
    ppermute x9 -> x15, starting transfers between devices: 26.3 us -> 51 us  [send_to(): lax.ppermute(x, 'rep', [(i, (i + step) % replicas) for i in range(replica...]
    all_to_all x1 -> x3, starting transfers between devices: 19 us -> 42.8 us  [the longest x1 18.6 us: on_device(): incoming = lax.all_to_all(outgoing, WIDE, 0, 0, tiled=True)]
    all_to_all x1 -> x3, waiting for transfers between devices: 21.1 us -> 36.5 us  [the longest x1 31.7 us: on_device(): returned = lax.all_to_all(joint, WIDE, 0, 0, tiled=True)]
    ppermute x9 -> x15, waiting for transfers between devices: 35.9 us -> 21.1 us  [send_to(): lax.ppermute(x, 'rep', [(i, (i + step) % replicas) for i in range(replica...]
    dot_general x12 -> x4, matrix products: 26.7 us -> 12.1 us  [dot(): return lax.dot_general(left, right, dims, preferred_element_type=F32)]
    unnamed x34 -> x42, local copies, waits for them, and re-layouts: 4.05 us -> 15.5 us
    pallas_call x1 -> x5, Pallas kernels: 5.98 us -> 14.4 us  [call(): pl.pallas_call(kernel, out_shape=outs, in_specs=in_specs, out_specs=[VMEM...]
  transfers between devices with their start and end apart: 12 -> 18, of which waited for: 8 -> 8; matrix products, arithmetic and copies ran while one was open for 8% -> 9% of each run, Pallas kernels for 3% -> 3%
where the time goes in v3:
time: 205 us; the launch traced here: 203 us
  starting transfers between devices  93.8 us (46%)
  waiting for transfers between devices  57.7 us (28%)
  local copies, waits for them, and re-layouts  20.8 us (10%)
  Pallas kernels  14.4 us (7%)
  matrix products  12.1 us (6%)
  other arithmetic  3.35 us (2%)
    ppermute x15, starting transfers between devices, send_to(): lax.ppermute(x, 'rep', [(i, (i + step) % replicas) for i in range(replica...  51 us
    all_to_all x1, waiting for transfers between devices, on_device(): returned = lax.all_to_all(joint, WIDE, 0, 0, tiled=True)  31.7 us
    ppermute x15, waiting for transfers between devices, send_to(): lax.ppermute(x, 'rep', [(i, (i + step) % replicas) for i in range(replica...  21.1 us
    all_to_all x1, starting transfers between devices, on_device(): incoming = lax.all_to_all(outgoing, WIDE, 0, 0, tiled=True)  18.6 us
    all_to_all x1, starting transfers between devices, on_device(): returned = lax.all_to_all(joint, WIDE, 0, 0, tiled=True)  16.6 us
    unnamed x42, local copies, waits for them, and re-layouts  15.5 us
    pallas_call x5, Pallas kernels, call(): pl.pallas_call(kernel, out_shape=outs, in_specs=in_specs, out_specs=[VMEM...  14.4 us
    dot_general x4, matrix products, dot(): return lax.dot_general(left, right, dims, preferred_element_type=F32)  12.1 us
  transfers between devices with their start and end apart: 18, of which 8 were waited for; matrix products, arithmetic and copies ran while one was open for 9% of the time, Pallas kernels for 3%

profile of v3, /device:TPU:1, one launch (start us, length us, event | category | flops | bytes accessed | tf_op | source)
XLA Modules:
  0.0 203.1 jit_solution(909060241010161043)
XLA Ops:
  1.5 3.5 %fusion.3 = bf16[128,8,512]{2,1,0:T(8,128)(2,1)} fusion(bf16[1024,512]{1,0:T(8,128)(2,1)} %param.9, s32[1024]{0:T(1024)S(1)} %eq.15), kind=kOutput, calls=%fused_computation.4 | convolution fusion | flops 1075314688 | bytes 2101248 | tf_op jit(solution)/shard_map/dot_general | solution.py:20
  5.0 18.6 %all-to-all-start = ((bf16[128,8,512]{2,1,0:T(8,128)(2,1)}), bf16[128,8,512]{2,1,0:T(8,128)(2,1)S(1)}, u32[]{:S(2)}, u32[]{:S(2)}) async-start(bf16[128,8,512]{2,1,0:T(8,128)(2,1)} %fusion.3), calls=%async_computation | async-start | bytes 2097152 | tf_op jit(solution)/shard_map/all_to_all | solution.py:186
  23.6 4.7 %collective-permute-start.1 = (bf16[256,512]{1,0:T(8,128)(2,1)}, bf16[256,512]{1,0:T(8,128)(2,1)}, u32[]{:S(2)}, u32[]{:S(2)}) collective-permute-start(bf16[256,512]{1,0:T(8,128)(2,1)} %param.17), channel_id=1, source_target_pairs={{0,2},{1,3},{2,0},{3,1},{4,6},{5,7},{6,4},{7,5},{8,10},{9,11},{10,... | collective-permute-start | bytes 786440 | tf_op jit(solution)/shard_map/ppermute | solution.py:153
  28.3 2.8 %collective-permute-start = (bf16[256,512]{1,0:T(8,128)(2,1)}, bf16[256,512]{1,0:T(8,128)(2,1)}, u32[]{:S(2)}, u32[]{:S(2)}) collective-permute-start(bf16[256,512]{1,0:T(8,128)(2,1)} %param.17), channel_id=1, source_target_pairs={{0,3},{1,0},{2,1},{3,2},{4,7},{5,4},{6,5},{7,6},{8,11},{9,8},{10,9... | collective-permute-start | bytes 786440 | tf_op jit(solution)/shard_map/ppermute | solution.py:153
  31.0 2.5 %collective-permute-start.2 = (bf16[256,512]{1,0:T(8,128)(2,1)}, bf16[256,512]{1,0:T(8,128)(2,1)}, u32[]{:S(2)}, u32[]{:S(2)}) collective-permute-start(bf16[256,512]{1,0:T(8,128)(2,1)} %param.17), channel_id=1, source_target_pairs={{0,1},{1,2},{2,3},{3,0},{4,5},{5,6},{6,7},{7,4},{8,9},{9,10},{10,1... | collective-permute-start | bytes 786440 | tf_op jit(solution)/shard_map/ppermute | solution.py:153
  33.8 6.2 %tile_counts.1 = (bf16[1024,1024]{1,0:T(8,128)(2,1)S(1)}, bf16[1024,1024]{1,0:T(8,128)(2,1)S(1)}) custom-call(s32[128]{0:T(128)S(1)} %fusion.11.place_ref, s32[256,128]{1,0:T(8,128)S(1)} %bitcast.35), custom_call_target="tpu_custom_call" | custom-call | flops 20971520 | bytes 4325888 | tf_op jit(solution)/shard_map/tile_counts/pallas_call | solution.py:27
  41.5 2.5 %copy.16 = bf16[1024,1024]{0,1:T(8,128)(2,1)} copy(bf16[1024,1024]{1,0:T(8,128)(2,1)S(1)} %get-tuple-element.35.counts_ref) | data formatting | bytes 4194304 | tf_op jit(solution)/shard_map/tile_counts/pallas_call | solution.py:27
  47.1 2.7 %fusion.6.local_ref = f32[1024,512]{1,0:T(8,128)} fusion(bf16[1024,1024]{1,0:T(8,128)(2,1)S(1)} %copy-done.10, bf16[2048,512]{1,0:T(8,128)(2,1)S(1)} %constant_dynamic-update-slice_fusion, s32[]{:T(128)S(6)} %select_n.42), kind=kOutput, calls=%fused_computation.8 | convolution fusion | flops 1073741824 | bytes 5242884 | tf_op jit(solution)/shard_map/dot_general | solution.py:20
  57.0 3.2 %collective-permute-start.3 = (bf16[256,512]{1,0:T(8,128)(2,1)S(1)}, bf16[256,512]{1,0:T(8,128)(2,1)S(1)}, u32[]{:S(2)}, u32[]{:S(2)}) collective-permute-start(bf16[256,512]{1,0:T(8,128)(2,1)S(1)} %get-tuple-element.39), channel_id=1, source_target_pairs={{0,1},{1,2},{2,3},{3,0},{4,5},{5,6},{6,7},{7,4},{8,9},{9,10},{10,1... | collective-permute-start | bytes 786440 | tf_op jit(solution)/shard_map/ppermute | solution.py:153
  60.2 4.4 %collective-permute-start.4 = (bf16[256,512]{1,0:T(8,128)(2,1)S(1)}, bf16[256,512]{1,0:T(8,128)(2,1)S(1)}, u32[]{:S(2)}, u32[]{:S(2)}) collective-permute-start(bf16[256,512]{1,0:T(8,128)(2,1)S(1)} %get-tuple-element.40), channel_id=1, source_target_pairs={{0,2},{1,3},{2,0},{3,1},{4,6},{5,7},{6,4},{7,5},{8,10},{9,11},{10,... | collective-permute-start | bytes 786440 | tf_op jit(solution)/shard_map/ppermute | solution.py:153
  64.6 3.1 %collective-permute-start.5 = (bf16[256,512]{1,0:T(8,128)(2,1)S(1)}, bf16[256,512]{1,0:T(8,128)(2,1)S(1)}, u32[]{:S(2)}, u32[]{:S(2)}) collective-permute-start(bf16[256,512]{1,0:T(8,128)(2,1)S(1)} %get-tuple-element.41), channel_id=1, source_target_pairs={{0,3},{1,0},{2,1},{3,2},{4,7},{5,4},{6,5},{7,6},{8,11},{9,8},{10,9... | collective-permute-start | bytes 786440 | tf_op jit(solution)/shard_map/ppermute | solution.py:153
  67.7 5.6 %collective-permute-done.4 = bf16[256,512]{1,0:T(8,128)(2,1)S(1)} collective-permute-done((bf16[256,512]{1,0:T(8,128)(2,1)S(1)}, bf16[256,512]{1,0:T(8,128)(2,1)S(1)}, u32[]{:S(2)}, u32[]{:S(2)}) %collective-permute-start.4) | collective-permute-done | bytes 262176 | tf_op jit(solution)/shard_map/ppermute | solution.py:153
  75.0 5.5 %collective-permute-start.8 = (bf16[256,512]{1,0:T(8,128)(2,1)S(1)}, bf16[256,512]{1,0:T(8,128)(2,1)S(1)}, u32[]{:S(2)}, u32[]{:S(2)}) collective-permute-start(bf16[256,512]{1,0:T(8,128)(2,1)S(1)} %multiply_convert_fusion.agg0), channel_id=1, source_target_pairs={{0,1},{1,2},{2,3},{3,0},{4,5},{5,6},{6,7},{7,4},{8,9},{9,10},{10,1... | collective-permute-start | bytes 786440 | tf_op jit(solution)/shard_map/ppermute | solution.py:153
  83.0 3.7 %collective-permute-start.6 = (bf16[256,512]{1,0:T(8,128)(2,1)S(1)}, bf16[256,512]{1,0:T(8,128)(2,1)}, u32[]{:S(2)}, u32[]{:S(2)}) collective-permute-start(bf16[256,512]{1,0:T(8,128)(2,1)S(1)} %multiply_convert_fusion.agg0), channel_id=1, source_target_pairs={{0,3},{1,0},{2,1},{3,2},{4,7},{5,4},{6,5},{7,6},{8,11},{9,8},{10,9... | collective-permute-start | bytes 786440 | tf_op jit(solution)/shard_map/ppermute | solution.py:153
  87.0 5.4 %collective-permute-done.7.agg2 = bf16[256,512]{1,0:T(8,128)(2,1)} collective-permute-done((bf16[256,512]{1,0:T(8,128)(2,1)S(1)}, bf16[256,512]{1,0:T(8,128)(2,1)}, u32[]{:S(2)}, u32[]{:S(2)}) %collective-permute-start.7) | collective-permute-done | bytes 262176 | tf_op jit(solution)/shard_map/ppermute | solution.py:153
  98.3 4.5 %dense.1 = (bf16[256,512]{1,0:T(8,128)(2,1)}, f32[256,512]{1,0:T(8,128)S(1)}, bf16[1024,512]{1,0:T(8,128)(2,1)S(1)}, bf16[1024,640]{1,0:T(8,128)(2,1)S(1)}) custom-call(s32[1]{0:T(128)} %bitcast.rep_ref, bf16[256,512]{1,0:T(8,128)(2,1)S(1)} %multiply_convert_fusion.agg0, bf16[256,512]{1,0:T(8,128)(2,1)} %collective-permute-done.6.agg1, ...), custom_call_target="tpu_custom_call" | custom-call | flops 2147483648 | bytes 10752004 | tf_op jit(solution)/shard_map/dense/pallas_call | solution.py:27
  105.6 16.6 %all-to-all-start.1 = ((bf16[128,8,640]{2,1,0:T(8,128)(2,1)}), bf16[128,8,640]{2,1,0:T(8,128)(2,1)S(1)}, u32[]{:S(2)}, u32[]{:S(2)}) async-start(bf16[128,8,640]{2,1,0:T(8,128)(2,1)} %bitcast.29), calls=%async_computation.1 | async-start | bytes 2621440 | tf_op jit(solution)/shard_map/all_to_all | solution.py:244
  122.2 3.9 %fusion.16.local_ref = f32[1024,512]{1,0:T(8,128)} fusion(bf16[1024,1024]{1,0:T(8,128)(2,1)S(1)} %copy-done.11, bf16[1024,512]{1,0:T(8,128)(2,1)} %copy-done.12), kind=kOutput, calls=%fused_computation.37 | convolution fusion | flops 1073741824 | bytes 5242880 | tf_op jit(solution)/shard_map/dot_general | solution.py:20
  126.1 31.7 %all-to-all-done.1 = bf16[128,8,640]{2,1,0:T(8,128)(2,1)S(1)} async-done(((bf16[128,8,640]{2,1,0:T(8,128)(2,1)}), bf16[128,8,640]{2,1,0:T(8,128)(2,1)S(1)}, u32[]{:S(2)}, u32[]{:S(2)}) %all-to-all-start.1) | async-done | bytes 1310752 | tf_op jit(solution)/shard_map/all_to_all | solution.py:244
  162.5 7.6 %all-to-all-start.2 = ((bf16[128,8,128]{2,1,0:T(8,128)(2,1)}), bf16[128,8,128]{2,1,0:T(8,128)(2,1)S(1)}, u32[]{:S(2)}, u32[]{:S(2)}) async-start(bf16[128,8,128]{2,1,0:T(8,128)(2,1)} %broadcast_in_dim.8), calls=%async_computation.2 | async-start | bytes 524288 | tf_op jit(solution)/shard_map/all_to_all | solution.py:261
  172.0 5.5 %collective-permute-start.10 = (bf16[256,512]{1,0:T(8,128)(2,1)S(1)}, bf16[256,512]{1,0:T(8,128)(2,1)S(1)}, u32[]{:S(2)}, u32[]{:S(2)}) collective-permute-start(bf16[256,512]{1,0:T(8,128)(2,1)S(1)} %get-tuple-element.57), channel_id=1, source_target_pairs={{0,2},{1,3},{2,0},{3,1},{4,6},{5,7},{6,4},{7,5},{8,10},{9,11},{10,... | collective-permute-start | bytes 786440 | tf_op jit(solution)/shard_map/ppermute | solution.py:153
  179.4 4.9 %all-to-all-done.2 = bf16[128,8,128]{2,1,0:T(8,128)(2,1)S(1)} async-done(((bf16[128,8,128]{2,1,0:T(8,128)(2,1)}), bf16[128,8,128]{2,1,0:T(8,128)(2,1)S(1)}, u32[]{:S(2)}, u32[]{:S(2)}) %all-to-all-start.2) | async-done | bytes 262176 | tf_op jit(solution)/shard_map/all_to_all | solution.py:261
  186.2 5.5 %collective-permute-start.13 = (bf16[256,512]{1,0:T(8,128)(2,1)S(1)}, bf16[256,512]{1,0:T(8,128)(2,1)S(1)}, u32[]{:S(2)}, u32[]{:S(2)}) collective-permute-start(bf16[256,512]{1,0:T(8,128)(2,1)S(1)} %bitcast.32), channel_id=1, source_target_pairs={{0,2},{1,3},{2,0},{3,1},{4,6},{5,7},{6,4},{7,5},{8,10},{9,11},{10,... | collective-permute-start | bytes 786440 | tf_op jit(solution)/shard_map/ppermute | solution.py:153
  194.5 5.4 %collective-permute-done.13.part2 = bf16[256,512]{1,0:T(8,128)(2,1)S(1)} collective-permute-done((bf16[256,512]{1,0:T(8,128)(2,1)S(1)}, bf16[256,512]{1,0:T(8,128)(2,1)S(1)}, u32[]{:S(2)}, u32[]{:S(2)}) %collective-permute-start.13) | collective-permute-done | bytes 262176 | tf_op jit(solution)/shard_map/ppermute | solution.py:153
  (80 shorter events, 42.3 us)
Async XLA Ops:
  5.0 28.6 %copy-start.16 = (s32[1,128,8]{1,2,0:T(8,128)S(1)}, s32[1,128,8]{1,2,0:T(8,128)}, u32[]{:S(2)}) copy-start(s32[1,128,8]{1,2,0:T(8,128)} %param.12) | copy-start | bytes 12292
  5.0 28.8 %copy-start.18 = (s32[1,1,128]{2,1,0:T(1,128)S(1)}, s32[1,1,128]{2,1,0:T(1,128)}, u32[]{:S(2)}) copy-start(s32[1,1,128]{2,1,0:T(1,128)} %param.14) | copy-start | bytes 1540
  5.0 28.8 %copy-start.19 = (s32[1,1,128]{2,1,0:T(1,128)S(1)}, s32[1,1,128]{2,1,0:T(1,128)}, u32[]{:S(2)}) copy-start(s32[1,1,128]{2,1,0:T(1,128)} %param.13) | copy-start | bytes 1540
  5.0 28.8 %copy-start.8 = (s32[1,1,32768]{2,1,0:T(1,128)S(1)}, s32[1,1,32768]{2,1,0:T(1,128)}, u32[]{:S(2)}) copy-start(s32[1,1,32768]{2,1,0:T(1,128)} %param.15) | copy-start | bytes 393220
  5.0 49.1 %all-to-all-start = ((bf16[128,8,512]{2,1,0:T(8,128)(2,1)}), bf16[128,8,512]{2,1,0:T(8,128)(2,1)S(1)}, u32[]{:S(2)}, u32[]{:S(2)}) async-start(bf16[128,8,512]{2,1,0:T(8,128)(2,1)} %fusion.3), calls=%async_computation | async-start | bytes 2097152 | tf_op jit(solution)/shard_map/all_to_all | solution.py:186
  23.6 28.2 %collective-permute-start.1 = (bf16[256,512]{1,0:T(8,128)(2,1)}, bf16[256,512]{1,0:T(8,128)(2,1)}, u32[]{:S(2)}, u32[]{:S(2)}) collective-permute-start(bf16[256,512]{1,0:T(8,128)(2,1)} %param.17), channel_id=1, source_target_pairs={{0,2},{1,3},{2,0},{3,1},{4,6},{5,7},{6,4},{7,5},{8,10},{9,11},{10,... | collective-permute-start | bytes 786440 | tf_op jit(solution)/shard_map/ppermute | solution.py:153
  28.3 23.6 %collective-permute-start = (bf16[256,512]{1,0:T(8,128)(2,1)}, bf16[256,512]{1,0:T(8,128)(2,1)}, u32[]{:S(2)}, u32[]{:S(2)}) collective-permute-start(bf16[256,512]{1,0:T(8,128)(2,1)} %param.17), channel_id=1, source_target_pairs={{0,3},{1,0},{2,1},{3,2},{4,7},{5,4},{6,5},{7,6},{8,11},{9,8},{10,9... | collective-permute-start | bytes 786440 | tf_op jit(solution)/shard_map/ppermute | solution.py:153
  31.0 20.8 %collective-permute-start.2 = (bf16[256,512]{1,0:T(8,128)(2,1)}, bf16[256,512]{1,0:T(8,128)(2,1)}, u32[]{:S(2)}, u32[]{:S(2)}) collective-permute-start(bf16[256,512]{1,0:T(8,128)(2,1)} %param.17), channel_id=1, source_target_pairs={{0,1},{1,2},{2,3},{3,0},{4,5},{5,6},{6,7},{7,4},{8,9},{9,10},{10,1... | collective-permute-start | bytes 786440 | tf_op jit(solution)/shard_map/ppermute | solution.py:153
  57.0 36.4 %copy-start = (bf16[1024,1024]{0,1:T(8,128)(2,1)S(1)}, bf16[1024,1024]{0,1:T(8,128)(2,1)}, u32[]{:S(2)}) copy-start(bf16[1024,1024]{0,1:T(8,128)(2,1)} %copy.16) | copy-start | bytes 6291460
  57.0 10.7 %collective-permute-start.3 = (bf16[256,512]{1,0:T(8,128)(2,1)S(1)}, bf16[256,512]{1,0:T(8,128)(2,1)S(1)}, u32[]{:S(2)}, u32[]{:S(2)}) collective-permute-start(bf16[256,512]{1,0:T(8,128)(2,1)S(1)} %get-tuple-element.39), channel_id=1, source_target_pairs={{0,1},{1,2},{2,3},{3,0},{4,5},{5,6},{6,7},{7,4},{8,9},{9,10},{10,1... | collective-permute-start | bytes 786440 | tf_op jit(solution)/shard_map/ppermute | solution.py:153
  60.2 13.0 %collective-permute-start.4 = (bf16[256,512]{1,0:T(8,128)(2,1)S(1)}, bf16[256,512]{1,0:T(8,128)(2,1)S(1)}, u32[]{:S(2)}, u32[]{:S(2)}) collective-permute-start(bf16[256,512]{1,0:T(8,128)(2,1)S(1)} %get-tuple-element.40), channel_id=1, source_target_pairs={{0,2},{1,3},{2,0},{3,1},{4,6},{5,7},{6,4},{7,5},{8,10},{9,11},{10,... | collective-permute-start | bytes 786440 | tf_op jit(solution)/shard_map/ppermute | solution.py:153
  64.6 10.2 %collective-permute-start.5 = (bf16[256,512]{1,0:T(8,128)(2,1)S(1)}, bf16[256,512]{1,0:T(8,128)(2,1)S(1)}, u32[]{:S(2)}, u32[]{:S(2)}) collective-permute-start(bf16[256,512]{1,0:T(8,128)(2,1)S(1)} %get-tuple-element.41), channel_id=1, source_target_pairs={{0,3},{1,0},{2,1},{3,2},{4,7},{5,4},{6,5},{7,6},{8,11},{9,8},{10,9... | collective-permute-start | bytes 786440 | tf_op jit(solution)/shard_map/ppermute | solution.py:153
  75.0 12.0 %collective-permute-start.8 = (bf16[256,512]{1,0:T(8,128)(2,1)S(1)}, bf16[256,512]{1,0:T(8,128)(2,1)S(1)}, u32[]{:S(2)}, u32[]{:S(2)}) collective-permute-start(bf16[256,512]{1,0:T(8,128)(2,1)S(1)} %multiply_convert_fusion.agg0), channel_id=1, source_target_pairs={{0,1},{1,2},{2,3},{3,0},{4,5},{5,6},{6,7},{7,4},{8,9},{9,10},{10,1... | collective-permute-start | bytes 786440 | tf_op jit(solution)/shard_map/ppermute | solution.py:153
  80.5 11.9 %collective-permute-start.7 = (bf16[256,512]{1,0:T(8,128)(2,1)S(1)}, bf16[256,512]{1,0:T(8,128)(2,1)}, u32[]{:S(2)}, u32[]{:S(2)}) collective-permute-start(bf16[256,512]{1,0:T(8,128)(2,1)S(1)} %multiply_convert_fusion.agg0), channel_id=1, source_target_pairs={{0,2},{1,3},{2,0},{3,1},{4,6},{5,7},{6,4},{7,5},{8,10},{9,11},{10,... | collective-permute-start | bytes 786440 | tf_op jit(solution)/shard_map/ppermute | solution.py:153
  83.0 10.4 %collective-permute-start.6 = (bf16[256,512]{1,0:T(8,128)(2,1)S(1)}, bf16[256,512]{1,0:T(8,128)(2,1)}, u32[]{:S(2)}, u32[]{:S(2)}) collective-permute-start(bf16[256,512]{1,0:T(8,128)(2,1)S(1)} %multiply_convert_fusion.agg0), channel_id=1, source_target_pairs={{0,3},{1,0},{2,1},{3,2},{4,7},{5,4},{6,5},{7,6},{8,11},{9,8},{10,9... | collective-permute-start | bytes 786440 | tf_op jit(solution)/shard_map/ppermute | solution.py:153
  105.6 16.6 %copy-start.11 = (bf16[1024,1024]{1,0:T(8,128)(2,1)S(1)}, bf16[1024,1024]{1,0:T(8,128)(2,1)}, u32[]{:S(2)}) copy-start(bf16[1024,1024]{1,0:T(8,128)(2,1)} %copy-done.9) | copy-start | bytes 6291460
  105.6 52.2 %all-to-all-start.1 = ((bf16[128,8,640]{2,1,0:T(8,128)(2,1)}), bf16[128,8,640]{2,1,0:T(8,128)(2,1)S(1)}, u32[]{:S(2)}, u32[]{:S(2)}) async-start(bf16[128,8,640]{2,1,0:T(8,128)(2,1)} %bitcast.29), calls=%async_computation.1 | async-start | bytes 2621440 | tf_op jit(solution)/shard_map/all_to_all | solution.py:244
  162.5 21.8 %all-to-all-start.2 = ((bf16[128,8,128]{2,1,0:T(8,128)(2,1)}), bf16[128,8,128]{2,1,0:T(8,128)(2,1)S(1)}, u32[]{:S(2)}, u32[]{:S(2)}) async-start(bf16[128,8,128]{2,1,0:T(8,128)(2,1)} %broadcast_in_dim.8), calls=%async_computation.2 | async-start | bytes 524288 | tf_op jit(solution)/shard_map/all_to_all | solution.py:261
  170.1 21.6 %collective-permute-start.9 = (bf16[256,512]{1,0:T(8,128)(2,1)S(1)}, bf16[256,512]{1,0:T(8,128)(2,1)S(1)}, u32[]{:S(2)}, u32[]{:S(2)}) collective-permute-start(bf16[256,512]{1,0:T(8,128)(2,1)S(1)} %get-tuple-element.56), channel_id=1, source_target_pairs={{0,1},{1,2},{2,3},{3,0},{4,5},{5,6},{6,7},{7,4},{8,9},{9,10},{10,1... | collective-permute-start | bytes 786440 | tf_op jit(solution)/shard_map/ppermute | solution.py:153
  172.0 21.7 %collective-permute-start.10 = (bf16[256,512]{1,0:T(8,128)(2,1)S(1)}, bf16[256,512]{1,0:T(8,128)(2,1)S(1)}, u32[]{:S(2)}, u32[]{:S(2)}) collective-permute-start(bf16[256,512]{1,0:T(8,128)(2,1)S(1)} %get-tuple-element.57), channel_id=1, source_target_pairs={{0,2},{1,3},{2,0},{3,1},{4,6},{5,7},{6,4},{7,5},{8,10},{9,11},{10,... | collective-permute-start | bytes 786440 | tf_op jit(solution)/shard_map/ppermute | solution.py:153
  177.5 16.2 %collective-permute-start.11 = (bf16[256,512]{1,0:T(8,128)(2,1)S(1)}, bf16[256,512]{1,0:T(8,128)(2,1)S(1)}, u32[]{:S(2)}, u32[]{:S(2)}) collective-permute-start(bf16[256,512]{1,0:T(8,128)(2,1)S(1)} %get-tuple-element.58), channel_id=1, source_target_pairs={{0,3},{1,0},{2,1},{3,2},{4,7},{5,4},{6,5},{7,6},{8,11},{9,8},{10,9... | collective-permute-start | bytes 786440 | tf_op jit(solution)/shard_map/ppermute | solution.py:153
  184.3 10.2 %collective-permute-start.14 = (bf16[256,512]{1,0:T(8,128)(2,1)S(1)}, bf16[256,512]{1,0:T(8,128)(2,1)S(1)}, u32[]{:S(2)}, u32[]{:S(2)}) collective-permute-start(bf16[256,512]{1,0:T(8,128)(2,1)S(1)} %bitcast.31), channel_id=1, source_target_pairs={{0,1},{1,2},{2,3},{3,0},{4,5},{5,6},{6,7},{7,4},{8,9},{9,10},{10,1... | collective-permute-start | bytes 786440 | tf_op jit(solution)/shard_map/ppermute | solution.py:153
  186.2 13.7 %collective-permute-start.13 = (bf16[256,512]{1,0:T(8,128)(2,1)S(1)}, bf16[256,512]{1,0:T(8,128)(2,1)S(1)}, u32[]{:S(2)}, u32[]{:S(2)}) collective-permute-start(bf16[256,512]{1,0:T(8,128)(2,1)S(1)} %bitcast.32), channel_id=1, source_target_pairs={{0,2},{1,3},{2,0},{3,1},{4,6},{5,7},{6,4},{7,5},{8,10},{9,11},{10,... | collective-permute-start | bytes 786440 | tf_op jit(solution)/shard_map/ppermute | solution.py:153
  191.7 10.3 %collective-permute-start.12 = (bf16[256,512]{1,0:T(8,128)(2,1)S(1)}, bf16[256,512]{1,0:T(8,128)(2,1)S(1)}, u32[]{:S(2)}, u32[]{:S(2)}) collective-permute-start(bf16[256,512]{1,0:T(8,128)(2,1)S(1)} %bitcast.33), channel_id=1, source_target_pairs={{0,3},{1,0},{2,1},{3,2},{4,7},{5,4},{6,5},{7,6},{8,11},{9,8},{10,9... | collective-permute-start | bytes 786440 | tf_op jit(solution)/shard_map/ppermute | solution.py:153
  (14 other events, 22.0 us)

commit v4 on v3

v4 whole, which is shorter than its diff:
```python
import functools

import jax
import jax.numpy as jnp
from jax import lax
from jax.experimental import pallas as pl
from jax.experimental.pallas import tpu as pltpu
from jax.sharding import Mesh
from jax.sharding import PartitionSpec as P

BLOCK = 64
LANES = 128
WIDE = ("y", "z", "core")
F32 = jnp.float32
BF16 = jnp.bfloat16
VMEM = pl.BlockSpec(memory_space=pltpu.VMEM)
HBM = pl.BlockSpec(memory_space=pltpu.HBM)
SMEM = pl.BlockSpec(memory_space=pltpu.SMEM)


def dot(left, right, left_dim, right_dim):
    dims = (((left_dim,), (right_dim,)), ((), ()))
    return lax.dot_general(left, right, dims, preferred_element_type=F32)


def call(kernel, name, outs, in_specs, args, flops, out_specs=None, scratch=(), vmem=24):
    moved = sum(a.size * a.dtype.itemsize for a in args) + sum(
        o.size * o.dtype.itemsize for o in outs
    )
    args = [
        pltpu.with_memory_space_constraint(a, pltpu.HBM) if spec is HBM else a
        for a, spec in zip(args, in_specs, strict=True)
    ]
    out_specs = out_specs or [VMEM] * len(outs)
    outs = [
        pltpu.HBM(o.shape, o.dtype) if spec is HBM else o
        for o, spec in zip(outs, out_specs, strict=True)
    ]
    return pl.pallas_call(
        kernel,
        out_shape=outs,
        in_specs=in_specs,
        out_specs=out_specs,
        scratch_shapes=scratch,
        compiler_params=pltpu.CompilerParams(vmem_limit_bytes=vmem << 20),
        cost_estimate=pl.CostEstimate(flops=flops, bytes_accessed=moved, transcendentals=0),
        name=name,
    )(*args)


def shape(rows, cols, dtype):
    return jax.ShapeDtypeStruct((rows, cols), dtype)


def started(source, target, sem):
    copy = pltpu.make_async_copy(source, target, sem)
    copy.start()
    return copy


def turned_quarters(rep_ref, feats_hbm, feats_ref, sems, replicas):
    quarter = feats_ref.shape[0] // replicas
    copies = []
    for k in range(replicas):
        at = pl.multiple_of(((rep_ref[0] + k) % replicas) * quarter, quarter)
        copies.append(
            started(
                feats_hbm.at[pl.ds(at, quarter), :],
                feats_ref.at[pl.ds(k * quarter, quarter), :],
                sems.at[k],
            )
        )
    return copies


def count_kernel(
    replicas, rep_ref, place_ref, words_ref, feats_hbm, local_hbm, halo_ref, halo_t_hbm, sums_hbm,
    counts_ref, halo_t_ref, feats_ref, sums_ref, sems,
):
    feats_copies = turned_quarters(rep_ref, feats_hbm, feats_ref, sems, replicas)
    counts_ref[...] = jnp.zeros_like(counts_ref)
    row = lax.broadcasted_iota(jnp.int32, (BLOCK, LANES), 0)
    lane = lax.broadcasted_iota(jnp.int32, (BLOCK, LANES), 1)
    word_lane = (row % 32) * 4 + (lane % BLOCK) // 16
    shift = lane % 16
    half = lane // BLOCK

    def add_tile(t, carry):
        place = place_ref[t]
        dst = pl.multiple_of((place // 64) * BLOCK, BLOCK)
        src = place % 64
        upper = jnp.broadcast_to(words_ref[pl.ds(2 * t, 1), :], (32, LANES))
        lower = jnp.broadcast_to(words_ref[pl.ds(2 * t + 1, 1), :], (32, LANES))
        words = jnp.concatenate([upper, lower], axis=0)
        picked = jnp.take_along_axis(words, word_lane, axis=1)
        bits = jnp.right_shift(picked, shift) & 1
        tile = jnp.where(half == src % 2, bits, 0).astype(F32).astype(BF16)
        rows = pl.ds(dst, BLOCK)
        cols = pl.ds(pl.multiple_of((src // 2) * LANES, LANES), LANES)
        counts_ref[rows, cols] = counts_ref[rows, cols] + tile
        return carry

    lax.fori_loop(0, place_ref.shape[0], add_tile, 0, unroll=4)
    split = local_hbm.shape[1]
    local_copy = started(counts_ref.at[:, pl.ds(0, split)], local_hbm, sems.at[replicas])
    halo_ref[...] = counts_ref[:, split:]
    halo_t_ref[...] = counts_ref[:, split:].T
    halo_t_copy = started(halo_t_ref, halo_t_hbm, sems.at[replicas + 1])
    for copy in feats_copies:
        copy.wait()
    rows_done = 256
    for at in range(0, counts_ref.shape[0], rows_done):
        rows = pl.ds(at, rows_done)
        sums_ref[rows, :] = dot(counts_ref[rows, :split], feats_ref[...], 1, 0)
    sums_copy = started(sums_ref, sums_hbm, sems.at[replicas + 2])
    local_copy.wait()
    halo_t_copy.wait()
    sums_copy.wait()


def sum_kernel(counts_ref, incoming_ref, local_hbm, own_ref, send1, send2, send3, local_ref, sems):
    quarter = own_ref.shape[0]
    order = (2, 1, 3, 0)
    quarters = {k: pl.ds(k * quarter, quarter) for k in order}
    copies = {
        k: started(local_hbm.at[rows, :], local_ref.at[rows, :], sems.at[k])
        for k, rows in quarters.items()
    }
    for k, rows in quarters.items():
        total = dot(counts_ref[rows, :], incoming_ref[...], 1, 0)
        copies[k].wait()
        total = total + local_ref[rows, :]
        if k:
            (send1, send2, send3)[k - 1][...] = total.astype(BF16)
        else:
            own_ref[...] = total


def dense_kernel(
    replicas, rep_ref, agg0, agg1, agg2, agg3, grad0, grad1, grad2, grad3, feats_hbm, w_self_hbm,
    w_neigh_hbm, scale_ref, halo_t_hbm, out_ref, grad_pre_ref, grad_agg_hbm, joint_hbm,
    grad_ref, feats_ref, w_self_ref, w_neigh_ref, halo_t_ref, grad_agg_ref, joint_ref, sems,
):
    aggs = (agg0, agg1, agg2, agg3)
    quarter, feat_width = agg0.shape
    share = feat_width // replicas
    halo_rows = halo_t_ref.shape[0]
    step = min(256, halo_rows)
    starts = range(0, halo_rows, step)
    neigh_copy = started(w_neigh_hbm, w_neigh_ref, sems.at[0])
    self_copy = started(w_self_hbm, w_self_ref, sems.at[1])
    feats_copies = turned_quarters(rep_ref, feats_hbm, feats_ref, sems.at[pl.ds(2, replicas)], replicas)
    grad_copies = [
        started(grad, grad_ref.at[pl.ds(k * quarter, quarter), :], sems.at[2 + replicas + k])
        for k, grad in enumerate((grad0, grad1, grad2, grad3))
    ]
    at = 2 + 2 * replicas
    halo_copies = [
        started(halo_t_hbm.at[pl.ds(i, step), :], halo_t_ref.at[pl.ds(i, step), :], sems.at[at + n])
        for n, i in enumerate(starts)
    ]
    at += len(starts)
    share_cols = pl.ds(pl.multiple_of(rep_ref[0] * share, LANES), share)
    grad_self = jnp.zeros((share, feat_width), F32)
    grad_neigh = jnp.zeros((share, feat_width), F32)
    neigh_copy.wait()
    self_copy.wait()
    w_neigh = w_neigh_ref[...]
    for k, agg_ref in enumerate(aggs):
        rows = pl.ds(k * quarter, quarter)
        feats_copies[k].wait()
        pre = dot(agg_ref[...], w_neigh, 1, 0) + dot(feats_ref[rows, :], w_self_ref[...], 1, 0)
        sigmoid = jax.nn.sigmoid(pre)
        grad_copies[k].wait()
        grad_pre = (
            grad_ref[rows, :].astype(F32) * sigmoid * (1.0 + pre * (1.0 - sigmoid))
        ).astype(BF16)
        if k == 0:
            out_ref[...] = (pre * sigmoid).astype(BF16)
            grad_pre_ref[...] = grad_pre
        grad_agg_ref[rows, :] = (dot(grad_pre, w_neigh, 1, 1) * scale_ref[rows, :]).astype(BF16)
        grad_self = grad_self + dot(feats_ref[rows, share_cols], grad_pre, 0, 0)
        grad_neigh = grad_neigh + dot(agg_ref[:, share_cols], grad_pre, 0, 0)
    grad_agg_copy = started(grad_agg_ref, grad_agg_hbm, sems.at[at])
    tile = 0
    per_peer = (joint_ref.shape[1] - feat_width) // LANES
    for part in (grad_self, grad_neigh):
        for g in range(0, share, 8):
            for c in range(0, feat_width, LANES):
                peer, slot = tile // per_peer, tile % per_peer
                lane = feat_width + slot * LANES
                joint_ref[peer * 8 : peer * 8 + 8, lane : lane + LANES] = part[
                    g : g + 8, c : c + LANES
                ].astype(BF16)
                tile += 1
    joint_copies = []
    for n, i in enumerate(starts):
        rows = pl.ds(i, step)
        halo_copies[n].wait()
        joint_ref[rows, :feat_width] = dot(halo_t_ref[rows, :], grad_agg_ref[...], 1, 0).astype(BF16)
        joint_copies.append(started(joint_ref.at[rows, :], joint_hbm.at[rows, :], sems.at[at + 1 + n]))
    grad_agg_copy.wait()
    for copy in joint_copies:
        copy.wait()


def return_kernel(
    replicas, slots_ref, joint_ref, local_hbm, base_hbm, copies_hbm, own_ref, send1, send2, send3,
    tiles_ref, local_ref, base_ref, sems,
):
    quarter, feat_width = own_ref.shape
    halo_rows = joint_ref.shape[0]
    order = (2, 1, 3, 0)
    local_copies = {
        k: started(
            local_hbm.at[pl.ds(k * quarter, quarter), :],
            local_ref.at[pl.ds(k * quarter, quarter), :],
            sems.at[k],
        )
        for k in order
    }
    base_copy = started(base_hbm, base_ref, sems.at[replicas])
    lanes = joint_ref.shape[1] - feat_width
    tiles = joint_ref[:, feat_width:].astype(F32).reshape(halo_rows // 8, 8, lanes)
    tile = tiles.sum(axis=0, keepdims=True)
    tiles_ref[...] = (
        jnp.broadcast_to(tile, tiles.shape).reshape(halo_rows, lanes).astype(BF16)
    )
    copies_copy = started(tiles_ref, copies_hbm, sems.at[replicas + 1])
    slots = jnp.broadcast_to(slots_ref[...], (quarter, halo_rows))
    row = lax.broadcasted_iota(jnp.int32, (quarter, halo_rows), 0)
    for k in order:
        pick = jnp.where(row + k * quarter == slots, 1.0, 0.0).astype(BF16)
        total = dot(pick, joint_ref[:, :feat_width], 1, 0)
        local_copies[k].wait()
        total = total + local_ref[pl.ds(k * quarter, quarter), :]
        if k:
            (send1, send2, send3)[k - 1][...] = total.astype(BF16)
        else:
            base_copy.wait()
            own_ref[...] = total + base_ref[...]
    copies_copy.wait()


def place_kernel(rep_ref, part0, part1, part2, part3, self_ref, neigh_ref):
    parts = (part0, part1, part2, part3)
    share = part0.shape[0] // 2
    for k, part in enumerate(parts):
        at = pl.ds(pl.multiple_of(((rep_ref[0] + k) % len(parts)) * share, share), share)
        self_ref[at, :] = part[:share, :]
        neigh_ref[at, :] = part[share:, :]


def send_to(x, step, replicas):
    return lax.ppermute(x, "rep", [(i, (i + step) % replicas) for i in range(replicas)])


def from_ahead(x, replicas):
    return [send_to(x, replicas - k, replicas) for k in range(1, replicas)]


def on_device(
    node_feats, w_self, w_neigh, send_rows, tile_dst, tile_src, tile_bits, norm_count, grad_out
):
    node_rows, feat_width = node_feats.shape
    peer_count = lax.axis_size(WIDE)
    replicas = lax.axis_size("rep")
    slot_count = send_rows.shape[2]
    tile_total = tile_dst.shape[2]
    quarter = node_rows // replicas
    share = feat_width // replicas
    rep_index = lax.axis_index("rep")
    rep_ref = rep_index.reshape(1).astype(jnp.int32)
    dst_count = node_rows // BLOCK
    halo_rows = peer_count * slot_count
    first_row = rep_index * quarter
    first_block = rep_index * (quarter // BLOCK)
    send_outs = [shape(quarter, feat_width, BF16)] * (replicas - 1)

    slot_rows = send_rows[0].reshape(-1)
    every_row = lax.broadcasted_iota(jnp.int32, (node_rows, halo_rows), 0)
    send_pick = (every_row == slot_rows[None, :]).astype(BF16)
    outgoing = dot(send_pick, node_feats, 0, 0).astype(BF16)
    incoming = lax.all_to_all(outgoing, WIDE, 0, 0, tiled=True)

    scale = lax.rsqrt(norm_count.astype(F32))
    scale = lax.dynamic_slice_in_dim(jnp.concatenate([scale, scale]), first_row, node_rows, 0)
    scale = scale[:, None]
    grad_outs = [grad_out] + from_ahead(grad_out, replicas)
    dst = (tile_dst[0, 0] - first_block) % dst_count
    src = tile_src[0, 0]
    src = jnp.where(src < dst_count, (src - first_block) % dst_count, src)
    block_flops = 2 * node_rows * halo_rows * feat_width
    counts_local, counts_halo, halo_t, sums_local = call(
        functools.partial(count_kernel, replicas),
        "tile_counts",
        [
            shape(node_rows, node_rows, BF16),
            shape(node_rows, halo_rows, BF16),
            shape(halo_rows, node_rows, BF16),
            shape(node_rows, feat_width, F32),
        ],
        [SMEM, SMEM, VMEM, HBM],
        (rep_ref, dst * 64 + src, tile_bits.reshape(tile_total * 2, LANES), node_feats),
        tile_total * BLOCK * LANES * 20 + block_flops,
        out_specs=[HBM, VMEM, HBM, HBM],
        scratch=[
            pltpu.VMEM((node_rows, node_rows + halo_rows), BF16),
            pltpu.VMEM((halo_rows, node_rows), BF16),
            pltpu.VMEM((node_rows, feat_width), BF16),
            pltpu.VMEM((node_rows, feat_width), F32),
            pltpu.SemaphoreType.DMA((replicas + 3,)),
        ],
    )
    turned_slots = ((slot_rows - first_row) % node_rows)[None, :]
    incoming, counts_halo, sums_local, scale, turned_slots, *grad_outs = lax.optimization_barrier(
        (incoming, counts_halo, sums_local, scale, turned_slots, *grad_outs)
    )

    own_sums, *sends = call(
        sum_kernel,
        "neighbour_sums",
        [shape(quarter, feat_width, F32)] + send_outs,
        [VMEM, VMEM, HBM],
        (counts_halo, incoming, sums_local),
        block_flops,
        scratch=[
            pltpu.VMEM((node_rows, feat_width), F32),
            pltpu.SemaphoreType.DMA((replicas,)),
        ],
    )
    for k in range(1, replicas):
        own_sums = own_sums + send_to(sends[k - 1], k, replicas).astype(F32)
    own_agg = (own_sums * scale[:quarter]).astype(BF16)
    aggs = [own_agg] + from_ahead(own_agg, replicas)
    joint_width = feat_width + 2 * share * feat_width // halo_rows
    halo_steps = max(1, halo_rows // 256)
    out_feats, grad_pre, grad_agg, joint = call(
        functools.partial(dense_kernel, replicas),
        "dense",
        [
            shape(quarter, feat_width, BF16),
            shape(quarter, feat_width, BF16),
            shape(node_rows, feat_width, BF16),
            shape(halo_rows, joint_width, BF16),
        ],
        [SMEM] + [VMEM] * 4 + [HBM] * 7 + [VMEM, HBM],
        (rep_ref, *aggs, *grad_outs, node_feats, w_self, w_neigh, scale, halo_t),
        2 * block_flops,
        out_specs=[VMEM, VMEM, HBM, HBM],
        scratch=[
            pltpu.VMEM((node_rows, feat_width), BF16),
            pltpu.VMEM((node_rows, feat_width), BF16),
            pltpu.VMEM((feat_width, feat_width), BF16),
            pltpu.VMEM((feat_width, feat_width), BF16),
            pltpu.VMEM((halo_rows, node_rows), BF16),
            pltpu.VMEM((node_rows, feat_width), BF16),
            pltpu.VMEM((halo_rows, joint_width), BF16),
            pltpu.SemaphoreType.DMA((3 + 2 * replicas + 2 * halo_steps,)),
        ],
    )
    returned = lax.all_to_all(joint, WIDE, 0, 0, tiled=True)
    grad_local = dot(counts_local, grad_agg, 0, 0)
    own_base = dot(grad_pre, w_self, 1, 1)
    returned, grad_local, own_base = lax.optimization_barrier((returned, grad_local, own_base))

    copies, own_grad, *sends = call(
        functools.partial(return_kernel, replicas),
        "returned_rows",
        [shape(halo_rows, joint_width - feat_width, BF16), shape(quarter, feat_width, F32)]
        + send_outs,
        [VMEM, VMEM, HBM, HBM],
        (turned_slots, returned, grad_local, own_base),
        block_flops,
        out_specs=[HBM] + [VMEM] * replicas,
        scratch=[
            pltpu.VMEM((halo_rows, joint_width - feat_width), BF16),
            pltpu.VMEM((node_rows, feat_width), F32),
            pltpu.VMEM((quarter, feat_width), F32),
            pltpu.SemaphoreType.DMA((replicas + 2,)),
        ],
    )
    for k in range(1, replicas):
        own_grad = own_grad + send_to(sends[k - 1], k, replicas).astype(F32)

    tiles = lax.all_to_all(copies, WIDE, 0, 0, tiled=True)
    lane_tiles = feat_width // LANES
    own_share = (
        tiles.reshape(peer_count, slot_count, -1, LANES)
        .transpose(0, 2, 1, 3)
        .reshape(-1, lane_tiles, slot_count, LANES)
        .transpose(0, 2, 1, 3)
        .reshape(2 * share, feat_width)
    )
    grad_self, grad_neigh = call(
        place_kernel,
        "place",
        [shape(feat_width, feat_width, BF16)] * 2,
        [SMEM] + [VMEM] * replicas,
        (rep_ref, own_share, *from_ahead(own_share, replicas)),
        0,
    )
    return out_feats, own_grad.astype(BF16), grad_self, grad_neigh


def solution(mesh):
    fine = Mesh(
        mesh.devices.reshape(8, mesh.shape["wide"] // 16, 2, mesh.shape["rep"]), WIDE + ("rep",)
    )
    in_specs = (
        P(WIDE, None),
        P(),
        P(),
        P(WIDE, None, "rep"),
        P(WIDE, "rep", None),
        P(WIDE, "rep", None),
        P(WIDE, "rep", None),
        P(WIDE),
        P(WIDE + ("rep",), None),
    )
    out_specs = (P(WIDE + ("rep",), None), P(WIDE + ("rep",), None), P(), P())
    return jax.shard_map(
        on_device, mesh=fine, in_specs=in_specs, out_specs=out_specs, check_vma=False
    )
```

time: 205 us -> 193 us (0.941)
  local copies, waits for them, and re-layouts: 20.8 us -> 1.34 us
  Pallas kernels: 14.4 us -> 24.5 us
  waiting for transfers between devices: 57.7 us -> 63.9 us
  starting transfers between devices: 93.8 us -> 89.1 us
  matrix products: 12.1 us -> 9.13 us
  other arithmetic: 3.35 us -> 1.12 us
    unnamed x42 -> x15, local copies, waits for them, and re-layouts: 15.5 us -> 0.82 us
    all_to_all x1, waiting for transfers between devices: 0.01 us -> 10.6 us  [on_device(): incoming = lax.all_to_all(outgoing, WIDE, 0, 0, tiled=True)]
    pallas_call x5, Pallas kernels: 14.4 us -> 24.5 us  [call(): pl.pallas_call(kernel, out_shape=outs, in_specs=in_specs, out_specs=out_s...]
    all_to_all x1, starting transfers between devices: 16.6 us -> 9.29 us  [on_device(): returned = lax.all_to_all(joint, WIDE, 0, 0, tiled=True)]
    dot_general x4 -> x3, matrix products: 12.1 us -> 9.13 us  [dot(): return lax.dot_general(left, right, dims, preferred_element_type=F32)]
    ppermute x15, starting transfers between devices: 51 us -> 53.6 us  [send_to(): lax.ppermute(x, 'rep', [(i, (i + step) % replicas) for i in range(replica...]
    pallas_call x1 -> x0, local copies, waits for them, and re-layouts: 2.53 us -> none  [call(): pl.pallas_call(kernel, out_shape=outs, in_specs=in_specs, out_specs=[VMEM...]
    concatenate x2 -> x1, other arithmetic: 2.31 us -> 0.08 us  [on_device(): jnp.concatenate([scale, scale])]
  transfers between devices with their start and end apart: 18 -> 18, of which waited for: 8 -> 9; matrix products, arithmetic and copies ran while one was open for 9% -> 4% of each run, Pallas kernels for 3% -> 5%
where the time goes in v4:
time: 193 us; the launch traced here: 190 us
  starting transfers between devices  89.1 us (46%)
  waiting for transfers between devices  63.9 us (33%)
  Pallas kernels  24.5 us (13%)
  matrix products  9.13 us (5%)
    ppermute x15, starting transfers between devices, send_to(): lax.ppermute(x, 'rep', [(i, (i + step) % replicas) for i in range(replica...  53.6 us
    all_to_all x1, waiting for transfers between devices, on_device(): returned = lax.all_to_all(joint, WIDE, 0, 0, tiled=True)  29.9 us
    pallas_call x5, Pallas kernels, call(): pl.pallas_call(kernel, out_shape=outs, in_specs=in_specs, out_specs=out_s...  24.5 us
    ppermute x15, waiting for transfers between devices, send_to(): lax.ppermute(x, 'rep', [(i, (i + step) % replicas) for i in range(replica...  19.7 us
    all_to_all x1, starting transfers between devices, on_device(): incoming = lax.all_to_all(outgoing, WIDE, 0, 0, tiled=True)  18.6 us
    all_to_all x1, waiting for transfers between devices, on_device(): incoming = lax.all_to_all(outgoing, WIDE, 0, 0, tiled=True)  10.6 us
    all_to_all x1, starting transfers between devices, on_device(): returned = lax.all_to_all(joint, WIDE, 0, 0, tiled=True)  9.29 us
    dot_general x3, matrix products, dot(): return lax.dot_general(left, right, dims, preferred_element_type=F32)  9.13 us
  transfers between devices with their start and end apart: 18, of which 9 were waited for; matrix products, arithmetic and copies ran while one was open for 4% of the time, Pallas kernels for 5%

profile of v4, /device:TPU:1, one launch (start us, length us, event | category | flops | bytes accessed | tf_op | source)
XLA Modules:
  0.0 190.0 jit_solution(555072671349443423)
XLA Ops:
  1.5 3.5 %fusion.3 = bf16[128,8,512]{2,1,0:T(8,128)(2,1)} fusion(bf16[1024,512]{1,0:T(8,128)(2,1)} %feats_hbm.3, s32[1024]{0:T(1024)S(1)} %eq.15), kind=kOutput, calls=%fused_computation.4 | convolution fusion | flops 1075314688 | bytes 2101248 | tf_op jit(solution)/shard_map/dot_general | solution.py:23
  5.1 18.6 %all-to-all-start = ((bf16[128,8,512]{2,1,0:T(8,128)(2,1)}), bf16[128,8,512]{2,1,0:T(8,128)(2,1)S(1)}, u32[]{:S(2)}, u32[]{:S(2)}) async-start(bf16[128,8,512]{2,1,0:T(8,128)(2,1)} %fusion.3), calls=%async_computation | async-start | bytes 2097152 | tf_op jit(solution)/shard_map/all_to_all | solution.py:284
  23.7 4.7 %collective-permute-start.1 = (bf16[256,512]{1,0:T(8,128)(2,1)S(1)}, bf16[256,512]{1,0:T(8,128)(2,1)}, u32[]{:S(2)}, u32[]{:S(2)}) collective-permute-start(bf16[256,512]{1,0:T(8,128)(2,1)S(1)} %copy-done.6), channel_id=1, source_target_pairs={{0,2},{1,3},{2,0},{3,1},{4,6},{5,7},{6,4},{7,5},{8,10},{9,11},{10,... | collective-permute-start | bytes 786440 | tf_op jit(solution)/shard_map/ppermute | solution.py:255
  33.8 9.4 %tile_counts.1 = (bf16[1024,1024]{1,0:T(8,128)(2,1)}, bf16[1024,1024]{1,0:T(8,128)(2,1)S(1)}, bf16[1024,1024]{1,0:T(8,128)(2,1)}, f32[1024,512]{1,0:T(8,128)}) custom-call(s32[1]{0:T(128)} %bitcast.rep_ref, s32[128]{0:T(128)S(1)} %fusion.7.place_ref, s32[256,128]{1,0:T(8,128)S(1)} %bitcast.33, bf16[1024,512]{1,0:T(8,128)(2,1)} %feats_hbm.3), custom_call_target="tpu_custom_call" | custom-call | flops 1094713344 | bytes 9568772 | tf_op jit(solution)/shard_map/tile_counts/pallas_call | solution.py:39
  43.5 10.6 %all-to-all-done = bf16[128,8,512]{2,1,0:T(8,128)(2,1)S(1)} async-done(((bf16[128,8,512]{2,1,0:T(8,128)(2,1)}), bf16[128,8,512]{2,1,0:T(8,128)(2,1)S(1)}, u32[]{:S(2)}, u32[]{:S(2)}) %all-to-all-start) | async-done | bytes 1048608 | tf_op jit(solution)/shard_map/all_to_all | solution.py:284
  57.0 3.1 %collective-permute-start.3 = (bf16[256,512]{1,0:T(8,128)(2,1)S(1)}, bf16[256,512]{1,0:T(8,128)(2,1)S(1)}, u32[]{:S(2)}, u32[]{:S(2)}) collective-permute-start(bf16[256,512]{1,0:T(8,128)(2,1)S(1)} %get-tuple-element.41), channel_id=1, source_target_pairs={{0,1},{1,2},{2,3},{3,0},{4,5},{5,6},{6,7},{7,4},{8,9},{9,10},{10,1... | collective-permute-start | bytes 786440 | tf_op jit(solution)/shard_map/ppermute | solution.py:255
  60.1 4.4 %collective-permute-start.4 = (bf16[256,512]{1,0:T(8,128)(2,1)S(1)}, bf16[256,512]{1,0:T(8,128)(2,1)S(1)}, u32[]{:S(2)}, u32[]{:S(2)}) collective-permute-start(bf16[256,512]{1,0:T(8,128)(2,1)S(1)} %get-tuple-element.42), channel_id=1, source_target_pairs={{0,2},{1,3},{2,0},{3,1},{4,6},{5,7},{6,4},{7,5},{8,10},{9,11},{10,... | collective-permute-start | bytes 786440 | tf_op jit(solution)/shard_map/ppermute | solution.py:255
  67.6 5.6 %collective-permute-done.4 = bf16[256,512]{1,0:T(8,128)(2,1)S(1)} collective-permute-done((bf16[256,512]{1,0:T(8,128)(2,1)S(1)}, bf16[256,512]{1,0:T(8,128)(2,1)S(1)}, u32[]{:S(2)}, u32[]{:S(2)}) %collective-permute-start.4) | collective-permute-done | bytes 262176 | tf_op jit(solution)/shard_map/ppermute | solution.py:255
  74.9 5.7 %collective-permute-start.8 = (bf16[256,512]{1,0:T(8,128)(2,1)S(1)}, bf16[256,512]{1,0:T(8,128)(2,1)S(1)}, u32[]{:S(2)}, u32[]{:S(2)}) collective-permute-start(bf16[256,512]{1,0:T(8,128)(2,1)S(1)} %multiply_convert_fusion.agg0), channel_id=1, source_target_pairs={{0,1},{1,2},{2,3},{3,0},{4,5},{5,6},{6,7},{7,4},{8,9},{9,10},{10,1... | collective-permute-start | bytes 786440 | tf_op jit(solution)/shard_map/ppermute | solution.py:255
  82.9 4.0 %collective-permute-start.6 = (bf16[256,512]{1,0:T(8,128)(2,1)S(1)}, bf16[256,512]{1,0:T(8,128)(2,1)S(1)}, u32[]{:S(2)}, u32[]{:S(2)}) collective-permute-start(bf16[256,512]{1,0:T(8,128)(2,1)S(1)} %multiply_convert_fusion.agg0), channel_id=1, source_target_pairs={{0,3},{1,0},{2,1},{3,2},{4,7},{5,4},{6,5},{7,6},{8,11},{9,8},{10,9... | collective-permute-start | bytes 786440 | tf_op jit(solution)/shard_map/ppermute | solution.py:255
  87.1 5.3 %collective-permute-done.7.agg2 = bf16[256,512]{1,0:T(8,128)(2,1)S(1)} collective-permute-done((bf16[256,512]{1,0:T(8,128)(2,1)S(1)}, bf16[256,512]{1,0:T(8,128)(2,1)S(1)}, u32[]{:S(2)}, u32[]{:S(2)}) %collective-permute-start.7) | collective-permute-done | bytes 262176 | tf_op jit(solution)/shard_map/ppermute | solution.py:255
  93.5 8.1 %dense.1 = (bf16[256,512]{1,0:T(8,128)(2,1)}, bf16[256,512]{1,0:T(8,128)(2,1)S(1)}, bf16[1024,512]{1,0:T(8,128)(2,1)}, bf16[1024,640]{1,0:T(8,128)(2,1)}) custom-call(s32[1]{0:T(128)} %bitcast.rep_ref, bf16[256,512]{1,0:T(8,128)(2,1)S(1)} %multiply_convert_fusion.agg0, bf16[256,512]{1,0:T(8,128)(2,1)S(1)} %collective-permute-done.6.agg1, ...), custom_call_target="tpu_custom_call" | custom-call | flops 2147483648 | bytes 9179140 | tf_op jit(solution)/shard_map/dense/pallas_call | solution.py:39
  101.6 9.3 %all-to-all-start.1 = ((bf16[128,8,640]{2,1,0:T(8,128)(2,1)}), bf16[128,8,640]{2,1,0:T(8,128)(2,1)S(1)}, u32[]{:S(2)}, u32[]{:S(2)}) async-start(bf16[128,8,640]{2,1,0:T(8,128)(2,1)} %bitcast.34), calls=%async_computation.1 | async-start | bytes 2621440 | tf_op jit(solution)/shard_map/all_to_all | solution.py:362
  112.0 4.5 %fusion.10.local_hbm = f32[1024,512]{1,0:T(8,128)} fusion(bf16[1024,1024]{1,0:T(8,128)(2,1)} %get-tuple-element.53, bf16[1024,512]{1,0:T(8,128)(2,1)} %get-tuple-element.54), kind=kOutput, calls=%fused_computation.28 | convolution fusion | flops 1073741824 | bytes 5242880 | tf_op jit(solution)/shard_map/dot_general | solution.py:23
  116.5 29.9 %all-to-all-done.1 = bf16[128,8,640]{2,1,0:T(8,128)(2,1)S(1)} async-done(((bf16[128,8,640]{2,1,0:T(8,128)(2,1)}), bf16[128,8,640]{2,1,0:T(8,128)(2,1)S(1)}, u32[]{:S(2)}, u32[]{:S(2)}) %all-to-all-start.1) | async-done | bytes 1310752 | tf_op jit(solution)/shard_map/all_to_all | solution.py:362
  149.4 7.6 %all-to-all-start.2 = ((bf16[128,8,128]{2,1,0:T(8,128)(2,1)}), bf16[128,8,128]{2,1,0:T(8,128)(2,1)S(1)}, u32[]{:S(2)}, u32[]{:S(2)}) async-start(bf16[128,8,128]{2,1,0:T(8,128)(2,1)} %bitcast.35), calls=%async_computation.2 | async-start | bytes 524288 | tf_op jit(solution)/shard_map/all_to_all | solution.py:386
  157.0 4.0 %collective-permute-start.9 = (bf16[256,512]{1,0:T(8,128)(2,1)S(1)}, bf16[256,512]{1,0:T(8,128)(2,1)S(1)}, u32[]{:S(2)}, u32[]{:S(2)}) collective-permute-start(bf16[256,512]{1,0:T(8,128)(2,1)S(1)} %get-tuple-element.60), channel_id=1, source_target_pairs={{0,1},{1,2},{2,3},{3,0},{4,5},{5,6},{6,7},{7,4},{8,9},{9,10},{10,1... | collective-permute-start | bytes 786440 | tf_op jit(solution)/shard_map/ppermute | solution.py:255
  161.1 3.4 %collective-permute-start.10 = (bf16[256,512]{1,0:T(8,128)(2,1)S(1)}, bf16[256,512]{1,0:T(8,128)(2,1)S(1)}, u32[]{:S(2)}, u32[]{:S(2)}) collective-permute-start(bf16[256,512]{1,0:T(8,128)(2,1)S(1)} %get-tuple-element.61), channel_id=1, source_target_pairs={{0,2},{1,3},{2,0},{3,1},{4,6},{5,7},{6,4},{7,5},{8,10},{9,11},{10,... | collective-permute-start | bytes 786440 | tf_op jit(solution)/shard_map/ppermute | solution.py:255
  164.5 3.2 %collective-permute-start.11 = (bf16[256,512]{1,0:T(8,128)(2,1)S(1)}, bf16[256,512]{1,0:T(8,128)(2,1)S(1)}, u32[]{:S(2)}, u32[]{:S(2)}) collective-permute-start(bf16[256,512]{1,0:T(8,128)(2,1)S(1)} %get-tuple-element.62), channel_id=1, source_target_pairs={{0,3},{1,0},{2,1},{3,2},{4,7},{5,4},{6,5},{7,6},{8,11},{9,8},{10,9... | collective-permute-start | bytes 786440 | tf_op jit(solution)/shard_map/ppermute | solution.py:255
  167.7 3.6 %all-to-all-done.2 = bf16[128,8,128]{2,1,0:T(8,128)(2,1)S(1)} async-done(((bf16[128,8,128]{2,1,0:T(8,128)(2,1)}), bf16[128,8,128]{2,1,0:T(8,128)(2,1)S(1)}, u32[]{:S(2)}, u32[]{:S(2)}) %all-to-all-start.2) | async-done | bytes 262176 | tf_op jit(solution)/shard_map/all_to_all | solution.py:386
  171.3 4.0 %collective-permute-start.14 = (bf16[256,512]{1,0:T(8,128)(2,1)S(1)}, bf16[256,512]{1,0:T(8,128)(2,1)S(1)}, u32[]{:S(2)}, u32[]{:S(2)}) collective-permute-start(bf16[256,512]{1,0:T(8,128)(2,1)S(1)} %bitcast.29), channel_id=1, source_target_pairs={{0,1},{1,2},{2,3},{3,0},{4,5},{5,6},{6,7},{7,4},{8,9},{9,10},{10,1... | collective-permute-start | bytes 786440 | tf_op jit(solution)/shard_map/ppermute | solution.py:255
  175.3 3.4 %collective-permute-start.13 = (bf16[256,512]{1,0:T(8,128)(2,1)S(1)}, bf16[256,512]{1,0:T(8,128)(2,1)S(1)}, u32[]{:S(2)}, u32[]{:S(2)}) collective-permute-start(bf16[256,512]{1,0:T(8,128)(2,1)S(1)} %bitcast.30), channel_id=1, source_target_pairs={{0,2},{1,3},{2,0},{3,1},{4,6},{5,7},{6,4},{7,5},{8,10},{9,11},{10,... | collective-permute-start | bytes 786440 | tf_op jit(solution)/shard_map/ppermute | solution.py:255
  178.7 3.2 %collective-permute-start.12 = (bf16[256,512]{1,0:T(8,128)(2,1)S(1)}, bf16[256,512]{1,0:T(8,128)(2,1)S(1)}, u32[]{:S(2)}, u32[]{:S(2)}) collective-permute-start(bf16[256,512]{1,0:T(8,128)(2,1)S(1)} %bitcast.31), channel_id=1, source_target_pairs={{0,3},{1,0},{2,1},{3,2},{4,7},{5,4},{6,5},{7,6},{8,11},{9,8},{10,9... | collective-permute-start | bytes 786440 | tf_op jit(solution)/shard_map/ppermute | solution.py:255
  182.8 4.3 %collective-permute-done.13.part2 = bf16[256,512]{1,0:T(8,128)(2,1)S(1)} collective-permute-done((bf16[256,512]{1,0:T(8,128)(2,1)S(1)}, bf16[256,512]{1,0:T(8,128)(2,1)S(1)}, u32[]{:S(2)}, u32[]{:S(2)}) %collective-permute-start.13) | collective-permute-done | bytes 262176 | tf_op jit(solution)/shard_map/ppermute | solution.py:255
  (47 shorter events, 25.7 us)
Async XLA Ops:
  1.5 22.1 %copy-start.6 = (bf16[256,512]{1,0:T(8,128)(2,1)S(1)}, bf16[256,512]{1,0:T(8,128)(2,1)}, u32[]{:S(2)}) copy-start(bf16[256,512]{1,0:T(8,128)(2,1)} %grad0) | copy-start | bytes 786436
  5.1 28.6 %copy-start.3 = (s32[1024]{0:T(1024)S(1)}, s32[1024]{0:T(1024)}, u32[]{:S(2)}) copy-start(s32[1024]{0:T(1024)} %param.16) | copy-start | bytes 12292
  5.1 28.7 %copy-start.4 = (s32[1,1,128]{2,1,0:T(1,128)S(1)}, s32[1,1,128]{2,1,0:T(1,128)}, u32[]{:S(2)}) copy-start(s32[1,1,128]{2,1,0:T(1,128)} %param.14) | copy-start | bytes 1540
  5.1 28.7 %copy-start.5 = (s32[1,1,128]{2,1,0:T(1,128)S(1)}, s32[1,1,128]{2,1,0:T(1,128)}, u32[]{:S(2)}) copy-start(s32[1,1,128]{2,1,0:T(1,128)} %param.13) | copy-start | bytes 1540
  5.1 28.7 %copy-start.2 = (s32[1,128,8]{1,2,0:T(8,128)S(1)}, s32[1,128,8]{1,2,0:T(8,128)}, u32[]{:S(2)}) copy-start(s32[1,128,8]{1,2,0:T(8,128)} %param.12) | copy-start | bytes 12292
  5.1 28.7 %copy-start = (s32[1,1,32768]{2,1,0:T(1,128)S(1)}, s32[1,1,32768]{2,1,0:T(1,128)}, u32[]{:S(2)}) copy-start(s32[1,1,32768]{2,1,0:T(1,128)} %param.15) | copy-start | bytes 393220
  5.1 49.0 %all-to-all-start = ((bf16[128,8,512]{2,1,0:T(8,128)(2,1)}), bf16[128,8,512]{2,1,0:T(8,128)(2,1)S(1)}, u32[]{:S(2)}, u32[]{:S(2)}) async-start(bf16[128,8,512]{2,1,0:T(8,128)(2,1)} %fusion.3), calls=%async_computation | async-start | bytes 2097152 | tf_op jit(solution)/shard_map/all_to_all | solution.py:284
  23.7 19.8 %collective-permute-start.1 = (bf16[256,512]{1,0:T(8,128)(2,1)S(1)}, bf16[256,512]{1,0:T(8,128)(2,1)}, u32[]{:S(2)}, u32[]{:S(2)}) collective-permute-start(bf16[256,512]{1,0:T(8,128)(2,1)S(1)} %copy-done.6), channel_id=1, source_target_pairs={{0,2},{1,3},{2,0},{3,1},{4,6},{5,7},{6,4},{7,5},{8,10},{9,11},{10,... | collective-permute-start | bytes 786440 | tf_op jit(solution)/shard_map/ppermute | solution.py:255
  28.3 15.1 %collective-permute-start = (bf16[256,512]{1,0:T(8,128)(2,1)S(1)}, bf16[256,512]{1,0:T(8,128)(2,1)}, u32[]{:S(2)}, u32[]{:S(2)}) collective-permute-start(bf16[256,512]{1,0:T(8,128)(2,1)S(1)} %copy-done.6), channel_id=1, source_target_pairs={{0,3},{1,0},{2,1},{3,2},{4,7},{5,4},{6,5},{7,6},{8,11},{9,8},{10,9... | collective-permute-start | bytes 786440 | tf_op jit(solution)/shard_map/ppermute | solution.py:255
  31.1 12.4 %collective-permute-start.2 = (bf16[256,512]{1,0:T(8,128)(2,1)S(1)}, bf16[256,512]{1,0:T(8,128)(2,1)}, u32[]{:S(2)}, u32[]{:S(2)}) collective-permute-start(bf16[256,512]{1,0:T(8,128)(2,1)S(1)} %copy-done.6), channel_id=1, source_target_pairs={{0,1},{1,2},{2,3},{3,0},{4,5},{5,6},{6,7},{7,4},{8,9},{9,10},{10,1... | collective-permute-start | bytes 786440 | tf_op jit(solution)/shard_map/ppermute | solution.py:255
  57.0 10.6 %collective-permute-start.3 = (bf16[256,512]{1,0:T(8,128)(2,1)S(1)}, bf16[256,512]{1,0:T(8,128)(2,1)S(1)}, u32[]{:S(2)}, u32[]{:S(2)}) collective-permute-start(bf16[256,512]{1,0:T(8,128)(2,1)S(1)} %get-tuple-element.41), channel_id=1, source_target_pairs={{0,1},{1,2},{2,3},{3,0},{4,5},{5,6},{6,7},{7,4},{8,9},{9,10},{10,1... | collective-permute-start | bytes 786440 | tf_op jit(solution)/shard_map/ppermute | solution.py:255
  60.1 13.0 %collective-permute-start.4 = (bf16[256,512]{1,0:T(8,128)(2,1)S(1)}, bf16[256,512]{1,0:T(8,128)(2,1)S(1)}, u32[]{:S(2)}, u32[]{:S(2)}) collective-permute-start(bf16[256,512]{1,0:T(8,128)(2,1)S(1)} %get-tuple-element.42), channel_id=1, source_target_pairs={{0,2},{1,3},{2,0},{3,1},{4,6},{5,7},{6,4},{7,5},{8,10},{9,11},{10,... | collective-permute-start | bytes 786440 | tf_op jit(solution)/shard_map/ppermute | solution.py:255
  64.5 10.3 %collective-permute-start.5 = (bf16[256,512]{1,0:T(8,128)(2,1)S(1)}, bf16[256,512]{1,0:T(8,128)(2,1)S(1)}, u32[]{:S(2)}, u32[]{:S(2)}) collective-permute-start(bf16[256,512]{1,0:T(8,128)(2,1)S(1)} %get-tuple-element.43), channel_id=1, source_target_pairs={{0,3},{1,0},{2,1},{3,2},{4,7},{5,4},{6,5},{7,6},{8,11},{9,8},{10,9... | collective-permute-start | bytes 786440 | tf_op jit(solution)/shard_map/ppermute | solution.py:255
  74.9 12.2 %collective-permute-start.8 = (bf16[256,512]{1,0:T(8,128)(2,1)S(1)}, bf16[256,512]{1,0:T(8,128)(2,1)S(1)}, u32[]{:S(2)}, u32[]{:S(2)}) collective-permute-start(bf16[256,512]{1,0:T(8,128)(2,1)S(1)} %multiply_convert_fusion.agg0), channel_id=1, source_target_pairs={{0,1},{1,2},{2,3},{3,0},{4,5},{5,6},{6,7},{7,4},{8,9},{9,10},{10,1... | collective-permute-start | bytes 786440 | tf_op jit(solution)/shard_map/ppermute | solution.py:255
  80.7 11.8 %collective-permute-start.7 = (bf16[256,512]{1,0:T(8,128)(2,1)S(1)}, bf16[256,512]{1,0:T(8,128)(2,1)S(1)}, u32[]{:S(2)}, u32[]{:S(2)}) collective-permute-start(bf16[256,512]{1,0:T(8,128)(2,1)S(1)} %multiply_convert_fusion.agg0), channel_id=1, source_target_pairs={{0,2},{1,3},{2,0},{3,1},{4,6},{5,7},{6,4},{7,5},{8,10},{9,11},{10,... | collective-permute-start | bytes 786440 | tf_op jit(solution)/shard_map/ppermute | solution.py:255
  82.9 10.5 %collective-permute-start.6 = (bf16[256,512]{1,0:T(8,128)(2,1)S(1)}, bf16[256,512]{1,0:T(8,128)(2,1)S(1)}, u32[]{:S(2)}, u32[]{:S(2)}) collective-permute-start(bf16[256,512]{1,0:T(8,128)(2,1)S(1)} %multiply_convert_fusion.agg0), channel_id=1, source_target_pairs={{0,3},{1,0},{2,1},{3,2},{4,7},{5,4},{6,5},{7,6},{8,11},{9,8},{10,9... | collective-permute-start | bytes 786440 | tf_op jit(solution)/shard_map/ppermute | solution.py:255
  101.6 44.9 %all-to-all-start.1 = ((bf16[128,8,640]{2,1,0:T(8,128)(2,1)}), bf16[128,8,640]{2,1,0:T(8,128)(2,1)S(1)}, u32[]{:S(2)}, u32[]{:S(2)}) async-start(bf16[128,8,640]{2,1,0:T(8,128)(2,1)} %bitcast.34), calls=%async_computation.1 | async-start | bytes 2621440 | tf_op jit(solution)/shard_map/all_to_all | solution.py:362
  149.4 21.8 %all-to-all-start.2 = ((bf16[128,8,128]{2,1,0:T(8,128)(2,1)}), bf16[128,8,128]{2,1,0:T(8,128)(2,1)S(1)}, u32[]{:S(2)}, u32[]{:S(2)}) async-start(bf16[128,8,128]{2,1,0:T(8,128)(2,1)} %bitcast.35), calls=%async_computation.2 | async-start | bytes 524288 | tf_op jit(solution)/shard_map/all_to_all | solution.py:386
  157.0 21.6 %collective-permute-start.9 = (bf16[256,512]{1,0:T(8,128)(2,1)S(1)}, bf16[256,512]{1,0:T(8,128)(2,1)S(1)}, u32[]{:S(2)}, u32[]{:S(2)}) collective-permute-start(bf16[256,512]{1,0:T(8,128)(2,1)S(1)} %get-tuple-element.60), channel_id=1, source_target_pairs={{0,1},{1,2},{2,3},{3,0},{4,5},{5,6},{6,7},{7,4},{8,9},{9,10},{10,1... | collective-permute-start | bytes 786440 | tf_op jit(solution)/shard_map/ppermute | solution.py:255
  161.1 20.8 %collective-permute-start.10 = (bf16[256,512]{1,0:T(8,128)(2,1)S(1)}, bf16[256,512]{1,0:T(8,128)(2,1)S(1)}, u32[]{:S(2)}, u32[]{:S(2)}) collective-permute-start(bf16[256,512]{1,0:T(8,128)(2,1)S(1)} %get-tuple-element.61), channel_id=1, source_target_pairs={{0,2},{1,3},{2,0},{3,1},{4,6},{5,7},{6,4},{7,5},{8,10},{9,11},{10,... | collective-permute-start | bytes 786440 | tf_op jit(solution)/shard_map/ppermute | solution.py:255
  164.5 17.4 %collective-permute-start.11 = (bf16[256,512]{1,0:T(8,128)(2,1)S(1)}, bf16[256,512]{1,0:T(8,128)(2,1)S(1)}, u32[]{:S(2)}, u32[]{:S(2)}) collective-permute-start(bf16[256,512]{1,0:T(8,128)(2,1)S(1)} %get-tuple-element.62), channel_id=1, source_target_pairs={{0,3},{1,0},{2,1},{3,2},{4,7},{5,4},{6,5},{7,6},{8,11},{9,8},{10,9... | collective-permute-start | bytes 786440 | tf_op jit(solution)/shard_map/ppermute | solution.py:255
  171.3 11.5 %collective-permute-start.14 = (bf16[256,512]{1,0:T(8,128)(2,1)S(1)}, bf16[256,512]{1,0:T(8,128)(2,1)S(1)}, u32[]{:S(2)}, u32[]{:S(2)}) collective-permute-start(bf16[256,512]{1,0:T(8,128)(2,1)S(1)} %bitcast.29), channel_id=1, source_target_pairs={{0,1},{1,2},{2,3},{3,0},{4,5},{5,6},{6,7},{7,4},{8,9},{9,10},{10,1... | collective-permute-start | bytes 786440 | tf_op jit(solution)/shard_map/ppermute | solution.py:255
  175.3 11.7 %collective-permute-start.13 = (bf16[256,512]{1,0:T(8,128)(2,1)S(1)}, bf16[256,512]{1,0:T(8,128)(2,1)S(1)}, u32[]{:S(2)}, u32[]{:S(2)}) collective-permute-start(bf16[256,512]{1,0:T(8,128)(2,1)S(1)} %bitcast.30), channel_id=1, source_target_pairs={{0,2},{1,3},{2,0},{3,1},{4,6},{5,7},{6,4},{7,5},{8,10},{9,11},{10,... | collective-permute-start | bytes 786440 | tf_op jit(solution)/shard_map/ppermute | solution.py:255
  178.7 10.2 %collective-permute-start.12 = (bf16[256,512]{1,0:T(8,128)(2,1)S(1)}, bf16[256,512]{1,0:T(8,128)(2,1)S(1)}, u32[]{:S(2)}, u32[]{:S(2)}) collective-permute-start(bf16[256,512]{1,0:T(8,128)(2,1)S(1)} %bitcast.31), channel_id=1, source_target_pairs={{0,3},{1,0},{2,1},{3,2},{4,7},{5,4},{6,5},{7,6},{8,11},{9,8},{10,9... | collective-permute-start | bytes 786440 | tf_op jit(solution)/shard_map/ppermute | solution.py:255
  (1 other events, 9.3 us)

commit v5 on v4

v5 whole, which is shorter than its diff:
```python
import functools

import jax
import jax.numpy as jnp
from jax import lax
from jax.experimental import pallas as pl
from jax.experimental.pallas import tpu as pltpu
from jax.sharding import Mesh
from jax.sharding import PartitionSpec as P

BLOCK = 64
LANES = 128
WIDE = ("y", "z", "core")
F32 = jnp.float32
BF16 = jnp.bfloat16
VMEM = pl.BlockSpec(memory_space=pltpu.VMEM)
HBM = pl.BlockSpec(memory_space=pltpu.HBM)
SMEM = pl.BlockSpec(memory_space=pltpu.SMEM)


def dot(left, right, left_dim, right_dim):
    dims = (((left_dim,), (right_dim,)), ((), ()))
    return lax.dot_general(left, right, dims, preferred_element_type=F32)


def call(kernel, name, outs, in_specs, args, flops, out_specs=None, scratch=(), vmem=24):
    moved = sum(a.size * a.dtype.itemsize for a in args) + sum(
        o.size * o.dtype.itemsize for o in outs
    )
    args = [
        pltpu.with_memory_space_constraint(a, pltpu.HBM) if spec is HBM else a
        for a, spec in zip(args, in_specs, strict=True)
    ]
    out_specs = out_specs or [VMEM] * len(outs)
    outs = [
        pltpu.HBM(o.shape, o.dtype) if spec is HBM else o
        for o, spec in zip(outs, out_specs, strict=True)
    ]
    return pl.pallas_call(
        kernel,
        out_shape=outs,
        in_specs=in_specs,
        out_specs=out_specs,
        scratch_shapes=scratch,
        compiler_params=pltpu.CompilerParams(vmem_limit_bytes=vmem << 20),
        cost_estimate=pl.CostEstimate(flops=flops, bytes_accessed=moved, transcendentals=0),
        name=name,
    )(*args)


def shape(rows, cols, dtype):
    return jax.ShapeDtypeStruct((rows, cols), dtype)


def started(source, target, sem):
    copy = pltpu.make_async_copy(source, target, sem)
    copy.start()
    return copy


def turned_quarters(rep_ref, feats_hbm, feats_ref, sems, replicas):
    quarter = feats_ref.shape[0] // replicas
    copies = []
    for k in range(replicas):
        at = pl.multiple_of(((rep_ref[0] + k) % replicas) * quarter, quarter)
        copies.append(
            started(
                feats_hbm.at[pl.ds(at, quarter), :],
                feats_ref.at[pl.ds(k * quarter, quarter), :],
                sems.at[k],
            )
        )
    return copies


def count_kernel(
    replicas, rep_ref, place_ref, words_ref, feats_hbm, local_t_hbm, halo_ref, halo_t_hbm, sums_hbm,
    counts_ref, turned_ref, feats_ref, sums_ref, sems,
):
    feats_copies = turned_quarters(rep_ref, feats_hbm, feats_ref, sems, replicas)
    counts_ref[...] = jnp.zeros_like(counts_ref)
    row = lax.broadcasted_iota(jnp.int32, (BLOCK, LANES), 0)
    lane = lax.broadcasted_iota(jnp.int32, (BLOCK, LANES), 1)
    word_lane = (row % 32) * 4 + (lane % BLOCK) // 16
    shift = lane % 16
    half = lane // BLOCK

    def add_tile(t, carry):
        place = place_ref[t]
        dst = pl.multiple_of((place // 64) * BLOCK, BLOCK)
        src = place % 64
        upper = jnp.broadcast_to(words_ref[pl.ds(2 * t, 1), :], (32, LANES))
        lower = jnp.broadcast_to(words_ref[pl.ds(2 * t + 1, 1), :], (32, LANES))
        words = jnp.concatenate([upper, lower], axis=0)
        picked = jnp.take_along_axis(words, word_lane, axis=1)
        bits = jnp.right_shift(picked, shift) & 1
        tile = jnp.where(half == src % 2, bits, 0).astype(F32).astype(BF16)
        rows = pl.ds(dst, BLOCK)
        cols = pl.ds(pl.multiple_of((src // 2) * LANES, LANES), LANES)
        counts_ref[rows, cols] = counts_ref[rows, cols] + tile
        return carry

    lax.fori_loop(0, place_ref.shape[0], add_tile, 0, unroll=4)
    split = local_t_hbm.shape[0]
    turned_ref[...] = counts_ref[...].T
    local_copy = started(turned_ref.at[pl.ds(0, split), :], local_t_hbm, sems.at[replicas])
    halo_copy = started(
        turned_ref.at[pl.ds(split, turned_ref.shape[0] - split), :], halo_t_hbm, sems.at[replicas + 1]
    )
    halo_ref[...] = counts_ref[:, split:]
    for copy in feats_copies:
        copy.wait()
    rows_done = 256
    for at in range(0, counts_ref.shape[0], rows_done):
        rows = pl.ds(at, rows_done)
        sums_ref[rows, :] = dot(counts_ref[rows, :split], feats_ref[...], 1, 0)
    sums_copy = started(sums_ref, sums_hbm, sems.at[replicas + 2])
    local_copy.wait()
    halo_copy.wait()
    sums_copy.wait()


def quarter_copies(local_hbm, local_ref, sems, order):
    quarter = local_ref.shape[0] // len(order)
    rows = {k: pl.ds(k * quarter, quarter) for k in order}
    return rows, {
        k: started(local_hbm.at[rows[k], :], local_ref.at[rows[k], :], sems.at[k]) for k in order
    }


def sum_kernel(
    counts_ref, incoming_ref, local_hbm, own_ref, send1, send2, send3, local_ref, total_ref, sems
):
    order = (2, 1, 3, 0)
    quarters, copies = quarter_copies(local_hbm, local_ref, sems, order)
    for rows in quarters.values():
        total_ref[rows, :] = dot(counts_ref[rows, :], incoming_ref[...], 1, 0)
    for k, rows in quarters.items():
        copies[k].wait()
        total = total_ref[rows, :] + local_ref[rows, :]
        if k:
            (send1, send2, send3)[k - 1][...] = total.astype(BF16)
        else:
            own_ref[...] = total


def dense_quarter(agg, feats, grad_out, scale, w_self, w_neigh):
    pre = dot(agg, w_neigh, 1, 0) + dot(feats, w_self, 1, 0)
    sigmoid = jax.nn.sigmoid(pre)
    grad_pre = (grad_out.astype(F32) * sigmoid * (1.0 + pre * (1.0 - sigmoid))).astype(BF16)
    grad_agg = (dot(grad_pre, w_neigh, 1, 1) * scale).astype(BF16)
    return pre * sigmoid, grad_pre, grad_agg


def own_kernel(
    replicas, rep_ref, agg_ref, grad_ref, feats_hbm, w_self_ref, w_neigh_ref, scale_ref,
    out_ref, base_hbm, grad_agg_ref, weights_ref, feats_ref, base_ref, sems,
):
    quarter, feat_width = agg_ref.shape
    share = feat_width // replicas
    own_rows = pl.ds(pl.multiple_of(rep_ref[0] * quarter, quarter), quarter)
    feats_copy = started(feats_hbm.at[own_rows, :], feats_ref, sems.at[0])
    feats_copy.wait()
    out, grad_pre, grad_agg = dense_quarter(
        agg_ref[...], feats_ref[...], grad_ref[...], scale_ref[:quarter, :], w_self_ref[...],
        w_neigh_ref[...],
    )
    out_ref[...] = out.astype(BF16)
    grad_agg_ref[...] = grad_agg
    base_ref[...] = dot(grad_pre, w_self_ref[...], 1, 1)
    base_copy = started(base_ref, base_hbm, sems.at[1])
    share_cols = pl.ds(pl.multiple_of(rep_ref[0] * share, LANES), share)
    weights_ref[:share, :] = dot(feats_ref[:, share_cols], grad_pre, 0, 0)
    weights_ref[share:, :] = dot(agg_ref[:, share_cols], grad_pre, 0, 0)
    base_copy.wait()


def dense_kernel(
    replicas, rep_ref, agg1, agg2, agg3, grad1, grad2, grad3, feats_hbm, w_self_ref, w_neigh_ref,
    scale_ref, halo_t_hbm, own_grad_ref, own_weights_ref, grad_agg_hbm, joint_hbm,
    grad_ref, feats_ref, halo_t_ref, grad_agg_ref, joint_ref, sems,
):
    aggs = {1: agg1, 2: agg2, 3: agg3}
    quarter, feat_width = agg1.shape
    share = feat_width // replicas
    halo_rows = halo_t_ref.shape[0]
    step = min(256, halo_rows)
    starts = range(0, halo_rows, step)
    feats_copies, grad_copies = {}, {}
    for k, grad in zip(aggs, (grad1, grad2, grad3), strict=True):
        at = pl.multiple_of(((rep_ref[0] + k) % replicas) * quarter, quarter)
        feats_copies[k] = started(feats_hbm.at[pl.ds(at, quarter), :], feats_ref.at[k - 1], sems.at[k - 1])
        grad_copies[k] = started(grad, grad_ref.at[k - 1], sems.at[replicas + k - 1])
    at = 2 * replicas
    halo_copies = [
        started(halo_t_hbm.at[pl.ds(i, step), :], halo_t_ref.at[pl.ds(i, step), :], sems.at[at + n])
        for n, i in enumerate(starts)
    ]
    at += len(starts)
    share_cols = pl.ds(pl.multiple_of(rep_ref[0] * share, LANES), share)
    grad_self = own_weights_ref[:share, :]
    grad_neigh = own_weights_ref[share:, :]
    grad_agg_ref[:quarter, :] = own_grad_ref[...]
    for k, agg_ref in aggs.items():
        rows = pl.ds(k * quarter, quarter)
        feats_copies[k].wait()
        grad_copies[k].wait()
        _, grad_pre, grad_agg = dense_quarter(
            agg_ref[...], feats_ref[k - 1], grad_ref[k - 1], scale_ref[rows, :], w_self_ref[...],
            w_neigh_ref[...],
        )
        grad_agg_ref[rows, :] = grad_agg
        grad_self = grad_self + dot(feats_ref[k - 1, :, share_cols], grad_pre, 0, 0)
        grad_neigh = grad_neigh + dot(agg_ref[:, share_cols], grad_pre, 0, 0)
    grad_agg_copy = started(grad_agg_ref, grad_agg_hbm, sems.at[at])
    per_peer = (joint_ref.shape[1] - feat_width) // LANES
    half = feat_width // LANES // 2
    weights = jnp.concatenate([grad_self, grad_neigh], axis=0)
    for core in range(2):
        for n in range(half):
            for g in range(2 * share // 8):
                tile = n * (2 * share // 8) + g
                row = (tile // per_peer * 2 + core) * 8
                lane = feat_width + tile % per_peer * LANES
                col = (core * half + n) * LANES
                joint_ref[row : row + 8, lane : lane + LANES] = weights[
                    g * 8 : g * 8 + 8, col : col + LANES
                ].astype(BF16)
    joint_copies = []
    for n, i in enumerate(starts):
        rows = pl.ds(i, step)
        halo_copies[n].wait()
        joint_ref[rows, :feat_width] = dot(halo_t_ref[rows, :], grad_agg_ref[...], 1, 0).astype(BF16)
        joint_copies.append(started(joint_ref.at[rows, :], joint_hbm.at[rows, :], sems.at[at + 1 + n]))
    grad_agg_copy.wait()
    for copy in joint_copies:
        copy.wait()


def local_kernel(
    replicas, counts_hbm, grad_hbm, base_hbm, local_hbm, counts_ref, grad_ref, base_ref, local_ref, sems
):
    copies = [
        started(*pair, sems.at[n])
        for n, pair in enumerate(
            ((counts_hbm, counts_ref), (grad_hbm, grad_ref), (base_hbm, base_ref))
        )
    ]
    for copy in copies:
        copy.wait()
    quarter = base_ref.shape[0]
    for k in range(replicas):
        rows = pl.ds(k * quarter, quarter)
        total = dot(counts_ref[rows, :], grad_ref[...], 1, 0)
        local_ref[rows, :] = total if k else total + base_ref[...]
    copy = started(local_ref, local_hbm, sems.at[3])
    copy.wait()


def return_kernel(
    replicas, slots_ref, joint_ref, local_hbm, tile_ref, own_ref, send1, send2, send3,
    local_ref, total_ref, sems,
):
    quarter, feat_width = own_ref.shape
    halo_rows = joint_ref.shape[0]
    order = (2, 1, 3, 0)
    quarters, copies = quarter_copies(local_hbm, local_ref, sems, order)
    lanes = joint_ref.shape[1] - feat_width
    tiles = joint_ref[:, feat_width:].astype(F32).reshape(halo_rows // 8, 8, lanes)
    tile = tiles.sum(axis=0, keepdims=True)
    many = tile_ref.shape[0]
    tile_ref[...] = (
        jnp.broadcast_to(tile, (many // 8, 8, lanes)).reshape(many, lanes).astype(BF16)
    )
    slots = jnp.broadcast_to(slots_ref[...], (quarter, halo_rows))
    row = lax.broadcasted_iota(jnp.int32, (quarter, halo_rows), 0)
    for k, rows in quarters.items():
        pick = jnp.where(row + k * quarter == slots, 1.0, 0.0).astype(BF16)
        total_ref[rows, :] = dot(pick, joint_ref[:, :feat_width], 1, 0)
    for k, rows in quarters.items():
        copies[k].wait()
        total = total_ref[rows, :] + local_ref[rows, :]
        if k:
            (send1, send2, send3)[k - 1][...] = total.astype(BF16)
        else:
            own_ref[...] = total


def place_kernel(replicas, parts_ref, self_ref, neigh_ref):
    share = self_ref.shape[0] // replicas
    cores = 2
    block = parts_ref.shape[0] // (cores * replicas)
    for core in range(cores):
        for rep in range(replicas):
            for n in range(block // (2 * share)):
                at = (core * replicas + rep) * block + n * 2 * share
                lane = (core * (block // (2 * share)) + n) * LANES
                rows = slice(rep * share, (rep + 1) * share)
                self_ref[rows, lane : lane + LANES] = parts_ref[at : at + share, :]
                neigh_ref[rows, lane : lane + LANES] = parts_ref[at + share : at + 2 * share, :]


def send_to(x, step, replicas):
    return lax.ppermute(x, "rep", [(i, (i + step) % replicas) for i in range(replicas)])


def from_ahead(x, replicas):
    return [send_to(x, replicas - k, replicas) for k in range(1, replicas)]


def on_device(
    node_feats, w_self, w_neigh, send_rows, tile_dst, tile_src, tile_bits, norm_count, grad_out
):
    node_rows, feat_width = node_feats.shape
    peer_count = lax.axis_size(WIDE)
    replicas = lax.axis_size("rep")
    slot_count = send_rows.shape[2]
    tile_total = tile_dst.shape[2]
    quarter = node_rows // replicas
    share = feat_width // replicas
    rep_index = lax.axis_index("rep")
    rep_ref = rep_index.reshape(1).astype(jnp.int32)
    dst_count = node_rows // BLOCK
    halo_rows = peer_count * slot_count
    first_row = rep_index * quarter
    first_block = rep_index * (quarter // BLOCK)
    send_outs = [shape(quarter, feat_width, BF16)] * (replicas - 1)

    slot_rows = send_rows[0].reshape(-1)
    every_row = lax.broadcasted_iota(jnp.int32, (node_rows, halo_rows), 0)
    send_pick = (every_row == slot_rows[None, :]).astype(BF16)
    outgoing = dot(send_pick, node_feats, 0, 0).astype(BF16)
    incoming = lax.all_to_all(outgoing, WIDE, 0, 0, tiled=True)

    scale = lax.rsqrt(norm_count.astype(F32))
    scale = lax.dynamic_slice_in_dim(jnp.concatenate([scale, scale]), first_row, node_rows, 0)
    scale = scale[:, None]
    grad_outs = [grad_out] + from_ahead(grad_out, replicas)
    dst = (tile_dst[0, 0] - first_block) % dst_count
    src = tile_src[0, 0]
    src = jnp.where(src < dst_count, (src - first_block) % dst_count, src)
    block_flops = 2 * node_rows * halo_rows * feat_width
    local_t, counts_halo, halo_t, sums_local = call(
        functools.partial(count_kernel, replicas),
        "tile_counts",
        [
            shape(node_rows, node_rows, BF16),
            shape(node_rows, halo_rows, BF16),
            shape(halo_rows, node_rows, BF16),
            shape(node_rows, feat_width, F32),
        ],
        [SMEM, SMEM, VMEM, HBM],
        (rep_ref, dst * 64 + src, tile_bits.reshape(tile_total * 2, LANES), node_feats),
        tile_total * BLOCK * LANES * 20 + block_flops,
        out_specs=[HBM, VMEM, HBM, HBM],
        scratch=[
            pltpu.VMEM((node_rows, node_rows + halo_rows), BF16),
            pltpu.VMEM((node_rows + halo_rows, node_rows), BF16),
            pltpu.VMEM((node_rows, feat_width), BF16),
            pltpu.VMEM((node_rows, feat_width), F32),
            pltpu.SemaphoreType.DMA((replicas + 3,)),
        ],
    )
    turned_slots = ((slot_rows - first_row) % node_rows)[None, :]
    incoming, counts_halo, sums_local, scale, turned_slots, *grad_outs = lax.optimization_barrier(
        (incoming, counts_halo, sums_local, scale, turned_slots, *grad_outs)
    )

    own_sums, *sends = call(
        sum_kernel,
        "neighbour_sums",
        [shape(quarter, feat_width, F32)] + send_outs,
        [VMEM, VMEM, HBM],
        (counts_halo, incoming, sums_local),
        block_flops,
        scratch=[pltpu.VMEM((node_rows, feat_width), F32)] * 2
        + [pltpu.SemaphoreType.DMA((replicas,))],
    )
    for k in range(1, replicas):
        own_sums = own_sums + send_to(sends[k - 1], k, replicas).astype(F32)
    own_agg = (own_sums * scale[:quarter]).astype(BF16)
    aggs = from_ahead(own_agg, replicas)
    joint_width = feat_width + 2 * share * feat_width // halo_rows
    halo_steps = max(1, halo_rows // 256)
    out_feats, own_base, own_grad_agg, own_weights = call(
        functools.partial(own_kernel, replicas),
        "dense_own",
        [
            shape(quarter, feat_width, BF16),
            shape(quarter, feat_width, F32),
            shape(quarter, feat_width, BF16),
            shape(2 * share, feat_width, F32),
        ],
        [SMEM, VMEM, VMEM, HBM, VMEM, VMEM, VMEM],
        (rep_ref, own_agg, grad_outs[0], node_feats, w_self, w_neigh, scale),
        block_flops // 2,
        out_specs=[VMEM, HBM, VMEM, VMEM],
        scratch=[
            pltpu.VMEM((quarter, feat_width), BF16),
            pltpu.VMEM((quarter, feat_width), F32),
            pltpu.SemaphoreType.DMA((2,)),
        ],
    )
    grad_agg, joint = call(
        functools.partial(dense_kernel, replicas),
        "dense_rest",
        [shape(node_rows, feat_width, BF16), shape(halo_rows, joint_width, BF16)],
        [SMEM] + [VMEM] * 3 + [HBM] * 4 + [VMEM] * 3 + [HBM, VMEM, VMEM],
        (
            rep_ref, *aggs, *grad_outs[1:], node_feats, w_self, w_neigh, scale, halo_t, own_grad_agg,
            own_weights,
        ),
        2 * block_flops,
        out_specs=[HBM, HBM],
        scratch=[
            pltpu.VMEM((replicas - 1, quarter, feat_width), BF16),
            pltpu.VMEM((replicas - 1, quarter, feat_width), BF16),
            pltpu.VMEM((halo_rows, node_rows), BF16),
            pltpu.VMEM((node_rows, feat_width), BF16),
            pltpu.VMEM((halo_rows, joint_width), BF16),
            pltpu.SemaphoreType.DMA((1 + 2 * replicas + 2 * halo_steps,)),
        ],
    )
    returned = lax.all_to_all(joint, WIDE, 0, 0, tiled=True)
    (local_grad,) = call(
        functools.partial(local_kernel, replicas),
        "local_rows",
        [shape(node_rows, feat_width, F32)],
        [HBM] * 3,
        (local_t, grad_agg, own_base),
        block_flops,
        out_specs=[HBM],
        scratch=[
            pltpu.VMEM((node_rows, node_rows), BF16),
            pltpu.VMEM((node_rows, feat_width), BF16),
            pltpu.VMEM((quarter, feat_width), F32),
            pltpu.VMEM((node_rows, feat_width), F32),
            pltpu.SemaphoreType.DMA((4,)),
        ],
    )

    lanes = joint_width - feat_width
    chips = peer_count // 2
    copies, own_grad, *sends = call(
        functools.partial(return_kernel, replicas),
        "returned_rows",
        [shape(chips * slot_count, lanes, BF16), shape(quarter, feat_width, F32)] + send_outs,
        [VMEM, VMEM, HBM],
        (turned_slots, returned, local_grad),
        block_flops,
        scratch=[pltpu.VMEM((node_rows, feat_width), F32)] * 2
        + [pltpu.SemaphoreType.DMA((replicas,))],
    )
    for k in range(1, replicas):
        own_grad = own_grad + send_to(sends[k - 1], k, replicas).astype(F32)

    tiles = lax.all_to_all(copies, ("y", "z"), 0, 0, tiled=True)
    halves = 2 * replicas
    parts = lax.all_to_all(
        jnp.broadcast_to(tiles, (halves,) + tiles.shape).reshape(-1, lanes), ("core", "rep"), 0, 0, tiled=True
    )
    parts = (
        parts.reshape(halves * chips, slot_count, -1, LANES)
        .transpose(0, 2, 1, 3)
        .reshape(-1, LANES)
    )
    grad_self, grad_neigh = call(
        functools.partial(place_kernel, replicas),
        "place",
        [shape(feat_width, feat_width, BF16)] * 2,
        [VMEM],
        (parts,),
        0,
    )
    return out_feats, own_grad.astype(BF16), grad_self, grad_neigh


def solution(mesh):
    fine = Mesh(
        mesh.devices.reshape(8, mesh.shape["wide"] // 16, 2, mesh.shape["rep"]), WIDE + ("rep",)
    )
    in_specs = (
        P(WIDE, None),
        P(),
        P(),
        P(WIDE, None, "rep"),
        P(WIDE, "rep", None),
        P(WIDE, "rep", None),
        P(WIDE, "rep", None),
        P(WIDE),
        P(WIDE + ("rep",), None),
    )
    out_specs = (P(WIDE + ("rep",), None), P(WIDE + ("rep",), None), P(), P())
    return jax.shard_map(
        on_device, mesh=fine, in_specs=in_specs, out_specs=out_specs, check_vma=False
    )
```

time: 193 us -> 201 us (1.041); the launches traced: 190 us -> 200 us
  blocking collectives: 0 us -> 17.6 us
  starting transfers between devices: 89.1 us -> 77.6 us
  Pallas kernels: 24.5 us -> 30.3 us
  matrix products: 9.13 us -> 3.53 us
  waiting for transfers between devices: 63.9 us -> 66.8 us
    all_to_all x0 -> x1, blocking collectives: none -> 17.6 us  [on_device(): tiles = lax.all_to_all(copies, ('y', 'z'), 0, 0, tiled=True)]
    ppermute x15 -> x12, starting transfers between devices: 53.6 us -> 43.2 us  [send_to(): lax.ppermute(x, 'rep', [(i, (i + step) % replicas) for i in range(replica...]
    ppermute x15 -> x12, waiting for transfers between devices: 19.7 us -> 25.8 us  [send_to(): lax.ppermute(x, 'rep', [(i, (i + step) % replicas) for i in range(replica...]
    pallas_call x5 -> x7, Pallas kernels: 24.5 us -> 30.3 us  [call(): pl.pallas_call(kernel, out_shape=outs, in_specs=in_specs, out_specs=out_s...]
    dot_general x3 -> x1, matrix products: 9.13 us -> 3.53 us  [dot(): return lax.dot_general(left, right, dims, preferred_element_type=F32)]
    all_to_all x1, waiting for transfers between devices: 3.6 us -> 0.01 us  [on_device(): lax.all_to_all(jnp.broadcast_to(tiles, (halves,) + tiles.shape).reshape(-...]
  transfers between devices with their start and end apart: 18 -> 15, of which waited for: 9 -> 8; matrix products, arithmetic and copies ran while one was open for 4% -> 1% of each run, Pallas kernels for 5% -> 9%
where the time goes in v5:
time: 201 us; the launch traced here: 200 us
  starting transfers between devices  77.6 us (39%)
  waiting for transfers between devices  66.8 us (33%)
  Pallas kernels  30.3 us (15%)
  blocking collectives  17.6 us (9%)
  matrix products  3.53 us (2%)
  local copies, waits for them, and re-layouts  2.46 us (1%)
    ppermute x12, starting transfers between devices, send_to(): lax.ppermute(x, 'rep', [(i, (i + step) % replicas) for i in range(replica...  43.2 us
    all_to_all x1, waiting for transfers between devices, on_device(): returned = lax.all_to_all(joint, WIDE, 0, 0, tiled=True)  31 us
    pallas_call x7, Pallas kernels, call(): pl.pallas_call(kernel, out_shape=outs, in_specs=in_specs, out_specs=out_s...  30.3 us
    ppermute x12, waiting for transfers between devices, send_to(): lax.ppermute(x, 'rep', [(i, (i + step) % replicas) for i in range(replica...  25.8 us
    all_to_all x1, starting transfers between devices, on_device(): incoming = lax.all_to_all(outgoing, WIDE, 0, 0, tiled=True)  18.6 us
    all_to_all x1, blocking collectives, on_device(): tiles = lax.all_to_all(copies, ('y', 'z'), 0, 0, tiled=True)  17.6 us
    all_to_all x1, waiting for transfers between devices, on_device(): incoming = lax.all_to_all(outgoing, WIDE, 0, 0, tiled=True)  10 us
    all_to_all x1, starting transfers between devices, on_device(): returned = lax.all_to_all(joint, WIDE, 0, 0, tiled=True)  9.34 us
  transfers between devices with their start and end apart: 15, of which 8 were waited for; matrix products, arithmetic and copies ran while one was open for 1% of the time, Pallas kernels for 9%

profile of v5, /device:TPU:1, one launch (start us, length us, event | category | flops | bytes accessed | tf_op | source)
XLA Modules:
  0.0 200.5 jit_solution(18159209604049222312)
XLA Ops:
  1.5 3.5 %fusion.3 = bf16[128,8,512]{2,1,0:T(8,128)(2,1)} fusion(bf16[1024,512]{1,0:T(8,128)(2,1)} %feats_hbm.5, s32[1024]{0:T(1024)S(1)} %eq.15), kind=kOutput, calls=%fused_computation.4 | convolution fusion | flops 1075314688 | bytes 2101248 | tf_op jit(solution)/shard_map/dot_general | solution.py:23
  5.1 18.6 %all-to-all-start = ((bf16[128,8,512]{2,1,0:T(8,128)(2,1)}), bf16[128,8,512]{2,1,0:T(8,128)(2,1)S(1)}, u32[]{:S(2)}, u32[]{:S(2)}) async-start(bf16[128,8,512]{2,1,0:T(8,128)(2,1)} %fusion.3), calls=%async_computation | async-start | bytes 2097152 | tf_op jit(solution)/shard_map/all_to_all | solution.py:333
  23.7 4.7 %collective-permute-start.1 = (bf16[256,512]{1,0:T(8,128)(2,1)S(1)}, bf16[256,512]{1,0:T(8,128)(2,1)}, u32[]{:S(2)}, u32[]{:S(2)}) collective-permute-start(bf16[256,512]{1,0:T(8,128)(2,1)S(1)} %copy-done.2), channel_id=1, source_target_pairs={{0,2},{1,3},{2,0},{3,1},{4,6},{5,7},{6,4},{7,5},{8,10},{9,11},{10,... | collective-permute-start | bytes 786440 | tf_op jit(solution)/shard_map/ppermute | solution.py:304
  28.3 2.8 %collective-permute-start = (bf16[256,512]{1,0:T(8,128)(2,1)S(1)}, bf16[256,512]{1,0:T(8,128)(2,1)}, u32[]{:S(2)}, u32[]{:S(2)}) collective-permute-start(bf16[256,512]{1,0:T(8,128)(2,1)S(1)} %copy-done.2), channel_id=1, source_target_pairs={{0,3},{1,0},{2,1},{3,2},{4,7},{5,4},{6,5},{7,6},{8,11},{9,8},{10,9... | collective-permute-start | bytes 786440 | tf_op jit(solution)/shard_map/ppermute | solution.py:304
  33.8 10.0 %tile_counts.1 = (bf16[1024,1024]{1,0:T(8,128)(2,1)}, bf16[1024,1024]{1,0:T(8,128)(2,1)S(1)}, bf16[1024,1024]{1,0:T(8,128)(2,1)}, f32[1024,512]{1,0:T(8,128)}) custom-call(s32[1]{0:T(128)} %bitcast.rep_ref, s32[128]{0:T(128)S(1)} %fusion.7.place_ref, s32[256,128]{1,0:T(8,128)S(1)} %bitcast.24, bf16[1024,512]{1,0:T(8,128)(2,1)} %feats_hbm.5), custom_call_target="tpu_custom_call" | custom-call | flops 1094713344 | bytes 9568772 | tf_op jit(solution)/shard_map/tile_counts/pallas_call | solution.py:39
  44.1 10.0 %all-to-all-done = bf16[128,8,512]{2,1,0:T(8,128)(2,1)S(1)} async-done(((bf16[128,8,512]{2,1,0:T(8,128)(2,1)}), bf16[128,8,512]{2,1,0:T(8,128)(2,1)S(1)}, u32[]{:S(2)}, u32[]{:S(2)}) %all-to-all-start) | async-done | bytes 1048608 | tf_op jit(solution)/shard_map/all_to_all | solution.py:333
  56.7 3.3 %collective-permute-start.3 = (bf16[256,512]{1,0:T(8,128)(2,1)S(1)}, bf16[256,512]{1,0:T(8,128)(2,1)S(1)}, u32[]{:S(2)}, u32[]{:S(2)}) collective-permute-start(bf16[256,512]{1,0:T(8,128)(2,1)S(1)} %get-tuple-element.40), channel_id=1, source_target_pairs={{0,1},{1,2},{2,3},{3,0},{4,5},{5,6},{6,7},{7,4},{8,9},{9,10},{10,1... | collective-permute-start | bytes 786440 | tf_op jit(solution)/shard_map/ppermute | solution.py:304
  59.9 4.4 %collective-permute-start.4 = (bf16[256,512]{1,0:T(8,128)(2,1)S(1)}, bf16[256,512]{1,0:T(8,128)(2,1)S(1)}, u32[]{:S(2)}, u32[]{:S(2)}) collective-permute-start(bf16[256,512]{1,0:T(8,128)(2,1)S(1)} %get-tuple-element.41), channel_id=1, source_target_pairs={{0,2},{1,3},{2,0},{3,1},{4,6},{5,7},{6,4},{7,5},{8,10},{9,11},{10,... | collective-permute-start | bytes 786440 | tf_op jit(solution)/shard_map/ppermute | solution.py:304
  64.3 3.1 %collective-permute-start.5 = (bf16[256,512]{1,0:T(8,128)(2,1)S(1)}, bf16[256,512]{1,0:T(8,128)(2,1)S(1)}, u32[]{:S(2)}, u32[]{:S(2)}) collective-permute-start(bf16[256,512]{1,0:T(8,128)(2,1)S(1)} %get-tuple-element.42), channel_id=1, source_target_pairs={{0,3},{1,0},{2,1},{3,2},{4,7},{5,4},{6,5},{7,6},{8,11},{9,8},{10,9... | collective-permute-start | bytes 786440 | tf_op jit(solution)/shard_map/ppermute | solution.py:304
  67.4 5.6 %collective-permute-done.4 = bf16[256,512]{1,0:T(8,128)(2,1)S(1)} collective-permute-done((bf16[256,512]{1,0:T(8,128)(2,1)S(1)}, bf16[256,512]{1,0:T(8,128)(2,1)S(1)}, u32[]{:S(2)}, u32[]{:S(2)}) %collective-permute-start.4) | collective-permute-done | bytes 262176 | tf_op jit(solution)/shard_map/ppermute | solution.py:304
  74.7 5.7 %collective-permute-start.8 = (bf16[256,512]{1,0:T(8,128)(2,1)S(1)}, bf16[256,512]{1,0:T(8,128)(2,1)S(1)}, u32[]{:S(2)}, u32[]{:S(2)}) collective-permute-start(bf16[256,512]{1,0:T(8,128)(2,1)S(1)} %multiply_convert_fusion.agg_ref), channel_id=1, source_target_pairs={{0,1},{1,2},{2,3},{3,0},{4,5},{5,6},{6,7},{7,4},{8,9},{9,10},{10,1... | collective-permute-start | bytes 786440 | tf_op jit(solution)/shard_map/ppermute | solution.py:304
  82.7 4.0 %collective-permute-start.6 = (bf16[256,512]{1,0:T(8,128)(2,1)S(1)}, bf16[256,512]{1,0:T(8,128)(2,1)S(1)}, u32[]{:S(2)}, u32[]{:S(2)}) collective-permute-start(bf16[256,512]{1,0:T(8,128)(2,1)S(1)} %multiply_convert_fusion.agg_ref), channel_id=1, source_target_pairs={{0,3},{1,0},{2,1},{3,2},{4,7},{5,4},{6,5},{7,6},{8,11},{9,8},{10,9... | collective-permute-start | bytes 786440 | tf_op jit(solution)/shard_map/ppermute | solution.py:304
  86.9 3.4 %dense_own.1 = (bf16[256,512]{1,0:T(8,128)(2,1)}, f32[256,512]{1,0:T(8,128)}, bf16[256,512]{1,0:T(8,128)(2,1)S(1)}, f32[256,512]{1,0:T(8,128)S(1)}) custom-call(s32[1]{0:T(128)} %bitcast.rep_ref, bf16[256,512]{1,0:T(8,128)(2,1)S(1)} %multiply_convert_fusion.agg_ref, bf16[256,512]{1,0:T(8,128)(2,1)S(1)} %copy-done.2, bf16[1024,512]{1,0:T(8,128)(2,1)} %feats_hbm.5, ...), custom_call_target="tpu_custom_call" | custom-call | flops 536870912 | bytes 4198404 | tf_op jit(solution)/shard_map/dense_own/pallas_call | solution.py:39
  93.3 6.0 %dense_rest.1 = (bf16[1024,512]{1,0:T(8,128)(2,1)}, bf16[1024,640]{1,0:T(8,128)(2,1)}) custom-call(s32[1]{0:T(128)} %bitcast.rep_ref, bf16[256,512]{1,0:T(8,128)(2,1)S(1)} %collective-permute-done.6.agg1, bf16[256,512]{1,0:T(8,128)(2,1)S(1)} %collective-permute-done.7.agg2, bf16[256,512]{1,0:T(8,128)(2,1)S(1)} %collective-permute-done.8.agg3, ...), custom_call_target="tpu_custom_call" | custom-call | flops 2147483648 | bytes 8916996 | tf_op jit(solution)/shard_map/dense_rest/pallas_call | solution.py:39
  99.2 9.3 %all-to-all-start.1 = ((bf16[128,8,640]{2,1,0:T(8,128)(2,1)}), bf16[128,8,640]{2,1,0:T(8,128)(2,1)S(1)}, u32[]{:S(2)}, u32[]{:S(2)}) async-start(bf16[128,8,640]{2,1,0:T(8,128)(2,1)} %bitcast.25), calls=%async_computation.1 | async-start | bytes 2621440 | tf_op jit(solution)/shard_map/all_to_all | solution.py:424
  108.6 4.6 %local_rows.1.local_hbm = f32[1024,512]{1,0:T(8,128)} custom-call(bf16[1024,1024]{1,0:T(8,128)(2,1)} %get-tuple-element.54.counts_hbm, bf16[1024,512]{1,0:T(8,128)(2,1)} %get-tuple-element.55.grad_hbm, f32[256,512]{1,0:T(8,128)} %get-tuple-element.56.base_hbm), custom_call_target="tpu_custom_call" | custom-call | flops 1073741824 | bytes 5767168 | tf_op jit(solution)/shard_map/local_rows/pallas_call | solution.py:39
  113.2 31.0 %all-to-all-done.1 = bf16[128,8,640]{2,1,0:T(8,128)(2,1)S(1)} async-done(((bf16[128,8,640]{2,1,0:T(8,128)(2,1)}), bf16[128,8,640]{2,1,0:T(8,128)(2,1)S(1)}, u32[]{:S(2)}, u32[]{:S(2)}) %all-to-all-start.1) | async-done | bytes 1310752 | tf_op jit(solution)/shard_map/all_to_all | solution.py:424
  146.8 17.6 %all_to_all.43 = bf16[64,8,128]{2,1,0:T(8,128)(2,1)S(1)} all-to-all(bf16[64,8,128]{2,1,0:T(8,128)(2,1)S(1)} %bitcast.23), channel_id=1, replica_groups=mesh['y'=8,'z'=8,'core'=2,'rep'=4] {'y','z'}, dimensions={0} | all-to-all | bytes 262144 | tf_op jit(solution)/shard_map/all_to_all | solution.py:457
  165.5 6.5 %all-to-all-start.3 = ((bf16[8,512,128]{2,1,0:T(8,128)(2,1)}), bf16[8,512,128]{2,1,0:T(8,128)(2,1)S(1)}, u32[]{:S(2)}, u32[]{:S(2)}) async-start(bf16[8,512,128]{2,1,0:T(8,128)(2,1)} %broadcast_in_dim.8), calls=%async_computation.3 | async-start | bytes 2097152 | tf_op jit(solution)/shard_map/all_to_all | solution.py:459
  172.1 3.3 %collective-permute-start.9 = (bf16[256,512]{1,0:T(8,128)(2,1)S(1)}, bf16[256,512]{1,0:T(8,128)(2,1)S(1)}, u32[]{:S(2)}, u32[]{:S(2)}) collective-permute-start(bf16[256,512]{1,0:T(8,128)(2,1)S(1)} %get-tuple-element.58), channel_id=1, source_target_pairs={{0,1},{1,2},{2,3},{3,0},{4,5},{5,6},{6,7},{7,4},{8,9},{9,10},{10,1... | collective-permute-start | bytes 786440 | tf_op jit(solution)/shard_map/ppermute | solution.py:304
  175.3 4.3 %collective-permute-start.10 = (bf16[256,512]{1,0:T(8,128)(2,1)S(1)}, bf16[256,512]{1,0:T(8,128)(2,1)S(1)}, u32[]{:S(2)}, u32[]{:S(2)}) collective-permute-start(bf16[256,512]{1,0:T(8,128)(2,1)S(1)} %get-tuple-element.59), channel_id=1, source_target_pairs={{0,2},{1,3},{2,0},{3,1},{4,6},{5,7},{6,4},{7,5},{8,10},{9,11},{10,... | collective-permute-start | bytes 786440 | tf_op jit(solution)/shard_map/ppermute | solution.py:304
  179.7 3.1 %collective-permute-start.11 = (bf16[256,512]{1,0:T(8,128)(2,1)S(1)}, bf16[256,512]{1,0:T(8,128)(2,1)S(1)}, u32[]{:S(2)}, u32[]{:S(2)}) collective-permute-start(bf16[256,512]{1,0:T(8,128)(2,1)S(1)} %get-tuple-element.60), channel_id=1, source_target_pairs={{0,3},{1,0},{2,1},{3,2},{4,7},{5,4},{6,5},{7,6},{8,11},{9,8},{10,9... | collective-permute-start | bytes 786440 | tf_op jit(solution)/shard_map/ppermute | solution.py:304
  182.8 9.9 %collective-permute-done.9 = bf16[256,512]{1,0:T(8,128)(2,1)S(1)} collective-permute-done((bf16[256,512]{1,0:T(8,128)(2,1)S(1)}, bf16[256,512]{1,0:T(8,128)(2,1)S(1)}, u32[]{:S(2)}, u32[]{:S(2)}) %collective-permute-start.9) | collective-permute-done | bytes 262176 | tf_op jit(solution)/shard_map/ppermute | solution.py:304
  192.6 5.8 %collective-permute-done.10 = bf16[256,512]{1,0:T(8,128)(2,1)S(1)} collective-permute-done((bf16[256,512]{1,0:T(8,128)(2,1)S(1)}, bf16[256,512]{1,0:T(8,128)(2,1)S(1)}, u32[]{:S(2)}, u32[]{:S(2)}) %collective-permute-start.10) | collective-permute-done | bytes 262176 | tf_op jit(solution)/shard_map/ppermute | solution.py:304
  (45 shorter events, 19.3 us)
Async XLA Ops:
  1.5 22.1 %copy-start.2 = (bf16[256,512]{1,0:T(8,128)(2,1)S(1)}, bf16[256,512]{1,0:T(8,128)(2,1)}, u32[]{:S(2)}) copy-start(bf16[256,512]{1,0:T(8,128)(2,1)} %grad_ref) | copy-start | bytes 786436
  5.1 28.6 %copy-start.5 = (s32[1024]{0:T(1024)S(1)}, s32[1024]{0:T(1024)}, u32[]{:S(2)}) copy-start(s32[1024]{0:T(1024)} %param.16) | copy-start | bytes 12292
  5.1 28.7 %copy-start.6 = (s32[1,1,128]{2,1,0:T(1,128)S(1)}, s32[1,1,128]{2,1,0:T(1,128)}, u32[]{:S(2)}) copy-start(s32[1,1,128]{2,1,0:T(1,128)} %param.14) | copy-start | bytes 1540
  5.1 28.7 %copy-start.7 = (s32[1,1,128]{2,1,0:T(1,128)S(1)}, s32[1,1,128]{2,1,0:T(1,128)}, u32[]{:S(2)}) copy-start(s32[1,1,128]{2,1,0:T(1,128)} %param.13) | copy-start | bytes 1540
  5.1 28.7 %copy-start.4 = (s32[1,128,8]{1,2,0:T(8,128)S(1)}, s32[1,128,8]{1,2,0:T(8,128)}, u32[]{:S(2)}) copy-start(s32[1,128,8]{1,2,0:T(8,128)} %param.12) | copy-start | bytes 12292
  5.1 28.7 %copy-start.3 = (s32[1,1,32768]{2,1,0:T(1,128)S(1)}, s32[1,1,32768]{2,1,0:T(1,128)}, u32[]{:S(2)}) copy-start(s32[1,1,32768]{2,1,0:T(1,128)} %param.15) | copy-start | bytes 393220
  5.1 49.0 %all-to-all-start = ((bf16[128,8,512]{2,1,0:T(8,128)(2,1)}), bf16[128,8,512]{2,1,0:T(8,128)(2,1)S(1)}, u32[]{:S(2)}, u32[]{:S(2)}) async-start(bf16[128,8,512]{2,1,0:T(8,128)(2,1)} %fusion.3), calls=%async_computation | async-start | bytes 2097152 | tf_op jit(solution)/shard_map/all_to_all | solution.py:333
  23.7 20.4 %collective-permute-start.1 = (bf16[256,512]{1,0:T(8,128)(2,1)S(1)}, bf16[256,512]{1,0:T(8,128)(2,1)}, u32[]{:S(2)}, u32[]{:S(2)}) collective-permute-start(bf16[256,512]{1,0:T(8,128)(2,1)S(1)} %copy-done.2), channel_id=1, source_target_pairs={{0,2},{1,3},{2,0},{3,1},{4,6},{5,7},{6,4},{7,5},{8,10},{9,11},{10,... | collective-permute-start | bytes 786440 | tf_op jit(solution)/shard_map/ppermute | solution.py:304
  28.3 15.7 %collective-permute-start = (bf16[256,512]{1,0:T(8,128)(2,1)S(1)}, bf16[256,512]{1,0:T(8,128)(2,1)}, u32[]{:S(2)}, u32[]{:S(2)}) collective-permute-start(bf16[256,512]{1,0:T(8,128)(2,1)S(1)} %copy-done.2), channel_id=1, source_target_pairs={{0,3},{1,0},{2,1},{3,2},{4,7},{5,4},{6,5},{7,6},{8,11},{9,8},{10,9... | collective-permute-start | bytes 786440 | tf_op jit(solution)/shard_map/ppermute | solution.py:304
  31.1 13.0 %collective-permute-start.2 = (bf16[256,512]{1,0:T(8,128)(2,1)S(1)}, bf16[256,512]{1,0:T(8,128)(2,1)}, u32[]{:S(2)}, u32[]{:S(2)}) collective-permute-start(bf16[256,512]{1,0:T(8,128)(2,1)S(1)} %copy-done.2), channel_id=1, source_target_pairs={{0,1},{1,2},{2,3},{3,0},{4,5},{5,6},{6,7},{7,4},{8,9},{9,10},{10,1... | collective-permute-start | bytes 786440 | tf_op jit(solution)/shard_map/ppermute | solution.py:304
  56.7 30.3 %copy-start = (bf16[512,512]{1,0:T(8,128)(2,1)S(1)}, bf16[512,512]{1,0:T(8,128)(2,1)}, u32[]{:S(2)}) copy-start(bf16[512,512]{1,0:T(8,128)(2,1)} %w_self_ref.3) | copy-start | bytes 1572868
  56.7 30.3 %copy-start.1 = (bf16[512,512]{1,0:T(8,128)(2,1)S(1)}, bf16[512,512]{1,0:T(8,128)(2,1)}, u32[]{:S(2)}) copy-start(bf16[512,512]{1,0:T(8,128)(2,1)} %w_neigh_ref.3) | copy-start | bytes 1572868
  56.7 10.7 %collective-permute-start.3 = (bf16[256,512]{1,0:T(8,128)(2,1)S(1)}, bf16[256,512]{1,0:T(8,128)(2,1)S(1)}, u32[]{:S(2)}, u32[]{:S(2)}) collective-permute-start(bf16[256,512]{1,0:T(8,128)(2,1)S(1)} %get-tuple-element.40), channel_id=1, source_target_pairs={{0,1},{1,2},{2,3},{3,0},{4,5},{5,6},{6,7},{7,4},{8,9},{9,10},{10,1... | collective-permute-start | bytes 786440 | tf_op jit(solution)/shard_map/ppermute | solution.py:304
  59.9 13.0 %collective-permute-start.4 = (bf16[256,512]{1,0:T(8,128)(2,1)S(1)}, bf16[256,512]{1,0:T(8,128)(2,1)S(1)}, u32[]{:S(2)}, u32[]{:S(2)}) collective-permute-start(bf16[256,512]{1,0:T(8,128)(2,1)S(1)} %get-tuple-element.41), channel_id=1, source_target_pairs={{0,2},{1,3},{2,0},{3,1},{4,6},{5,7},{6,4},{7,5},{8,10},{9,11},{10,... | collective-permute-start | bytes 786440 | tf_op jit(solution)/shard_map/ppermute | solution.py:304
  64.3 10.3 %collective-permute-start.5 = (bf16[256,512]{1,0:T(8,128)(2,1)S(1)}, bf16[256,512]{1,0:T(8,128)(2,1)S(1)}, u32[]{:S(2)}, u32[]{:S(2)}) collective-permute-start(bf16[256,512]{1,0:T(8,128)(2,1)S(1)} %get-tuple-element.42), channel_id=1, source_target_pairs={{0,3},{1,0},{2,1},{3,2},{4,7},{5,4},{6,5},{7,6},{8,11},{9,8},{10,9... | collective-permute-start | bytes 786440 | tf_op jit(solution)/shard_map/ppermute | solution.py:304
  74.7 15.6 %collective-permute-start.8 = (bf16[256,512]{1,0:T(8,128)(2,1)S(1)}, bf16[256,512]{1,0:T(8,128)(2,1)S(1)}, u32[]{:S(2)}, u32[]{:S(2)}) collective-permute-start(bf16[256,512]{1,0:T(8,128)(2,1)S(1)} %multiply_convert_fusion.agg_ref), channel_id=1, source_target_pairs={{0,1},{1,2},{2,3},{3,0},{4,5},{5,6},{6,7},{7,4},{8,9},{9,10},{10,1... | collective-permute-start | bytes 786440 | tf_op jit(solution)/shard_map/ppermute | solution.py:304
  80.5 11.8 %collective-permute-start.7 = (bf16[256,512]{1,0:T(8,128)(2,1)S(1)}, bf16[256,512]{1,0:T(8,128)(2,1)S(1)}, u32[]{:S(2)}, u32[]{:S(2)}) collective-permute-start(bf16[256,512]{1,0:T(8,128)(2,1)S(1)} %multiply_convert_fusion.agg_ref), channel_id=1, source_target_pairs={{0,2},{1,3},{2,0},{3,1},{4,6},{5,7},{6,4},{7,5},{8,10},{9,11},{10,... | collective-permute-start | bytes 786440 | tf_op jit(solution)/shard_map/ppermute | solution.py:304
  82.7 10.5 %collective-permute-start.6 = (bf16[256,512]{1,0:T(8,128)(2,1)S(1)}, bf16[256,512]{1,0:T(8,128)(2,1)S(1)}, u32[]{:S(2)}, u32[]{:S(2)}) collective-permute-start(bf16[256,512]{1,0:T(8,128)(2,1)S(1)} %multiply_convert_fusion.agg_ref), channel_id=1, source_target_pairs={{0,3},{1,0},{2,1},{3,2},{4,7},{5,4},{6,5},{7,6},{8,11},{9,8},{10,9... | collective-permute-start | bytes 786440 | tf_op jit(solution)/shard_map/ppermute | solution.py:304
  99.2 44.9 %all-to-all-start.1 = ((bf16[128,8,640]{2,1,0:T(8,128)(2,1)}), bf16[128,8,640]{2,1,0:T(8,128)(2,1)S(1)}, u32[]{:S(2)}, u32[]{:S(2)}) async-start(bf16[128,8,640]{2,1,0:T(8,128)(2,1)} %bitcast.25), calls=%async_computation.1 | async-start | bytes 2621440 | tf_op jit(solution)/shard_map/all_to_all | solution.py:424
  165.5 33.8 %all-to-all-start.3 = ((bf16[8,512,128]{2,1,0:T(8,128)(2,1)}), bf16[8,512,128]{2,1,0:T(8,128)(2,1)S(1)}, u32[]{:S(2)}, u32[]{:S(2)}) async-start(bf16[8,512,128]{2,1,0:T(8,128)(2,1)} %broadcast_in_dim.8), calls=%async_computation.3 | async-start | bytes 2097152 | tf_op jit(solution)/shard_map/all_to_all | solution.py:459
  172.1 20.6 %collective-permute-start.9 = (bf16[256,512]{1,0:T(8,128)(2,1)S(1)}, bf16[256,512]{1,0:T(8,128)(2,1)S(1)}, u32[]{:S(2)}, u32[]{:S(2)}) collective-permute-start(bf16[256,512]{1,0:T(8,128)(2,1)S(1)} %get-tuple-element.58), channel_id=1, source_target_pairs={{0,1},{1,2},{2,3},{3,0},{4,5},{5,6},{6,7},{7,4},{8,9},{9,10},{10,1... | collective-permute-start | bytes 786440 | tf_op jit(solution)/shard_map/ppermute | solution.py:304
  175.3 23.1 %collective-permute-start.10 = (bf16[256,512]{1,0:T(8,128)(2,1)S(1)}, bf16[256,512]{1,0:T(8,128)(2,1)S(1)}, u32[]{:S(2)}, u32[]{:S(2)}) collective-permute-start(bf16[256,512]{1,0:T(8,128)(2,1)S(1)} %get-tuple-element.59), channel_id=1, source_target_pairs={{0,2},{1,3},{2,0},{3,1},{4,6},{5,7},{6,4},{7,5},{8,10},{9,11},{10,... | collective-permute-start | bytes 786440 | tf_op jit(solution)/shard_map/ppermute | solution.py:304
  179.7 18.8 %collective-permute-start.11 = (bf16[256,512]{1,0:T(8,128)(2,1)S(1)}, bf16[256,512]{1,0:T(8,128)(2,1)S(1)}, u32[]{:S(2)}, u32[]{:S(2)}) collective-permute-start(bf16[256,512]{1,0:T(8,128)(2,1)S(1)} %get-tuple-element.60), channel_id=1, source_target_pairs={{0,3},{1,0},{2,1},{3,2},{4,7},{5,4},{6,5},{7,6},{8,11},{9,8},{10,9... | collective-permute-start | bytes 786440 | tf_op jit(solution)/shard_map/ppermute | solution.py:304

commit v6 on v5

--- a/solution.py
+++ b/solution.py
@@ -11,6 +11,7 @@
 BLOCK = 64
 LANES = 128
 WIDE = ("y", "z", "core")
+FAR_FIRST = (2, 1, 3)
 F32 = jnp.float32
 BF16 = jnp.bfloat16
 VMEM = pl.BlockSpec(memory_space=pltpu.VMEM)
@@ -128,6 +129,35 @@
     }
 
 
+def gather_kernel(slots_hbm, feats_hbm, rows_hbm, slots_ref, feats_ref, rows_ref, sems):
+    slots_copy = started(slots_hbm, slots_ref, sems.at[0])
+    feats_copy = started(feats_hbm, feats_ref, sems.at[1])
+    slots_copy.wait()
+    slot_count, peers = slots_ref.shape
+    node_rows = feats_ref.shape[0]
+    lane = lax.broadcasted_iota(jnp.int32, (slot_count, node_rows), 1)
+    slots = slots_ref[...]
+    step = min(32, peers)
+    copies = []
+    for at in range(0, peers, step):
+        pick = jnp.concatenate(
+            [
+                jnp.where(lane == slots[:, s : s + 1], 1.0, 0.0).astype(F32)
+                for s in range(at, at + step)
+            ],
+            axis=0,
+        ).astype(BF16)
+        if at == 0:
+            feats_copy.wait()
+        rows = pl.ds(at * slot_count, step * slot_count)
+        rows_ref[rows, :] = dot(pick, feats_ref[...], 1, 0).astype(BF16)
+        copies.append(
+            started(rows_ref.at[rows, :], rows_hbm.at[rows, :], sems.at[2 + at // step])
+        )
+    for copy in copies:
+        copy.wait()
+
+
 def sum_kernel(
     counts_ref, incoming_ref, local_hbm, own_ref, send1, send2, send3, local_ref, total_ref, sems
 ):
@@ -176,7 +206,7 @@
 
 
 def dense_kernel(
-    replicas, rep_ref, agg1, agg2, agg3, grad1, grad2, grad3, feats_hbm, w_self_ref, w_neigh_ref,
+    replicas, rep_ref, agg1, agg3, agg2, grad1, grad2, grad3, feats_hbm, w_self_ref, w_neigh_ref,
     scale_ref, halo_t_hbm, own_grad_ref, own_weights_ref, grad_agg_hbm, joint_hbm,
     grad_ref, feats_ref, halo_t_ref, grad_agg_ref, joint_ref, sems,
 ):
@@ -213,19 +243,17 @@
         grad_self = grad_self + dot(feats_ref[k - 1, :, share_cols], grad_pre, 0, 0)
         grad_neigh = grad_neigh + dot(agg_ref[:, share_cols], grad_pre, 0, 0)
     grad_agg_copy = started(grad_agg_ref, grad_agg_hbm, sems.at[at])
+    tile = 0
     per_peer = (joint_ref.shape[1] - feat_width) // LANES
-    half = feat_width // LANES // 2
-    weights = jnp.concatenate([grad_self, grad_neigh], axis=0)
-    for core in range(2):
-        for n in range(half):
-            for g in range(2 * share // 8):
-                tile = n * (2 * share // 8) + g
-                row = (tile // per_peer * 2 + core) * 8
-                lane = feat_width + tile % per_peer * LANES
-                col = (core * half + n) * LANES
-                joint_ref[row : row + 8, lane : lane + LANES] = weights[
-                    g * 8 : g * 8 + 8, col : col + LANES
+    for part in (grad_self, grad_neigh):
+        for g in range(0, share, 8):
+            for c in range(0, feat_width, LANES):
+                peer, slot = tile // per_peer, tile % per_peer
+                lane = feat_width + slot * LANES
+                joint_ref[peer * 8 : peer * 8 + 8, lane : lane + LANES] = part[
+                    g : g + 8, c : c + LANES
                 ].astype(BF16)
+                tile += 1
     joint_copies = []
     for n, i in enumerate(starts):
         rows = pl.ds(i, step)
@@ -258,8 +286,8 @@
 
 
 def return_kernel(
-    replicas, slots_ref, joint_ref, local_hbm, tile_ref, own_ref, send1, send2, send3,
-    local_ref, total_ref, sems,
+    replicas, slots_ref, joint_ref, local_hbm, copies_hbm, own_ref, send1, send2, send3,
+    tiles_ref, local_ref, total_ref, sems,
 ):
     quarter, feat_width = own_ref.shape
     halo_rows = joint_ref.shape[0]
@@ -268,10 +296,8 @@
     lanes = joint_ref.shape[1] - feat_width
     tiles = joint_ref[:, feat_width:].astype(F32).reshape(halo_rows // 8, 8, lanes)
     tile = tiles.sum(axis=0, keepdims=True)
-    many = tile_ref.shape[0]
-    tile_ref[...] = (
-        jnp.broadcast_to(tile, (many // 8, 8, lanes)).reshape(many, lanes).astype(BF16)
-    )
+    tiles_ref[...] = jnp.broadcast_to(tile, tiles.shape).reshape(halo_rows, lanes).astype(BF16)
+    copies_copy = started(tiles_ref, copies_hbm, sems.at[replicas])
     slots = jnp.broadcast_to(slots_ref[...], (quarter, halo_rows))
     row = lax.broadcasted_iota(jnp.int32, (quarter, halo_rows), 0)
     for k, rows in quarters.items():
@@ -284,20 +310,16 @@
             (send1, send2, send3)[k - 1][...] = total.astype(BF16)
         else:
             own_ref[...] = total
-
-
-def place_kernel(replicas, parts_ref, self_ref, neigh_ref):
-    share = self_ref.shape[0] // replicas
-    cores = 2
-    block = parts_ref.shape[0] // (cores * replicas)
-    for core in range(cores):
-        for rep in range(replicas):
-            for n in range(block // (2 * share)):
-                at = (core * replicas + rep) * block + n * 2 * share
-                lane = (core * (block // (2 * share)) + n) * LANES
-                rows = slice(rep * share, (rep + 1) * share)
-                self_ref[rows, lane : lane + LANES] = parts_ref[at : at + share, :]
-                neigh_ref[rows, lane : lane + LANES] = parts_ref[at + share : at + 2 * share, :]
+    copies_copy.wait()
+
+
+def place_kernel(rep_ref, part0, part1, part3, part2, self_ref, neigh_ref):
+    parts = (part0, part1, part2, part3)
+    share = part0.shape[0] // 2
+    for k, part in enumerate(parts):
+        at = pl.ds(pl.multiple_of(((rep_ref[0] + k) % len(parts)) * share, share), share)
+        self_ref[at, :] = part[:share, :]
+        neigh_ref[at, :] = part[share:, :]
 
 
 def send_to(x, step, replicas):
@@ -305,7 +327,8 @@
 
 
 def from_ahead(x, replicas):
-    return [send_to(x, replicas - k, replicas) for k in range(1, replicas)]
+    ahead = {k: send_to(x, replicas - k, replicas) for k in reversed(FAR_FIRST)}
+    return [ahead[k] for k in range(1, replicas)]
 
 
 def on_device(
@@ -327,9 +350,21 @@
     send_outs = [shape(quarter, feat_width, BF16)] * (replicas - 1)
 
     slot_rows = send_rows[0].reshape(-1)
-    every_row = lax.broadcasted_iota(jnp.int32, (node_rows, halo_rows), 0)
-    send_pick = (every_row == slot_rows[None, :]).astype(BF16)
-    outgoing = dot(send_pick, node_feats, 0, 0).astype(BF16)
+    (outgoing,) = call(
+        gather_kernel,
+        "gather_rows",
+        [shape(halo_rows, feat_width, BF16)],
+        [HBM, HBM],
+        (send_rows[0].T, node_feats),
+        2 * node_rows * halo_rows * feat_width,
+        out_specs=[HBM],
+        scratch=[
+            pltpu.VMEM((slot_count, peer_count), jnp.int32),
+            pltpu.VMEM((node_rows, feat_width), BF16),
+            pltpu.VMEM((halo_rows, feat_width), BF16),
+            pltpu.SemaphoreType.DMA((2 + max(1, peer_count // 32),)),
+        ],
+    )
     incoming = lax.all_to_all(outgoing, WIDE, 0, 0, tiled=True)
 
     scale = lax.rsqrt(norm_count.astype(F32))
@@ -376,7 +411,7 @@
         scratch=[pltpu.VMEM((node_rows, feat_width), F32)] * 2
         + [pltpu.SemaphoreType.DMA((replicas,))],
     )
-    for k in range(1, replicas):
+    for k in FAR_FIRST:
         own_sums = own_sums + send_to(sends[k - 1], k, replicas).astype(F32)
     own_agg = (own_sums * scale[:quarter]).astype(BF16)
     aggs = from_ahead(own_agg, replicas)
@@ -407,7 +442,7 @@
         [shape(node_rows, feat_width, BF16), shape(halo_rows, joint_width, BF16)],
         [SMEM] + [VMEM] * 3 + [HBM] * 4 + [VMEM] * 3 + [HBM, VMEM, VMEM],
         (
-            rep_ref, *aggs, *grad_outs[1:], node_feats, w_self, w_neigh, scale, halo_t, own_grad_agg,
+            rep_ref, aggs[0], aggs[2], aggs[1], *grad_outs[1:], node_feats, w_self, w_neigh, scale, halo_t, own_grad_agg,
             own_weights,
         ),
         2 * block_flops,
@@ -440,36 +475,37 @@
     )
 
     lanes = joint_width - feat_width
-    chips = peer_count // 2
     copies, own_grad, *sends = call(
         functools.partial(return_kernel, replicas),
         "returned_rows",
-        [shape(chips * slot_count, lanes, BF16), shape(quarter, feat_width, F32)] + send_outs,
+        [shape(halo_rows, lanes, BF16), shape(quarter, feat_width, F32)] + send_outs,
         [VMEM, VMEM, HBM],
         (turned_slots, returned, local_grad),
         block_flops,
-        scratch=[pltpu.VMEM((node_rows, feat_width), F32)] * 2
-        + [pltpu.SemaphoreType.DMA((replicas,))],
-    )
-    for k in range(1, replicas):
+        out_specs=[HBM] + [VMEM] * replicas,
+        scratch=[pltpu.VMEM((halo_rows, lanes), BF16)]
+        + [pltpu.VMEM((node_rows, feat_width), F32)] * 2
+        + [pltpu.SemaphoreType.DMA((replicas + 1,))],
+    )
+    for k in FAR_FIRST:
         own_grad = own_grad + send_to(sends[k - 1], k, replicas).astype(F32)
 
-    tiles = lax.all_to_all(copies, ("y", "z"), 0, 0, tiled=True)
-    halves = 2 * replicas
-    parts = lax.all_to_all(
-        jnp.broadcast_to(tiles, (halves,) + tiles.shape).reshape(-1, lanes), ("core", "rep"), 0, 0, tiled=True
-    )
-    parts = (
-        parts.reshape(halves * chips, slot_count, -1, LANES)
+    tiles = lax.all_to_all(copies, WIDE, 0, 0, tiled=True)
+    lane_tiles = feat_width // LANES
+    own_share = (
+        tiles.reshape(peer_count, slot_count, -1, LANES)
         .transpose(0, 2, 1, 3)
-        .reshape(-1, LANES)
-    )
+        .reshape(-1, lane_tiles, slot_count, LANES)
+        .transpose(0, 2, 1, 3)
+        .reshape(2 * share, feat_width)
+    )
+    shares = from_ahead(own_share, replicas)
     grad_self, grad_neigh = call(
-        functools.partial(place_kernel, replicas),
+        place_kernel,
         "place",
         [shape(feat_width, feat_width, BF16)] * 2,
-        [VMEM],
-        (parts,),
+        [SMEM] + [VMEM] * replicas,
+        (rep_ref, own_share, shares[0], shares[2], shares[1]),
         0,
     )
     return out_feats, own_grad.astype(BF16), grad_self, grad_neigh

time: 201 us -> 182 us (0.905)
  blocking collectives: 17.6 us -> 0 us
  starting transfers between devices: 77.6 us -> 88.9 us
  waiting for transfers between devices: 66.8 us -> 55.7 us
  matrix products: 3.53 us -> 0 us
  Pallas kernels: 30.3 us -> 33 us
    all_to_all x1 -> x0, blocking collectives: 17.6 us -> none  [on_device(): tiles = lax.all_to_all(copies, ('y', 'z'), 0, 0, tiled=True)]
    ppermute x12 -> x15, waiting for transfers between devices: 25.8 us -> 11.6 us  [send_to(): lax.ppermute(x, 'rep', [(i, (i + step) % replicas) for i in range(replica...]
    ppermute x12 -> x15, starting transfers between devices: 43.2 us -> 55.2 us  [send_to(): lax.ppermute(x, 'rep', [(i, (i + step) % replicas) for i in range(replica...]
    dot_general x1 -> x0, matrix products: 3.53 us -> none  [dot(): return lax.dot_general(left, right, dims, preferred_element_type=F32)]
    all_to_all x1, waiting for transfers between devices: 0.01 us -> 3.13 us  [on_device(): tiles = lax.all_to_all(copies, WIDE, 0, 0, tiled=True)]
    pallas_call x7 -> x8, Pallas kernels: 30.3 us -> 33 us  [call(): pl.pallas_call(kernel, out_shape=outs, in_specs=in_specs, out_specs=out_s...]
  transfers between devices with their start and end apart: 15 -> 18, of which waited for: 8 -> 6; matrix products, arithmetic and copies ran while one was open for 1% -> 1% of each run, Pallas kernels for 9% -> 10%
where the time goes in v6:
time: 182 us; the launch traced here: 180 us
  starting transfers between devices  88.9 us (49%)
  waiting for transfers between devices  55.7 us (31%)
  Pallas kernels  33 us (18%)
    ppermute x15, starting transfers between devices, send_to(): lax.ppermute(x, 'rep', [(i, (i + step) % replicas) for i in range(replica...  55.2 us
    pallas_call x8, Pallas kernels, call(): pl.pallas_call(kernel, out_shape=outs, in_specs=in_specs, out_specs=out_s...  33 us
    all_to_all x1, waiting for transfers between devices, on_device(): returned = lax.all_to_all(joint, WIDE, 0, 0, tiled=True)  31 us
    all_to_all x1, starting transfers between devices, on_device(): incoming = lax.all_to_all(outgoing, WIDE, 0, 0, tiled=True)  18.4 us
    ppermute x15, waiting for transfers between devices, send_to(): lax.ppermute(x, 'rep', [(i, (i + step) % replicas) for i in range(replica...  11.6 us
    all_to_all x1, waiting for transfers between devices, on_device(): incoming = lax.all_to_all(outgoing, WIDE, 0, 0, tiled=True)  10 us
    all_to_all x1, starting transfers between devices, on_device(): returned = lax.all_to_all(joint, WIDE, 0, 0, tiled=True)  7.67 us
    all_to_all x1, starting transfers between devices, on_device(): tiles = lax.all_to_all(copies, WIDE, 0, 0, tiled=True)  7.61 us
  transfers between devices with their start and end apart: 18, of which 6 were waited for; matrix products, arithmetic and copies ran while one was open for 1% of the time, Pallas kernels for 10%

profile of v6, /device:TPU:1, one launch (start us, length us, event | category | flops | bytes accessed | tf_op | source)
XLA Modules:
  0.0 180.2 jit_solution(4167457756475867694)
XLA Ops:
  0.7 3.4 %gather_rows.1 = bf16[1024,512]{1,0:T(8,128)(2,1)} custom-call(s32[8,128]{1,0:T(8,128)} %bitcast.36, bf16[1024,512]{1,0:T(8,128)(2,1)} %feats_hbm.7), custom_call_target="tpu_custom_call" | custom-call | flops 1073741824 | bytes 2101248 | tf_op jit(solution)/shard_map/gather_rows/pallas_call | solution.py:40
  4.1 18.4 %all-to-all-start = ((bf16[128,8,512]{2,1,0:T(8,128)(2,1)}), bf16[128,8,512]{2,1,0:T(8,128)(2,1)S(1)}, u32[]{:S(2)}, u32[]{:S(2)}) async-start(bf16[128,8,512]{2,1,0:T(8,128)(2,1)} %bitcast.32), calls=%async_computation | async-start | bytes 2097152 | tf_op jit(solution)/shard_map/all_to_all | solution.py:368
  22.6 4.7 %collective-permute-start.1 = (bf16[256,512]{1,0:T(8,128)(2,1)S(1)}, bf16[256,512]{1,0:T(8,128)(2,1)}, u32[]{:S(2)}, u32[]{:S(2)}) collective-permute-start(bf16[256,512]{1,0:T(8,128)(2,1)S(1)} %copy-done.2), channel_id=1, source_target_pairs={{0,2},{1,3},{2,0},{3,1},{4,6},{5,7},{6,4},{7,5},{8,10},{9,11},{10,... | collective-permute-start | bytes 786440 | tf_op jit(solution)/shard_map/ppermute | solution.py:326
  32.7 10.0 %tile_counts.1 = (bf16[1024,1024]{1,0:T(8,128)(2,1)}, bf16[1024,1024]{1,0:T(8,128)(2,1)S(1)}, bf16[1024,1024]{1,0:T(8,128)(2,1)}, f32[1024,512]{1,0:T(8,128)}) custom-call(s32[1]{0:T(128)} %bitcast.rep_ref, s32[128]{0:T(128)S(1)} %fusion.3.place_ref, s32[256,128]{1,0:T(8,128)S(1)} %bitcast.30, bf16[1024,512]{1,0:T(8,128)(2,1)} %feats_hbm.7), custom_call_target="tpu_custom_call" | custom-call | flops 1094713344 | bytes 9568772 | tf_op jit(solution)/shard_map/tile_counts/pallas_call | solution.py:40
  43.0 10.0 %all-to-all-done = bf16[128,8,512]{2,1,0:T(8,128)(2,1)S(1)} async-done(((bf16[128,8,512]{2,1,0:T(8,128)(2,1)}), bf16[128,8,512]{2,1,0:T(8,128)(2,1)S(1)}, u32[]{:S(2)}, u32[]{:S(2)}) %all-to-all-start) | async-done | bytes 1048608 | tf_op jit(solution)/shard_map/all_to_all | solution.py:368
  55.6 4.8 %collective-permute-start.3 = (bf16[256,512]{1,0:T(8,128)(2,1)S(1)}, bf16[256,512]{1,0:T(8,128)(2,1)S(1)}, u32[]{:S(2)}, u32[]{:S(2)}) collective-permute-start(bf16[256,512]{1,0:T(8,128)(2,1)S(1)} %get-tuple-element.40), channel_id=1, source_target_pairs={{0,2},{1,3},{2,0},{3,1},{4,6},{5,7},{6,4},{7,5},{8,10},{9,11},{10,... | collective-permute-start | bytes 786440 | tf_op jit(solution)/shard_map/ppermute | solution.py:326
  62.6 4.3 %collective-permute-start.5 = (bf16[256,512]{1,0:T(8,128)(2,1)S(1)}, bf16[256,512]{1,0:T(8,128)(2,1)S(1)}, u32[]{:S(2)}, u32[]{:S(2)}) collective-permute-start(bf16[256,512]{1,0:T(8,128)(2,1)S(1)} %get-tuple-element.42), channel_id=1, source_target_pairs={{0,3},{1,0},{2,1},{3,2},{4,7},{5,4},{6,5},{7,6},{8,11},{9,8},{10,9... | collective-permute-start | bytes 786440 | tf_op jit(solution)/shard_map/ppermute | solution.py:326
  66.9 5.4 %collective-permute-done.4 = bf16[256,512]{1,0:T(8,128)(2,1)S(1)} collective-permute-done((bf16[256,512]{1,0:T(8,128)(2,1)S(1)}, bf16[256,512]{1,0:T(8,128)(2,1)S(1)}, u32[]{:S(2)}, u32[]{:S(2)}) %collective-permute-start.4) | collective-permute-done | bytes 262176 | tf_op jit(solution)/shard_map/ppermute | solution.py:326
  72.4 5.4 %collective-permute-start.8 = (bf16[256,512]{1,0:T(8,128)(2,1)S(1)}, bf16[256,512]{1,0:T(8,128)(2,1)S(1)}, u32[]{:S(2)}, u32[]{:S(2)}) collective-permute-start(bf16[256,512]{1,0:T(8,128)(2,1)S(1)} %multiply_convert_fusion.agg_ref), channel_id=1, source_target_pairs={{0,2},{1,3},{2,0},{3,1},{4,6},{5,7},{6,4},{7,5},{8,10},{9,11},{10,... | collective-permute-start | bytes 786440 | tf_op jit(solution)/shard_map/ppermute | solution.py:326
  79.7 4.6 %collective-permute-start.6 = (bf16[256,512]{1,0:T(8,128)(2,1)S(1)}, bf16[256,512]{1,0:T(8,128)(2,1)S(1)}, u32[]{:S(2)}, u32[]{:S(2)}) collective-permute-start(bf16[256,512]{1,0:T(8,128)(2,1)S(1)} %multiply_convert_fusion.agg_ref), channel_id=1, source_target_pairs={{0,3},{1,0},{2,1},{3,2},{4,7},{5,4},{6,5},{7,6},{8,11},{9,8},{10,9... | collective-permute-start | bytes 786440 | tf_op jit(solution)/shard_map/ppermute | solution.py:326
  84.5 3.4 %dense_own.1 = (bf16[256,512]{1,0:T(8,128)(2,1)}, f32[256,512]{1,0:T(8,128)}, bf16[256,512]{1,0:T(8,128)(2,1)S(1)}, f32[256,512]{1,0:T(8,128)S(1)}) custom-call(s32[1]{0:T(128)} %bitcast.rep_ref, bf16[256,512]{1,0:T(8,128)(2,1)S(1)} %multiply_convert_fusion.agg_ref, bf16[256,512]{1,0:T(8,128)(2,1)S(1)} %copy-done.2, bf16[1024,512]{1,0:T(8,128)(2,1)} %feats_hbm.7, ...), custom_call_target="tpu_custom_call" | custom-call | flops 536870912 | bytes 4198404 | tf_op jit(solution)/shard_map/dense_own/pallas_call | solution.py:40
  89.8 6.0 %dense_rest.1 = (bf16[1024,512]{1,0:T(8,128)(2,1)}, bf16[1024,640]{1,0:T(8,128)(2,1)}) custom-call(s32[1]{0:T(128)} %bitcast.rep_ref, bf16[256,512]{1,0:T(8,128)(2,1)S(1)} %collective-permute-done.6.agg1, bf16[256,512]{1,0:T(8,128)(2,1)S(1)} %collective-permute-done.7.agg3, bf16[256,512]{1,0:T(8,128)(2,1)S(1)} %collective-permute-done.8.agg2, ...), custom_call_target="tpu_custom_call" | custom-call | flops 2147483648 | bytes 8916996 | tf_op jit(solution)/shard_map/dense_rest/pallas_call | solution.py:40
  95.8 7.7 %all-to-all-start.1 = ((bf16[128,8,640]{2,1,0:T(8,128)(2,1)}), bf16[128,8,640]{2,1,0:T(8,128)(2,1)S(1)}, u32[]{:S(2)}, u32[]{:S(2)}) async-start(bf16[128,8,640]{2,1,0:T(8,128)(2,1)} %bitcast.31), calls=%async_computation.1 | async-start | bytes 2621440 | tf_op jit(solution)/shard_map/all_to_all | solution.py:459
  103.5 4.6 %local_rows.1.local_hbm = f32[1024,512]{1,0:T(8,128)} custom-call(bf16[1024,1024]{1,0:T(8,128)(2,1)} %get-tuple-element.54.counts_hbm, bf16[1024,512]{1,0:T(8,128)(2,1)} %get-tuple-element.55.grad_hbm, f32[256,512]{1,0:T(8,128)} %get-tuple-element.56.base_hbm), custom_call_target="tpu_custom_call" | custom-call | flops 1073741824 | bytes 5767168 | tf_op jit(solution)/shard_map/local_rows/pallas_call | solution.py:40
  108.1 31.0 %all-to-all-done.1 = bf16[128,8,640]{2,1,0:T(8,128)(2,1)S(1)} async-done(((bf16[128,8,640]{2,1,0:T(8,128)(2,1)}), bf16[128,8,640]{2,1,0:T(8,128)(2,1)S(1)}, u32[]{:S(2)}, u32[]{:S(2)}) %all-to-all-start.1) | async-done | bytes 1310752 | tf_op jit(solution)/shard_map/all_to_all | solution.py:459
  141.0 7.6 %all-to-all-start.2 = ((bf16[128,8,128]{2,1,0:T(8,128)(2,1)}), bf16[128,8,128]{2,1,0:T(8,128)(2,1)S(1)}, u32[]{:S(2)}, u32[]{:S(2)}) async-start(bf16[128,8,128]{2,1,0:T(8,128)(2,1)} %bitcast.33), calls=%async_computation.2 | async-start | bytes 524288 | tf_op jit(solution)/shard_map/all_to_all | solution.py:493
  148.7 4.6 %collective-permute-start.9 = (bf16[256,512]{1,0:T(8,128)(2,1)S(1)}, bf16[256,512]{1,0:T(8,128)(2,1)S(1)}, u32[]{:S(2)}, u32[]{:S(2)}) collective-permute-start(bf16[256,512]{1,0:T(8,128)(2,1)S(1)} %get-tuple-element.58), channel_id=1, source_target_pairs={{0,2},{1,3},{2,0},{3,1},{4,6},{5,7},{6,4},{7,5},{8,10},{9,11},{10,... | collective-permute-start | bytes 786440 | tf_op jit(solution)/shard_map/ppermute | solution.py:326
  153.2 3.1 %collective-permute-start.10 = (bf16[256,512]{1,0:T(8,128)(2,1)S(1)}, bf16[256,512]{1,0:T(8,128)(2,1)S(1)}, u32[]{:S(2)}, u32[]{:S(2)}) collective-permute-start(bf16[256,512]{1,0:T(8,128)(2,1)S(1)} %get-tuple-element.59), channel_id=1, source_target_pairs={{0,1},{1,2},{2,3},{3,0},{4,5},{5,6},{6,7},{7,4},{8,9},{9,10},{10,1... | collective-permute-start | bytes 786440 | tf_op jit(solution)/shard_map/ppermute | solution.py:326
  156.3 3.4 %collective-permute-start.11 = (bf16[256,512]{1,0:T(8,128)(2,1)S(1)}, bf16[256,512]{1,0:T(8,128)(2,1)S(1)}, u32[]{:S(2)}, u32[]{:S(2)}) collective-permute-start(bf16[256,512]{1,0:T(8,128)(2,1)S(1)} %get-tuple-element.60), channel_id=1, source_target_pairs={{0,3},{1,0},{2,1},{3,2},{4,7},{5,4},{6,5},{7,6},{8,11},{9,8},{10,9... | collective-permute-start | bytes 786440 | tf_op jit(solution)/shard_map/ppermute | solution.py:326
  159.7 3.1 %all-to-all-done.2 = bf16[128,8,128]{2,1,0:T(8,128)(2,1)S(1)} async-done(((bf16[128,8,128]{2,1,0:T(8,128)(2,1)}), bf16[128,8,128]{2,1,0:T(8,128)(2,1)S(1)}, u32[]{:S(2)}, u32[]{:S(2)}) %all-to-all-start.2) | async-done | bytes 262176 | tf_op jit(solution)/shard_map/all_to_all | solution.py:493
  162.9 4.6 %collective-permute-start.14 = (bf16[256,512]{1,0:T(8,128)(2,1)S(1)}, bf16[256,512]{1,0:T(8,128)(2,1)S(1)}, u32[]{:S(2)}, u32[]{:S(2)}) collective-permute-start(bf16[256,512]{1,0:T(8,128)(2,1)S(1)} %bitcast.26), channel_id=1, source_target_pairs={{0,2},{1,3},{2,0},{3,1},{4,6},{5,7},{6,4},{7,5},{8,10},{9,11},{10,... | collective-permute-start | bytes 786440 | tf_op jit(solution)/shard_map/ppermute | solution.py:326
  167.4 3.1 %collective-permute-start.13 = (bf16[256,512]{1,0:T(8,128)(2,1)S(1)}, bf16[256,512]{1,0:T(8,128)(2,1)S(1)}, u32[]{:S(2)}, u32[]{:S(2)}) collective-permute-start(bf16[256,512]{1,0:T(8,128)(2,1)S(1)} %bitcast.27), channel_id=1, source_target_pairs={{0,1},{1,2},{2,3},{3,0},{4,5},{5,6},{6,7},{7,4},{8,9},{9,10},{10,1... | collective-permute-start | bytes 786440 | tf_op jit(solution)/shard_map/ppermute | solution.py:326
  170.5 3.4 %collective-permute-start.12 = (bf16[256,512]{1,0:T(8,128)(2,1)S(1)}, bf16[256,512]{1,0:T(8,128)(2,1)S(1)}, u32[]{:S(2)}, u32[]{:S(2)}) collective-permute-start(bf16[256,512]{1,0:T(8,128)(2,1)S(1)} %bitcast.28), channel_id=1, source_target_pairs={{0,3},{1,0},{2,1},{3,2},{4,7},{5,4},{6,5},{7,6},{8,11},{9,8},{10,9... | collective-permute-start | bytes 786440 | tf_op jit(solution)/shard_map/ppermute | solution.py:326
  174.8 4.3 %collective-permute-done.13.part3 = bf16[256,512]{1,0:T(8,128)(2,1)S(1)} collective-permute-done((bf16[256,512]{1,0:T(8,128)(2,1)S(1)}, bf16[256,512]{1,0:T(8,128)(2,1)S(1)}, u32[]{:S(2)}, u32[]{:S(2)}) %collective-permute-start.13) | collective-permute-done | bytes 262176 | tf_op jit(solution)/shard_map/ppermute | solution.py:326
  (47 shorter events, 18.5 us)
Async XLA Ops:
  0.6 31.9 %copy-start.4 = (s32[1024]{0:T(1024)S(1)}, s32[1024]{0:T(1024)}, u32[]{:S(2)}) copy-start(s32[1024]{0:T(1024)} %param.16) | copy-start | bytes 12292
  0.7 32.0 %copy-start.6 = (s32[1,1,128]{2,1,0:T(1,128)S(1)}, s32[1,1,128]{2,1,0:T(1,128)}, u32[]{:S(2)}) copy-start(s32[1,1,128]{2,1,0:T(1,128)} %param.14) | copy-start | bytes 1540
  0.7 32.0 %copy-start.7 = (s32[1,1,128]{2,1,0:T(1,128)S(1)}, s32[1,1,128]{2,1,0:T(1,128)}, u32[]{:S(2)}) copy-start(s32[1,1,128]{2,1,0:T(1,128)} %param.13) | copy-start | bytes 1540
  0.7 32.0 %copy-start.5 = (s32[1,128,8]{1,2,0:T(8,128)S(1)}, s32[1,128,8]{1,2,0:T(8,128)}, u32[]{:S(2)}) copy-start(s32[1,128,8]{1,2,0:T(8,128)} %param.12) | copy-start | bytes 12292
  0.7 32.0 %copy-start.3 = (s32[1,1,32768]{2,1,0:T(1,128)S(1)}, s32[1,1,32768]{2,1,0:T(1,128)}, u32[]{:S(2)}) copy-start(s32[1,1,32768]{2,1,0:T(1,128)} %param.15) | copy-start | bytes 393220
  4.1 48.9 %all-to-all-start = ((bf16[128,8,512]{2,1,0:T(8,128)(2,1)}), bf16[128,8,512]{2,1,0:T(8,128)(2,1)S(1)}, u32[]{:S(2)}, u32[]{:S(2)}) async-start(bf16[128,8,512]{2,1,0:T(8,128)(2,1)} %bitcast.32), calls=%async_computation | async-start | bytes 2097152 | tf_op jit(solution)/shard_map/all_to_all | solution.py:368
  22.6 20.4 %collective-permute-start.1 = (bf16[256,512]{1,0:T(8,128)(2,1)S(1)}, bf16[256,512]{1,0:T(8,128)(2,1)}, u32[]{:S(2)}, u32[]{:S(2)}) collective-permute-start(bf16[256,512]{1,0:T(8,128)(2,1)S(1)} %copy-done.2), channel_id=1, source_target_pairs={{0,2},{1,3},{2,0},{3,1},{4,6},{5,7},{6,4},{7,5},{8,10},{9,11},{10,... | collective-permute-start | bytes 786440 | tf_op jit(solution)/shard_map/ppermute | solution.py:326
  27.2 15.7 %collective-permute-start = (bf16[256,512]{1,0:T(8,128)(2,1)S(1)}, bf16[256,512]{1,0:T(8,128)(2,1)}, u32[]{:S(2)}, u32[]{:S(2)}) collective-permute-start(bf16[256,512]{1,0:T(8,128)(2,1)S(1)} %copy-done.2), channel_id=1, source_target_pairs={{0,3},{1,0},{2,1},{3,2},{4,7},{5,4},{6,5},{7,6},{8,11},{9,8},{10,9... | collective-permute-start | bytes 786440 | tf_op jit(solution)/shard_map/ppermute | solution.py:326
  30.0 13.0 %collective-permute-start.2 = (bf16[256,512]{1,0:T(8,128)(2,1)S(1)}, bf16[256,512]{1,0:T(8,128)(2,1)}, u32[]{:S(2)}, u32[]{:S(2)}) collective-permute-start(bf16[256,512]{1,0:T(8,128)(2,1)S(1)} %copy-done.2), channel_id=1, source_target_pairs={{0,1},{1,2},{2,3},{3,0},{4,5},{5,6},{6,7},{7,4},{8,9},{9,10},{10,1... | collective-permute-start | bytes 786440 | tf_op jit(solution)/shard_map/ppermute | solution.py:326
  55.6 29.0 %copy-start = (bf16[512,512]{1,0:T(8,128)(2,1)S(1)}, bf16[512,512]{1,0:T(8,128)(2,1)}, u32[]{:S(2)}) copy-start(bf16[512,512]{1,0:T(8,128)(2,1)} %w_self_ref.3) | copy-start | bytes 1572868
  55.6 11.3 %collective-permute-start.3 = (bf16[256,512]{1,0:T(8,128)(2,1)S(1)}, bf16[256,512]{1,0:T(8,128)(2,1)S(1)}, u32[]{:S(2)}, u32[]{:S(2)}) collective-permute-start(bf16[256,512]{1,0:T(8,128)(2,1)S(1)} %get-tuple-element.40), channel_id=1, source_target_pairs={{0,2},{1,3},{2,0},{3,1},{4,6},{5,7},{6,4},{7,5},{8,10},{9,11},{10,... | collective-permute-start | bytes 786440 | tf_op jit(solution)/shard_map/ppermute | solution.py:326
  60.4 11.9 %collective-permute-start.4 = (bf16[256,512]{1,0:T(8,128)(2,1)S(1)}, bf16[256,512]{1,0:T(8,128)(2,1)S(1)}, u32[]{:S(2)}, u32[]{:S(2)}) collective-permute-start(bf16[256,512]{1,0:T(8,128)(2,1)S(1)} %get-tuple-element.41), channel_id=1, source_target_pairs={{0,1},{1,2},{2,3},{3,0},{4,5},{5,6},{6,7},{7,4},{8,9},{9,10},{10,1... | collective-permute-start | bytes 786440 | tf_op jit(solution)/shard_map/ppermute | solution.py:326
  62.6 9.7 %collective-permute-start.5 = (bf16[256,512]{1,0:T(8,128)(2,1)S(1)}, bf16[256,512]{1,0:T(8,128)(2,1)S(1)}, u32[]{:S(2)}, u32[]{:S(2)}) collective-permute-start(bf16[256,512]{1,0:T(8,128)(2,1)S(1)} %get-tuple-element.42), channel_id=1, source_target_pairs={{0,3},{1,0},{2,1},{3,2},{4,7},{5,4},{6,5},{7,6},{8,11},{9,8},{10,9... | collective-permute-start | bytes 786440 | tf_op jit(solution)/shard_map/ppermute | solution.py:326
  72.4 15.5 %collective-permute-start.8 = (bf16[256,512]{1,0:T(8,128)(2,1)S(1)}, bf16[256,512]{1,0:T(8,128)(2,1)S(1)}, u32[]{:S(2)}, u32[]{:S(2)}) collective-permute-start(bf16[256,512]{1,0:T(8,128)(2,1)S(1)} %multiply_convert_fusion.agg_ref), channel_id=1, source_target_pairs={{0,2},{1,3},{2,0},{3,1},{4,6},{5,7},{6,4},{7,5},{8,10},{9,11},{10,... | collective-permute-start | bytes 786440 | tf_op jit(solution)/shard_map/ppermute | solution.py:326
  77.8 12.1 %collective-permute-start.7 = (bf16[256,512]{1,0:T(8,128)(2,1)S(1)}, bf16[256,512]{1,0:T(8,128)(2,1)S(1)}, u32[]{:S(2)}, u32[]{:S(2)}) collective-permute-start(bf16[256,512]{1,0:T(8,128)(2,1)S(1)} %multiply_convert_fusion.agg_ref), channel_id=1, source_target_pairs={{0,1},{1,2},{2,3},{3,0},{4,5},{5,6},{6,7},{7,4},{8,9},{9,10},{10,1... | collective-permute-start | bytes 786440 | tf_op jit(solution)/shard_map/ppermute | solution.py:326
  79.7 10.1 %collective-permute-start.6 = (bf16[256,512]{1,0:T(8,128)(2,1)S(1)}, bf16[256,512]{1,0:T(8,128)(2,1)S(1)}, u32[]{:S(2)}, u32[]{:S(2)}) collective-permute-start(bf16[256,512]{1,0:T(8,128)(2,1)S(1)} %multiply_convert_fusion.agg_ref), channel_id=1, source_target_pairs={{0,3},{1,0},{2,1},{3,2},{4,7},{5,4},{6,5},{7,6},{8,11},{9,8},{10,9... | collective-permute-start | bytes 786440 | tf_op jit(solution)/shard_map/ppermute | solution.py:326
  95.8 43.2 %all-to-all-start.1 = ((bf16[128,8,640]{2,1,0:T(8,128)(2,1)}), bf16[128,8,640]{2,1,0:T(8,128)(2,1)S(1)}, u32[]{:S(2)}, u32[]{:S(2)}) async-start(bf16[128,8,640]{2,1,0:T(8,128)(2,1)} %bitcast.31), calls=%async_computation.1 | async-start | bytes 2621440 | tf_op jit(solution)/shard_map/all_to_all | solution.py:459
  141.0 21.8 %all-to-all-start.2 = ((bf16[128,8,128]{2,1,0:T(8,128)(2,1)}), bf16[128,8,128]{2,1,0:T(8,128)(2,1)S(1)}, u32[]{:S(2)}, u32[]{:S(2)}) async-start(bf16[128,8,128]{2,1,0:T(8,128)(2,1)} %bitcast.33), calls=%async_computation.2 | async-start | bytes 524288 | tf_op jit(solution)/shard_map/all_to_all | solution.py:493
  148.7 21.9 %collective-permute-start.9 = (bf16[256,512]{1,0:T(8,128)(2,1)S(1)}, bf16[256,512]{1,0:T(8,128)(2,1)S(1)}, u32[]{:S(2)}, u32[]{:S(2)}) collective-permute-start(bf16[256,512]{1,0:T(8,128)(2,1)S(1)} %get-tuple-element.58), channel_id=1, source_target_pairs={{0,2},{1,3},{2,0},{3,1},{4,6},{5,7},{6,4},{7,5},{8,10},{9,11},{10,... | collective-permute-start | bytes 786440 | tf_op jit(solution)/shard_map/ppermute | solution.py:326
  153.2 20.7 %collective-permute-start.10 = (bf16[256,512]{1,0:T(8,128)(2,1)S(1)}, bf16[256,512]{1,0:T(8,128)(2,1)S(1)}, u32[]{:S(2)}, u32[]{:S(2)}) collective-permute-start(bf16[256,512]{1,0:T(8,128)(2,1)S(1)} %get-tuple-element.59), channel_id=1, source_target_pairs={{0,1},{1,2},{2,3},{3,0},{4,5},{5,6},{6,7},{7,4},{8,9},{9,10},{10,1... | collective-permute-start | bytes 786440 | tf_op jit(solution)/shard_map/ppermute | solution.py:326
  156.3 17.7 %collective-permute-start.11 = (bf16[256,512]{1,0:T(8,128)(2,1)S(1)}, bf16[256,512]{1,0:T(8,128)(2,1)S(1)}, u32[]{:S(2)}, u32[]{:S(2)}) collective-permute-start(bf16[256,512]{1,0:T(8,128)(2,1)S(1)} %get-tuple-element.60), channel_id=1, source_target_pairs={{0,3},{1,0},{2,1},{3,2},{4,7},{5,4},{6,5},{7,6},{8,11},{9,8},{10,9... | collective-permute-start | bytes 786440 | tf_op jit(solution)/shard_map/ppermute | solution.py:326
  162.9 12.0 %collective-permute-start.14 = (bf16[256,512]{1,0:T(8,128)(2,1)S(1)}, bf16[256,512]{1,0:T(8,128)(2,1)S(1)}, u32[]{:S(2)}, u32[]{:S(2)}) collective-permute-start(bf16[256,512]{1,0:T(8,128)(2,1)S(1)} %bitcast.26), channel_id=1, source_target_pairs={{0,2},{1,3},{2,0},{3,1},{4,6},{5,7},{6,4},{7,5},{8,10},{9,11},{10,... | collective-permute-start | bytes 786440 | tf_op jit(solution)/shard_map/ppermute | solution.py:326
  167.4 11.7 %collective-permute-start.13 = (bf16[256,512]{1,0:T(8,128)(2,1)S(1)}, bf16[256,512]{1,0:T(8,128)(2,1)S(1)}, u32[]{:S(2)}, u32[]{:S(2)}) collective-permute-start(bf16[256,512]{1,0:T(8,128)(2,1)S(1)} %bitcast.27), channel_id=1, source_target_pairs={{0,1},{1,2},{2,3},{3,0},{4,5},{5,6},{6,7},{7,4},{8,9},{9,10},{10,1... | collective-permute-start | bytes 786440 | tf_op jit(solution)/shard_map/ppermute | solution.py:326
  170.5 8.6 %collective-permute-start.12 = (bf16[256,512]{1,0:T(8,128)(2,1)S(1)}, bf16[256,512]{1,0:T(8,128)(2,1)S(1)}, u32[]{:S(2)}, u32[]{:S(2)}) collective-permute-start(bf16[256,512]{1,0:T(8,128)(2,1)S(1)} %bitcast.28), channel_id=1, source_target_pairs={{0,3},{1,0},{2,1},{3,2},{4,7},{5,4},{6,5},{7,6},{8,11},{9,8},{10,9... | collective-permute-start | bytes 786440 | tf_op jit(solution)/shard_map/ppermute | solution.py:326
  (2 other events, 50.9 us)

commit v7 on v6

--- a/solution.py
+++ b/solution.py
@@ -205,42 +205,64 @@
     base_copy.wait()
 
 
+def far_kernel(
+    replicas, step, rep_ref, agg_ref, grad_hbm, feats_hbm, w_self_ref, w_neigh_ref, scale_ref, before_ref,
+    grad_agg_ref, weights_ref, grad_ref, feats_ref, sems,
+):
+    quarter, feat_width = agg_ref.shape
+    share = feat_width // replicas
+    at = pl.multiple_of(((rep_ref[0] + step) % replicas) * quarter, quarter)
+    feats_copy = started(feats_hbm.at[pl.ds(at, quarter), :], feats_ref, sems.at[0])
+    grad_copy = started(grad_hbm, grad_ref, sems.at[1])
+    feats_copy.wait()
+    grad_copy.wait()
+    _, grad_pre, grad_agg = dense_quarter(
+        agg_ref[...], feats_ref[...], grad_ref[...], scale_ref[pl.ds(step * quarter, quarter), :],
+        w_self_ref[...], w_neigh_ref[...],
+    )
+    grad_agg_ref[...] = grad_agg
+    share_cols = pl.ds(pl.multiple_of(rep_ref[0] * share, LANES), share)
+    weights_ref[:share, :] = before_ref[:share, :] + dot(feats_ref[:, share_cols], grad_pre, 0, 0)
+    weights_ref[share:, :] = before_ref[share:, :] + dot(agg_ref[:, share_cols], grad_pre, 0, 0)
+
+
 def dense_kernel(
-    replicas, rep_ref, agg1, agg3, agg2, grad1, grad2, grad3, feats_hbm, w_self_ref, w_neigh_ref,
-    scale_ref, halo_t_hbm, own_grad_ref, own_weights_ref, grad_agg_hbm, joint_hbm,
+    replicas, rep_ref, agg1, agg3, grad1, grad3, feats_hbm, w_self_ref, w_neigh_ref, scale_ref,
+    halo_t_hbm, grad_agg0_ref, grad_agg2_ref, weights_ref, grad_agg_hbm, joint_hbm,
     grad_ref, feats_ref, halo_t_ref, grad_agg_ref, joint_ref, sems,
 ):
-    aggs = {1: agg1, 2: agg2, 3: agg3}
+    aggs = {1: agg1, 3: agg3}
     quarter, feat_width = agg1.shape
     share = feat_width // replicas
     halo_rows = halo_t_ref.shape[0]
     step = min(256, halo_rows)
     starts = range(0, halo_rows, step)
-    feats_copies, grad_copies = {}, {}
-    for k, grad in zip(aggs, (grad1, grad2, grad3), strict=True):
+    feats_copies, grad_copies = [], []
+    for n, (k, grad) in enumerate(zip(aggs, (grad1, grad3), strict=True)):
         at = pl.multiple_of(((rep_ref[0] + k) % replicas) * quarter, quarter)
-        feats_copies[k] = started(feats_hbm.at[pl.ds(at, quarter), :], feats_ref.at[k - 1], sems.at[k - 1])
-        grad_copies[k] = started(grad, grad_ref.at[k - 1], sems.at[replicas + k - 1])
-    at = 2 * replicas
+        feats_copies.append(started(feats_hbm.at[pl.ds(at, quarter), :], feats_ref.at[n], sems.at[n]))
+        grad_copies.append(started(grad, grad_ref.at[n], sems.at[2 + n]))
+    at = 4
     halo_copies = [
         started(halo_t_hbm.at[pl.ds(i, step), :], halo_t_ref.at[pl.ds(i, step), :], sems.at[at + n])
         for n, i in enumerate(starts)
     ]
     at += len(starts)
     share_cols = pl.ds(pl.multiple_of(rep_ref[0] * share, LANES), share)
-    grad_self = own_weights_ref[:share, :]
-    grad_neigh = own_weights_ref[share:, :]
-    grad_agg_ref[:quarter, :] = own_grad_ref[...]
-    for k, agg_ref in aggs.items():
+    grad_self = weights_ref[:share, :]
+    grad_neigh = weights_ref[share:, :]
+    grad_agg_ref[:quarter, :] = grad_agg0_ref[...]
+    grad_agg_ref[pl.ds(2 * quarter, quarter), :] = grad_agg2_ref[...]
+    for n, (k, agg_ref) in enumerate(aggs.items()):
         rows = pl.ds(k * quarter, quarter)
-        feats_copies[k].wait()
-        grad_copies[k].wait()
+        feats_copies[n].wait()
+        grad_copies[n].wait()
         _, grad_pre, grad_agg = dense_quarter(
-            agg_ref[...], feats_ref[k - 1], grad_ref[k - 1], scale_ref[rows, :], w_self_ref[...],
+            agg_ref[...], feats_ref[n], grad_ref[n], scale_ref[rows, :], w_self_ref[...],
             w_neigh_ref[...],
         )
         grad_agg_ref[rows, :] = grad_agg
-        grad_self = grad_self + dot(feats_ref[k - 1, :, share_cols], grad_pre, 0, 0)
+        grad_self = grad_self + dot(feats_ref[n, :, share_cols], grad_pre, 0, 0)
         grad_neigh = grad_neigh + dot(agg_ref[:, share_cols], grad_pre, 0, 0)
     grad_agg_copy = started(grad_agg_ref, grad_agg_hbm, sems.at[at])
     tile = 0
@@ -285,23 +307,37 @@
     copy.wait()
 
 
+def tile_kernel(joint_ref, copies_hbm, tiles_ref, sems):
+    halo_rows, lanes = tiles_ref.shape
+    feat_width = joint_ref.shape[1] - lanes
+    tiles = joint_ref[:, feat_width:].astype(F32).reshape(halo_rows // 8, 8, lanes)
+    tile = tiles.sum(axis=0, keepdims=True)
+    tiles_ref[...] = jnp.broadcast_to(tile, tiles.shape).reshape(halo_rows, lanes).astype(BF16)
+    copy = started(tiles_ref, copies_hbm, sems.at[0])
+    copy.wait()
+
+
 def return_kernel(
-    replicas, slots_ref, joint_ref, local_hbm, copies_hbm, own_ref, send1, send2, send3,
-    tiles_ref, local_ref, total_ref, sems,
+    replicas, rep_ref, slots_ref, joint_ref, local_hbm, own_ref, send1, send2, send3, local_ref,
+    total_ref, sems,
 ):
     quarter, feat_width = own_ref.shape
     halo_rows = joint_ref.shape[0]
     order = (2, 1, 3, 0)
     quarters, copies = quarter_copies(local_hbm, local_ref, sems, order)
-    lanes = joint_ref.shape[1] - feat_width
-    tiles = joint_ref[:, feat_width:].astype(F32).reshape(halo_rows // 8, 8, lanes)
-    tile = tiles.sum(axis=0, keepdims=True)
-    tiles_ref[...] = jnp.broadcast_to(tile, tiles.shape).reshape(halo_rows, lanes).astype(BF16)
-    copies_copy = started(tiles_ref, copies_hbm, sems.at[replicas])
-    slots = jnp.broadcast_to(slots_ref[...], (quarter, halo_rows))
+    slots = slots_ref[...]
+    slot = lax.broadcasted_iota(jnp.int32, slots.shape, 0)
+    lane = lax.broadcasted_iota(jnp.int32, slots.shape, 1)
+    pieces = []
+    for at in range(0, halo_rows, LANES):
+        picked = jnp.take_along_axis(slots, at // 8 + lane // 8, axis=1)
+        pieces.append(jnp.where(slot == lane % 8, picked, 0).sum(axis=0, keepdims=True))
+    turned = jnp.concatenate(pieces, axis=1) - rep_ref[0] * quarter
+    turned = jnp.where(turned < 0, turned + quarter * replicas, turned)
+    turned = jnp.broadcast_to(turned, (quarter, halo_rows))
     row = lax.broadcasted_iota(jnp.int32, (quarter, halo_rows), 0)
     for k, rows in quarters.items():
-        pick = jnp.where(row + k * quarter == slots, 1.0, 0.0).astype(BF16)
+        pick = jnp.where(row + k * quarter == turned, 1.0, 0.0).astype(BF16)
         total_ref[rows, :] = dot(pick, joint_ref[:, :feat_width], 1, 0)
     for k, rows in quarters.items():
         copies[k].wait()
@@ -310,7 +346,6 @@
             (send1, send2, send3)[k - 1][...] = total.astype(BF16)
         else:
             own_ref[...] = total
-    copies_copy.wait()
 
 
 def place_kernel(rep_ref, part0, part1, part3, part2, self_ref, neigh_ref):
@@ -349,13 +384,13 @@
     first_block = rep_index * (quarter // BLOCK)
     send_outs = [shape(quarter, feat_width, BF16)] * (replicas - 1)
 
-    slot_rows = send_rows[0].reshape(-1)
+    slots = send_rows[0].T
     (outgoing,) = call(
         gather_kernel,
         "gather_rows",
         [shape(halo_rows, feat_width, BF16)],
         [HBM, HBM],
-        (send_rows[0].T, node_feats),
+        (slots, node_feats),
         2 * node_rows * halo_rows * feat_width,
         out_specs=[HBM],
         scratch=[
@@ -396,9 +431,8 @@
             pltpu.SemaphoreType.DMA((replicas + 3,)),
         ],
     )
-    turned_slots = ((slot_rows - first_row) % node_rows)[None, :]
-    incoming, counts_halo, sums_local, scale, turned_slots, *grad_outs = lax.optimization_barrier(
-        (incoming, counts_halo, sums_local, scale, turned_slots, *grad_outs)
+    incoming, counts_halo, sums_local, scale, *grad_outs = lax.optimization_barrier(
+        (incoming, counts_halo, sums_local, scale, *grad_outs)
     )
 
     own_sums, *sends = call(
@@ -436,24 +470,33 @@
             pltpu.SemaphoreType.DMA((2,)),
         ],
     )
+    far_grad_agg, far_weights = call(
+        functools.partial(far_kernel, replicas, 2),
+        "dense_far",
+        [shape(quarter, feat_width, BF16), shape(2 * share, feat_width, F32)],
+        [SMEM, VMEM, HBM, HBM, VMEM, VMEM, VMEM, VMEM],
+        (rep_ref, aggs[1], grad_outs[2], node_feats, w_self, w_neigh, scale, own_weights),
+        block_flops // 2,
+        scratch=[pltpu.VMEM((quarter, feat_width), BF16)] * 2 + [pltpu.SemaphoreType.DMA((2,))],
+    )
     grad_agg, joint = call(
         functools.partial(dense_kernel, replicas),
         "dense_rest",
         [shape(node_rows, feat_width, BF16), shape(halo_rows, joint_width, BF16)],
-        [SMEM] + [VMEM] * 3 + [HBM] * 4 + [VMEM] * 3 + [HBM, VMEM, VMEM],
+        [SMEM] + [VMEM] * 2 + [HBM] * 3 + [VMEM] * 3 + [HBM] + [VMEM] * 3,
         (
-            rep_ref, aggs[0], aggs[2], aggs[1], *grad_outs[1:], node_feats, w_self, w_neigh, scale, halo_t, own_grad_agg,
-            own_weights,
+            rep_ref, aggs[0], aggs[2], grad_outs[1], grad_outs[3], node_feats, w_self, w_neigh, scale, halo_t,
+            own_grad_agg, far_grad_agg, far_weights,
         ),
         2 * block_flops,
         out_specs=[HBM, HBM],
         scratch=[
-            pltpu.VMEM((replicas - 1, quarter, feat_width), BF16),
-            pltpu.VMEM((replicas - 1, quarter, feat_width), BF16),
+            pltpu.VMEM((2, quarter, feat_width), BF16),
+            pltpu.VMEM((2, quarter, feat_width), BF16),
             pltpu.VMEM((halo_rows, node_rows), BF16),
             pltpu.VMEM((node_rows, feat_width), BF16),
             pltpu.VMEM((halo_rows, joint_width), BF16),
-            pltpu.SemaphoreType.DMA((1 + 2 * replicas + 2 * halo_steps,)),
+            pltpu.SemaphoreType.DMA((5 + 2 * halo_steps,)),
         ],
     )
     returned = lax.all_to_all(joint, WIDE, 0, 0, tiled=True)
@@ -475,17 +518,25 @@
     )
 
     lanes = joint_width - feat_width
-    copies, own_grad, *sends = call(
+    (copies,) = call(
+        tile_kernel,
+        "weight_tile",
+        [shape(halo_rows, lanes, BF16)],
+        [VMEM],
+        (returned,),
+        halo_rows * lanes,
+        out_specs=[HBM],
+        scratch=[pltpu.VMEM((halo_rows, lanes), BF16), pltpu.SemaphoreType.DMA((1,))],
+    )
+    own_grad, *sends = call(
         functools.partial(return_kernel, replicas),
         "returned_rows",
-        [shape(halo_rows, lanes, BF16), shape(quarter, feat_width, F32)] + send_outs,
-        [VMEM, VMEM, HBM],
-        (turned_slots, returned, local_grad),
+        [shape(quarter, feat_width, F32)] + send_outs,
+        [SMEM, VMEM, VMEM, HBM],
+        (rep_ref, jnp.pad(slots, ((0, 0), (0, -peer_count % LANES))), returned, local_grad),
         block_flops,
-        out_specs=[HBM] + [VMEM] * replicas,
-        scratch=[pltpu.VMEM((halo_rows, lanes), BF16)]
-        + [pltpu.VMEM((node_rows, feat_width), F32)] * 2
-        + [pltpu.SemaphoreType.DMA((replicas + 1,))],
+        scratch=[pltpu.VMEM((node_rows, feat_width), F32)] * 2
+        + [pltpu.SemaphoreType.DMA((replicas,))],
     )
     for k in FAR_FIRST:
         own_grad = own_grad + send_to(sends[k - 1], k, replicas).astype(F32)

time: 182 us -> 183 us (level)
  blocking collectives: 0 us -> 43.2 us
  waiting for transfers between devices: 55.7 us -> 23.6 us
  starting transfers between devices: 88.9 us -> 78.7 us
    all_to_all x0 -> x1, blocking collectives: none -> 43.2 us  [on_device(): returned = lax.all_to_all(joint, WIDE, 0, 0, tiled=True)]
    all_to_all x1 -> x0, waiting for transfers between devices: 31 us -> none  [on_device(): returned = lax.all_to_all(joint, WIDE, 0, 0, tiled=True)]
    all_to_all x1 -> x0, starting transfers between devices: 7.67 us -> none  [on_device(): returned = lax.all_to_all(joint, WIDE, 0, 0, tiled=True)]
    all_to_all x1, waiting for transfers between devices: 3.13 us -> 0.01 us  [on_device(): tiles = lax.all_to_all(copies, WIDE, 0, 0, tiled=True)]
    ppermute x15, starting transfers between devices: 55.2 us -> 52.7 us  [send_to(): lax.ppermute(x, 'rep', [(i, (i + step) % replicas) for i in range(replica...]
    pallas_call x8 -> x10, Pallas kernels: 33 us -> 34.5 us  [call(): pl.pallas_call(kernel, out_shape=outs, in_specs=in_specs, out_specs=out_s...]
  transfers between devices with their start and end apart: 18 -> 17, of which waited for: 6 -> 5; matrix products, arithmetic and copies ran while one was open for 1% -> 1% of each run, Pallas kernels for 10% -> 12%
where the time goes in v7:
time: 183 us; the launch traced here: 182 us
  starting transfers between devices  78.7 us (43%)
  blocking collectives  43.2 us (24%)
  Pallas kernels  34.5 us (19%)
  waiting for transfers between devices  23.6 us (13%)
    ppermute x15, starting transfers between devices, send_to(): lax.ppermute(x, 'rep', [(i, (i + step) % replicas) for i in range(replica...  52.7 us
    all_to_all x1, blocking collectives, on_device(): returned = lax.all_to_all(joint, WIDE, 0, 0, tiled=True)  43.2 us
    pallas_call x10, Pallas kernels, call(): pl.pallas_call(kernel, out_shape=outs, in_specs=in_specs, out_specs=out_s...  34.5 us
    all_to_all x1, starting transfers between devices, on_device(): incoming = lax.all_to_all(outgoing, WIDE, 0, 0, tiled=True)  18.4 us
    ppermute x15, waiting for transfers between devices, send_to(): lax.ppermute(x, 'rep', [(i, (i + step) % replicas) for i in range(replica...  13.3 us
    all_to_all x1, waiting for transfers between devices, on_device(): incoming = lax.all_to_all(outgoing, WIDE, 0, 0, tiled=True)  10.2 us
    all_to_all x1, starting transfers between devices, on_device(): tiles = lax.all_to_all(copies, WIDE, 0, 0, tiled=True)  7.61 us
  transfers between devices with their start and end apart: 17, of which 5 were waited for; matrix products, arithmetic and copies ran while one was open for 1% of the time, Pallas kernels for 12%

profile of v7, /device:TPU:1, one launch (start us, length us, event | category | flops | bytes accessed | tf_op | source)
XLA Modules:
  0.0 182.4 jit_solution(13582775069473389211)
XLA Ops:
  0.7 3.4 %gather_rows.1 = bf16[1024,512]{1,0:T(8,128)(2,1)} custom-call(s32[8,128]{1,0:T(8,128)} %bitcast.32, bf16[1024,512]{1,0:T(8,128)(2,1)} %feats_hbm.9), custom_call_target="tpu_custom_call" | custom-call | flops 1073741824 | bytes 2101248 | tf_op jit(solution)/shard_map/gather_rows/pallas_call | solution.py:40
  4.1 18.4 %all-to-all-start = ((bf16[128,8,512]{2,1,0:T(8,128)(2,1)}), bf16[128,8,512]{2,1,0:T(8,128)(2,1)S(1)}, u32[]{:S(2)}, u32[]{:S(2)}) async-start(bf16[128,8,512]{2,1,0:T(8,128)(2,1)} %bitcast.35), calls=%async_computation | async-start | bytes 2097152 | tf_op jit(solution)/shard_map/all_to_all | solution.py:403
  22.5 4.7 %collective-permute-start.1 = (bf16[256,512]{1,0:T(8,128)(2,1)S(1)}, bf16[256,512]{1,0:T(8,128)(2,1)}, u32[]{:S(2)}, u32[]{:S(2)}) collective-permute-start(bf16[256,512]{1,0:T(8,128)(2,1)S(1)} %copy-done.2), channel_id=1, source_target_pairs={{0,2},{1,3},{2,0},{3,1},{4,6},{5,7},{6,4},{7,5},{8,10},{9,11},{10,... | collective-permute-start | bytes 786440 | tf_op jit(solution)/shard_map/ppermute | solution.py:361
  27.2 2.8 %collective-permute-start = (bf16[256,512]{1,0:T(8,128)(2,1)S(1)}, bf16[256,512]{1,0:T(8,128)(2,1)}, u32[]{:S(2)}, u32[]{:S(2)}) collective-permute-start(bf16[256,512]{1,0:T(8,128)(2,1)S(1)} %copy-done.2), channel_id=1, source_target_pairs={{0,3},{1,0},{2,1},{3,2},{4,7},{5,4},{6,5},{7,6},{8,11},{9,8},{10,9... | collective-permute-start | bytes 786440 | tf_op jit(solution)/shard_map/ppermute | solution.py:361
  29.9 2.5 %collective-permute-start.2 = (bf16[256,512]{1,0:T(8,128)(2,1)S(1)}, bf16[256,512]{1,0:T(8,128)(2,1)}, u32[]{:S(2)}, u32[]{:S(2)}) collective-permute-start(bf16[256,512]{1,0:T(8,128)(2,1)S(1)} %copy-done.2), channel_id=1, source_target_pairs={{0,1},{1,2},{2,3},{3,0},{4,5},{5,6},{6,7},{7,4},{8,9},{9,10},{10,1... | collective-permute-start | bytes 786440 | tf_op jit(solution)/shard_map/ppermute | solution.py:361
  32.5 10.0 %tile_counts.1 = (bf16[1024,1024]{1,0:T(8,128)(2,1)}, bf16[1024,1024]{1,0:T(8,128)(2,1)S(1)}, bf16[1024,1024]{1,0:T(8,128)(2,1)}, f32[1024,512]{1,0:T(8,128)}) custom-call(s32[1]{0:T(128)} %bitcast.rep_ref, s32[128]{0:T(128)S(1)} %fusion.2.place_ref, s32[256,128]{1,0:T(8,128)S(1)} %bitcast.31, bf16[1024,512]{1,0:T(8,128)(2,1)} %feats_hbm.9), custom_call_target="tpu_custom_call" | custom-call | flops 1094713344 | bytes 9568772 | tf_op jit(solution)/shard_map/tile_counts/pallas_call | solution.py:40
  42.7 10.2 %all-to-all-done = bf16[128,8,512]{2,1,0:T(8,128)(2,1)S(1)} async-done(((bf16[128,8,512]{2,1,0:T(8,128)(2,1)}), bf16[128,8,512]{2,1,0:T(8,128)(2,1)S(1)}, u32[]{:S(2)}, u32[]{:S(2)}) %all-to-all-start) | async-done | bytes 1048608 | tf_op jit(solution)/shard_map/all_to_all | solution.py:403
  52.9 2.6 %neighbour_sums.1 = (f32[256,512]{1,0:T(8,128)S(1)}, bf16[256,512]{1,0:T(8,128)(2,1)S(1)}, bf16[256,512]{1,0:T(8,128)(2,1)S(1)}, bf16[256,512]{1,0:T(8,128)(2,1)S(1)}) custom-call(bf16[1024,1024]{1,0:T(8,128)(2,1)S(1)} %get-tuple-element.36.counts_ref, bf16[1024,512]{1,0:T(8,128)(2,1)S(1)} %bitcast.26, f32[1024,512]{1,0:T(8,128)} %get-tuple-element.38.local_hbm), custom_call_target="tpu_custom_call" | custom-call | flops 1073741824 | bytes 6553600 | tf_op jit(solution)/shard_map/neighbour_sums/pallas_call | solution.py:40
  55.5 4.8 %collective-permute-start.3 = (bf16[256,512]{1,0:T(8,128)(2,1)S(1)}, bf16[256,512]{1,0:T(8,128)(2,1)S(1)}, u32[]{:S(2)}, u32[]{:S(2)}) collective-permute-start(bf16[256,512]{1,0:T(8,128)(2,1)S(1)} %get-tuple-element.40), channel_id=1, source_target_pairs={{0,2},{1,3},{2,0},{3,1},{4,6},{5,7},{6,4},{7,5},{8,10},{9,11},{10,... | collective-permute-start | bytes 786440 | tf_op jit(solution)/shard_map/ppermute | solution.py:361
  62.5 4.3 %collective-permute-start.5 = (bf16[256,512]{1,0:T(8,128)(2,1)S(1)}, bf16[256,512]{1,0:T(8,128)(2,1)S(1)}, u32[]{:S(2)}, u32[]{:S(2)}) collective-permute-start(bf16[256,512]{1,0:T(8,128)(2,1)S(1)} %get-tuple-element.42), channel_id=1, source_target_pairs={{0,3},{1,0},{2,1},{3,2},{4,7},{5,4},{6,5},{7,6},{8,11},{9,8},{10,9... | collective-permute-start | bytes 786440 | tf_op jit(solution)/shard_map/ppermute | solution.py:361
  66.8 5.4 %collective-permute-done.4 = bf16[256,512]{1,0:T(8,128)(2,1)S(1)} collective-permute-done((bf16[256,512]{1,0:T(8,128)(2,1)S(1)}, bf16[256,512]{1,0:T(8,128)(2,1)S(1)}, u32[]{:S(2)}, u32[]{:S(2)}) %collective-permute-start.4) | collective-permute-done | bytes 262176 | tf_op jit(solution)/shard_map/ppermute | solution.py:361
  72.3 5.4 %collective-permute-start.8 = (bf16[256,512]{1,0:T(8,128)(2,1)S(1)}, bf16[256,512]{1,0:T(8,128)(2,1)S(1)}, u32[]{:S(2)}, u32[]{:S(2)}) collective-permute-start(bf16[256,512]{1,0:T(8,128)(2,1)S(1)} %multiply_convert_fusion.agg_ref), channel_id=1, source_target_pairs={{0,2},{1,3},{2,0},{3,1},{4,6},{5,7},{6,4},{7,5},{8,10},{9,11},{10,... | collective-permute-start | bytes 786440 | tf_op jit(solution)/shard_map/ppermute | solution.py:361
  79.6 4.6 %collective-permute-start.6 = (bf16[256,512]{1,0:T(8,128)(2,1)S(1)}, bf16[256,512]{1,0:T(8,128)(2,1)S(1)}, u32[]{:S(2)}, u32[]{:S(2)}) collective-permute-start(bf16[256,512]{1,0:T(8,128)(2,1)S(1)} %multiply_convert_fusion.agg_ref), channel_id=1, source_target_pairs={{0,3},{1,0},{2,1},{3,2},{4,7},{5,4},{6,5},{7,6},{8,11},{9,8},{10,9... | collective-permute-start | bytes 786440 | tf_op jit(solution)/shard_map/ppermute | solution.py:361
  84.5 3.4 %dense_own.1 = (bf16[256,512]{1,0:T(8,128)(2,1)}, f32[256,512]{1,0:T(8,128)}, bf16[256,512]{1,0:T(8,128)(2,1)S(1)}, f32[256,512]{1,0:T(8,128)S(1)}) custom-call(s32[1]{0:T(128)} %bitcast.rep_ref, bf16[256,512]{1,0:T(8,128)(2,1)S(1)} %multiply_convert_fusion.agg_ref, bf16[256,512]{1,0:T(8,128)(2,1)S(1)} %copy-done.2, bf16[1024,512]{1,0:T(8,128)(2,1)} %feats_hbm.9, ...), custom_call_target="tpu_custom_call" | custom-call | flops 536870912 | bytes 4198404 | tf_op jit(solution)/shard_map/dense_own/pallas_call | solution.py:40
  89.8 5.2 %dense_rest.1 = (bf16[1024,512]{1,0:T(8,128)(2,1)}, bf16[1024,640]{1,0:T(8,128)(2,1)}) custom-call(s32[1]{0:T(128)} %bitcast.rep_ref, bf16[256,512]{1,0:T(8,128)(2,1)S(1)} %collective-permute-done.6.agg1, bf16[256,512]{1,0:T(8,128)(2,1)S(1)} %collective-permute-done.7.agg3, bf16[256,512]{1,0:T(8,128)(2,1)} %collective-permute-done.grad1, ...), custom_call_target="tpu_custom_call" | custom-call | flops 2147483648 | bytes 8654852 | tf_op jit(solution)/shard_map/dense_rest/pallas_call | solution.py:40
  94.9 43.2 %all_to_all.32 = bf16[128,8,640]{2,1,0:T(8,128)(2,1)S(1)} all-to-all(bf16[128,8,640]{2,1,0:T(8,128)(2,1)} %bitcast.34), channel_id=1, replica_groups=mesh['y'=8,'z'=8,'core'=2,'rep'=4] {'y','z','core'}, dimensions={0} | all-to-all | bytes 2621440 | tf_op jit(solution)/shard_map/all_to_all | solution.py:502
  139.0 7.6 %all-to-all-start.2 = ((bf16[128,8,128]{2,1,0:T(8,128)(2,1)}), bf16[128,8,128]{2,1,0:T(8,128)(2,1)S(1)}, u32[]{:S(2)}, u32[]{:S(2)}) async-start(bf16[128,8,128]{2,1,0:T(8,128)(2,1)} %bitcast.36), calls=%async_computation.2 | async-start | bytes 524288 | tf_op jit(solution)/shard_map/all_to_all | solution.py:544
  146.6 4.6 %local_rows.1.local_hbm = f32[1024,512]{1,0:T(8,128)} custom-call(bf16[1024,1024]{1,0:T(8,128)(2,1)} %get-tuple-element.55.counts_hbm, bf16[1024,512]{1,0:T(8,128)(2,1)} %get-tuple-element.56.grad_hbm, f32[256,512]{1,0:T(8,128)} %get-tuple-element.57.base_hbm), custom_call_target="tpu_custom_call" | custom-call | flops 1073741824 | bytes 5767168 | tf_op jit(solution)/shard_map/local_rows/pallas_call | solution.py:40
  152.9 4.4 %collective-permute-start.9 = (bf16[256,512]{1,0:T(8,128)(2,1)S(1)}, bf16[256,512]{1,0:T(8,128)(2,1)S(1)}, u32[]{:S(2)}, u32[]{:S(2)}) collective-permute-start(bf16[256,512]{1,0:T(8,128)(2,1)S(1)} %get-tuple-element.59), channel_id=1, source_target_pairs={{0,2},{1,3},{2,0},{3,1},{4,6},{5,7},{6,4},{7,5},{8,10},{9,11},{10,... | collective-permute-start | bytes 786440 | tf_op jit(solution)/shard_map/ppermute | solution.py:361
  157.4 3.1 %collective-permute-start.10 = (bf16[256,512]{1,0:T(8,128)(2,1)S(1)}, bf16[256,512]{1,0:T(8,128)(2,1)S(1)}, u32[]{:S(2)}, u32[]{:S(2)}) collective-permute-start(bf16[256,512]{1,0:T(8,128)(2,1)S(1)} %get-tuple-element.60), channel_id=1, source_target_pairs={{0,1},{1,2},{2,3},{3,0},{4,5},{5,6},{6,7},{7,4},{8,9},{9,10},{10,1... | collective-permute-start | bytes 786440 | tf_op jit(solution)/shard_map/ppermute | solution.py:361
  160.4 3.4 %collective-permute-start.11 = (bf16[256,512]{1,0:T(8,128)(2,1)S(1)}, bf16[256,512]{1,0:T(8,128)(2,1)S(1)}, u32[]{:S(2)}, u32[]{:S(2)}) collective-permute-start(bf16[256,512]{1,0:T(8,128)(2,1)S(1)} %get-tuple-element.61), channel_id=1, source_target_pairs={{0,3},{1,0},{2,1},{3,2},{4,7},{5,4},{6,5},{7,6},{8,11},{9,8},{10,9... | collective-permute-start | bytes 786440 | tf_op jit(solution)/shard_map/ppermute | solution.py:361
  166.1 2.3 %collective-permute-start.13 = (bf16[256,512]{1,0:T(8,128)(2,1)S(1)}, bf16[256,512]{1,0:T(8,128)(2,1)S(1)}, u32[]{:S(2)}, u32[]{:S(2)}) collective-permute-start(bf16[256,512]{1,0:T(8,128)(2,1)S(1)} %bitcast.28), channel_id=1, source_target_pairs={{0,1},{1,2},{2,3},{3,0},{4,5},{5,6},{6,7},{7,4},{8,9},{9,10},{10,1... | collective-permute-start | bytes 786440 | tf_op jit(solution)/shard_map/ppermute | solution.py:361
  168.4 4.2 %collective-permute-start.12 = (bf16[256,512]{1,0:T(8,128)(2,1)S(1)}, bf16[256,512]{1,0:T(8,128)(2,1)S(1)}, u32[]{:S(2)}, u32[]{:S(2)}) collective-permute-start(bf16[256,512]{1,0:T(8,128)(2,1)S(1)} %bitcast.29), channel_id=1, source_target_pairs={{0,3},{1,0},{2,1},{3,2},{4,7},{5,4},{6,5},{7,6},{8,11},{9,8},{10,9... | collective-permute-start | bytes 786440 | tf_op jit(solution)/shard_map/ppermute | solution.py:361
  173.9 7.4 %collective-permute-done.13.part3 = bf16[256,512]{1,0:T(8,128)(2,1)S(1)} collective-permute-done((bf16[256,512]{1,0:T(8,128)(2,1)S(1)}, bf16[256,512]{1,0:T(8,128)(2,1)S(1)}, u32[]{:S(2)}, u32[]{:S(2)}) %collective-permute-start.13) | collective-permute-done | bytes 262176 | tf_op jit(solution)/shard_map/ppermute | solution.py:361
  (44 shorter events, 13.6 us)
Async XLA Ops:
  0.6 21.9 %copy-start.2 = (bf16[256,512]{1,0:T(8,128)(2,1)S(1)}, bf16[256,512]{1,0:T(8,128)(2,1)}, u32[]{:S(2)}) copy-start(bf16[256,512]{1,0:T(8,128)(2,1)} %grad_ref) | copy-start | bytes 786436
  0.6 31.8 %copy-start.5 = (s32[1024]{0:T(1024)S(1)}, s32[1024]{0:T(1024)}, u32[]{:S(2)}) copy-start(s32[1024]{0:T(1024)} %param.16) | copy-start | bytes 12292
  0.7 31.8 %copy-start.6 = (s32[1,1,128]{2,1,0:T(1,128)S(1)}, s32[1,1,128]{2,1,0:T(1,128)}, u32[]{:S(2)}) copy-start(s32[1,1,128]{2,1,0:T(1,128)} %param.14) | copy-start | bytes 1540
  0.7 31.8 %copy-start.7 = (s32[1,1,128]{2,1,0:T(1,128)S(1)}, s32[1,1,128]{2,1,0:T(1,128)}, u32[]{:S(2)}) copy-start(s32[1,1,128]{2,1,0:T(1,128)} %param.13) | copy-start | bytes 1540
  0.7 31.9 %copy-start.3 = (s32[1,1,32768]{2,1,0:T(1,128)S(1)}, s32[1,1,32768]{2,1,0:T(1,128)}, u32[]{:S(2)}) copy-start(s32[1,1,32768]{2,1,0:T(1,128)} %param.15) | copy-start | bytes 393220
  4.1 48.9 %all-to-all-start = ((bf16[128,8,512]{2,1,0:T(8,128)(2,1)}), bf16[128,8,512]{2,1,0:T(8,128)(2,1)S(1)}, u32[]{:S(2)}, u32[]{:S(2)}) async-start(bf16[128,8,512]{2,1,0:T(8,128)(2,1)} %bitcast.35), calls=%async_computation | async-start | bytes 2097152 | tf_op jit(solution)/shard_map/all_to_all | solution.py:403
  22.5 20.2 %collective-permute-start.1 = (bf16[256,512]{1,0:T(8,128)(2,1)S(1)}, bf16[256,512]{1,0:T(8,128)(2,1)}, u32[]{:S(2)}, u32[]{:S(2)}) collective-permute-start(bf16[256,512]{1,0:T(8,128)(2,1)S(1)} %copy-done.2), channel_id=1, source_target_pairs={{0,2},{1,3},{2,0},{3,1},{4,6},{5,7},{6,4},{7,5},{8,10},{9,11},{10,... | collective-permute-start | bytes 786440 | tf_op jit(solution)/shard_map/ppermute | solution.py:361
  27.2 15.5 %collective-permute-start = (bf16[256,512]{1,0:T(8,128)(2,1)S(1)}, bf16[256,512]{1,0:T(8,128)(2,1)}, u32[]{:S(2)}, u32[]{:S(2)}) collective-permute-start(bf16[256,512]{1,0:T(8,128)(2,1)S(1)} %copy-done.2), channel_id=1, source_target_pairs={{0,3},{1,0},{2,1},{3,2},{4,7},{5,4},{6,5},{7,6},{8,11},{9,8},{10,9... | collective-permute-start | bytes 786440 | tf_op jit(solution)/shard_map/ppermute | solution.py:361
  29.9 12.7 %collective-permute-start.2 = (bf16[256,512]{1,0:T(8,128)(2,1)S(1)}, bf16[256,512]{1,0:T(8,128)(2,1)}, u32[]{:S(2)}, u32[]{:S(2)}) collective-permute-start(bf16[256,512]{1,0:T(8,128)(2,1)S(1)} %copy-done.2), channel_id=1, source_target_pairs={{0,1},{1,2},{2,3},{3,0},{4,5},{5,6},{6,7},{7,4},{8,9},{9,10},{10,1... | collective-permute-start | bytes 786440 | tf_op jit(solution)/shard_map/ppermute | solution.py:361
  55.5 28.9 %copy-start = (bf16[512,512]{1,0:T(8,128)(2,1)S(1)}, bf16[512,512]{1,0:T(8,128)(2,1)}, u32[]{:S(2)}) copy-start(bf16[512,512]{1,0:T(8,128)(2,1)} %w_self_ref.5) | copy-start | bytes 1572868
  55.5 28.9 %copy-start.1 = (bf16[512,512]{1,0:T(8,128)(2,1)S(1)}, bf16[512,512]{1,0:T(8,128)(2,1)}, u32[]{:S(2)}) copy-start(bf16[512,512]{1,0:T(8,128)(2,1)} %w_neigh_ref.5) | copy-start | bytes 1572868
  55.5 11.3 %collective-permute-start.3 = (bf16[256,512]{1,0:T(8,128)(2,1)S(1)}, bf16[256,512]{1,0:T(8,128)(2,1)S(1)}, u32[]{:S(2)}, u32[]{:S(2)}) collective-permute-start(bf16[256,512]{1,0:T(8,128)(2,1)S(1)} %get-tuple-element.40), channel_id=1, source_target_pairs={{0,2},{1,3},{2,0},{3,1},{4,6},{5,7},{6,4},{7,5},{8,10},{9,11},{10,... | collective-permute-start | bytes 786440 | tf_op jit(solution)/shard_map/ppermute | solution.py:361
  60.3 11.9 %collective-permute-start.4 = (bf16[256,512]{1,0:T(8,128)(2,1)S(1)}, bf16[256,512]{1,0:T(8,128)(2,1)S(1)}, u32[]{:S(2)}, u32[]{:S(2)}) collective-permute-start(bf16[256,512]{1,0:T(8,128)(2,1)S(1)} %get-tuple-element.41), channel_id=1, source_target_pairs={{0,1},{1,2},{2,3},{3,0},{4,5},{5,6},{6,7},{7,4},{8,9},{9,10},{10,1... | collective-permute-start | bytes 786440 | tf_op jit(solution)/shard_map/ppermute | solution.py:361
  62.5 9.7 %collective-permute-start.5 = (bf16[256,512]{1,0:T(8,128)(2,1)S(1)}, bf16[256,512]{1,0:T(8,128)(2,1)S(1)}, u32[]{:S(2)}, u32[]{:S(2)}) collective-permute-start(bf16[256,512]{1,0:T(8,128)(2,1)S(1)} %get-tuple-element.42), channel_id=1, source_target_pairs={{0,3},{1,0},{2,1},{3,2},{4,7},{5,4},{6,5},{7,6},{8,11},{9,8},{10,9... | collective-permute-start | bytes 786440 | tf_op jit(solution)/shard_map/ppermute | solution.py:361
  72.3 15.5 %collective-permute-start.8 = (bf16[256,512]{1,0:T(8,128)(2,1)S(1)}, bf16[256,512]{1,0:T(8,128)(2,1)S(1)}, u32[]{:S(2)}, u32[]{:S(2)}) collective-permute-start(bf16[256,512]{1,0:T(8,128)(2,1)S(1)} %multiply_convert_fusion.agg_ref), channel_id=1, source_target_pairs={{0,2},{1,3},{2,0},{3,1},{4,6},{5,7},{6,4},{7,5},{8,10},{9,11},{10,... | collective-permute-start | bytes 786440 | tf_op jit(solution)/shard_map/ppermute | solution.py:361
  77.7 12.1 %collective-permute-start.7 = (bf16[256,512]{1,0:T(8,128)(2,1)S(1)}, bf16[256,512]{1,0:T(8,128)(2,1)S(1)}, u32[]{:S(2)}, u32[]{:S(2)}) collective-permute-start(bf16[256,512]{1,0:T(8,128)(2,1)S(1)} %multiply_convert_fusion.agg_ref), channel_id=1, source_target_pairs={{0,1},{1,2},{2,3},{3,0},{4,5},{5,6},{6,7},{7,4},{8,9},{9,10},{10,1... | collective-permute-start | bytes 786440 | tf_op jit(solution)/shard_map/ppermute | solution.py:361
  79.6 10.1 %collective-permute-start.6 = (bf16[256,512]{1,0:T(8,128)(2,1)S(1)}, bf16[256,512]{1,0:T(8,128)(2,1)S(1)}, u32[]{:S(2)}, u32[]{:S(2)}) collective-permute-start(bf16[256,512]{1,0:T(8,128)(2,1)S(1)} %multiply_convert_fusion.agg_ref), channel_id=1, source_target_pairs={{0,3},{1,0},{2,1},{3,2},{4,7},{5,4},{6,5},{7,6},{8,11},{9,8},{10,9... | collective-permute-start | bytes 786440 | tf_op jit(solution)/shard_map/ppermute | solution.py:361
  139.0 24.9 %all-to-all-start.2 = ((bf16[128,8,128]{2,1,0:T(8,128)(2,1)}), bf16[128,8,128]{2,1,0:T(8,128)(2,1)S(1)}, u32[]{:S(2)}, u32[]{:S(2)}) async-start(bf16[128,8,128]{2,1,0:T(8,128)(2,1)} %bitcast.36), calls=%async_computation.2 | async-start | bytes 524288 | tf_op jit(solution)/shard_map/all_to_all | solution.py:544
  152.9 15.5 %collective-permute-start.9 = (bf16[256,512]{1,0:T(8,128)(2,1)S(1)}, bf16[256,512]{1,0:T(8,128)(2,1)S(1)}, u32[]{:S(2)}, u32[]{:S(2)}) collective-permute-start(bf16[256,512]{1,0:T(8,128)(2,1)S(1)} %get-tuple-element.59), channel_id=1, source_target_pairs={{0,2},{1,3},{2,0},{3,1},{4,6},{5,7},{6,4},{7,5},{8,10},{9,11},{10,... | collective-permute-start | bytes 786440 | tf_op jit(solution)/shard_map/ppermute | solution.py:361
  157.4 15.3 %collective-permute-start.10 = (bf16[256,512]{1,0:T(8,128)(2,1)S(1)}, bf16[256,512]{1,0:T(8,128)(2,1)S(1)}, u32[]{:S(2)}, u32[]{:S(2)}) collective-permute-start(bf16[256,512]{1,0:T(8,128)(2,1)S(1)} %get-tuple-element.60), channel_id=1, source_target_pairs={{0,1},{1,2},{2,3},{3,0},{4,5},{5,6},{6,7},{7,4},{8,9},{9,10},{10,1... | collective-permute-start | bytes 786440 | tf_op jit(solution)/shard_map/ppermute | solution.py:361
  160.4 12.2 %collective-permute-start.11 = (bf16[256,512]{1,0:T(8,128)(2,1)S(1)}, bf16[256,512]{1,0:T(8,128)(2,1)S(1)}, u32[]{:S(2)}, u32[]{:S(2)}) collective-permute-start(bf16[256,512]{1,0:T(8,128)(2,1)S(1)} %get-tuple-element.61), channel_id=1, source_target_pairs={{0,3},{1,0},{2,1},{3,2},{4,7},{5,4},{6,5},{7,6},{8,11},{9,8},{10,9... | collective-permute-start | bytes 786440 | tf_op jit(solution)/shard_map/ppermute | solution.py:361
  163.9 10.0 %collective-permute-start.14 = (bf16[256,512]{1,0:T(8,128)(2,1)S(1)}, bf16[256,512]{1,0:T(8,128)(2,1)S(1)}, u32[]{:S(2)}, u32[]{:S(2)}) collective-permute-start(bf16[256,512]{1,0:T(8,128)(2,1)S(1)} %bitcast.27), channel_id=1, source_target_pairs={{0,2},{1,3},{2,0},{3,1},{4,6},{5,7},{6,4},{7,5},{8,10},{9,11},{10,... | collective-permute-start | bytes 786440 | tf_op jit(solution)/shard_map/ppermute | solution.py:361
  166.1 15.3 %collective-permute-start.13 = (bf16[256,512]{1,0:T(8,128)(2,1)S(1)}, bf16[256,512]{1,0:T(8,128)(2,1)S(1)}, u32[]{:S(2)}, u32[]{:S(2)}) collective-permute-start(bf16[256,512]{1,0:T(8,128)(2,1)S(1)} %bitcast.28), channel_id=1, source_target_pairs={{0,1},{1,2},{2,3},{3,0},{4,5},{5,6},{6,7},{7,4},{8,9},{9,10},{10,1... | collective-permute-start | bytes 786440 | tf_op jit(solution)/shard_map/ppermute | solution.py:361
  168.4 13.0 %collective-permute-start.12 = (bf16[256,512]{1,0:T(8,128)(2,1)S(1)}, bf16[256,512]{1,0:T(8,128)(2,1)S(1)}, u32[]{:S(2)}, u32[]{:S(2)}) collective-permute-start(bf16[256,512]{1,0:T(8,128)(2,1)S(1)} %bitcast.29), channel_id=1, source_target_pairs={{0,3},{1,0},{2,1},{3,2},{4,7},{5,4},{6,5},{7,6},{8,11},{9,8},{10,9... | collective-permute-start | bytes 786440 | tf_op jit(solution)/shard_map/ppermute | solution.py:361
  (1 other events, 4.6 us)

commit v8 on v7

--- a/solution.py
+++ b/solution.py
@@ -517,6 +517,7 @@
         ],
     )
 
+    returned, local_grad = lax.optimization_barrier((returned, local_grad))
     lanes = joint_width - feat_width
     (copies,) = call(
         tile_kernel,

time: 183 us -> 180 us (0.984)
  blocking collectives: 43.2 us -> 0 us
  waiting for transfers between devices: 23.6 us -> 52.7 us
  starting transfers between devices: 78.7 us -> 88.6 us
    all_to_all x1 -> x0, blocking collectives: 43.2 us -> none  [on_device(): returned = lax.all_to_all(joint, WIDE, 0, 0, tiled=True)]
    all_to_all x0 -> x1, waiting for transfers between devices: none -> 30.9 us  [on_device(): returned = lax.all_to_all(joint, WIDE, 0, 0, tiled=True)]
    all_to_all x0 -> x1, starting transfers between devices: none -> 7.63 us  [on_device(): returned = lax.all_to_all(joint, WIDE, 0, 0, tiled=True)]
    ppermute x15, waiting for transfers between devices: 13.3 us -> 9.88 us  [send_to(): lax.ppermute(x, 'rep', [(i, (i + step) % replicas) for i in range(replica...]
    ppermute x15, starting transfers between devices: 52.7 us -> 54.9 us  [send_to(): lax.ppermute(x, 'rep', [(i, (i + step) % replicas) for i in range(replica...]
  transfers between devices with their start and end apart: 17 -> 18, of which waited for: 5 -> 6; matrix products, arithmetic and copies ran while one was open for 1% -> 1% of each run, Pallas kernels for 12% -> 12%
where the time goes in v8:
time: 180 us; the launch traced here: 178 us
  starting transfers between devices  88.6 us (49%)
  waiting for transfers between devices  52.7 us (29%)
  Pallas kernels  34.5 us (19%)
    ppermute x15, starting transfers between devices, send_to(): lax.ppermute(x, 'rep', [(i, (i + step) % replicas) for i in range(replica...  54.9 us
    pallas_call x10, Pallas kernels, call(): pl.pallas_call(kernel, out_shape=outs, in_specs=in_specs, out_specs=out_s...  34.5 us
    all_to_all x1, waiting for transfers between devices, on_device(): returned = lax.all_to_all(joint, WIDE, 0, 0, tiled=True)  30.9 us
    all_to_all x1, starting transfers between devices, on_device(): incoming = lax.all_to_all(outgoing, WIDE, 0, 0, tiled=True)  18.4 us
    all_to_all x1, waiting for transfers between devices, on_device(): incoming = lax.all_to_all(outgoing, WIDE, 0, 0, tiled=True)  10.3 us
    ppermute x15, waiting for transfers between devices, send_to(): lax.ppermute(x, 'rep', [(i, (i + step) % replicas) for i in range(replica...  9.88 us
    all_to_all x1, starting transfers between devices, on_device(): returned = lax.all_to_all(joint, WIDE, 0, 0, tiled=True)  7.63 us
    all_to_all x1, starting transfers between devices, on_device(): tiles = lax.all_to_all(copies, WIDE, 0, 0, tiled=True)  7.61 us
  transfers between devices with their start and end apart: 18, of which 6 were waited for; matrix products, arithmetic and copies ran while one was open for 1% of the time, Pallas kernels for 12%

profile of v8, /device:TPU:1, one launch (start us, length us, event | category | flops | bytes accessed | tf_op | source)
XLA Modules:
  0.0 178.2 jit_solution(7329874975646616403)
XLA Ops:
  0.7 3.4 %gather_rows.1 = bf16[1024,512]{1,0:T(8,128)(2,1)} custom-call(s32[8,128]{1,0:T(8,128)} %bitcast.32, bf16[1024,512]{1,0:T(8,128)(2,1)} %feats_hbm.9), custom_call_target="tpu_custom_call" | custom-call | flops 1073741824 | bytes 2101248 | tf_op jit(solution)/shard_map/gather_rows/pallas_call | solution.py:40
  4.1 18.4 %all-to-all-start = ((bf16[128,8,512]{2,1,0:T(8,128)(2,1)}), bf16[128,8,512]{2,1,0:T(8,128)(2,1)S(1)}, u32[]{:S(2)}, u32[]{:S(2)}) async-start(bf16[128,8,512]{2,1,0:T(8,128)(2,1)} %bitcast.35), calls=%async_computation | async-start | bytes 2097152 | tf_op jit(solution)/shard_map/all_to_all | solution.py:403
  22.5 4.7 %collective-permute-start.1 = (bf16[256,512]{1,0:T(8,128)(2,1)S(1)}, bf16[256,512]{1,0:T(8,128)(2,1)}, u32[]{:S(2)}, u32[]{:S(2)}) collective-permute-start(bf16[256,512]{1,0:T(8,128)(2,1)S(1)} %copy-done.2), channel_id=1, source_target_pairs={{0,2},{1,3},{2,0},{3,1},{4,6},{5,7},{6,4},{7,5},{8,10},{9,11},{10,... | collective-permute-start | bytes 786440 | tf_op jit(solution)/shard_map/ppermute | solution.py:361
  27.2 2.8 %collective-permute-start = (bf16[256,512]{1,0:T(8,128)(2,1)S(1)}, bf16[256,512]{1,0:T(8,128)(2,1)}, u32[]{:S(2)}, u32[]{:S(2)}) collective-permute-start(bf16[256,512]{1,0:T(8,128)(2,1)S(1)} %copy-done.2), channel_id=1, source_target_pairs={{0,3},{1,0},{2,1},{3,2},{4,7},{5,4},{6,5},{7,6},{8,11},{9,8},{10,9... | collective-permute-start | bytes 786440 | tf_op jit(solution)/shard_map/ppermute | solution.py:361
  32.6 10.0 %tile_counts.1 = (bf16[1024,1024]{1,0:T(8,128)(2,1)}, bf16[1024,1024]{1,0:T(8,128)(2,1)S(1)}, bf16[1024,1024]{1,0:T(8,128)(2,1)}, f32[1024,512]{1,0:T(8,128)}) custom-call(s32[1]{0:T(128)} %bitcast.rep_ref, s32[128]{0:T(128)S(1)} %fusion.2.place_ref, s32[256,128]{1,0:T(8,128)S(1)} %bitcast.31, bf16[1024,512]{1,0:T(8,128)(2,1)} %feats_hbm.9), custom_call_target="tpu_custom_call" | custom-call | flops 1094713344 | bytes 9568772 | tf_op jit(solution)/shard_map/tile_counts/pallas_call | solution.py:40
  42.7 10.3 %all-to-all-done = bf16[128,8,512]{2,1,0:T(8,128)(2,1)S(1)} async-done(((bf16[128,8,512]{2,1,0:T(8,128)(2,1)}), bf16[128,8,512]{2,1,0:T(8,128)(2,1)S(1)}, u32[]{:S(2)}, u32[]{:S(2)}) %all-to-all-start) | async-done | bytes 1048608 | tf_op jit(solution)/shard_map/all_to_all | solution.py:403
  55.5 4.8 %collective-permute-start.3 = (bf16[256,512]{1,0:T(8,128)(2,1)S(1)}, bf16[256,512]{1,0:T(8,128)(2,1)S(1)}, u32[]{:S(2)}, u32[]{:S(2)}) collective-permute-start(bf16[256,512]{1,0:T(8,128)(2,1)S(1)} %get-tuple-element.42), channel_id=1, source_target_pairs={{0,2},{1,3},{2,0},{3,1},{4,6},{5,7},{6,4},{7,5},{8,10},{9,11},{10,... | collective-permute-start | bytes 786440 | tf_op jit(solution)/shard_map/ppermute | solution.py:361
  62.5 4.3 %collective-permute-start.5 = (bf16[256,512]{1,0:T(8,128)(2,1)S(1)}, bf16[256,512]{1,0:T(8,128)(2,1)S(1)}, u32[]{:S(2)}, u32[]{:S(2)}) collective-permute-start(bf16[256,512]{1,0:T(8,128)(2,1)S(1)} %get-tuple-element.44), channel_id=1, source_target_pairs={{0,3},{1,0},{2,1},{3,2},{4,7},{5,4},{6,5},{7,6},{8,11},{9,8},{10,9... | collective-permute-start | bytes 786440 | tf_op jit(solution)/shard_map/ppermute | solution.py:361
  66.8 5.4 %collective-permute-done.4 = bf16[256,512]{1,0:T(8,128)(2,1)S(1)} collective-permute-done((bf16[256,512]{1,0:T(8,128)(2,1)S(1)}, bf16[256,512]{1,0:T(8,128)(2,1)S(1)}, u32[]{:S(2)}, u32[]{:S(2)}) %collective-permute-start.4) | collective-permute-done | bytes 262176 | tf_op jit(solution)/shard_map/ppermute | solution.py:361
  72.3 5.4 %collective-permute-start.8 = (bf16[256,512]{1,0:T(8,128)(2,1)S(1)}, bf16[256,512]{1,0:T(8,128)(2,1)S(1)}, u32[]{:S(2)}, u32[]{:S(2)}) collective-permute-start(bf16[256,512]{1,0:T(8,128)(2,1)S(1)} %multiply_convert_fusion.agg_ref), channel_id=1, source_target_pairs={{0,2},{1,3},{2,0},{3,1},{4,6},{5,7},{6,4},{7,5},{8,10},{9,11},{10,... | collective-permute-start | bytes 786440 | tf_op jit(solution)/shard_map/ppermute | solution.py:361
  79.6 4.6 %collective-permute-start.6 = (bf16[256,512]{1,0:T(8,128)(2,1)S(1)}, bf16[256,512]{1,0:T(8,128)(2,1)S(1)}, u32[]{:S(2)}, u32[]{:S(2)}) collective-permute-start(bf16[256,512]{1,0:T(8,128)(2,1)S(1)} %multiply_convert_fusion.agg_ref), channel_id=1, source_target_pairs={{0,3},{1,0},{2,1},{3,2},{4,7},{5,4},{6,5},{7,6},{8,11},{9,8},{10,9... | collective-permute-start | bytes 786440 | tf_op jit(solution)/shard_map/ppermute | solution.py:361
  84.5 3.4 %dense_own.1 = (bf16[256,512]{1,0:T(8,128)(2,1)}, f32[256,512]{1,0:T(8,128)}, bf16[256,512]{1,0:T(8,128)(2,1)S(1)}, f32[256,512]{1,0:T(8,128)S(1)}) custom-call(s32[1]{0:T(128)} %bitcast.rep_ref, bf16[256,512]{1,0:T(8,128)(2,1)S(1)} %multiply_convert_fusion.agg_ref, bf16[256,512]{1,0:T(8,128)(2,1)S(1)} %copy-done.2, bf16[1024,512]{1,0:T(8,128)(2,1)} %feats_hbm.9, ...), custom_call_target="tpu_custom_call" | custom-call | flops 536870912 | bytes 4198404 | tf_op jit(solution)/shard_map/dense_own/pallas_call | solution.py:40
  89.8 5.2 %dense_rest.1 = (bf16[1024,512]{1,0:T(8,128)(2,1)}, bf16[1024,640]{1,0:T(8,128)(2,1)}) custom-call(s32[1]{0:T(128)} %bitcast.rep_ref, bf16[256,512]{1,0:T(8,128)(2,1)S(1)} %collective-permute-done.6.agg1, bf16[256,512]{1,0:T(8,128)(2,1)S(1)} %collective-permute-done.7.agg3, bf16[256,512]{1,0:T(8,128)(2,1)} %collective-permute-done.grad1, ...), custom_call_target="tpu_custom_call" | custom-call | flops 2147483648 | bytes 8654852 | tf_op jit(solution)/shard_map/dense_rest/pallas_call | solution.py:40
  94.9 7.6 %all-to-all-start.1 = ((bf16[128,8,640]{2,1,0:T(8,128)(2,1)}), bf16[128,8,640]{2,1,0:T(8,128)(2,1)S(1)}, u32[]{:S(2)}, u32[]{:S(2)}) async-start(bf16[128,8,640]{2,1,0:T(8,128)(2,1)} %bitcast.34), calls=%async_computation.1 | async-start | bytes 2621440 | tf_op jit(solution)/shard_map/all_to_all | solution.py:502
  102.6 4.6 %local_rows.1.local_hbm = f32[1024,512]{1,0:T(8,128)} custom-call(bf16[1024,1024]{1,0:T(8,128)(2,1)} %get-tuple-element.57.counts_hbm, bf16[1024,512]{1,0:T(8,128)(2,1)} %get-tuple-element.58.grad_hbm, f32[256,512]{1,0:T(8,128)} %get-tuple-element.59.base_hbm), custom_call_target="tpu_custom_call" | custom-call | flops 1073741824 | bytes 5767168 | tf_op jit(solution)/shard_map/local_rows/pallas_call | solution.py:40
  107.2 30.9 %all-to-all-done.1 = bf16[128,8,640]{2,1,0:T(8,128)(2,1)S(1)} async-done(((bf16[128,8,640]{2,1,0:T(8,128)(2,1)}), bf16[128,8,640]{2,1,0:T(8,128)(2,1)S(1)}, u32[]{:S(2)}, u32[]{:S(2)}) %all-to-all-start.1) | async-done | bytes 1310752 | tf_op jit(solution)/shard_map/all_to_all | solution.py:502
  139.0 7.6 %all-to-all-start.2 = ((bf16[128,8,128]{2,1,0:T(8,128)(2,1)}), bf16[128,8,128]{2,1,0:T(8,128)(2,1)S(1)}, u32[]{:S(2)}, u32[]{:S(2)}) async-start(bf16[128,8,128]{2,1,0:T(8,128)(2,1)} %bitcast.36), calls=%async_computation.2 | async-start | bytes 524288 | tf_op jit(solution)/shard_map/all_to_all | solution.py:545
  148.3 4.4 %collective-permute-start.9 = (bf16[256,512]{1,0:T(8,128)(2,1)S(1)}, bf16[256,512]{1,0:T(8,128)(2,1)S(1)}, u32[]{:S(2)}, u32[]{:S(2)}) collective-permute-start(bf16[256,512]{1,0:T(8,128)(2,1)S(1)} %get-tuple-element.63), channel_id=1, source_target_pairs={{0,2},{1,3},{2,0},{3,1},{4,6},{5,7},{6,4},{7,5},{8,10},{9,11},{10,... | collective-permute-start | bytes 786440 | tf_op jit(solution)/shard_map/ppermute | solution.py:361
  152.8 3.1 %collective-permute-start.10 = (bf16[256,512]{1,0:T(8,128)(2,1)S(1)}, bf16[256,512]{1,0:T(8,128)(2,1)S(1)}, u32[]{:S(2)}, u32[]{:S(2)}) collective-permute-start(bf16[256,512]{1,0:T(8,128)(2,1)S(1)} %get-tuple-element.64), channel_id=1, source_target_pairs={{0,1},{1,2},{2,3},{3,0},{4,5},{5,6},{6,7},{7,4},{8,9},{9,10},{10,1... | collective-permute-start | bytes 786440 | tf_op jit(solution)/shard_map/ppermute | solution.py:361
  155.8 3.4 %collective-permute-start.11 = (bf16[256,512]{1,0:T(8,128)(2,1)S(1)}, bf16[256,512]{1,0:T(8,128)(2,1)S(1)}, u32[]{:S(2)}, u32[]{:S(2)}) collective-permute-start(bf16[256,512]{1,0:T(8,128)(2,1)S(1)} %get-tuple-element.65), channel_id=1, source_target_pairs={{0,3},{1,0},{2,1},{3,2},{4,7},{5,4},{6,5},{7,6},{8,11},{9,8},{10,9... | collective-permute-start | bytes 786440 | tf_op jit(solution)/shard_map/ppermute | solution.py:361
  160.9 4.4 %collective-permute-start.14 = (bf16[256,512]{1,0:T(8,128)(2,1)S(1)}, bf16[256,512]{1,0:T(8,128)(2,1)S(1)}, u32[]{:S(2)}, u32[]{:S(2)}) collective-permute-start(bf16[256,512]{1,0:T(8,128)(2,1)S(1)} %bitcast.27), channel_id=1, source_target_pairs={{0,2},{1,3},{2,0},{3,1},{4,6},{5,7},{6,4},{7,5},{8,10},{9,11},{10,... | collective-permute-start | bytes 786440 | tf_op jit(solution)/shard_map/ppermute | solution.py:361
  165.3 3.1 %collective-permute-start.13 = (bf16[256,512]{1,0:T(8,128)(2,1)S(1)}, bf16[256,512]{1,0:T(8,128)(2,1)S(1)}, u32[]{:S(2)}, u32[]{:S(2)}) collective-permute-start(bf16[256,512]{1,0:T(8,128)(2,1)S(1)} %bitcast.28), channel_id=1, source_target_pairs={{0,1},{1,2},{2,3},{3,0},{4,5},{5,6},{6,7},{7,4},{8,9},{9,10},{10,1... | collective-permute-start | bytes 786440 | tf_op jit(solution)/shard_map/ppermute | solution.py:361
  168.4 3.4 %collective-permute-start.12 = (bf16[256,512]{1,0:T(8,128)(2,1)S(1)}, bf16[256,512]{1,0:T(8,128)(2,1)S(1)}, u32[]{:S(2)}, u32[]{:S(2)}) collective-permute-start(bf16[256,512]{1,0:T(8,128)(2,1)S(1)} %bitcast.29), channel_id=1, source_target_pairs={{0,3},{1,0},{2,1},{3,2},{4,7},{5,4},{6,5},{7,6},{8,11},{9,8},{10,9... | collective-permute-start | bytes 786440 | tf_op jit(solution)/shard_map/ppermute | solution.py:361
  172.7 4.4 %collective-permute-done.13.part3 = bf16[256,512]{1,0:T(8,128)(2,1)S(1)} collective-permute-done((bf16[256,512]{1,0:T(8,128)(2,1)S(1)}, bf16[256,512]{1,0:T(8,128)(2,1)S(1)}, u32[]{:S(2)}, u32[]{:S(2)}) %collective-permute-start.13) | collective-permute-done | bytes 262176 | tf_op jit(solution)/shard_map/ppermute | solution.py:361
  (45 shorter events, 17.7 us)
Async XLA Ops:
  0.6 31.8 %copy-start.5 = (s32[1024]{0:T(1024)S(1)}, s32[1024]{0:T(1024)}, u32[]{:S(2)}) copy-start(s32[1024]{0:T(1024)} %param.16) | copy-start | bytes 12292
  0.7 31.8 %copy-start.6 = (s32[1,1,128]{2,1,0:T(1,128)S(1)}, s32[1,1,128]{2,1,0:T(1,128)}, u32[]{:S(2)}) copy-start(s32[1,1,128]{2,1,0:T(1,128)} %param.14) | copy-start | bytes 1540
  0.7 31.8 %copy-start.7 = (s32[1,1,128]{2,1,0:T(1,128)S(1)}, s32[1,1,128]{2,1,0:T(1,128)}, u32[]{:S(2)}) copy-start(s32[1,1,128]{2,1,0:T(1,128)} %param.13) | copy-start | bytes 1540
  0.7 31.9 %copy-start.3 = (s32[1,1,32768]{2,1,0:T(1,128)S(1)}, s32[1,1,32768]{2,1,0:T(1,128)}, u32[]{:S(2)}) copy-start(s32[1,1,32768]{2,1,0:T(1,128)} %param.15) | copy-start | bytes 393220
  4.1 48.9 %all-to-all-start = ((bf16[128,8,512]{2,1,0:T(8,128)(2,1)}), bf16[128,8,512]{2,1,0:T(8,128)(2,1)S(1)}, u32[]{:S(2)}, u32[]{:S(2)}) async-start(bf16[128,8,512]{2,1,0:T(8,128)(2,1)} %bitcast.35), calls=%async_computation | async-start | bytes 2097152 | tf_op jit(solution)/shard_map/all_to_all | solution.py:403
  22.5 20.2 %collective-permute-start.1 = (bf16[256,512]{1,0:T(8,128)(2,1)S(1)}, bf16[256,512]{1,0:T(8,128)(2,1)}, u32[]{:S(2)}, u32[]{:S(2)}) collective-permute-start(bf16[256,512]{1,0:T(8,128)(2,1)S(1)} %copy-done.2), channel_id=1, source_target_pairs={{0,2},{1,3},{2,0},{3,1},{4,6},{5,7},{6,4},{7,5},{8,10},{9,11},{10,... | collective-permute-start | bytes 786440 | tf_op jit(solution)/shard_map/ppermute | solution.py:361
  27.2 15.5 %collective-permute-start = (bf16[256,512]{1,0:T(8,128)(2,1)S(1)}, bf16[256,512]{1,0:T(8,128)(2,1)}, u32[]{:S(2)}, u32[]{:S(2)}) collective-permute-start(bf16[256,512]{1,0:T(8,128)(2,1)S(1)} %copy-done.2), channel_id=1, source_target_pairs={{0,3},{1,0},{2,1},{3,2},{4,7},{5,4},{6,5},{7,6},{8,11},{9,8},{10,9... | collective-permute-start | bytes 786440 | tf_op jit(solution)/shard_map/ppermute | solution.py:361
  29.9 12.7 %collective-permute-start.2 = (bf16[256,512]{1,0:T(8,128)(2,1)S(1)}, bf16[256,512]{1,0:T(8,128)(2,1)}, u32[]{:S(2)}, u32[]{:S(2)}) collective-permute-start(bf16[256,512]{1,0:T(8,128)(2,1)S(1)} %copy-done.2), channel_id=1, source_target_pairs={{0,1},{1,2},{2,3},{3,0},{4,5},{5,6},{6,7},{7,4},{8,9},{9,10},{10,1... | collective-permute-start | bytes 786440 | tf_op jit(solution)/shard_map/ppermute | solution.py:361
  55.5 28.9 %copy-start = (bf16[512,512]{1,0:T(8,128)(2,1)S(1)}, bf16[512,512]{1,0:T(8,128)(2,1)}, u32[]{:S(2)}) copy-start(bf16[512,512]{1,0:T(8,128)(2,1)} %w_self_ref.5) | copy-start | bytes 1572868
  55.5 11.3 %collective-permute-start.3 = (bf16[256,512]{1,0:T(8,128)(2,1)S(1)}, bf16[256,512]{1,0:T(8,128)(2,1)S(1)}, u32[]{:S(2)}, u32[]{:S(2)}) collective-permute-start(bf16[256,512]{1,0:T(8,128)(2,1)S(1)} %get-tuple-element.42), channel_id=1, source_target_pairs={{0,2},{1,3},{2,0},{3,1},{4,6},{5,7},{6,4},{7,5},{8,10},{9,11},{10,... | collective-permute-start | bytes 786440 | tf_op jit(solution)/shard_map/ppermute | solution.py:361
  60.3 11.9 %collective-permute-start.4 = (bf16[256,512]{1,0:T(8,128)(2,1)S(1)}, bf16[256,512]{1,0:T(8,128)(2,1)S(1)}, u32[]{:S(2)}, u32[]{:S(2)}) collective-permute-start(bf16[256,512]{1,0:T(8,128)(2,1)S(1)} %get-tuple-element.43), channel_id=1, source_target_pairs={{0,1},{1,2},{2,3},{3,0},{4,5},{5,6},{6,7},{7,4},{8,9},{9,10},{10,1... | collective-permute-start | bytes 786440 | tf_op jit(solution)/shard_map/ppermute | solution.py:361
  62.5 9.7 %collective-permute-start.5 = (bf16[256,512]{1,0:T(8,128)(2,1)S(1)}, bf16[256,512]{1,0:T(8,128)(2,1)S(1)}, u32[]{:S(2)}, u32[]{:S(2)}) collective-permute-start(bf16[256,512]{1,0:T(8,128)(2,1)S(1)} %get-tuple-element.44), channel_id=1, source_target_pairs={{0,3},{1,0},{2,1},{3,2},{4,7},{5,4},{6,5},{7,6},{8,11},{9,8},{10,9... | collective-permute-start | bytes 786440 | tf_op jit(solution)/shard_map/ppermute | solution.py:361
  72.3 15.5 %collective-permute-start.8 = (bf16[256,512]{1,0:T(8,128)(2,1)S(1)}, bf16[256,512]{1,0:T(8,128)(2,1)S(1)}, u32[]{:S(2)}, u32[]{:S(2)}) collective-permute-start(bf16[256,512]{1,0:T(8,128)(2,1)S(1)} %multiply_convert_fusion.agg_ref), channel_id=1, source_target_pairs={{0,2},{1,3},{2,0},{3,1},{4,6},{5,7},{6,4},{7,5},{8,10},{9,11},{10,... | collective-permute-start | bytes 786440 | tf_op jit(solution)/shard_map/ppermute | solution.py:361
  77.7 12.1 %collective-permute-start.7 = (bf16[256,512]{1,0:T(8,128)(2,1)S(1)}, bf16[256,512]{1,0:T(8,128)(2,1)S(1)}, u32[]{:S(2)}, u32[]{:S(2)}) collective-permute-start(bf16[256,512]{1,0:T(8,128)(2,1)S(1)} %multiply_convert_fusion.agg_ref), channel_id=1, source_target_pairs={{0,1},{1,2},{2,3},{3,0},{4,5},{5,6},{6,7},{7,4},{8,9},{9,10},{10,1... | collective-permute-start | bytes 786440 | tf_op jit(solution)/shard_map/ppermute | solution.py:361
  79.6 10.1 %collective-permute-start.6 = (bf16[256,512]{1,0:T(8,128)(2,1)S(1)}, bf16[256,512]{1,0:T(8,128)(2,1)S(1)}, u32[]{:S(2)}, u32[]{:S(2)}) collective-permute-start(bf16[256,512]{1,0:T(8,128)(2,1)S(1)} %multiply_convert_fusion.agg_ref), channel_id=1, source_target_pairs={{0,3},{1,0},{2,1},{3,2},{4,7},{5,4},{6,5},{7,6},{8,11},{9,8},{10,9... | collective-permute-start | bytes 786440 | tf_op jit(solution)/shard_map/ppermute | solution.py:361
  94.9 43.2 %all-to-all-start.1 = ((bf16[128,8,640]{2,1,0:T(8,128)(2,1)}), bf16[128,8,640]{2,1,0:T(8,128)(2,1)S(1)}, u32[]{:S(2)}, u32[]{:S(2)}) async-start(bf16[128,8,640]{2,1,0:T(8,128)(2,1)} %bitcast.34), calls=%async_computation.1 | async-start | bytes 2621440 | tf_op jit(solution)/shard_map/all_to_all | solution.py:502
  107.2 39.4 %copy-start.4 = (s32[1,128,8]{1,2,0:T(8,128)S(1)}, s32[1,128,8]{1,2,0:T(8,128)}, u32[]{:S(2)}) copy-start(s32[1,128,8]{1,2,0:T(8,128)} %param.12) | copy-start | bytes 12292
  139.0 21.8 %all-to-all-start.2 = ((bf16[128,8,128]{2,1,0:T(8,128)(2,1)}), bf16[128,8,128]{2,1,0:T(8,128)(2,1)S(1)}, u32[]{:S(2)}, u32[]{:S(2)}) async-start(bf16[128,8,128]{2,1,0:T(8,128)(2,1)} %bitcast.36), calls=%async_computation.2 | async-start | bytes 524288 | tf_op jit(solution)/shard_map/all_to_all | solution.py:545
  148.3 20.1 %collective-permute-start.9 = (bf16[256,512]{1,0:T(8,128)(2,1)S(1)}, bf16[256,512]{1,0:T(8,128)(2,1)S(1)}, u32[]{:S(2)}, u32[]{:S(2)}) collective-permute-start(bf16[256,512]{1,0:T(8,128)(2,1)S(1)} %get-tuple-element.63), channel_id=1, source_target_pairs={{0,2},{1,3},{2,0},{3,1},{4,6},{5,7},{6,4},{7,5},{8,10},{9,11},{10,... | collective-permute-start | bytes 786440 | tf_op jit(solution)/shard_map/ppermute | solution.py:361
  152.8 19.1 %collective-permute-start.10 = (bf16[256,512]{1,0:T(8,128)(2,1)S(1)}, bf16[256,512]{1,0:T(8,128)(2,1)S(1)}, u32[]{:S(2)}, u32[]{:S(2)}) collective-permute-start(bf16[256,512]{1,0:T(8,128)(2,1)S(1)} %get-tuple-element.64), channel_id=1, source_target_pairs={{0,1},{1,2},{2,3},{3,0},{4,5},{5,6},{6,7},{7,4},{8,9},{9,10},{10,1... | collective-permute-start | bytes 786440 | tf_op jit(solution)/shard_map/ppermute | solution.py:361
  155.8 16.0 %collective-permute-start.11 = (bf16[256,512]{1,0:T(8,128)(2,1)S(1)}, bf16[256,512]{1,0:T(8,128)(2,1)S(1)}, u32[]{:S(2)}, u32[]{:S(2)}) collective-permute-start(bf16[256,512]{1,0:T(8,128)(2,1)S(1)} %get-tuple-element.65), channel_id=1, source_target_pairs={{0,3},{1,0},{2,1},{3,2},{4,7},{5,4},{6,5},{7,6},{8,11},{9,8},{10,9... | collective-permute-start | bytes 786440 | tf_op jit(solution)/shard_map/ppermute | solution.py:361
  160.9 11.8 %collective-permute-start.14 = (bf16[256,512]{1,0:T(8,128)(2,1)S(1)}, bf16[256,512]{1,0:T(8,128)(2,1)S(1)}, u32[]{:S(2)}, u32[]{:S(2)}) collective-permute-start(bf16[256,512]{1,0:T(8,128)(2,1)S(1)} %bitcast.27), channel_id=1, source_target_pairs={{0,2},{1,3},{2,0},{3,1},{4,6},{5,7},{6,4},{7,5},{8,10},{9,11},{10,... | collective-permute-start | bytes 786440 | tf_op jit(solution)/shard_map/ppermute | solution.py:361
  165.3 11.8 %collective-permute-start.13 = (bf16[256,512]{1,0:T(8,128)(2,1)S(1)}, bf16[256,512]{1,0:T(8,128)(2,1)S(1)}, u32[]{:S(2)}, u32[]{:S(2)}) collective-permute-start(bf16[256,512]{1,0:T(8,128)(2,1)S(1)} %bitcast.28), channel_id=1, source_target_pairs={{0,1},{1,2},{2,3},{3,0},{4,5},{5,6},{6,7},{7,4},{8,9},{9,10},{10,1... | collective-permute-start | bytes 786440 | tf_op jit(solution)/shard_map/ppermute | solution.py:361
  168.4 8.7 %collective-permute-start.12 = (bf16[256,512]{1,0:T(8,128)(2,1)S(1)}, bf16[256,512]{1,0:T(8,128)(2,1)S(1)}, u32[]{:S(2)}, u32[]{:S(2)}) collective-permute-start(bf16[256,512]{1,0:T(8,128)(2,1)S(1)} %bitcast.29), channel_id=1, source_target_pairs={{0,3},{1,0},{2,1},{3,2},{4,7},{5,4},{6,5},{7,6},{8,11},{9,8},{10,9... | collective-permute-start | bytes 786440 | tf_op jit(solution)/shard_map/ppermute | solution.py:361
  (2 other events, 50.8 us)

commit v9 on v8

--- a/solution.py
+++ b/solution.py
@@ -183,13 +183,19 @@
 
 
 def own_kernel(
-    replicas, rep_ref, agg_ref, grad_ref, feats_hbm, w_self_ref, w_neigh_ref, scale_ref,
-    out_ref, base_hbm, grad_agg_ref, weights_ref, feats_ref, base_ref, sems,
+    replicas, rep_ref, agg_ref, grad_ref, grad1, grad2, grad3, feats_hbm, w_self_ref, w_neigh_ref, scale_ref,
+    out_ref, base_hbm, grad_agg_ref, weights_ref, feats_all_ref, grads_ref, feats_ref, base_ref, sems,
 ):
     quarter, feat_width = agg_ref.shape
     share = feat_width // replicas
     own_rows = pl.ds(pl.multiple_of(rep_ref[0] * quarter, quarter), quarter)
     feats_copy = started(feats_hbm.at[own_rows, :], feats_ref, sems.at[0])
+    ahead = []
+    for k, grad in ((2, grad2), (1, grad1), (3, grad3)):
+        at = pl.multiple_of(((rep_ref[0] + k) % replicas) * quarter, quarter)
+        to = pl.ds((k - 1) * quarter, quarter)
+        ahead.append(started(feats_hbm.at[pl.ds(at, quarter), :], feats_all_ref.at[to, :], sems.at[2 * k]))
+        ahead.append(started(grad, grads_ref.at[to, :], sems.at[2 * k + 1]))
     feats_copy.wait()
     out, grad_pre, grad_agg = dense_quarter(
         agg_ref[...], feats_ref[...], grad_ref[...], scale_ref[:quarter, :], w_self_ref[...],
@@ -202,34 +208,32 @@
     share_cols = pl.ds(pl.multiple_of(rep_ref[0] * share, LANES), share)
     weights_ref[:share, :] = dot(feats_ref[:, share_cols], grad_pre, 0, 0)
     weights_ref[share:, :] = dot(agg_ref[:, share_cols], grad_pre, 0, 0)
+    for copy in ahead:
+        copy.wait()
     base_copy.wait()
 
 
 def far_kernel(
-    replicas, step, rep_ref, agg_ref, grad_hbm, feats_hbm, w_self_ref, w_neigh_ref, scale_ref, before_ref,
-    grad_agg_ref, weights_ref, grad_ref, feats_ref, sems,
+    replicas, step, rep_ref, agg_ref, grads_ref, feats_ref, w_self_ref, w_neigh_ref, scale_ref, before_ref,
+    grad_agg_ref, weights_ref,
 ):
     quarter, feat_width = agg_ref.shape
     share = feat_width // replicas
-    at = pl.multiple_of(((rep_ref[0] + step) % replicas) * quarter, quarter)
-    feats_copy = started(feats_hbm.at[pl.ds(at, quarter), :], feats_ref, sems.at[0])
-    grad_copy = started(grad_hbm, grad_ref, sems.at[1])
-    feats_copy.wait()
-    grad_copy.wait()
+    at = pl.ds((step - 1) * quarter, quarter)
     _, grad_pre, grad_agg = dense_quarter(
-        agg_ref[...], feats_ref[...], grad_ref[...], scale_ref[pl.ds(step * quarter, quarter), :],
+        agg_ref[...], feats_ref[at, :], grads_ref[at, :], scale_ref[pl.ds(step * quarter, quarter), :],
         w_self_ref[...], w_neigh_ref[...],
     )
     grad_agg_ref[...] = grad_agg
     share_cols = pl.ds(pl.multiple_of(rep_ref[0] * share, LANES), share)
-    weights_ref[:share, :] = before_ref[:share, :] + dot(feats_ref[:, share_cols], grad_pre, 0, 0)
+    weights_ref[:share, :] = before_ref[:share, :] + dot(feats_ref[at, share_cols], grad_pre, 0, 0)
     weights_ref[share:, :] = before_ref[share:, :] + dot(agg_ref[:, share_cols], grad_pre, 0, 0)
 
 
 def dense_kernel(
-    replicas, rep_ref, agg1, agg3, grad1, grad3, feats_hbm, w_self_ref, w_neigh_ref, scale_ref,
+    replicas, rep_ref, agg1, agg3, grads_ref, feats_ref, w_self_ref, w_neigh_ref, scale_ref,
     halo_t_hbm, grad_agg0_ref, grad_agg2_ref, weights_ref, grad_agg_hbm, joint_hbm,
-    grad_ref, feats_ref, halo_t_ref, grad_agg_ref, joint_ref, sems,
+    halo_t_ref, grad_agg_ref, joint_ref, sems,
 ):
     aggs = {1: agg1, 3: agg3}
     quarter, feat_width = agg1.shape
@@ -237,12 +241,7 @@
     halo_rows = halo_t_ref.shape[0]
     step = min(256, halo_rows)
     starts = range(0, halo_rows, step)
-    feats_copies, grad_copies = [], []
-    for n, (k, grad) in enumerate(zip(aggs, (grad1, grad3), strict=True)):
-        at = pl.multiple_of(((rep_ref[0] + k) % replicas) * quarter, quarter)
-        feats_copies.append(started(feats_hbm.at[pl.ds(at, quarter), :], feats_ref.at[n], sems.at[n]))
-        grad_copies.append(started(grad, grad_ref.at[n], sems.at[2 + n]))
-    at = 4
+    at = 0
     halo_copies = [
         started(halo_t_hbm.at[pl.ds(i, step), :], halo_t_ref.at[pl.ds(i, step), :], sems.at[at + n])
         for n, i in enumerate(starts)
@@ -253,16 +252,15 @@
     grad_neigh = weights_ref[share:, :]
     grad_agg_ref[:quarter, :] = grad_agg0_ref[...]
     grad_agg_ref[pl.ds(2 * quarter, quarter), :] = grad_agg2_ref[...]
-    for n, (k, agg_ref) in enumerate(aggs.items()):
+    for k, agg_ref in aggs.items():
         rows = pl.ds(k * quarter, quarter)
-        feats_copies[n].wait()
-        grad_copies[n].wait()
+        past = pl.ds((k - 1) * quarter, quarter)
         _, grad_pre, grad_agg = dense_quarter(
-            agg_ref[...], feats_ref[n], grad_ref[n], scale_ref[rows, :], w_self_ref[...],
+            agg_ref[...], feats_ref[past, :], grads_ref[past, :], scale_ref[rows, :], w_self_ref[...],
             w_neigh_ref[...],
         )
         grad_agg_ref[rows, :] = grad_agg
-        grad_self = grad_self + dot(feats_ref[n, :, share_cols], grad_pre, 0, 0)
+        grad_self = grad_self + dot(feats_ref[past, share_cols], grad_pre, 0, 0)
         grad_neigh = grad_neigh + dot(agg_ref[:, share_cols], grad_pre, 0, 0)
     grad_agg_copy = started(grad_agg_ref, grad_agg_hbm, sems.at[at])
     tile = 0
@@ -451,7 +449,7 @@
     aggs = from_ahead(own_agg, replicas)
     joint_width = feat_width + 2 * share * feat_width // halo_rows
     halo_steps = max(1, halo_rows // 256)
-    out_feats, own_base, own_grad_agg, own_weights = call(
+    out_feats, own_base, own_grad_agg, own_weights, feats_ahead, grads_ahead = call(
         functools.partial(own_kernel, replicas),
         "dense_own",
         [
@@ -459,44 +457,43 @@
             shape(quarter, feat_width, F32),
             shape(quarter, feat_width, BF16),
             shape(2 * share, feat_width, F32),
-        ],
-        [SMEM, VMEM, VMEM, HBM, VMEM, VMEM, VMEM],
-        (rep_ref, own_agg, grad_outs[0], node_feats, w_self, w_neigh, scale),
+            shape(node_rows - quarter, feat_width, BF16),
+            shape(node_rows - quarter, feat_width, BF16),
+        ],
+        [SMEM, VMEM, VMEM, HBM, HBM, HBM, HBM, VMEM, VMEM, VMEM],
+        (rep_ref, own_agg, *grad_outs, node_feats, w_self, w_neigh, scale),
         block_flops // 2,
-        out_specs=[VMEM, HBM, VMEM, VMEM],
+        out_specs=[VMEM, HBM, VMEM, VMEM, VMEM, VMEM],
         scratch=[
             pltpu.VMEM((quarter, feat_width), BF16),
             pltpu.VMEM((quarter, feat_width), F32),
-            pltpu.SemaphoreType.DMA((2,)),
+            pltpu.SemaphoreType.DMA((2 * replicas,)),
         ],
     )
     far_grad_agg, far_weights = call(
         functools.partial(far_kernel, replicas, 2),
         "dense_far",
         [shape(quarter, feat_width, BF16), shape(2 * share, feat_width, F32)],
-        [SMEM, VMEM, HBM, HBM, VMEM, VMEM, VMEM, VMEM],
-        (rep_ref, aggs[1], grad_outs[2], node_feats, w_self, w_neigh, scale, own_weights),
+        [SMEM] + [VMEM] * 7,
+        (rep_ref, aggs[1], grads_ahead, feats_ahead, w_self, w_neigh, scale, own_weights),
         block_flops // 2,
-        scratch=[pltpu.VMEM((quarter, feat_width), BF16)] * 2 + [pltpu.SemaphoreType.DMA((2,))],
     )
     grad_agg, joint = call(
         functools.partial(dense_kernel, replicas),
         "dense_rest",
         [shape(node_rows, feat_width, BF16), shape(halo_rows, joint_width, BF16)],
-        [SMEM] + [VMEM] * 2 + [HBM] * 3 + [VMEM] * 3 + [HBM] + [VMEM] * 3,
+        [SMEM] + [VMEM] * 7 + [HBM] + [VMEM] * 3,
         (
-            rep_ref, aggs[0], aggs[2], grad_outs[1], grad_outs[3], node_feats, w_self, w_neigh, scale, halo_t,
+            rep_ref, aggs[0], aggs[2], grads_ahead, feats_ahead, w_self, w_neigh, scale, halo_t,
             own_grad_agg, far_grad_agg, far_weights,
         ),
         2 * block_flops,
         out_specs=[HBM, HBM],
         scratch=[
-            pltpu.VMEM((2, quarter, feat_width), BF16),
-            pltpu.VMEM((2, quarter, feat_width), BF16),
             pltpu.VMEM((halo_rows, node_rows), BF16),
             pltpu.VMEM((node_rows, feat_width), BF16),
             pltpu.VMEM((halo_rows, joint_width), BF16),
-            pltpu.SemaphoreType.DMA((5 + 2 * halo_steps,)),
+            pltpu.SemaphoreType.DMA((1 + 2 * halo_steps,)),
         ],
     )
     returned = lax.all_to_all(joint, WIDE, 0, 0, tiled=True)

time: 180 us -> 179 us (level)
  no operation moved by 1% of the time
where the time goes in v9:
time: 179 us; the launch traced here: 178 us
  starting transfers between devices  88.7 us (50%)
  waiting for transfers between devices  53.4 us (30%)
  Pallas kernels  33.1 us (18%)
    ppermute x15, starting transfers between devices, send_to(): lax.ppermute(x, 'rep', [(i, (i + step) % replicas) for i in range(replica...  55.2 us
    pallas_call x10, Pallas kernels, call(): pl.pallas_call(kernel, out_shape=outs, in_specs=in_specs, out_specs=out_s...  33.1 us
    all_to_all x1, waiting for transfers between devices, on_device(): returned = lax.all_to_all(joint, WIDE, 0, 0, tiled=True)  30.9 us
    all_to_all x1, starting transfers between devices, on_device(): incoming = lax.all_to_all(outgoing, WIDE, 0, 0, tiled=True)  18.4 us
    ppermute x15, waiting for transfers between devices, send_to(): lax.ppermute(x, 'rep', [(i, (i + step) % replicas) for i in range(replica...  10.7 us
    all_to_all x1, waiting for transfers between devices, on_device(): incoming = lax.all_to_all(outgoing, WIDE, 0, 0, tiled=True)  10.3 us
    all_to_all x1, starting transfers between devices, on_device(): tiles = lax.all_to_all(copies, WIDE, 0, 0, tiled=True)  7.61 us
    all_to_all x1, starting transfers between devices, on_device(): returned = lax.all_to_all(joint, WIDE, 0, 0, tiled=True)  7.49 us
  transfers between devices with their start and end apart: 18, of which 6 were waited for; matrix products, arithmetic and copies ran while one was open for 1% of the time, Pallas kernels for 12%

profile of v9, /device:TPU:1, one launch (start us, length us, event | category | flops | bytes accessed | tf_op | source)
XLA Modules:
  0.0 177.7 jit_solution(3862157558445959041)
XLA Ops:
  0.7 3.4 %gather_rows.1 = bf16[1024,512]{1,0:T(8,128)(2,1)} custom-call(s32[8,128]{1,0:T(8,128)} %bitcast.32, bf16[1024,512]{1,0:T(8,128)(2,1)} %feats_hbm.5), custom_call_target="tpu_custom_call" | custom-call | flops 1073741824 | bytes 2101248 | tf_op jit(solution)/shard_map/gather_rows/pallas_call | solution.py:40
  4.1 18.4 %all-to-all-start = ((bf16[128,8,512]{2,1,0:T(8,128)(2,1)}), bf16[128,8,512]{2,1,0:T(8,128)(2,1)S(1)}, u32[]{:S(2)}, u32[]{:S(2)}) async-start(bf16[128,8,512]{2,1,0:T(8,128)(2,1)} %bitcast.35), calls=%async_computation | async-start | bytes 2097152 | tf_op jit(solution)/shard_map/all_to_all | solution.py:401
  22.5 4.7 %collective-permute-start.1 = (bf16[256,512]{1,0:T(8,128)(2,1)S(1)}, bf16[256,512]{1,0:T(8,128)(2,1)}, u32[]{:S(2)}, u32[]{:S(2)}) collective-permute-start(bf16[256,512]{1,0:T(8,128)(2,1)S(1)} %copy-done.2), channel_id=1, source_target_pairs={{0,2},{1,3},{2,0},{3,1},{4,6},{5,7},{6,4},{7,5},{8,10},{9,11},{10,... | collective-permute-start | bytes 786440 | tf_op jit(solution)/shard_map/ppermute | solution.py:359
  27.2 2.8 %collective-permute-start = (bf16[256,512]{1,0:T(8,128)(2,1)S(1)}, bf16[256,512]{1,0:T(8,128)(2,1)}, u32[]{:S(2)}, u32[]{:S(2)}) collective-permute-start(bf16[256,512]{1,0:T(8,128)(2,1)S(1)} %copy-done.2), channel_id=1, source_target_pairs={{0,3},{1,0},{2,1},{3,2},{4,7},{5,4},{6,5},{7,6},{8,11},{9,8},{10,9... | collective-permute-start | bytes 786440 | tf_op jit(solution)/shard_map/ppermute | solution.py:359
  32.6 10.0 %tile_counts.1 = (bf16[1024,1024]{1,0:T(8,128)(2,1)}, bf16[1024,1024]{1,0:T(8,128)(2,1)S(1)}, bf16[1024,1024]{1,0:T(8,128)(2,1)}, f32[1024,512]{1,0:T(8,128)}) custom-call(s32[1]{0:T(128)} %bitcast.rep_ref, s32[128]{0:T(128)S(1)} %fusion.2.place_ref, s32[256,128]{1,0:T(8,128)S(1)} %bitcast.31, bf16[1024,512]{1,0:T(8,128)(2,1)} %feats_hbm.5), custom_call_target="tpu_custom_call" | custom-call | flops 1094713344 | bytes 9568772 | tf_op jit(solution)/shard_map/tile_counts/pallas_call | solution.py:40
  42.7 10.3 %all-to-all-done = bf16[128,8,512]{2,1,0:T(8,128)(2,1)S(1)} async-done(((bf16[128,8,512]{2,1,0:T(8,128)(2,1)}), bf16[128,8,512]{2,1,0:T(8,128)(2,1)S(1)}, u32[]{:S(2)}, u32[]{:S(2)}) %all-to-all-start) | async-done | bytes 1048608 | tf_op jit(solution)/shard_map/all_to_all | solution.py:401
  55.5 4.8 %collective-permute-start.3 = (bf16[256,512]{1,0:T(8,128)(2,1)S(1)}, bf16[256,512]{1,0:T(8,128)(2,1)S(1)}, u32[]{:S(2)}, u32[]{:S(2)}) collective-permute-start(bf16[256,512]{1,0:T(8,128)(2,1)S(1)} %get-tuple-element.44), channel_id=1, source_target_pairs={{0,2},{1,3},{2,0},{3,1},{4,6},{5,7},{6,4},{7,5},{8,10},{9,11},{10,... | collective-permute-start | bytes 786440 | tf_op jit(solution)/shard_map/ppermute | solution.py:359
  62.5 4.3 %collective-permute-start.5 = (bf16[256,512]{1,0:T(8,128)(2,1)S(1)}, bf16[256,512]{1,0:T(8,128)(2,1)S(1)}, u32[]{:S(2)}, u32[]{:S(2)}) collective-permute-start(bf16[256,512]{1,0:T(8,128)(2,1)S(1)} %get-tuple-element.46), channel_id=1, source_target_pairs={{0,3},{1,0},{2,1},{3,2},{4,7},{5,4},{6,5},{7,6},{8,11},{9,8},{10,9... | collective-permute-start | bytes 786440 | tf_op jit(solution)/shard_map/ppermute | solution.py:359
  66.8 5.4 %collective-permute-done.4 = bf16[256,512]{1,0:T(8,128)(2,1)S(1)} collective-permute-done((bf16[256,512]{1,0:T(8,128)(2,1)S(1)}, bf16[256,512]{1,0:T(8,128)(2,1)S(1)}, u32[]{:S(2)}, u32[]{:S(2)}) %collective-permute-start.4) | collective-permute-done | bytes 262176 | tf_op jit(solution)/shard_map/ppermute | solution.py:359
  72.3 5.4 %collective-permute-start.8 = (bf16[256,512]{1,0:T(8,128)(2,1)S(1)}, bf16[256,512]{1,0:T(8,128)(2,1)S(1)}, u32[]{:S(2)}, u32[]{:S(2)}) collective-permute-start(bf16[256,512]{1,0:T(8,128)(2,1)S(1)} %multiply_convert_fusion.agg_ref), channel_id=1, source_target_pairs={{0,2},{1,3},{2,0},{3,1},{4,6},{5,7},{6,4},{7,5},{8,10},{9,11},{10,... | collective-permute-start | bytes 786440 | tf_op jit(solution)/shard_map/ppermute | solution.py:359
  79.6 4.6 %collective-permute-start.6 = (bf16[256,512]{1,0:T(8,128)(2,1)S(1)}, bf16[256,512]{1,0:T(8,128)(2,1)S(1)}, u32[]{:S(2)}, u32[]{:S(2)}) collective-permute-start(bf16[256,512]{1,0:T(8,128)(2,1)S(1)} %multiply_convert_fusion.agg_ref), channel_id=1, source_target_pairs={{0,3},{1,0},{2,1},{3,2},{4,7},{5,4},{6,5},{7,6},{8,11},{9,8},{10,9... | collective-permute-start | bytes 786440 | tf_op jit(solution)/shard_map/ppermute | solution.py:359
  84.5 3.4 %dense_own.1 = (bf16[256,512]{1,0:T(8,128)(2,1)}, f32[256,512]{1,0:T(8,128)}, bf16[256,512]{1,0:T(8,128)(2,1)S(1)}, f32[256,512]{1,0:T(8,128)S(1)}, bf16[768,512...) custom-call(s32[1]{0:T(128)} %bitcast.rep_ref, bf16[256,512]{1,0:T(8,128)(2,1)S(1)} %multiply_convert_fusion.agg_ref, ...), custom_call_target="tpu_custom_call" | custom-call | flops 536870912 | bytes 6557700 | tf_op jit(solution)/shard_map/dense_own/pallas_call | solution.py:40
  89.8 4.8 %dense_rest.1 = (bf16[1024,512]{1,0:T(8,128)(2,1)}, bf16[1024,640]{1,0:T(8,128)(2,1)}) custom-call(s32[1]{0:T(128)} %bitcast.rep_ref, bf16[256,512]{1,0:T(8,128)(2,1)S(1)} %collective-permute-done.6.agg1, bf16[256,512]{1,0:T(8,128)(2,1)S(1)} %collective-permute-done.7.agg3, bf16[768,512]{1,0:T(8,128)(2,1)S(1)} %get-tuple-element.53.grads_ref, ...), custom_call_target="tpu_custom_call" | custom-call | flops 2147483648 | bytes 8654852 | tf_op jit(solution)/shard_map/dense_rest/pallas_call | solution.py:40
  94.6 7.5 %all-to-all-start.1 = ((bf16[128,8,640]{2,1,0:T(8,128)(2,1)}), bf16[128,8,640]{2,1,0:T(8,128)(2,1)S(1)}, u32[]{:S(2)}, u32[]{:S(2)}) async-start(bf16[128,8,640]{2,1,0:T(8,128)(2,1)} %bitcast.34), calls=%async_computation.1 | async-start | bytes 2621440 | tf_op jit(solution)/shard_map/all_to_all | solution.py:499
  102.1 4.6 %local_rows.1.local_hbm = f32[1024,512]{1,0:T(8,128)} custom-call(bf16[1024,1024]{1,0:T(8,128)(2,1)} %get-tuple-element.61.counts_hbm, bf16[1024,512]{1,0:T(8,128)(2,1)} %get-tuple-element.62.grad_hbm, f32[256,512]{1,0:T(8,128)} %get-tuple-element.63.base_hbm), custom_call_target="tpu_custom_call" | custom-call | flops 1073741824 | bytes 5767168 | tf_op jit(solution)/shard_map/local_rows/pallas_call | solution.py:40
  106.7 30.9 %all-to-all-done.1 = bf16[128,8,640]{2,1,0:T(8,128)(2,1)S(1)} async-done(((bf16[128,8,640]{2,1,0:T(8,128)(2,1)}), bf16[128,8,640]{2,1,0:T(8,128)(2,1)S(1)}, u32[]{:S(2)}, u32[]{:S(2)}) %all-to-all-start.1) | async-done | bytes 1310752 | tf_op jit(solution)/shard_map/all_to_all | solution.py:499
  138.5 7.6 %all-to-all-start.2 = ((bf16[128,8,128]{2,1,0:T(8,128)(2,1)}), bf16[128,8,128]{2,1,0:T(8,128)(2,1)S(1)}, u32[]{:S(2)}, u32[]{:S(2)}) async-start(bf16[128,8,128]{2,1,0:T(8,128)(2,1)} %bitcast.36), calls=%async_computation.2 | async-start | bytes 524288 | tf_op jit(solution)/shard_map/all_to_all | solution.py:542
  147.8 4.6 %collective-permute-start.9 = (bf16[256,512]{1,0:T(8,128)(2,1)S(1)}, bf16[256,512]{1,0:T(8,128)(2,1)S(1)}, u32[]{:S(2)}, u32[]{:S(2)}) collective-permute-start(bf16[256,512]{1,0:T(8,128)(2,1)S(1)} %get-tuple-element.67), channel_id=1, source_target_pairs={{0,2},{1,3},{2,0},{3,1},{4,6},{5,7},{6,4},{7,5},{8,10},{9,11},{10,... | collective-permute-start | bytes 786440 | tf_op jit(solution)/shard_map/ppermute | solution.py:359
  152.4 3.1 %collective-permute-start.10 = (bf16[256,512]{1,0:T(8,128)(2,1)S(1)}, bf16[256,512]{1,0:T(8,128)(2,1)S(1)}, u32[]{:S(2)}, u32[]{:S(2)}) collective-permute-start(bf16[256,512]{1,0:T(8,128)(2,1)S(1)} %get-tuple-element.68), channel_id=1, source_target_pairs={{0,1},{1,2},{2,3},{3,0},{4,5},{5,6},{6,7},{7,4},{8,9},{9,10},{10,1... | collective-permute-start | bytes 786440 | tf_op jit(solution)/shard_map/ppermute | solution.py:359
  155.5 3.4 %collective-permute-start.11 = (bf16[256,512]{1,0:T(8,128)(2,1)S(1)}, bf16[256,512]{1,0:T(8,128)(2,1)S(1)}, u32[]{:S(2)}, u32[]{:S(2)}) collective-permute-start(bf16[256,512]{1,0:T(8,128)(2,1)S(1)} %get-tuple-element.69), channel_id=1, source_target_pairs={{0,3},{1,0},{2,1},{3,2},{4,7},{5,4},{6,5},{7,6},{8,11},{9,8},{10,9... | collective-permute-start | bytes 786440 | tf_op jit(solution)/shard_map/ppermute | solution.py:359
  160.4 4.6 %collective-permute-start.14 = (bf16[256,512]{1,0:T(8,128)(2,1)S(1)}, bf16[256,512]{1,0:T(8,128)(2,1)S(1)}, u32[]{:S(2)}, u32[]{:S(2)}) collective-permute-start(bf16[256,512]{1,0:T(8,128)(2,1)S(1)} %bitcast.27), channel_id=1, source_target_pairs={{0,2},{1,3},{2,0},{3,1},{4,6},{5,7},{6,4},{7,5},{8,10},{9,11},{10,... | collective-permute-start | bytes 786440 | tf_op jit(solution)/shard_map/ppermute | solution.py:359
  164.9 3.1 %collective-permute-start.13 = (bf16[256,512]{1,0:T(8,128)(2,1)S(1)}, bf16[256,512]{1,0:T(8,128)(2,1)S(1)}, u32[]{:S(2)}, u32[]{:S(2)}) collective-permute-start(bf16[256,512]{1,0:T(8,128)(2,1)S(1)} %bitcast.28), channel_id=1, source_target_pairs={{0,1},{1,2},{2,3},{3,0},{4,5},{5,6},{6,7},{7,4},{8,9},{9,10},{10,1... | collective-permute-start | bytes 786440 | tf_op jit(solution)/shard_map/ppermute | solution.py:359
  168.0 3.4 %collective-permute-start.12 = (bf16[256,512]{1,0:T(8,128)(2,1)S(1)}, bf16[256,512]{1,0:T(8,128)(2,1)S(1)}, u32[]{:S(2)}, u32[]{:S(2)}) collective-permute-start(bf16[256,512]{1,0:T(8,128)(2,1)S(1)} %bitcast.29), channel_id=1, source_target_pairs={{0,3},{1,0},{2,1},{3,2},{4,7},{5,4},{6,5},{7,6},{8,11},{9,8},{10,9... | collective-permute-start | bytes 786440 | tf_op jit(solution)/shard_map/ppermute | solution.py:359
  172.3 4.3 %collective-permute-done.13.part3 = bf16[256,512]{1,0:T(8,128)(2,1)S(1)} collective-permute-done((bf16[256,512]{1,0:T(8,128)(2,1)S(1)}, bf16[256,512]{1,0:T(8,128)(2,1)S(1)}, u32[]{:S(2)}, u32[]{:S(2)}) %collective-permute-start.13) | collective-permute-done | bytes 262176 | tf_op jit(solution)/shard_map/ppermute | solution.py:359
  (45 shorter events, 17.5 us)
Async XLA Ops:
  0.6 31.8 %copy-start.5 = (s32[1024]{0:T(1024)S(1)}, s32[1024]{0:T(1024)}, u32[]{:S(2)}) copy-start(s32[1024]{0:T(1024)} %param.16) | copy-start | bytes 12292
  0.7 31.8 %copy-start.6 = (s32[1,1,128]{2,1,0:T(1,128)S(1)}, s32[1,1,128]{2,1,0:T(1,128)}, u32[]{:S(2)}) copy-start(s32[1,1,128]{2,1,0:T(1,128)} %param.14) | copy-start | bytes 1540
  0.7 31.8 %copy-start.7 = (s32[1,1,128]{2,1,0:T(1,128)S(1)}, s32[1,1,128]{2,1,0:T(1,128)}, u32[]{:S(2)}) copy-start(s32[1,1,128]{2,1,0:T(1,128)} %param.13) | copy-start | bytes 1540
  0.7 31.9 %copy-start.3 = (s32[1,1,32768]{2,1,0:T(1,128)S(1)}, s32[1,1,32768]{2,1,0:T(1,128)}, u32[]{:S(2)}) copy-start(s32[1,1,32768]{2,1,0:T(1,128)} %param.15) | copy-start | bytes 393220
  4.1 48.9 %all-to-all-start = ((bf16[128,8,512]{2,1,0:T(8,128)(2,1)}), bf16[128,8,512]{2,1,0:T(8,128)(2,1)S(1)}, u32[]{:S(2)}, u32[]{:S(2)}) async-start(bf16[128,8,512]{2,1,0:T(8,128)(2,1)} %bitcast.35), calls=%async_computation | async-start | bytes 2097152 | tf_op jit(solution)/shard_map/all_to_all | solution.py:401
  22.5 20.2 %collective-permute-start.1 = (bf16[256,512]{1,0:T(8,128)(2,1)S(1)}, bf16[256,512]{1,0:T(8,128)(2,1)}, u32[]{:S(2)}, u32[]{:S(2)}) collective-permute-start(bf16[256,512]{1,0:T(8,128)(2,1)S(1)} %copy-done.2), channel_id=1, source_target_pairs={{0,2},{1,3},{2,0},{3,1},{4,6},{5,7},{6,4},{7,5},{8,10},{9,11},{10,... | collective-permute-start | bytes 786440 | tf_op jit(solution)/shard_map/ppermute | solution.py:359
  27.2 15.5 %collective-permute-start = (bf16[256,512]{1,0:T(8,128)(2,1)S(1)}, bf16[256,512]{1,0:T(8,128)(2,1)}, u32[]{:S(2)}, u32[]{:S(2)}) collective-permute-start(bf16[256,512]{1,0:T(8,128)(2,1)S(1)} %copy-done.2), channel_id=1, source_target_pairs={{0,3},{1,0},{2,1},{3,2},{4,7},{5,4},{6,5},{7,6},{8,11},{9,8},{10,9... | collective-permute-start | bytes 786440 | tf_op jit(solution)/shard_map/ppermute | solution.py:359
  29.9 12.7 %collective-permute-start.2 = (bf16[256,512]{1,0:T(8,128)(2,1)S(1)}, bf16[256,512]{1,0:T(8,128)(2,1)}, u32[]{:S(2)}, u32[]{:S(2)}) collective-permute-start(bf16[256,512]{1,0:T(8,128)(2,1)S(1)} %copy-done.2), channel_id=1, source_target_pairs={{0,1},{1,2},{2,3},{3,0},{4,5},{5,6},{6,7},{7,4},{8,9},{9,10},{10,1... | collective-permute-start | bytes 786440 | tf_op jit(solution)/shard_map/ppermute | solution.py:359
  55.5 28.9 %copy-start = (bf16[512,512]{1,0:T(8,128)(2,1)S(1)}, bf16[512,512]{1,0:T(8,128)(2,1)}, u32[]{:S(2)}) copy-start(bf16[512,512]{1,0:T(8,128)(2,1)} %w_self_ref.5) | copy-start | bytes 1572868
  55.5 11.3 %collective-permute-start.3 = (bf16[256,512]{1,0:T(8,128)(2,1)S(1)}, bf16[256,512]{1,0:T(8,128)(2,1)S(1)}, u32[]{:S(2)}, u32[]{:S(2)}) collective-permute-start(bf16[256,512]{1,0:T(8,128)(2,1)S(1)} %get-tuple-element.44), channel_id=1, source_target_pairs={{0,2},{1,3},{2,0},{3,1},{4,6},{5,7},{6,4},{7,5},{8,10},{9,11},{10,... | collective-permute-start | bytes 786440 | tf_op jit(solution)/shard_map/ppermute | solution.py:359
  60.3 11.9 %collective-permute-start.4 = (bf16[256,512]{1,0:T(8,128)(2,1)S(1)}, bf16[256,512]{1,0:T(8,128)(2,1)S(1)}, u32[]{:S(2)}, u32[]{:S(2)}) collective-permute-start(bf16[256,512]{1,0:T(8,128)(2,1)S(1)} %get-tuple-element.45), channel_id=1, source_target_pairs={{0,1},{1,2},{2,3},{3,0},{4,5},{5,6},{6,7},{7,4},{8,9},{9,10},{10,1... | collective-permute-start | bytes 786440 | tf_op jit(solution)/shard_map/ppermute | solution.py:359
  62.5 9.7 %collective-permute-start.5 = (bf16[256,512]{1,0:T(8,128)(2,1)S(1)}, bf16[256,512]{1,0:T(8,128)(2,1)S(1)}, u32[]{:S(2)}, u32[]{:S(2)}) collective-permute-start(bf16[256,512]{1,0:T(8,128)(2,1)S(1)} %get-tuple-element.46), channel_id=1, source_target_pairs={{0,3},{1,0},{2,1},{3,2},{4,7},{5,4},{6,5},{7,6},{8,11},{9,8},{10,9... | collective-permute-start | bytes 786440 | tf_op jit(solution)/shard_map/ppermute | solution.py:359
  72.3 15.5 %collective-permute-start.8 = (bf16[256,512]{1,0:T(8,128)(2,1)S(1)}, bf16[256,512]{1,0:T(8,128)(2,1)S(1)}, u32[]{:S(2)}, u32[]{:S(2)}) collective-permute-start(bf16[256,512]{1,0:T(8,128)(2,1)S(1)} %multiply_convert_fusion.agg_ref), channel_id=1, source_target_pairs={{0,2},{1,3},{2,0},{3,1},{4,6},{5,7},{6,4},{7,5},{8,10},{9,11},{10,... | collective-permute-start | bytes 786440 | tf_op jit(solution)/shard_map/ppermute | solution.py:359
  77.7 12.1 %collective-permute-start.7 = (bf16[256,512]{1,0:T(8,128)(2,1)S(1)}, bf16[256,512]{1,0:T(8,128)(2,1)S(1)}, u32[]{:S(2)}, u32[]{:S(2)}) collective-permute-start(bf16[256,512]{1,0:T(8,128)(2,1)S(1)} %multiply_convert_fusion.agg_ref), channel_id=1, source_target_pairs={{0,1},{1,2},{2,3},{3,0},{4,5},{5,6},{6,7},{7,4},{8,9},{9,10},{10,1... | collective-permute-start | bytes 786440 | tf_op jit(solution)/shard_map/ppermute | solution.py:359
  79.6 10.1 %collective-permute-start.6 = (bf16[256,512]{1,0:T(8,128)(2,1)S(1)}, bf16[256,512]{1,0:T(8,128)(2,1)S(1)}, u32[]{:S(2)}, u32[]{:S(2)}) collective-permute-start(bf16[256,512]{1,0:T(8,128)(2,1)S(1)} %multiply_convert_fusion.agg_ref), channel_id=1, source_target_pairs={{0,3},{1,0},{2,1},{3,2},{4,7},{5,4},{6,5},{7,6},{8,11},{9,8},{10,9... | collective-permute-start | bytes 786440 | tf_op jit(solution)/shard_map/ppermute | solution.py:359
  94.6 43.1 %all-to-all-start.1 = ((bf16[128,8,640]{2,1,0:T(8,128)(2,1)}), bf16[128,8,640]{2,1,0:T(8,128)(2,1)S(1)}, u32[]{:S(2)}, u32[]{:S(2)}) async-start(bf16[128,8,640]{2,1,0:T(8,128)(2,1)} %bitcast.34), calls=%async_computation.1 | async-start | bytes 2621440 | tf_op jit(solution)/shard_map/all_to_all | solution.py:499
  106.7 39.4 %copy-start.4 = (s32[1,128,8]{1,2,0:T(8,128)S(1)}, s32[1,128,8]{1,2,0:T(8,128)}, u32[]{:S(2)}) copy-start(s32[1,128,8]{1,2,0:T(8,128)} %param.12) | copy-start | bytes 12292
  138.5 21.8 %all-to-all-start.2 = ((bf16[128,8,128]{2,1,0:T(8,128)(2,1)}), bf16[128,8,128]{2,1,0:T(8,128)(2,1)S(1)}, u32[]{:S(2)}, u32[]{:S(2)}) async-start(bf16[128,8,128]{2,1,0:T(8,128)(2,1)} %bitcast.36), calls=%async_computation.2 | async-start | bytes 524288 | tf_op jit(solution)/shard_map/all_to_all | solution.py:542
  147.8 20.2 %collective-permute-start.9 = (bf16[256,512]{1,0:T(8,128)(2,1)S(1)}, bf16[256,512]{1,0:T(8,128)(2,1)S(1)}, u32[]{:S(2)}, u32[]{:S(2)}) collective-permute-start(bf16[256,512]{1,0:T(8,128)(2,1)S(1)} %get-tuple-element.67), channel_id=1, source_target_pairs={{0,2},{1,3},{2,0},{3,1},{4,6},{5,7},{6,4},{7,5},{8,10},{9,11},{10,... | collective-permute-start | bytes 786440 | tf_op jit(solution)/shard_map/ppermute | solution.py:359
  152.4 19.1 %collective-permute-start.10 = (bf16[256,512]{1,0:T(8,128)(2,1)S(1)}, bf16[256,512]{1,0:T(8,128)(2,1)S(1)}, u32[]{:S(2)}, u32[]{:S(2)}) collective-permute-start(bf16[256,512]{1,0:T(8,128)(2,1)S(1)} %get-tuple-element.68), channel_id=1, source_target_pairs={{0,1},{1,2},{2,3},{3,0},{4,5},{5,6},{6,7},{7,4},{8,9},{9,10},{10,1... | collective-permute-start | bytes 786440 | tf_op jit(solution)/shard_map/ppermute | solution.py:359
  155.5 16.0 %collective-permute-start.11 = (bf16[256,512]{1,0:T(8,128)(2,1)S(1)}, bf16[256,512]{1,0:T(8,128)(2,1)S(1)}, u32[]{:S(2)}, u32[]{:S(2)}) collective-permute-start(bf16[256,512]{1,0:T(8,128)(2,1)S(1)} %get-tuple-element.69), channel_id=1, source_target_pairs={{0,3},{1,0},{2,1},{3,2},{4,7},{5,4},{6,5},{7,6},{8,11},{9,8},{10,9... | collective-permute-start | bytes 786440 | tf_op jit(solution)/shard_map/ppermute | solution.py:359
  160.4 12.0 %collective-permute-start.14 = (bf16[256,512]{1,0:T(8,128)(2,1)S(1)}, bf16[256,512]{1,0:T(8,128)(2,1)S(1)}, u32[]{:S(2)}, u32[]{:S(2)}) collective-permute-start(bf16[256,512]{1,0:T(8,128)(2,1)S(1)} %bitcast.27), channel_id=1, source_target_pairs={{0,2},{1,3},{2,0},{3,1},{4,6},{5,7},{6,4},{7,5},{8,10},{9,11},{10,... | collective-permute-start | bytes 786440 | tf_op jit(solution)/shard_map/ppermute | solution.py:359
  164.9 11.7 %collective-permute-start.13 = (bf16[256,512]{1,0:T(8,128)(2,1)S(1)}, bf16[256,512]{1,0:T(8,128)(2,1)S(1)}, u32[]{:S(2)}, u32[]{:S(2)}) collective-permute-start(bf16[256,512]{1,0:T(8,128)(2,1)S(1)} %bitcast.28), channel_id=1, source_target_pairs={{0,1},{1,2},{2,3},{3,0},{4,5},{5,6},{6,7},{7,4},{8,9},{9,10},{10,1... | collective-permute-start | bytes 786440 | tf_op jit(solution)/shard_map/ppermute | solution.py:359
  168.0 8.6 %collective-permute-start.12 = (bf16[256,512]{1,0:T(8,128)(2,1)S(1)}, bf16[256,512]{1,0:T(8,128)(2,1)S(1)}, u32[]{:S(2)}, u32[]{:S(2)}) collective-permute-start(bf16[256,512]{1,0:T(8,128)(2,1)S(1)} %bitcast.29), channel_id=1, source_target_pairs={{0,3},{1,0},{2,1},{3,2},{4,7},{5,4},{6,5},{7,6},{8,11},{9,8},{10,9... | collective-permute-start | bytes 786440 | tf_op jit(solution)/shard_map/ppermute | solution.py:359
  (2 other events, 50.8 us)

commit v10 on v9

--- a/solution.py
+++ b/solution.py
@@ -184,7 +184,7 @@
 
 def own_kernel(
     replicas, rep_ref, agg_ref, grad_ref, grad1, grad2, grad3, feats_hbm, w_self_ref, w_neigh_ref, scale_ref,
-    out_ref, base_hbm, grad_agg_ref, weights_ref, feats_all_ref, grads_ref, feats_ref, base_ref, sems,
+    halo_t_hbm, out_ref, base_hbm, grad_agg_ref, weights_ref, feats_all_ref, grads_ref, halo_t_ref, feats_ref, base_ref, sems,
 ):
     quarter, feat_width = agg_ref.shape
     share = feat_width // replicas
@@ -196,6 +196,7 @@
         to = pl.ds((k - 1) * quarter, quarter)
         ahead.append(started(feats_hbm.at[pl.ds(at, quarter), :], feats_all_ref.at[to, :], sems.at[2 * k]))
         ahead.append(started(grad, grads_ref.at[to, :], sems.at[2 * k + 1]))
+    ahead.append(started(halo_t_hbm, halo_t_ref, sems.at[2 * replicas]))
     feats_copy.wait()
     out, grad_pre, grad_agg = dense_quarter(
         agg_ref[...], feats_ref[...], grad_ref[...], scale_ref[:quarter, :], w_self_ref[...],
@@ -232,8 +233,8 @@
 
 def dense_kernel(
     replicas, rep_ref, agg1, agg3, grads_ref, feats_ref, w_self_ref, w_neigh_ref, scale_ref,
-    halo_t_hbm, grad_agg0_ref, grad_agg2_ref, weights_ref, grad_agg_hbm, joint_hbm,
-    halo_t_ref, grad_agg_ref, joint_ref, sems,
+    halo_t_ref, grad_agg0_ref, grad_agg2_ref, weights_ref, grad_agg_hbm, joint_hbm,
+    grad_agg_ref, joint_ref, sems,
 ):
     aggs = {1: agg1, 3: agg3}
     quarter, feat_width = agg1.shape
@@ -241,12 +242,6 @@
     halo_rows = halo_t_ref.shape[0]
     step = min(256, halo_rows)
     starts = range(0, halo_rows, step)
-    at = 0
-    halo_copies = [
-        started(halo_t_hbm.at[pl.ds(i, step), :], halo_t_ref.at[pl.ds(i, step), :], sems.at[at + n])
-        for n, i in enumerate(starts)
-    ]
-    at += len(starts)
     share_cols = pl.ds(pl.multiple_of(rep_ref[0] * share, LANES), share)
     grad_self = weights_ref[:share, :]
     grad_neigh = weights_ref[share:, :]
@@ -262,7 +257,7 @@
         grad_agg_ref[rows, :] = grad_agg
         grad_self = grad_self + dot(feats_ref[past, share_cols], grad_pre, 0, 0)
         grad_neigh = grad_neigh + dot(agg_ref[:, share_cols], grad_pre, 0, 0)
-    grad_agg_copy = started(grad_agg_ref, grad_agg_hbm, sems.at[at])
+    grad_agg_copy = started(grad_agg_ref, grad_agg_hbm, sems.at[0])
     tile = 0
     per_peer = (joint_ref.shape[1] - feat_width) // LANES
     for part in (grad_self, grad_neigh):
@@ -277,9 +272,8 @@
     joint_copies = []
     for n, i in enumerate(starts):
         rows = pl.ds(i, step)
-        halo_copies[n].wait()
         joint_ref[rows, :feat_width] = dot(halo_t_ref[rows, :], grad_agg_ref[...], 1, 0).astype(BF16)
-        joint_copies.append(started(joint_ref.at[rows, :], joint_hbm.at[rows, :], sems.at[at + 1 + n]))
+        joint_copies.append(started(joint_ref.at[rows, :], joint_hbm.at[rows, :], sems.at[1 + n]))
     grad_agg_copy.wait()
     for copy in joint_copies:
         copy.wait()
@@ -449,7 +443,7 @@
     aggs = from_ahead(own_agg, replicas)
     joint_width = feat_width + 2 * share * feat_width // halo_rows
     halo_steps = max(1, halo_rows // 256)
-    out_feats, own_base, own_grad_agg, own_weights, feats_ahead, grads_ahead = call(
+    out_feats, own_base, own_grad_agg, own_weights, feats_ahead, grads_ahead, halo_ahead = call(
         functools.partial(own_kernel, replicas),
         "dense_own",
         [
@@ -459,15 +453,16 @@
             shape(2 * share, feat_width, F32),
             shape(node_rows - quarter, feat_width, BF16),
             shape(node_rows - quarter, feat_width, BF16),
-        ],
-        [SMEM, VMEM, VMEM, HBM, HBM, HBM, HBM, VMEM, VMEM, VMEM],
-        (rep_ref, own_agg, *grad_outs, node_feats, w_self, w_neigh, scale),
+            shape(halo_rows, node_rows, BF16),
+        ],
+        [SMEM, VMEM, VMEM, HBM, HBM, HBM, HBM, VMEM, VMEM, VMEM, HBM],
+        (rep_ref, own_agg, *grad_outs, node_feats, w_self, w_neigh, scale, halo_t),
         block_flops // 2,
-        out_specs=[VMEM, HBM, VMEM, VMEM, VMEM, VMEM],
+        out_specs=[VMEM, HBM, VMEM, VMEM, VMEM, VMEM, VMEM],
         scratch=[
             pltpu.VMEM((quarter, feat_width), BF16),
             pltpu.VMEM((quarter, feat_width), F32),
-            pltpu.SemaphoreType.DMA((2 * replicas,)),
+            pltpu.SemaphoreType.DMA((2 * replicas + 1,)),
         ],
     )
     far_grad_agg, far_weights = call(
@@ -482,18 +477,17 @@
         functools.partial(dense_kernel, replicas),
         "dense_rest",
         [shape(node_rows, feat_width, BF16), shape(halo_rows, joint_width, BF16)],
-        [SMEM] + [VMEM] * 7 + [HBM] + [VMEM] * 3,
+        [SMEM] + [VMEM] * 11,
         (
-            rep_ref, aggs[0], aggs[2], grads_ahead, feats_ahead, w_self, w_neigh, scale, halo_t,
+            rep_ref, aggs[0], aggs[2], grads_ahead, feats_ahead, w_self, w_neigh, scale, halo_ahead,
             own_grad_agg, far_grad_agg, far_weights,
         ),
         2 * block_flops,
         out_specs=[HBM, HBM],
         scratch=[
-            pltpu.VMEM((halo_rows, node_rows), BF16),
             pltpu.VMEM((node_rows, feat_width), BF16),
             pltpu.VMEM((halo_rows, joint_width), BF16),
-            pltpu.SemaphoreType.DMA((1 + 2 * halo_steps,)),
+            pltpu.SemaphoreType.DMA((1 + halo_steps,)),
         ],
     )
     returned = lax.all_to_all(joint, WIDE, 0, 0, tiled=True)

time: 179 us -> 181 us (1.011)
  waiting for transfers between devices: 53.4 us -> 60.6 us
  starting transfers between devices: 88.7 us -> 83.8 us
    ppermute x15, starting transfers between devices: 55.2 us -> 48.1 us  [send_to(): lax.ppermute(x, 'rep', [(i, (i + step) % replicas) for i in range(replica...]
    ppermute x15, waiting for transfers between devices: 10.7 us -> 16.8 us  [send_to(): lax.ppermute(x, 'rep', [(i, (i + step) % replicas) for i in range(replica...]
    all_to_all x1, waiting for transfers between devices: 1.47 us -> 4.1 us  [on_device(): tiles = lax.all_to_all(copies, WIDE, 0, 0, tiled=True)]
    all_to_all x1, starting transfers between devices: 7.49 us -> 9.64 us  [on_device(): returned = lax.all_to_all(joint, WIDE, 0, 0, tiled=True)]
  transfers between devices with their start and end apart: 18 -> 18, of which waited for: 6 -> 10; matrix products, arithmetic and copies ran while one was open for 1% -> 1% of each run, Pallas kernels for 12% -> 11%
where the time goes in v10:
time: 181 us; the launch traced here: 178 us
  starting transfers between devices  83.8 us (46%)
  waiting for transfers between devices  60.6 us (33%)
  Pallas kernels  31.6 us (17%)
    ppermute x15, starting transfers between devices, send_to(): lax.ppermute(x, 'rep', [(i, (i + step) % replicas) for i in range(replica...  48.1 us
    pallas_call x10, Pallas kernels, call(): pl.pallas_call(kernel, out_shape=outs, in_specs=in_specs, out_specs=out_s...  31.6 us
    all_to_all x1, waiting for transfers between devices, on_device(): returned = lax.all_to_all(joint, WIDE, 0, 0, tiled=True)  30.9 us
    all_to_all x1, starting transfers between devices, on_device(): incoming = lax.all_to_all(outgoing, WIDE, 0, 0, tiled=True)  18.4 us
    ppermute x15, waiting for transfers between devices, send_to(): lax.ppermute(x, 'rep', [(i, (i + step) % replicas) for i in range(replica...  16.8 us
    all_to_all x1, starting transfers between devices, on_device(): returned = lax.all_to_all(joint, WIDE, 0, 0, tiled=True)  9.64 us
    all_to_all x1, waiting for transfers between devices, on_device(): incoming = lax.all_to_all(outgoing, WIDE, 0, 0, tiled=True)  8.69 us
    all_to_all x1, starting transfers between devices, on_device(): tiles = lax.all_to_all(copies, WIDE, 0, 0, tiled=True)  7.61 us
  transfers between devices with their start and end apart: 18, of which 10 were waited for; matrix products, arithmetic and copies ran while one was open for 1% of the time, Pallas kernels for 11%

profile of v10, /device:TPU:1, one launch (start us, length us, event | category | flops | bytes accessed | tf_op | source)
XLA Modules:
  0.0 178.3 jit_solution(6450491669928143029)
XLA Ops:
  0.7 3.4 %gather_rows.1 = bf16[1024,512]{1,0:T(8,128)(2,1)} custom-call(s32[8,128]{1,0:T(8,128)} %bitcast.32, bf16[1024,512]{1,0:T(8,128)(2,1)} %feats_hbm.5), custom_call_target="tpu_custom_call" | custom-call | flops 1073741824 | bytes 2101248 | tf_op jit(solution)/shard_map/gather_rows/pallas_call | solution.py:40
  4.1 18.4 %all-to-all-start = ((bf16[128,8,512]{2,1,0:T(8,128)(2,1)}), bf16[128,8,512]{2,1,0:T(8,128)(2,1)S(1)}, u32[]{:S(2)}, u32[]{:S(2)}) async-start(bf16[128,8,512]{2,1,0:T(8,128)(2,1)} %bitcast.35), calls=%async_computation | async-start | bytes 2097152 | tf_op jit(solution)/shard_map/all_to_all | solution.py:395
  22.5 4.4 %collective-permute-start = (bf16[256,512]{1,0:T(8,128)(2,1)S(1)}, bf16[256,512]{1,0:T(8,128)(2,1)}, u32[]{:S(2)}, u32[]{:S(2)}) collective-permute-start(bf16[256,512]{1,0:T(8,128)(2,1)S(1)} %copy-done.2), channel_id=1, source_target_pairs={{0,3},{1,0},{2,1},{3,2},{4,7},{5,4},{6,5},{7,6},{8,11},{9,8},{10,9... | collective-permute-start | bytes 786440 | tf_op jit(solution)/shard_map/ppermute | solution.py:353
  26.9 2.4 %collective-permute-start.1 = (bf16[256,512]{1,0:T(8,128)(2,1)S(1)}, bf16[256,512]{1,0:T(8,128)(2,1)}, u32[]{:S(2)}, u32[]{:S(2)}) collective-permute-start(bf16[256,512]{1,0:T(8,128)(2,1)S(1)} %copy-done.2), channel_id=1, source_target_pairs={{0,2},{1,3},{2,0},{3,1},{4,6},{5,7},{6,4},{7,5},{8,10},{9,11},{10,... | collective-permute-start | bytes 786440 | tf_op jit(solution)/shard_map/ppermute | solution.py:353
  29.3 2.5 %collective-permute-start.2 = (bf16[256,512]{1,0:T(8,128)(2,1)S(1)}, bf16[256,512]{1,0:T(8,128)(2,1)}, u32[]{:S(2)}, u32[]{:S(2)}) collective-permute-start(bf16[256,512]{1,0:T(8,128)(2,1)S(1)} %copy-done.2), channel_id=1, source_target_pairs={{0,1},{1,2},{2,3},{3,0},{4,5},{5,6},{6,7},{7,4},{8,9},{9,10},{10,1... | collective-permute-start | bytes 786440 | tf_op jit(solution)/shard_map/ppermute | solution.py:353
  31.9 10.0 %tile_counts.1 = (bf16[1024,1024]{1,0:T(8,128)(2,1)}, bf16[1024,1024]{1,0:T(8,128)(2,1)S(1)}, bf16[1024,1024]{1,0:T(8,128)(2,1)}, f32[1024,512]{1,0:T(8,128)}) custom-call(s32[1]{0:T(128)} %bitcast.rep_ref, s32[128]{0:T(128)S(1)} %fusion.2.place_ref, s32[256,128]{1,0:T(8,128)S(1)} %bitcast.31, bf16[1024,512]{1,0:T(8,128)(2,1)} %feats_hbm.5), custom_call_target="tpu_custom_call" | custom-call | flops 1094713344 | bytes 9568772 | tf_op jit(solution)/shard_map/tile_counts/pallas_call | solution.py:40
  44.3 8.7 %all-to-all-done = bf16[128,8,512]{2,1,0:T(8,128)(2,1)S(1)} async-done(((bf16[128,8,512]{2,1,0:T(8,128)(2,1)}), bf16[128,8,512]{2,1,0:T(8,128)(2,1)S(1)}, u32[]{:S(2)}, u32[]{:S(2)}) %all-to-all-start) | async-done | bytes 1048608 | tf_op jit(solution)/shard_map/all_to_all | solution.py:395
  52.9 2.6 %neighbour_sums.1 = (f32[256,512]{1,0:T(8,128)S(1)}, bf16[256,512]{1,0:T(8,128)(2,1)S(1)}, bf16[256,512]{1,0:T(8,128)(2,1)S(1)}, bf16[256,512]{1,0:T(8,128)(2,1)S(1)}) custom-call(bf16[1024,1024]{1,0:T(8,128)(2,1)S(1)} %get-tuple-element.41.counts_ref, bf16[1024,512]{1,0:T(8,128)(2,1)S(1)} %bitcast.26, f32[1024,512]{1,0:T(8,128)} %get-tuple-element.43.local_hbm), custom_call_target="tpu_custom_call" | custom-call | flops 1073741824 | bytes 6553600 | tf_op jit(solution)/shard_map/neighbour_sums/pallas_call | solution.py:40
  55.5 4.8 %collective-permute-start.3 = (bf16[256,512]{1,0:T(8,128)(2,1)S(1)}, bf16[256,512]{1,0:T(8,128)(2,1)S(1)}, u32[]{:S(2)}, u32[]{:S(2)}) collective-permute-start(bf16[256,512]{1,0:T(8,128)(2,1)S(1)} %get-tuple-element.45), channel_id=1, source_target_pairs={{0,2},{1,3},{2,0},{3,1},{4,6},{5,7},{6,4},{7,5},{8,10},{9,11},{10,... | collective-permute-start | bytes 786440 | tf_op jit(solution)/shard_map/ppermute | solution.py:353
  62.5 4.3 %collective-permute-start.5 = (bf16[256,512]{1,0:T(8,128)(2,1)S(1)}, bf16[256,512]{1,0:T(8,128)(2,1)S(1)}, u32[]{:S(2)}, u32[]{:S(2)}) collective-permute-start(bf16[256,512]{1,0:T(8,128)(2,1)S(1)} %get-tuple-element.47), channel_id=1, source_target_pairs={{0,3},{1,0},{2,1},{3,2},{4,7},{5,4},{6,5},{7,6},{8,11},{9,8},{10,9... | collective-permute-start | bytes 786440 | tf_op jit(solution)/shard_map/ppermute | solution.py:353
  66.8 5.4 %collective-permute-done.4 = bf16[256,512]{1,0:T(8,128)(2,1)S(1)} collective-permute-done((bf16[256,512]{1,0:T(8,128)(2,1)S(1)}, bf16[256,512]{1,0:T(8,128)(2,1)S(1)}, u32[]{:S(2)}, u32[]{:S(2)}) %collective-permute-start.4) | collective-permute-done | bytes 262176 | tf_op jit(solution)/shard_map/ppermute | solution.py:353
  72.3 5.4 %collective-permute-start.8 = (bf16[256,512]{1,0:T(8,128)(2,1)S(1)}, bf16[256,512]{1,0:T(8,128)(2,1)S(1)}, u32[]{:S(2)}, u32[]{:S(2)}) collective-permute-start(bf16[256,512]{1,0:T(8,128)(2,1)S(1)} %multiply_convert_fusion.agg_ref), channel_id=1, source_target_pairs={{0,2},{1,3},{2,0},{3,1},{4,6},{5,7},{6,4},{7,5},{8,10},{9,11},{10,... | collective-permute-start | bytes 786440 | tf_op jit(solution)/shard_map/ppermute | solution.py:353
  79.9 3.1 %collective-permute-start.7 = (bf16[256,512]{1,0:T(8,128)(2,1)S(1)}, bf16[256,512]{1,0:T(8,128)(2,1)S(1)}, u32[]{:S(2)}, u32[]{:S(2)}) collective-permute-start(bf16[256,512]{1,0:T(8,128)(2,1)S(1)} %multiply_convert_fusion.agg_ref), channel_id=1, source_target_pairs={{0,1},{1,2},{2,3},{3,0},{4,5},{5,6},{6,7},{7,4},{8,9},{9,10},{10,1... | collective-permute-start | bytes 786440 | tf_op jit(solution)/shard_map/ppermute | solution.py:353
  83.2 3.4 %dense_own.1 = (bf16[256,512]{1,0:T(8,128)(2,1)}, f32[256,512]{1,0:T(8,128)}, bf16[256,512]{1,0:T(8,128)(2,1)S(1)}, f32[256,512]{1,0:T(8,128)S(1)}, bf16[768,512...) custom-call(s32[1]{0:T(128)} %bitcast.rep_ref, ...), custom_call_target="tpu_custom_call" | custom-call | flops 536870912 | bytes 10752004 | tf_op jit(solution)/shard_map/dense_own/pallas_call | solution.py:40
  89.0 3.3 %dense_rest.1 = (bf16[1024,512]{1,0:T(8,128)(2,1)}, bf16[1024,640]{1,0:T(8,128)(2,1)}) custom-call(s32[1]{0:T(128)} %bitcast.rep_ref, bf16[256,512]{1,0:T(8,128)(2,1)S(1)} %collective-permute-done.6.agg1, bf16[256,512]{1,0:T(8,128)(2,1)S(1)} %collective-permute-done.7.agg3, bf16[768,512]{1,0:T(8,128)(2,1)S(1)} %get-tuple-element.55.grads_ref, ...), custom_call_target="tpu_custom_call" | custom-call | flops 2147483648 | bytes 8654852 | tf_op jit(solution)/shard_map/dense_rest/pallas_call | solution.py:40
  92.3 9.6 %all-to-all-start.1 = ((bf16[128,8,640]{2,1,0:T(8,128)(2,1)}), bf16[128,8,640]{2,1,0:T(8,128)(2,1)S(1)}, u32[]{:S(2)}, u32[]{:S(2)}) async-start(bf16[128,8,640]{2,1,0:T(8,128)(2,1)} %bitcast.34), calls=%async_computation.1 | async-start | bytes 2621440 | tf_op jit(solution)/shard_map/all_to_all | solution.py:493
  101.9 4.6 %local_rows.1.local_hbm = f32[1024,512]{1,0:T(8,128)} custom-call(bf16[1024,1024]{1,0:T(8,128)(2,1)} %get-tuple-element.63.counts_hbm, bf16[1024,512]{1,0:T(8,128)(2,1)} %get-tuple-element.64.grad_hbm, f32[256,512]{1,0:T(8,128)} %get-tuple-element.65.base_hbm), custom_call_target="tpu_custom_call" | custom-call | flops 1073741824 | bytes 5767168 | tf_op jit(solution)/shard_map/local_rows/pallas_call | solution.py:40
  106.6 30.9 %all-to-all-done.1 = bf16[128,8,640]{2,1,0:T(8,128)(2,1)S(1)} async-done(((bf16[128,8,640]{2,1,0:T(8,128)(2,1)}), bf16[128,8,640]{2,1,0:T(8,128)(2,1)S(1)}, u32[]{:S(2)}, u32[]{:S(2)}) %all-to-all-start.1) | async-done | bytes 1310752 | tf_op jit(solution)/shard_map/all_to_all | solution.py:493
  138.4 7.6 %all-to-all-start.2 = ((bf16[128,8,128]{2,1,0:T(8,128)(2,1)}), bf16[128,8,128]{2,1,0:T(8,128)(2,1)S(1)}, u32[]{:S(2)}, u32[]{:S(2)}) async-start(bf16[128,8,128]{2,1,0:T(8,128)(2,1)} %bitcast.36), calls=%async_computation.2 | async-start | bytes 524288 | tf_op jit(solution)/shard_map/all_to_all | solution.py:536
  149.6 4.6 %collective-permute-start.11 = (bf16[256,512]{1,0:T(8,128)(2,1)S(1)}, bf16[256,512]{1,0:T(8,128)(2,1)S(1)}, u32[]{:S(2)}, u32[]{:S(2)}) collective-permute-start(bf16[256,512]{1,0:T(8,128)(2,1)S(1)} %get-tuple-element.71), channel_id=1, source_target_pairs={{0,3},{1,0},{2,1},{3,2},{4,7},{5,4},{6,5},{7,6},{8,11},{9,8},{10,9... | collective-permute-start | bytes 786440 | tf_op jit(solution)/shard_map/ppermute | solution.py:353
  156.1 4.1 %all-to-all-done.2 = bf16[128,8,128]{2,1,0:T(8,128)(2,1)S(1)} async-done(((bf16[128,8,128]{2,1,0:T(8,128)(2,1)}), bf16[128,8,128]{2,1,0:T(8,128)(2,1)S(1)}, u32[]{:S(2)}, u32[]{:S(2)}) %all-to-all-start.2) | async-done | bytes 262176 | tf_op jit(solution)/shard_map/all_to_all | solution.py:536
  160.2 2.9 %collective-permute-start.12 = (bf16[256,512]{1,0:T(8,128)(2,1)S(1)}, bf16[256,512]{1,0:T(8,128)(2,1)S(1)}, u32[]{:S(2)}, u32[]{:S(2)}) collective-permute-start(bf16[256,512]{1,0:T(8,128)(2,1)S(1)} %bitcast.27), channel_id=1, source_target_pairs={{0,3},{1,0},{2,1},{3,2},{4,7},{5,4},{6,5},{7,6},{8,11},{9,8},{10,9... | collective-permute-start | bytes 786440 | tf_op jit(solution)/shard_map/ppermute | solution.py:353
  165.5 3.2 %collective-permute-start.14 = (bf16[256,512]{1,0:T(8,128)(2,1)S(1)}, bf16[256,512]{1,0:T(8,128)(2,1)S(1)}, u32[]{:S(2)}, u32[]{:S(2)}) collective-permute-start(bf16[256,512]{1,0:T(8,128)(2,1)S(1)} %bitcast.29), channel_id=1, source_target_pairs={{0,2},{1,3},{2,0},{3,1},{4,6},{5,7},{6,4},{7,5},{8,10},{9,11},{10,... | collective-permute-start | bytes 786440 | tf_op jit(solution)/shard_map/ppermute | solution.py:353
  172.2 5.1 %collective-permute-done.14.part2 = bf16[256,512]{1,0:T(8,128)(2,1)S(1)} collective-permute-done((bf16[256,512]{1,0:T(8,128)(2,1)S(1)}, bf16[256,512]{1,0:T(8,128)(2,1)S(1)}, u32[]{:S(2)}, u32[]{:S(2)}) %collective-permute-start.14) | collective-permute-done | bytes 262176 | tf_op jit(solution)/shard_map/ppermute | solution.py:353
  (45 shorter events, 22.7 us)
Async XLA Ops:
  0.6 31.2 %copy-start.5 = (s32[1024]{0:T(1024)S(1)}, s32[1024]{0:T(1024)}, u32[]{:S(2)}) copy-start(s32[1024]{0:T(1024)} %param.16) | copy-start | bytes 12292
  0.7 31.2 %copy-start.6 = (s32[1,1,128]{2,1,0:T(1,128)S(1)}, s32[1,1,128]{2,1,0:T(1,128)}, u32[]{:S(2)}) copy-start(s32[1,1,128]{2,1,0:T(1,128)} %param.14) | copy-start | bytes 1540
  0.7 31.2 %copy-start.7 = (s32[1,1,128]{2,1,0:T(1,128)S(1)}, s32[1,1,128]{2,1,0:T(1,128)}, u32[]{:S(2)}) copy-start(s32[1,1,128]{2,1,0:T(1,128)} %param.13) | copy-start | bytes 1540
  0.7 31.3 %copy-start.3 = (s32[1,1,32768]{2,1,0:T(1,128)S(1)}, s32[1,1,32768]{2,1,0:T(1,128)}, u32[]{:S(2)}) copy-start(s32[1,1,32768]{2,1,0:T(1,128)} %param.15) | copy-start | bytes 393220
  4.1 48.9 %all-to-all-start = ((bf16[128,8,512]{2,1,0:T(8,128)(2,1)}), bf16[128,8,512]{2,1,0:T(8,128)(2,1)S(1)}, u32[]{:S(2)}, u32[]{:S(2)}) async-start(bf16[128,8,512]{2,1,0:T(8,128)(2,1)} %bitcast.35), calls=%async_computation | async-start | bytes 2097152 | tf_op jit(solution)/shard_map/all_to_all | solution.py:395
  22.5 19.6 %collective-permute-start = (bf16[256,512]{1,0:T(8,128)(2,1)S(1)}, bf16[256,512]{1,0:T(8,128)(2,1)}, u32[]{:S(2)}, u32[]{:S(2)}) collective-permute-start(bf16[256,512]{1,0:T(8,128)(2,1)S(1)} %copy-done.2), channel_id=1, source_target_pairs={{0,3},{1,0},{2,1},{3,2},{4,7},{5,4},{6,5},{7,6},{8,11},{9,8},{10,9... | collective-permute-start | bytes 786440 | tf_op jit(solution)/shard_map/ppermute | solution.py:353
  26.9 15.2 %collective-permute-start.1 = (bf16[256,512]{1,0:T(8,128)(2,1)S(1)}, bf16[256,512]{1,0:T(8,128)(2,1)}, u32[]{:S(2)}, u32[]{:S(2)}) collective-permute-start(bf16[256,512]{1,0:T(8,128)(2,1)S(1)} %copy-done.2), channel_id=1, source_target_pairs={{0,2},{1,3},{2,0},{3,1},{4,6},{5,7},{6,4},{7,5},{8,10},{9,11},{10,... | collective-permute-start | bytes 786440 | tf_op jit(solution)/shard_map/ppermute | solution.py:353
  29.3 14.9 %collective-permute-start.2 = (bf16[256,512]{1,0:T(8,128)(2,1)S(1)}, bf16[256,512]{1,0:T(8,128)(2,1)}, u32[]{:S(2)}, u32[]{:S(2)}) collective-permute-start(bf16[256,512]{1,0:T(8,128)(2,1)S(1)} %copy-done.2), channel_id=1, source_target_pairs={{0,1},{1,2},{2,3},{3,0},{4,5},{5,6},{6,7},{7,4},{8,9},{9,10},{10,1... | collective-permute-start | bytes 786440 | tf_op jit(solution)/shard_map/ppermute | solution.py:353
  55.5 27.7 %copy-start = (bf16[512,512]{1,0:T(8,128)(2,1)S(1)}, bf16[512,512]{1,0:T(8,128)(2,1)}, u32[]{:S(2)}) copy-start(bf16[512,512]{1,0:T(8,128)(2,1)} %w_self_ref.5) | copy-start | bytes 1572868
  55.5 11.3 %collective-permute-start.3 = (bf16[256,512]{1,0:T(8,128)(2,1)S(1)}, bf16[256,512]{1,0:T(8,128)(2,1)S(1)}, u32[]{:S(2)}, u32[]{:S(2)}) collective-permute-start(bf16[256,512]{1,0:T(8,128)(2,1)S(1)} %get-tuple-element.45), channel_id=1, source_target_pairs={{0,2},{1,3},{2,0},{3,1},{4,6},{5,7},{6,4},{7,5},{8,10},{9,11},{10,... | collective-permute-start | bytes 786440 | tf_op jit(solution)/shard_map/ppermute | solution.py:353
  60.3 11.9 %collective-permute-start.4 = (bf16[256,512]{1,0:T(8,128)(2,1)S(1)}, bf16[256,512]{1,0:T(8,128)(2,1)S(1)}, u32[]{:S(2)}, u32[]{:S(2)}) collective-permute-start(bf16[256,512]{1,0:T(8,128)(2,1)S(1)} %get-tuple-element.46), channel_id=1, source_target_pairs={{0,1},{1,2},{2,3},{3,0},{4,5},{5,6},{6,7},{7,4},{8,9},{9,10},{10,1... | collective-permute-start | bytes 786440 | tf_op jit(solution)/shard_map/ppermute | solution.py:353
  62.5 9.7 %collective-permute-start.5 = (bf16[256,512]{1,0:T(8,128)(2,1)S(1)}, bf16[256,512]{1,0:T(8,128)(2,1)S(1)}, u32[]{:S(2)}, u32[]{:S(2)}) collective-permute-start(bf16[256,512]{1,0:T(8,128)(2,1)S(1)} %get-tuple-element.47), channel_id=1, source_target_pairs={{0,3},{1,0},{2,1},{3,2},{4,7},{5,4},{6,5},{7,6},{8,11},{9,8},{10,9... | collective-permute-start | bytes 786440 | tf_op jit(solution)/shard_map/ppermute | solution.py:353
  72.3 14.3 %collective-permute-start.8 = (bf16[256,512]{1,0:T(8,128)(2,1)S(1)}, bf16[256,512]{1,0:T(8,128)(2,1)S(1)}, u32[]{:S(2)}, u32[]{:S(2)}) collective-permute-start(bf16[256,512]{1,0:T(8,128)(2,1)S(1)} %multiply_convert_fusion.agg_ref), channel_id=1, source_target_pairs={{0,2},{1,3},{2,0},{3,1},{4,6},{5,7},{6,4},{7,5},{8,10},{9,11},{10,... | collective-permute-start | bytes 786440 | tf_op jit(solution)/shard_map/ppermute | solution.py:353
  77.7 10.3 %collective-permute-start.6 = (bf16[256,512]{1,0:T(8,128)(2,1)S(1)}, bf16[256,512]{1,0:T(8,128)(2,1)S(1)}, u32[]{:S(2)}, u32[]{:S(2)}) collective-permute-start(bf16[256,512]{1,0:T(8,128)(2,1)S(1)} %multiply_convert_fusion.agg_ref), channel_id=1, source_target_pairs={{0,3},{1,0},{2,1},{3,2},{4,7},{5,4},{6,5},{7,6},{8,11},{9,8},{10,9... | collective-permute-start | bytes 786440 | tf_op jit(solution)/shard_map/ppermute | solution.py:353
  79.9 9.2 %collective-permute-start.7 = (bf16[256,512]{1,0:T(8,128)(2,1)S(1)}, bf16[256,512]{1,0:T(8,128)(2,1)S(1)}, u32[]{:S(2)}, u32[]{:S(2)}) collective-permute-start(bf16[256,512]{1,0:T(8,128)(2,1)S(1)} %multiply_convert_fusion.agg_ref), channel_id=1, source_target_pairs={{0,1},{1,2},{2,3},{3,0},{4,5},{5,6},{6,7},{7,4},{8,9},{9,10},{10,1... | collective-permute-start | bytes 786440 | tf_op jit(solution)/shard_map/ppermute | solution.py:353
  92.3 45.2 %all-to-all-start.1 = ((bf16[128,8,640]{2,1,0:T(8,128)(2,1)}), bf16[128,8,640]{2,1,0:T(8,128)(2,1)S(1)}, u32[]{:S(2)}, u32[]{:S(2)}) async-start(bf16[128,8,640]{2,1,0:T(8,128)(2,1)} %bitcast.34), calls=%async_computation.1 | async-start | bytes 2621440 | tf_op jit(solution)/shard_map/all_to_all | solution.py:493
  106.6 39.4 %copy-start.4 = (s32[1,128,8]{1,2,0:T(8,128)S(1)}, s32[1,128,8]{1,2,0:T(8,128)}, u32[]{:S(2)}) copy-start(s32[1,128,8]{1,2,0:T(8,128)} %param.12) | copy-start | bytes 12292
  138.4 21.8 %all-to-all-start.2 = ((bf16[128,8,128]{2,1,0:T(8,128)(2,1)}), bf16[128,8,128]{2,1,0:T(8,128)(2,1)S(1)}, u32[]{:S(2)}, u32[]{:S(2)}) async-start(bf16[128,8,128]{2,1,0:T(8,128)(2,1)} %bitcast.36), calls=%async_computation.2 | async-start | bytes 524288 | tf_op jit(solution)/shard_map/all_to_all | solution.py:536
  147.7 17.9 %collective-permute-start.10 = (bf16[256,512]{1,0:T(8,128)(2,1)S(1)}, bf16[256,512]{1,0:T(8,128)(2,1)S(1)}, u32[]{:S(2)}, u32[]{:S(2)}) collective-permute-start(bf16[256,512]{1,0:T(8,128)(2,1)S(1)} %get-tuple-element.70), channel_id=1, source_target_pairs={{0,1},{1,2},{2,3},{3,0},{4,5},{5,6},{6,7},{7,4},{8,9},{9,10},{10,1... | collective-permute-start | bytes 786440 | tf_op jit(solution)/shard_map/ppermute | solution.py:353
  149.6 19.1 %collective-permute-start.11 = (bf16[256,512]{1,0:T(8,128)(2,1)S(1)}, bf16[256,512]{1,0:T(8,128)(2,1)S(1)}, u32[]{:S(2)}, u32[]{:S(2)}) collective-permute-start(bf16[256,512]{1,0:T(8,128)(2,1)S(1)} %get-tuple-element.71), channel_id=1, source_target_pairs={{0,3},{1,0},{2,1},{3,2},{4,7},{5,4},{6,5},{7,6},{8,11},{9,8},{10,9... | collective-permute-start | bytes 786440 | tf_op jit(solution)/shard_map/ppermute | solution.py:353
  154.2 14.5 %collective-permute-start.9 = (bf16[256,512]{1,0:T(8,128)(2,1)S(1)}, bf16[256,512]{1,0:T(8,128)(2,1)S(1)}, u32[]{:S(2)}, u32[]{:S(2)}) collective-permute-start(bf16[256,512]{1,0:T(8,128)(2,1)S(1)} %get-tuple-element.69), channel_id=1, source_target_pairs={{0,2},{1,3},{2,0},{3,1},{4,6},{5,7},{6,4},{7,5},{8,10},{9,11},{10,... | collective-permute-start | bytes 786440 | tf_op jit(solution)/shard_map/ppermute | solution.py:353
  160.2 10.0 %collective-permute-start.12 = (bf16[256,512]{1,0:T(8,128)(2,1)S(1)}, bf16[256,512]{1,0:T(8,128)(2,1)S(1)}, u32[]{:S(2)}, u32[]{:S(2)}) collective-permute-start(bf16[256,512]{1,0:T(8,128)(2,1)S(1)} %bitcast.27), channel_id=1, source_target_pairs={{0,3},{1,0},{2,1},{3,2},{4,7},{5,4},{6,5},{7,6},{8,11},{9,8},{10,9... | collective-permute-start | bytes 786440 | tf_op jit(solution)/shard_map/ppermute | solution.py:353
  163.1 9.1 %collective-permute-start.13 = (bf16[256,512]{1,0:T(8,128)(2,1)S(1)}, bf16[256,512]{1,0:T(8,128)(2,1)S(1)}, u32[]{:S(2)}, u32[]{:S(2)}) collective-permute-start(bf16[256,512]{1,0:T(8,128)(2,1)S(1)} %bitcast.28), channel_id=1, source_target_pairs={{0,1},{1,2},{2,3},{3,0},{4,5},{5,6},{6,7},{7,4},{8,9},{9,10},{10,1... | collective-permute-start | bytes 786440 | tf_op jit(solution)/shard_map/ppermute | solution.py:353
  165.5 11.8 %collective-permute-start.14 = (bf16[256,512]{1,0:T(8,128)(2,1)S(1)}, bf16[256,512]{1,0:T(8,128)(2,1)S(1)}, u32[]{:S(2)}, u32[]{:S(2)}) collective-permute-start(bf16[256,512]{1,0:T(8,128)(2,1)S(1)} %bitcast.29), channel_id=1, source_target_pairs={{0,2},{1,3},{2,0},{3,1},{4,6},{5,7},{6,4},{7,5},{8,10},{9,11},{10,... | collective-permute-start | bytes 786440 | tf_op jit(solution)/shard_map/ppermute | solution.py:353
  (2 other events, 49.6 us)
